TPU v7x, 128 devices: a whole 4x4x4 slice. The times are simulated.
128 devices in a mesh: depth: 32 (over x, z_hi, y), filt: 4 (over z_lo, core).
Axes of the slice: x: 4, y: 4, z: 4 (z_hi: 2, z_lo: 2; z = z_hi * 2 + z_lo), core: 2. Of those that a mesh axis runs over, the one named last changes fastest.
Arguments:
- upper_level: bfloat16 [64, 128, 16, 256], P(None, 'depth', 'filt'), may hold values from -6 to 6
- stride_weight: bfloat16 [8, 128, 64], P(None, 'filt'), may hold values from -0.25 to 0.25
- middle_weight: bfloat16 [27, 128, 128], P(None, 'filt'), may hold values from -0.109375 to 0.109375
- last_weight: bfloat16 [27, 128, 128], P(None, 'filt'), may hold values from -0.109375 to 0.109375
- cotangent: bfloat16 [128, 64, 8, 128], P('filt', 'depth'), may hold values from -0.0234375 to 0.0234375
Outputs:
- result: bfloat16 [128, 64, 8, 128], P('filt', 'depth')
- grad_stride: float32 [8, 128, 64], P(None, 'filt')
- grad_middle: float32 [27, 128, 128], P(None, 'filt')
- grad_last: float32 [27, 128, 128], P(None, 'filt')
All inputs are finite; a program needn't handle non-finite values.
Results may differ from a plain program's by a relative error of at most 0.0059.
Values may be sent and summed in bfloat16 or wider, within the bound.
No kernel may reach another device: no remote copies, remote signals or barrier semaphores. Data moves between devices by JAX's collectives and lax.ppermute only.
A program may use at most 64 MiB of HBM per device.

v0:
```python
import functools

import jax
import jax.numpy as jnp
from jax import lax
from jax.experimental import pallas as pl
from jax.experimental.pallas import tpu as pltpu
from jax.sharding import PartitionSpec as P

AXES = ("depth", "filt")
CELLS = 128
VMEM = pl.BlockSpec(memory_space=pltpu.VMEM)
SMEM = pl.BlockSpec(memory_space=pltpu.SMEM)
TAPS = [(a, b) for a in range(3) for b in range(3)]


def silu_slope(value):
    sigma = jax.nn.sigmoid(value)
    return sigma * (1.0 + value * (1.0 - sigma))


def pairs_of(move):
    depth, filt = lax.axis_size("depth"), lax.axis_size("filt")
    found = []
    for d in range(depth):
        for f in range(filt):
            e, g = move(d, f)
            if 0 <= e < depth and 0 <= g < filt:
                found.append((d * filt + f, e * filt + g))
    return found


def shifted(value, move):
    return lax.ppermute(value, AXES, pairs_of(move))


def swap_core(value):
    return shifted(value, lambda d, f: (d, f ^ 1))


def swap_chip(value):
    return shifted(value, lambda d, f: (d, f ^ 2))


def swap_chip_across(value):
    return shifted(value, lambda d, f: (d ^ 4, f ^ 2))


def four_parts(value, swap):
    far = swap(value)
    return [value, swap_core(value), far, swap_core(far)]


def call(body, out_shape, scratch=(), flops=0, moved=0, in_specs=None):
    many = isinstance(out_shape, (list, tuple))
    return pl.pallas_call(
        body,
        out_shape=out_shape,
        in_specs=in_specs,
        out_specs=[VMEM] * len(out_shape) if many else VMEM,
        scratch_shapes=list(scratch),
        cost_estimate=pl.CostEstimate(flops=flops, bytes_accessed=moved, transcendentals=0),
    )


def shape(dims, dtype=jnp.bfloat16):
    return jax.ShapeDtypeStruct(dims, dtype)


def dot(left, right):
    return jnp.dot(left, right, preferred_element_type=jnp.float32)


def dot_rows(left, right):
    return lax.dot_general(
        left, right, (((1,), (1,)), ((), ())), preferred_element_type=jnp.float32
    )


def stride_body(info, u_ref, s0, s1, s2, s3, act_ref, pre_ref, columns_ref, weights):
    filt = info[1]
    for j, part in enumerate((s0, s1, s2, s3)):
        start = pl.multiple_of((filt ^ j) * 32, 32)
        weights[pl.ds(start, 32), :] = part[...]
    source = lax.broadcasted_iota(jnp.int32, (256, 256), 0)
    target = lax.broadcasted_iota(jnp.int32, (256, 256), 1)
    pick = source == 2 * (target % 128) + target // 128
    pick = jnp.where(pick, 1.0, 0.0).astype(jnp.bfloat16)
    for p in range(2):
        for r in range(2):
            cell = 2 * p + r
            rows = []
            for a in range(2):
                for b in range(2):
                    split = dot(u_ref[2 * p + a, 2 * r + b], pick).astype(jnp.bfloat16)
                    rows += [split[:, :128], split[:, 128:]]
            block = jnp.concatenate(rows, axis=0)
            columns_ref[:, cell * 128 : cell * 128 + 128] = block
            pre = dot(weights[...], block).T
            pre_ref[p, r] = pre
            act_ref[p, r] = (pre * jax.nn.sigmoid(pre)).astype(jnp.bfloat16)


def turn_body(cot_ref, out_ref):
    for p in range(2):
        for r in range(2):
            block = jnp.concatenate([cot_ref[j, p, r] for j in range(4)], axis=0)
            out_ref[p, r] = block.astype(jnp.float32).T.astype(jnp.bfloat16)


def fill_window(window, left, middle, right):
    window[:, 0:2] = left[...]
    window[:, 2:4] = middle[...]
    window[:, 4:6] = right[...]


def fill_forward(weights, parts, filt):
    for j, part in enumerate(parts):
        start = (filt ^ j) * 32
        for n, (a, b) in enumerate(TAPS):
            for c in range(3):
                at = pl.multiple_of(start + c * 128, 32)
                weights[pl.ds(at, 32), n * 128 : n * 128 + 128] = part[9 * a + 3 * b + c]


def fill_backward(weights, parts, filt):
    for j, part in enumerate(parts):
        start = (filt ^ j) * 32
        for n, (a, b) in enumerate(TAPS):
            at = pl.multiple_of(start + n * 128, 32)
            for c in range(3):
                weights[pl.ds(at, 32), c * 128 : c * 128 + 128] = part[9 * a + 3 * b + c]


def column_of(size):
    return lax.broadcasted_iota(jnp.int32, (size, 1), 0) % CELLS


def from_before(value):
    size = value.shape[0]
    return jnp.where(column_of(size) == 0, 0.0, pltpu.roll(value, 1, 0))


def from_after(value):
    size = value.shape[0]
    return jnp.where(column_of(size) == CELLS - 1, 0.0, pltpu.roll(value, size - 1, 0))


def block_of(ref, p, planes, r, rows):
    return ref[pl.ds(p, planes), r : r + rows].reshape(planes * rows * CELLS, 128)


def conv_forward(ref, p, planes, r, rows, weights):
    wide = jnp.concatenate([block_of(ref, p + a, planes, r + b, rows) for a, b in TAPS], axis=1)
    out = dot_rows(wide, weights[...])
    return from_before(out[:, :128]) + out[:, 128:256] + from_after(out[:, 256:])


def conv_backward(ref, p, planes, r, rows, weights):
    wide = jnp.concatenate(
        [block_of(ref, p + 2 - a, planes, r + 2 - b, rows) for a, b in TAPS], axis=1
    )
    out = dot(wide, weights[...])
    return from_after(out[:, :128]) + out[:, 128:256] + from_before(out[:, 256:])


def inside(info, p):
    depth, filt = info[0], info[1]
    row = lax.broadcasted_iota(jnp.int32, (4 * CELLS, 1), 0) // CELLS
    bad = ((depth == 0) & (p == 0)) | ((depth == info[2] - 1) & (p == 3))
    low = jnp.where(filt == 0, 1, 0)
    high = jnp.where(filt == 3, 2, 3)
    low = jnp.where(bad, 4, low)
    return (row >= low) & (row <= high)


def middle_body(
    info, left, mid, right, m0, m1, m2, m3, l0, l1, l2, l3,
    act_ref, pre_ref, result_ref, window, weights_m, weights_l,
):
    filt = info[1]
    fill_window(window, left, mid, right)
    fill_forward(weights_m, (m0, m1, m2, m3), filt)
    fill_forward(weights_l, (l0, l1, l2, l3), filt)

    def plane(p, carry):
        pre = conv_forward(window, p, 1, 0, 4, weights_m)
        act = jnp.where(inside(info, p), pre * jax.nn.sigmoid(pre), 0.0)
        pre_ref[pl.ds(p, 1)] = pre.reshape(1, 4, CELLS, 128)
        act_ref[pl.ds(p, 1)] = act.astype(jnp.bfloat16).reshape(1, 4, CELLS, 128)
        return carry

    lax.fori_loop(0, 4, plane, 0)
    out = conv_forward(act_ref, 0, 2, 0, 2, weights_l)
    for p in range(2):
        for r in range(2):
            at = (2 * p + r) * CELLS
            block = out[at : at + CELLS].T.astype(jnp.bfloat16)
            for f in range(4):
                result_ref[f, p, r] = block[f * 32 : f * 32 + 32]


def shifts_of(value):
    lane = lax.broadcasted_iota(jnp.int32, value.shape, 1) % CELLS
    size = value.shape[1]
    after = jnp.where(lane == CELLS - 1, 0.0, pltpu.roll(value, size - 1, 1))
    before = jnp.where(lane == 0, 0.0, pltpu.roll(value, 1, 1))
    return jnp.concatenate([after, value, before], axis=0).astype(jnp.bfloat16)


def put_kernel_grad(grads_ref, first, grad):
    for n, (a, b) in enumerate(TAPS):
        for c in range(3):
            for f in range(4):
                at = c * 128 + f * 32
                piece = grad[at : at + 32, n * 128 : n * 128 + 128]
                grads_ref[f, first + 9 * a + 3 * b + c] = piece.astype(jnp.bfloat16)


def back_body(
    info, act_l, act_m, act_r, cot_l, cot_m, cot_r, m0, m1, m2, m3, l0, l1, l2, l3,
    mid_act, mid_pre, level_pre, columns, cot_own,
    grads_ref, window, act_window, weights_m, weights_l, delta,
):
    filt = info[1]
    fill_window(window, cot_l, cot_m, cot_r)
    fill_window(act_window, act_l, act_m, act_r)
    fill_backward(weights_l, (l0, l1, l2, l3), filt)
    fill_backward(weights_m, (m0, m1, m2, m3), filt)

    def plane(p, carry):
        back = conv_backward(window, p, 1, 0, 4, weights_l)
        pre = mid_pre[pl.ds(p, 1)].reshape(4 * CELLS, 128)
        here = jnp.where(inside(info, p), back * silu_slope(pre), 0.0)
        delta[pl.ds(p, 1)] = here.astype(jnp.bfloat16).reshape(1, 4, CELLS, 128)
        return carry

    lax.fori_loop(0, 4, plane, 0)

    own = [
        jnp.concatenate([cot_own[j, p, r] for j in range(4)], axis=0).astype(jnp.float32)
        for p in range(2)
        for r in range(2)
    ]
    cot_rows = shifts_of(jnp.concatenate(own, axis=1))
    wide = jnp.concatenate([block_of(mid_act, a, 2, b, 2) for a, b in TAPS], axis=1)
    put_kernel_grad(grads_ref, 0, dot(cot_rows, wide))

    own = [delta[1 + p, 1 + r].astype(jnp.float32).T for p in range(2) for r in range(2)]
    delta_rows = shifts_of(jnp.concatenate(own, axis=1))
    wide = jnp.concatenate([block_of(act_window, 1 + a, 2, 1 + b, 2) for a, b in TAPS], axis=1)
    put_kernel_grad(grads_ref, 27, dot(delta_rows, wide))

    back = conv_backward(delta, 0, 2, 0, 2, weights_m)
    pre = level_pre[...].reshape(4 * CELLS, 128)
    level_delta = (back * silu_slope(pre)).astype(jnp.bfloat16)
    grad = dot(columns[...], level_delta)
    for n in range(4):
        block = grad[n * 128 : n * 128 + 128].T.astype(jnp.bfloat16)
        for f in range(4):
            grads_ref[f, 54 + n] = block[f * 32 : f * 32 + 32]
    for n in range(58, 64):
        for f in range(4):
            grads_ref[f, n] = jnp.zeros((32, 128), jnp.bfloat16)


def neighbourhood(block):
    low = shifted(block, lambda d, f: (d + 1, f))
    high = shifted(block, lambda d, f: (d - 1, f))
    column = jnp.concatenate([low, block, high], axis=0)
    left = shifted(column, lambda d, f: (d, f + 1))
    right = shifted(column, lambda d, f: (d, f - 1))
    return left, column, right


def per_device(upper_level, stride_weight, middle_weight, last_weight, cotangent):
    depth = lax.axis_size("depth")
    info = jnp.stack([lax.axis_index("depth"), lax.axis_index("filt"), jnp.int32(depth)])
    stride_parts = four_parts(stride_weight.transpose(1, 0, 2).reshape(32, 512), swap_chip)
    middle_parts = four_parts(middle_weight, swap_chip)
    last_parts = four_parts(last_weight, swap_chip_across)

    cot_own = cotangent.reshape(32, 2, 4, 2, 128).transpose(2, 1, 3, 0, 4)
    cot_own = lax.all_to_all(cot_own, "filt", 0, 0, tiled=True)
    cot_cells = call(turn_body, shape((2, 2, 128, 128)), in_specs=[VMEM])(cot_own)
    cot_near = neighbourhood(cot_cells)

    upper = upper_level.transpose(1, 2, 0, 3)
    level_act, level_pre, columns = call(
        stride_body,
        [shape((2, 2, 128, 128)), shape((2, 2, 128, 128), jnp.float32), shape((512, 512))],
        [pltpu.VMEM((128, 512), jnp.bfloat16)],
        flops=200_000_000,
        moved=1_500_000,
        in_specs=[SMEM] + [VMEM] * 5,
    )(info, upper, *stride_parts)
    act_near = neighbourhood(level_act)

    mid_act, mid_pre, result = call(
        middle_body,
        [
            shape((4, 4, 128, 128)),
            shape((4, 4, 128, 128), jnp.float32),
            shape((4, 2, 2, 32, 128)),
        ],
        [
            pltpu.VMEM((6, 6, 128, 128), jnp.bfloat16),
            pltpu.VMEM((384, 1152), jnp.bfloat16),
            pltpu.VMEM((384, 1152), jnp.bfloat16),
        ],
        flops=3_000_000_000,
        moved=5_000_000,
        in_specs=[SMEM] + [VMEM] * 11,
    )(info, *act_near, *middle_parts, *last_parts)

    grads = call(
        back_body,
        shape((4, 64, 32, 128)),
        [
            pltpu.VMEM((6, 6, 128, 128), jnp.bfloat16),
            pltpu.VMEM((6, 6, 128, 128), jnp.bfloat16),
            pltpu.VMEM((1152, 384), jnp.bfloat16),
            pltpu.VMEM((1152, 384), jnp.bfloat16),
            pltpu.VMEM((4, 4, 128, 128), jnp.bfloat16),
        ],
        flops=4_000_000_000,
        moved=8_000_000,
        in_specs=[SMEM] + [VMEM] * 19,
    )(
        info, *act_near, *cot_near, *middle_parts, *last_parts,
        mid_act, mid_pre, level_pre, columns, cot_own,
    )

    result = lax.all_to_all(result, "filt", 0, 0, tiled=True)
    result = result.transpose(3, 1, 0, 2, 4).reshape(32, 2, 8, 128)

    terms = grads.reshape(4 * depth, 64, 128)
    terms = lax.all_to_all(terms, ("filt", "depth"), 0, 0, tiled=True)
    mine = jnp.sum(terms.astype(jnp.float32), axis=0).astype(jnp.bfloat16)
    spread = jnp.broadcast_to(mine[None], (depth, 64, 128))
    full = lax.all_to_all(spread, "depth", 0, 0, tiled=True)
    full = full.reshape(64, 32, 128).astype(jnp.float32)
    grad_stride = full[54:58].reshape(4, 32, 2, 64).transpose(0, 2, 1, 3).reshape(8, 32, 64)
    return (result, grad_stride, full[27:54], full[:27])


def solution(mesh):
    placed = (
        P(None, "depth", "filt", None),
        P(None, "filt", None),
        P(None, "filt", None),
        P(None, "filt", None),
        P("filt", "depth", None, None),
    )
    return jax.shard_map(
        per_device,
        mesh=mesh,
        in_specs=placed,
        out_specs=(
            P("filt", "depth", None, None),
            P(None, "filt", None),
            P(None, "filt", None),
            P(None, "filt", None),
        ),
        check_vma=False,
    )
```

profile of v0, /device:TPU:0, one launch (start us, length us, event | category | flops | bytes accessed | tf_op | source)
XLA Modules:
  0.0 144.7 jit_solution(4510760568569514034)
XLA Ops:
  0.6 0.0 copy-start.9
  0.7 0.0 copy-start.10
  0.7 0.9 copy.12
  1.6 0.1 reshape.28.s0
  1.7 0.0 copy-start.4
  1.7 2.1 %collective-permute-start.1 = (bf16[32,512]{1,0:T(8,128)(2,1)S(1)}, bf16[32,512]{1,0:T(8,128)(2,1)S(1)}, u32[]{:S(2)}, u32[]{:S(2)}) collective-permute-start(bf16[32,512]{1,0:T(8,128)(2,1)S(1)} %reshape.28.s0), channel_id=1, source_target_pairs={{0,2},{1,3},{2,0},{3,1},{4,6},{5,7},{6,4},{7,5},{8,10},{9,11},{10,... | collective-permute-start | bytes 98312 | tf_op jit(solution)/shard_map/ppermute | solution.py:34
  3.8 0.0 collective-permute-start
  3.8 1.9 %collective-permute-done.1.s2 = bf16[32,512]{1,0:T(8,128)(2,1)S(1)} collective-permute-done((bf16[32,512]{1,0:T(8,128)(2,1)S(1)}, bf16[32,512]{1,0:T(8,128)(2,1)S(1)}, u32[]{:S(2)}, u32[]{:S(2)}) %collective-permute-start.1) | collective-permute-done | bytes 32800 | tf_op jit(solution)/shard_map/ppermute | solution.py:34
  5.7 0.0 collective-permute-start.2
  5.7 0.6 pad_add_fusion.info
  6.4 2.0 %copy.21 = bf16[64,4,4,256]{3,0,2,1:T(8,128)(2,1)} copy(bf16[64,4,4,256]{3,2,1,0:T(4,128)(2,1)} %param.5) | data formatting | bytes 1048576 | tf_op args[0]
  8.4 0.0 collective-permute-done.s1
  8.4 0.0 collective-permute-done.2.s3
  8.4 0.6 copy-done.17
  9.0 3.1 %shard_map.84 = (bf16[2,2,128,128]{3,2,1,0:T(8,128)(2,1)}, f32[2,2,128,128]{3,2,1,0:T(8,128)}, bf16[512,512]{1,0:T(8,128)(2,1)}) custom-call(s32[3]{0:T(128)} %pad_add_fusion.info, bf16[4,4,64,256]{3,2,1,0:T(8,128)(2,1)} %bitcast.19, bf16[32,512]{1,0:T(8,128)(2,1)} %copy-done.4, bf16[32,512]{1,0:T(8,128)(2,1)} %copy-done.17, bf16[32,512]{1,0:T(8,128)(2,1)} %copy-done.16, ...), custom_call_target="tpu_custom_call" | custom-call | flops 200000000 | bytes 1500000 | tf_op jit(solution)/shard_map/pallas_call | solution.py:289
  12.1 3.6 %collective-permute-start.3 = (bf16[2,2,128,128]{3,2,1,0:T(8,128)(2,1)}, bf16[2,2,128,128]{3,2,1,0:T(8,128)(2,1)S(1)}, u32[]{:S(2)}, u32[]{:S(2)}) collective-permute-start(bf16[2,2,128,128]{3,2,1,0:T(8,128)(2,1)} %get-tuple-element.10), channel_id=1, source_target_pairs={{0,4},{1,5},{2,6},{3,7},{4,8},{5,9},{6,10},{7,11},{8,12},{9,13},{1... | collective-permute-start | bytes 393224 | tf_op jit(solution)/shard_map/ppermute | solution.py:34
  15.7 0.7 copy.22
  16.4 3.3 %all-to-all-start.1 = ((bf16[4,2,2,32,128]{4,3,2,1,0:T(8,128)(2,1)}), bf16[4,2,2,32,128]{4,3,2,1,0:T(8,128)(2,1)S(1)}, u32[]{:S(2)}, u32[]{:S(2)}) async-start(bf16[4,2,2,32,128]{4,3,2,1,0:T(8,128)(2,1)} %bitcast.15), calls=%async_computation.1 | async-start | bytes 262144 | tf_op jit(solution)/shard_map/all_to_all | solution.py:284
  19.7 0.5 collective-permute-start.7
  20.2 1.8 %collective-permute-start.8 = (bf16[27,32,128]{2,1,0:T(8,128)(2,1)S(1)}, bf16[27,32,128]{2,1,0:T(8,128)(2,1)S(1)}, u32[]{:S(2)}, u32[]{:S(2)}) collective-permute-start(bf16[27,32,128]{2,1,0:T(8,128)(2,1)S(1)} %copy-done.9), channel_id=1, source_target_pairs={{0,2},{1,3},{2,0},{3,1},{4,6},{5,7},{6,4},{7,5},{8,10},{9,11},{10,... | collective-permute-start | bytes 663560 | tf_op jit(solution)/shard_map/ppermute | solution.py:34
  21.9 2.7 %collective-permute-start.11 = (bf16[27,32,128]{2,1,0:T(8,128)(2,1)S(1)}, bf16[27,32,128]{2,1,0:T(8,128)(2,1)S(1)}, u32[]{:S(2)}, u32[]{:S(2)}) collective-permute-start(bf16[27,32,128]{2,1,0:T(8,128)(2,1)S(1)} %copy-done.10), channel_id=1, source_target_pairs={{0,18},{1,19},{2,16},{3,17},{4,22},{5,23},{6,20},{7,21},{8,26},{9,... | collective-permute-start | bytes 663560 | tf_op jit(solution)/shard_map/ppermute | solution.py:34
  24.6 1.3 collective-permute-start.4
  25.9 0.7 all-to-all-done.1.cot_ref.cot_own
  26.6 0.7 copy-done
  27.3 1.7 %shard_map.86 = bf16[2,2,128,128]{3,2,1,0:T(8,128)(2,1)} custom-call(bf16[4,2,2,32,128]{4,3,2,1,0:T(8,128)(2,1)} %copy-done), custom_call_target="tpu_custom_call" | custom-call | tf_op jit(solution)/shard_map/pallas_call | solution.py:285
  28.9 0.0 collective-permute-done.3
  28.9 1.3 collective-permute-start.14
  30.3 0.9 constant_dynamic-update-slice_fusion.1
  31.2 0.7 collective-permute-done.4
  31.9 0.0 copy-start.3
  31.9 1.3 collective-permute-start.5
  33.2 0.0 collective-permute-done.7.m1
  33.2 1.3 collective-permute-start.6
  34.5 0.0 collective-permute-done.8.m2
  34.5 4.2 %collective-permute-start.13 = (bf16[2,2,128,128]{3,2,1,0:T(8,128)(2,1)}, bf16[2,2,128,128]{3,2,1,0:T(8,128)(2,1)S(1)}, u32[]{:S(2)}, u32[]{:S(2)}) collective-permute-start(bf16[2,2,128,128]{3,2,1,0:T(8,128)(2,1)} %shard_map.86), channel_id=1, source_target_pairs={{0,4},{1,5},{2,6},{3,7},{4,8},{5,9},{6,10},{7,11},{8,12},{9,13},{1... | collective-permute-start | bytes 393224 | tf_op jit(solution)/shard_map/ppermute | solution.py:34
  38.8 0.0 collective-permute-done.11.l2
  38.8 1.8 %collective-permute-start.10 = (bf16[27,32,128]{2,1,0:T(8,128)(2,1)S(1)}, bf16[27,32,128]{2,1,0:T(8,128)(2,1)S(1)}, u32[]{:S(2)}, u32[]{:S(2)}) collective-permute-start(bf16[27,32,128]{2,1,0:T(8,128)(2,1)S(1)} %copy-done.10), channel_id=1, source_target_pairs={{0,1},{1,0},{2,3},{3,2},{4,5},{5,4},{6,7},{7,6},{8,9},{9,8},{10,11... | collective-permute-start | bytes 663560 | tf_op jit(solution)/shard_map/ppermute | solution.py:34
  40.7 0.1 collective-permute-start.9
  40.8 1.2 collective-permute-done.13
  41.9 1.2 collective-permute-start.12
  43.1 0.9 pad_maximum_fusion.cot_m
  44.1 1.9 %collective-permute-start.15 = (bf16[6,2,128,128]{3,2,1,0:T(8,128)(2,1)S(1)}, bf16[6,2,128,128]{3,2,1,0:T(8,128)(2,1)S(1)}, u32[]{:S(2)}, u32[]{:S(2)}) collective-permute-start(bf16[6,2,128,128]{3,2,1,0:T(8,128)(2,1)S(1)} %pad_maximum_fusion.cot_m), channel_id=1, source_target_pairs={{0,1},{1,2},{2,3},{4,5},{5,6},{6,7},{8,9},{9,10},{10,11},{12,13},{... | collective-permute-start | bytes 1179656 | tf_op jit(solution)/shard_map/ppermute | solution.py:34
  46.0 1.3 collective-permute-start.16
  47.3 0.0 collective-permute-done.12.l3
  47.3 0.0 collective-permute-done.5.left.act_l
  47.4 0.7 copy-done.15
  48.1 0.7 copy-done.5
  48.8 0.8 copy-done.6
  49.5 7.2 %shard_map.85 = (bf16[4,4,128,128]{3,2,1,0:T(8,128)(2,1)}, f32[4,4,128,128]{3,2,1,0:T(8,128)}, bf16[4,2,2,32,128]{4,3,2,1,0:T(8,128)(2,1)}) custom-call(s32[3]{0:T(128)} %pad_add_fusion.info, bf16[6,2,128,128]{3,2,1,0:T(8,128)(2,1)} %copy-done.5, bf16[6,2,128,128]{3,2,1,0:T(8,128)(2,1)} %copy-done.3, bf16[6,2,128,128]{3,2,1,0:T(8,128)(2,1)} %copy-done.6, ...), custom_call_target="tpu_custom_call" | custom-call | flops 3000000000 | bytes 5000000 | tf_op jit(solution)/shard_map/pallas_call | solution.py:299
  56.8 0.0 collective-permute-done.15.cot_l
  56.8 0.7 copy-done.7
  57.5 0.2 copy-done.8
  57.7 10.7 %shard_map.87 = bf16[4,64,32,128]{3,2,1,0:T(8,128)(2,1)} custom-call(s32[3]{0:T(128)} %pad_add_fusion.info, bf16[6,2,128,128]{3,2,1,0:T(8,128)(2,1)} %copy-done.5, bf16[6,2,128,128]{3,2,1,0:T(8,128)(2,1)} %copy-done.3, bf16[6,2,128,128]{3,2,1,0:T(8,128)(2,1)} %copy-done.6, bf16[6,2,128,128]{3,2,1,0:T(8,128)(2,1)} %copy-done.7, ...), custom_call_target="tpu_custom_call" | custom-call | flops 4000000000 | bytes 8000000 | tf_op jit(solution)/shard_map/pallas_call | solution.py:316
  68.3 48.7 %all_to_all.20 = bf16[128,64,128]{2,1,0:T(8,128)(2,1)S(1)} all-to-all(bf16[128,64,128]{2,1,0:T(8,128)(2,1)} %bitcast.18), channel_id=1, replica_groups=mesh['depth'=32,'filt'=4] {'filt','depth'}, dimensions={0} | all-to-all | bytes 4194304 | tf_op jit(solution)/shard_map/all_to_all | solution.py:338
  117.1 3.3 %all-to-all-start = ((bf16[4,2,2,32,128]{4,3,2,1,0:T(8,128)(2,1)}), bf16[4,2,2,32,128]{4,3,2,1,0:T(8,128)(2,1)S(1)}, u32[]{:S(2)}, u32[]{:S(2)}) async-start(bf16[4,2,2,32,128]{4,3,2,1,0:T(8,128)(2,1)} %get-tuple-element.11), calls=%async_computation | async-start | bytes 262144 | tf_op jit(solution)/shard_map/all_to_all | solution.py:334
  120.4 0.4 reduce_sum.12
  120.8 4.2 %all-to-all-done = bf16[4,2,2,32,128]{4,3,2,1,0:T(8,128)(2,1)S(1)} async-done(((bf16[4,2,2,32,128]{4,3,2,1,0:T(8,128)(2,1)}), bf16[4,2,2,32,128]{4,3,2,1,0:T(8,128)(2,1)S(1)}, u32[]{:S(2)}, u32[]{:S(2)}) %all-to-all-start) | async-done | bytes 131104 | tf_op jit(solution)/shard_map/all_to_all | solution.py:334
  125.0 0.9 broadcast_in_dim.2
  125.9 4.1 %all-to-all-start.3 = ((bf16[32,64,128]{2,1,0:T(8,128)(2,1)}), bf16[32,64,128]{2,1,0:T(8,128)(2,1)S(1)}, u32[]{:S(2)}, u32[]{:S(2)}) async-start(bf16[32,64,128]{2,1,0:T(8,128)(2,1)} %broadcast_in_dim.2), calls=%async_computation.3 | async-start | bytes 1048576 | tf_op jit(solution)/shard_map/all_to_all | solution.py:341
  130.0 0.7 copy.16
  130.7 12.2 %all-to-all-done.3 = bf16[32,64,128]{2,1,0:T(8,128)(2,1)S(1)} async-done(((bf16[32,64,128]{2,1,0:T(8,128)(2,1)}), bf16[32,64,128]{2,1,0:T(8,128)(2,1)S(1)}, u32[]{:S(2)}, u32[]{:S(2)}) %all-to-all-start.3) | async-done | bytes 524320 | tf_op jit(solution)/shard_map/all_to_all | solution.py:341
  142.9 0.1 fusion.1
  143.0 1.0 fusion
  144.0 0.7 pad_maximum_fusion.1
  (35 shorter events, 0.1 us)
Async XLA Ops:
  0.6 15.0 %copy-start.2 = (bf16[32,2,8,128]{3,2,1,0:T(8,128)(2,1)S(1)}, bf16[32,2,8,128]{3,2,1,0:T(8,128)(2,1)}, u32[]{:S(2)}) copy-start(bf16[32,2,8,128]{3,2,1,0:T(8,128)(2,1)} %param.9) | copy-start | bytes 393220
  0.6 19.1 %copy-start.9 = (bf16[27,32,128]{2,1,0:T(8,128)(2,1)S(1)}, bf16[27,32,128]{2,1,0:T(8,128)(2,1)}, u32[]{:S(2)}) copy-start(bf16[27,32,128]{2,1,0:T(8,128)(2,1)} %m0.3) | copy-start | bytes 663556
  0.7 21.3 %copy-start.10 = (bf16[27,32,128]{2,1,0:T(8,128)(2,1)S(1)}, bf16[27,32,128]{2,1,0:T(8,128)(2,1)}, u32[]{:S(2)}) copy-start(bf16[27,32,128]{2,1,0:T(8,128)(2,1)} %l0.3) | copy-start | bytes 663556
  1.7 6.7 %copy-start.4 = (bf16[32,512]{1,0:T(8,128)(2,1)}, bf16[32,512]{1,0:T(8,128)(2,1)S(1)}, u32[]{:S(2)}) copy-start(bf16[32,512]{1,0:T(8,128)(2,1)S(1)} %reshape.28.s0) | copy-start | bytes 98308
  1.7 4.0 %collective-permute-start.1 = (bf16[32,512]{1,0:T(8,128)(2,1)S(1)}, bf16[32,512]{1,0:T(8,128)(2,1)S(1)}, u32[]{:S(2)}, u32[]{:S(2)}) collective-permute-start(bf16[32,512]{1,0:T(8,128)(2,1)S(1)} %reshape.28.s0), channel_id=1, source_target_pairs={{0,2},{1,3},{2,0},{3,1},{4,6},{5,7},{6,4},{7,5},{8,10},{9,11},{10,... | collective-permute-start | bytes 98312 | tf_op jit(solution)/shard_map/ppermute | solution.py:34
  3.8 4.5 %collective-permute-start = (bf16[32,512]{1,0:T(8,128)(2,1)S(1)}, bf16[32,512]{1,0:T(8,128)(2,1)S(1)}, u32[]{:S(2)}, u32[]{:S(2)}) collective-permute-start(bf16[32,512]{1,0:T(8,128)(2,1)S(1)} %reshape.28.s0), channel_id=1, source_target_pairs={{0,1},{1,0},{2,3},{3,2},{4,5},{5,4},{6,7},{7,6},{8,9},{9,8},{10,11... | collective-permute-start | bytes 98312 | tf_op jit(solution)/shard_map/ppermute | solution.py:34
  5.7 2.7 %copy-start.16 = (bf16[32,512]{1,0:T(8,128)(2,1)}, bf16[32,512]{1,0:T(8,128)(2,1)S(1)}, u32[]{:S(2)}) copy-start(bf16[32,512]{1,0:T(8,128)(2,1)S(1)} %collective-permute-done.1.s2) | copy-start | bytes 98308
  5.7 2.6 %collective-permute-start.2 = (bf16[32,512]{1,0:T(8,128)(2,1)S(1)}, bf16[32,512]{1,0:T(8,128)(2,1)S(1)}, u32[]{:S(2)}, u32[]{:S(2)}) collective-permute-start(bf16[32,512]{1,0:T(8,128)(2,1)S(1)} %collective-permute-done.1.s2), channel_id=1, source_target_pairs={{0,1},{1,0},{2,3},{3,2},{4,5},{5,4},{6,7},{7,6},{8,9},{9,8},{10,11... | collective-permute-start | bytes 98312 | tf_op jit(solution)/shard_map/ppermute | solution.py:34
  8.4 0.6 copy-start.17
  8.4 0.6 copy-start.18
  12.1 16.9 %collective-permute-start.3 = (bf16[2,2,128,128]{3,2,1,0:T(8,128)(2,1)}, bf16[2,2,128,128]{3,2,1,0:T(8,128)(2,1)S(1)}, u32[]{:S(2)}, u32[]{:S(2)}) collective-permute-start(bf16[2,2,128,128]{3,2,1,0:T(8,128)(2,1)} %get-tuple-element.10), channel_id=1, source_target_pairs={{0,4},{1,5},{2,6},{3,7},{4,8},{5,9},{6,10},{7,11},{8,12},{9,13},{1... | collective-permute-start | bytes 393224 | tf_op jit(solution)/shard_map/ppermute | solution.py:34
  16.4 10.2 %all-to-all-start.1 = ((bf16[4,2,2,32,128]{4,3,2,1,0:T(8,128)(2,1)}), bf16[4,2,2,32,128]{4,3,2,1,0:T(8,128)(2,1)S(1)}, u32[]{:S(2)}, u32[]{:S(2)}) async-start(bf16[4,2,2,32,128]{4,3,2,1,0:T(8,128)(2,1)} %bitcast.15), calls=%async_computation.1 | async-start | bytes 262144 | tf_op jit(solution)/shard_map/all_to_all | solution.py:284
  19.7 13.5 %collective-permute-start.7 = (bf16[27,32,128]{2,1,0:T(8,128)(2,1)S(1)}, bf16[27,32,128]{2,1,0:T(8,128)(2,1)S(1)}, u32[]{:S(2)}, u32[]{:S(2)}) collective-permute-start(bf16[27,32,128]{2,1,0:T(8,128)(2,1)S(1)} %copy-done.9), channel_id=1, source_target_pairs={{0,1},{1,0},{2,3},{3,2},{4,5},{5,4},{6,7},{7,6},{8,9},{9,8},{10,11... | collective-permute-start | bytes 663560 | tf_op jit(solution)/shard_map/ppermute | solution.py:34
  20.2 14.4 %collective-permute-start.8 = (bf16[27,32,128]{2,1,0:T(8,128)(2,1)S(1)}, bf16[27,32,128]{2,1,0:T(8,128)(2,1)S(1)}, u32[]{:S(2)}, u32[]{:S(2)}) collective-permute-start(bf16[27,32,128]{2,1,0:T(8,128)(2,1)S(1)} %copy-done.9), channel_id=1, source_target_pairs={{0,2},{1,3},{2,0},{3,1},{4,6},{5,7},{6,4},{7,5},{8,10},{9,11},{10,... | collective-permute-start | bytes 663560 | tf_op jit(solution)/shard_map/ppermute | solution.py:34
  21.9 16.9 %collective-permute-start.11 = (bf16[27,32,128]{2,1,0:T(8,128)(2,1)S(1)}, bf16[27,32,128]{2,1,0:T(8,128)(2,1)S(1)}, u32[]{:S(2)}, u32[]{:S(2)}) collective-permute-start(bf16[27,32,128]{2,1,0:T(8,128)(2,1)S(1)} %copy-done.10), channel_id=1, source_target_pairs={{0,18},{1,19},{2,16},{3,17},{4,22},{5,23},{6,20},{7,21},{8,26},{9,... | collective-permute-start | bytes 663560 | tf_op jit(solution)/shard_map/ppermute | solution.py:34
  24.6 7.2 %collective-permute-start.4 = (bf16[2,2,128,128]{3,2,1,0:T(8,128)(2,1)}, bf16[2,2,128,128]{3,2,1,0:T(8,128)(2,1)S(1)}, u32[]{:S(2)}, u32[]{:S(2)}) collective-permute-start(bf16[2,2,128,128]{3,2,1,0:T(8,128)(2,1)} %get-tuple-element.10), channel_id=1, source_target_pairs={{4,0},{5,1},{6,2},{7,3},{8,4},{9,5},{10,6},{11,7},{12,8},{13,9},{1... | collective-permute-start | bytes 393224 | tf_op jit(solution)/shard_map/ppermute | solution.py:34
  26.6 0.7 copy-start
  28.9 11.7 %collective-permute-start.14 = (bf16[2,2,128,128]{3,2,1,0:T(8,128)(2,1)}, bf16[2,2,128,128]{3,2,1,0:T(8,128)(2,1)S(1)}, u32[]{:S(2)}, u32[]{:S(2)}) collective-permute-start(bf16[2,2,128,128]{3,2,1,0:T(8,128)(2,1)} %shard_map.86), channel_id=1, source_target_pairs={{4,0},{5,1},{6,2},{7,3},{8,4},{9,5},{10,6},{11,7},{12,8},{13,9},{1... | collective-permute-start | bytes 393224 | tf_op jit(solution)/shard_map/ppermute | solution.py:34
  31.9 16.2 %copy-start.3 = (bf16[6,2,128,128]{3,2,1,0:T(8,128)(2,1)}, bf16[6,2,128,128]{3,2,1,0:T(8,128)(2,1)S(1)}, u32[]{:S(2)}) copy-start(bf16[6,2,128,128]{3,2,1,0:T(8,128)(2,1)S(1)} %constant_dynamic-update-slice_fusion.mid.act_m) | copy-start | bytes 1179652
  31.9 15.5 %collective-permute-start.5 = (bf16[6,2,128,128]{3,2,1,0:T(8,128)(2,1)S(1)}, bf16[6,2,128,128]{3,2,1,0:T(8,128)(2,1)S(1)}, u32[]{:S(2)}, u32[]{:S(2)}) collective-permute-start(bf16[6,2,128,128]{3,2,1,0:T(8,128)(2,1)S(1)} %constant_dynamic-update-slice_fusion.mid.act_m), channel_id=1, source_target_pairs={{0,1},{1,2},{2,3},{4,5},{5,6},{6,7},{8,9},{9,10},{10,11},{12,13},{... | collective-permute-start | bytes 1179656 | tf_op jit(solution)/shard_map/ppermute | solution.py:34
  33.2 14.8 %copy-start.11 = (bf16[27,32,128]{2,1,0:T(8,128)(2,1)}, bf16[27,32,128]{2,1,0:T(8,128)(2,1)S(1)}, u32[]{:S(2)}) copy-start(bf16[27,32,128]{2,1,0:T(8,128)(2,1)S(1)} %collective-permute-done.7.m1) | copy-start | bytes 663556
  33.2 14.8 %collective-permute-start.6 = (bf16[6,2,128,128]{3,2,1,0:T(8,128)(2,1)S(1)}, bf16[6,2,128,128]{3,2,1,0:T(8,128)(2,1)S(1)}, u32[]{:S(2)}, u32[]{:S(2)}) collective-permute-start(bf16[6,2,128,128]{3,2,1,0:T(8,128)(2,1)S(1)} %constant_dynamic-update-slice_fusion.mid.act_m), channel_id=1, source_target_pairs={{1,0},{2,1},{3,2},{5,4},{6,5},{7,6},{9,8},{10,9},{11,10},{13,12},{... | collective-permute-start | bytes 1179656 | tf_op jit(solution)/shard_map/ppermute | solution.py:34
  34.5 13.5 %copy-start.12 = (bf16[27,32,128]{2,1,0:T(8,128)(2,1)}, bf16[27,32,128]{2,1,0:T(8,128)(2,1)S(1)}, u32[]{:S(2)}) copy-start(bf16[27,32,128]{2,1,0:T(8,128)(2,1)S(1)} %collective-permute-done.8.m2) | copy-start | bytes 663556
  34.5 7.4 %collective-permute-start.13 = (bf16[2,2,128,128]{3,2,1,0:T(8,128)(2,1)}, bf16[2,2,128,128]{3,2,1,0:T(8,128)(2,1)S(1)}, u32[]{:S(2)}, u32[]{:S(2)}) collective-permute-start(bf16[2,2,128,128]{3,2,1,0:T(8,128)(2,1)} %shard_map.86), channel_id=1, source_target_pairs={{0,4},{1,5},{2,6},{3,7},{4,8},{5,9},{6,10},{7,11},{8,12},{9,13},{1... | collective-permute-start | bytes 393224 | tf_op jit(solution)/shard_map/ppermute | solution.py:34
  38.8 9.2 %copy-start.13 = (bf16[27,32,128]{2,1,0:T(8,128)(2,1)}, bf16[27,32,128]{2,1,0:T(8,128)(2,1)S(1)}, u32[]{:S(2)}) copy-start(bf16[27,32,128]{2,1,0:T(8,128)(2,1)S(1)} %collective-permute-done.11.l2) | copy-start | bytes 663556
  38.8 5.2 %collective-permute-start.10 = (bf16[27,32,128]{2,1,0:T(8,128)(2,1)S(1)}, bf16[27,32,128]{2,1,0:T(8,128)(2,1)S(1)}, u32[]{:S(2)}, u32[]{:S(2)}) collective-permute-start(bf16[27,32,128]{2,1,0:T(8,128)(2,1)S(1)} %copy-done.10), channel_id=1, source_target_pairs={{0,1},{1,0},{2,3},{3,2},{4,5},{5,4},{6,7},{7,6},{8,9},{9,8},{10,11... | collective-permute-start | bytes 663560 | tf_op jit(solution)/shard_map/ppermute | solution.py:34
  40.7 5.4 %collective-permute-start.9 = (bf16[27,32,128]{2,1,0:T(8,128)(2,1)S(1)}, bf16[27,32,128]{2,1,0:T(8,128)(2,1)}, u32[]{:S(2)}, u32[]{:S(2)}) collective-permute-start(bf16[27,32,128]{2,1,0:T(8,128)(2,1)S(1)} %collective-permute-done.8.m2), channel_id=1, source_target_pairs={{0,1},{1,0},{2,3},{3,2},{4,5},{5,4},{6,7},{7,6},{8,9},{9,8},{10,11... | collective-permute-start | bytes 663560 | tf_op jit(solution)/shard_map/ppermute | solution.py:34
  41.9 5.4 %collective-permute-start.12 = (bf16[27,32,128]{2,1,0:T(8,128)(2,1)S(1)}, bf16[27,32,128]{2,1,0:T(8,128)(2,1)S(1)}, u32[]{:S(2)}, u32[]{:S(2)}) collective-permute-start(bf16[27,32,128]{2,1,0:T(8,128)(2,1)S(1)} %collective-permute-done.11.l2), channel_id=1, source_target_pairs={{0,1},{1,0},{2,3},{3,2},{4,5},{5,4},{6,7},{7,6},{8,9},{9,8},{10,11... | collective-permute-start | bytes 663560 | tf_op jit(solution)/shard_map/ppermute | solution.py:34
  44.0 12.7 %copy-start.1 = (bf16[6,2,128,128]{3,2,1,0:T(8,128)(2,1)}, bf16[6,2,128,128]{3,2,1,0:T(8,128)(2,1)S(1)}, u32[]{:S(2)}) copy-start(bf16[6,2,128,128]{3,2,1,0:T(8,128)(2,1)S(1)} %pad_maximum_fusion.cot_m) | copy-start | bytes 1179652
  44.1 4.0 %copy-start.14 = (bf16[27,32,128]{2,1,0:T(8,128)(2,1)}, bf16[27,32,128]{2,1,0:T(8,128)(2,1)S(1)}, u32[]{:S(2)}) copy-start(bf16[27,32,128]{2,1,0:T(8,128)(2,1)S(1)} %collective-permute-done.10.l1) | copy-start | bytes 663556
  44.1 12.7 %collective-permute-start.15 = (bf16[6,2,128,128]{3,2,1,0:T(8,128)(2,1)S(1)}, bf16[6,2,128,128]{3,2,1,0:T(8,128)(2,1)S(1)}, u32[]{:S(2)}, u32[]{:S(2)}) collective-permute-start(bf16[6,2,128,128]{3,2,1,0:T(8,128)(2,1)S(1)} %pad_maximum_fusion.cot_m), channel_id=1, source_target_pairs={{0,1},{1,2},{2,3},{4,5},{5,6},{6,7},{8,9},{9,10},{10,11},{12,13},{... | collective-permute-start | bytes 1179656 | tf_op jit(solution)/shard_map/ppermute | solution.py:34
  46.0 10.8 %collective-permute-start.16 = (bf16[6,2,128,128]{3,2,1,0:T(8,128)(2,1)S(1)}, bf16[6,2,128,128]{3,2,1,0:T(8,128)(2,1)S(1)}, u32[]{:S(2)}, u32[]{:S(2)}) collective-permute-start(bf16[6,2,128,128]{3,2,1,0:T(8,128)(2,1)S(1)} %pad_maximum_fusion.cot_m), channel_id=1, source_target_pairs={{1,0},{2,1},{3,2},{5,4},{6,5},{7,6},{9,8},{10,9},{11,10},{13,12},{... | collective-permute-start | bytes 1179656 | tf_op jit(solution)/shard_map/ppermute | solution.py:34
  47.3 0.7 copy-start.15
  48.0 0.7 copy-start.5
  48.8 0.8 copy-start.6
  56.8 0.8 copy-start.7
  56.8 0.9 copy-start.8
  117.1 7.9 %all-to-all-start = ((bf16[4,2,2,32,128]{4,3,2,1,0:T(8,128)(2,1)}), bf16[4,2,2,32,128]{4,3,2,1,0:T(8,128)(2,1)S(1)}, u32[]{:S(2)}, u32[]{:S(2)}) async-start(bf16[4,2,2,32,128]{4,3,2,1,0:T(8,128)(2,1)} %get-tuple-element.11), calls=%async_computation | async-start | bytes 262144 | tf_op jit(solution)/shard_map/all_to_all | solution.py:334
  125.9 17.0 %all-to-all-start.3 = ((bf16[32,64,128]{2,1,0:T(8,128)(2,1)}), bf16[32,64,128]{2,1,0:T(8,128)(2,1)S(1)}, u32[]{:S(2)}, u32[]{:S(2)}) async-start(bf16[32,64,128]{2,1,0:T(8,128)(2,1)} %broadcast_in_dim.2), calls=%async_computation.3 | async-start | bytes 1048576 | tf_op jit(solution)/shard_map/all_to_all | solution.py:341
where the time goes:
time: 146 us; the launch traced here: 145 us
  blocking collectives  48.7 us (33%)
  starting transfers between devices  37.1 us (25%)
  Pallas kernels  22.7 us (16%)
  waiting for transfers between devices  20.8 us (14%)
  local copies, waits for them, and re-layouts  11.7 us (8%)
  other arithmetic  2.62 us (2%)
    all_to_all x1, blocking collectives, per_device(): terms = lax.all_to_all(terms, ('filt', 'depth'), 0, 0, tiled=True)  48.7 us
    ppermute x17, starting transfers between devices, shifted(): return lax.ppermute(value, AXES, pairs_of(move))  26.4 us
    all_to_all x1, waiting for transfers between devices, per_device(): full = lax.all_to_all(spread, 'depth', 0, 0, tiled=True)  12.2 us
    pallas_call x1, Pallas kernels, per_device(): call(back_body, shape((4, 64, 32, 128)), [pltpu.VMEM((6, 6, 128, 128), jn...  10.7 us
    unnamed x42, local copies, waits for them, and re-layouts  7.93 us
    pallas_call x1, Pallas kernels, per_device(): call(middle_body, [shape((4, 4, 128, 128)), shape((4, 4, 128, 128), jnp.f...  7.23 us
    all_to_all x1, waiting for transfers between devices, per_device(): result = lax.all_to_all(result, 'filt', 0, 0, tiled=True)  4.2 us
    all_to_all x1, starting transfers between devices, per_device(): full = lax.all_to_all(spread, 'depth', 0, 0, tiled=True)  4.12 us
  transfers between devices with their start and end apart: 20, of which 6 were waited for; matrix products, arithmetic and copies ran while one was open for 4% of the time, Pallas kernels for 6%

commit v1 on v0

--- a/solution.py
+++ b/solution.py
@@ -1,13 +1,14 @@
-import functools
-
 import jax
 import jax.numpy as jnp
 from jax import lax
 from jax.experimental import pallas as pl
 from jax.experimental.pallas import tpu as pltpu
+from jax.sharding import Mesh
 from jax.sharding import PartitionSpec as P
 
-AXES = ("depth", "filt")
+
+AXES = ("depth", "chip", "core")
+FILT = ("chip", "core")
 CELLS = 128
 VMEM = pl.BlockSpec(memory_space=pltpu.VMEM)
 SMEM = pl.BlockSpec(memory_space=pltpu.SMEM)
@@ -20,7 +21,7 @@
 
 
 def pairs_of(move):
-    depth, filt = lax.axis_size("depth"), lax.axis_size("filt")
+    depth, filt = lax.axis_size("depth"), lax.axis_size(FILT)
     found = []
     for d in range(depth):
         for f in range(filt):
@@ -42,13 +43,16 @@
     return shifted(value, lambda d, f: (d, f ^ 2))
 
 
-def swap_chip_across(value):
-    return shifted(value, lambda d, f: (d ^ 4, f ^ 2))
-
-
-def four_parts(value, swap):
-    far = swap(value)
+def four_parts(value):
+    far = swap_chip(value)
     return [value, swap_core(value), far, swap_core(far)]
+
+
+def four_parts_across(value):
+    near = swap_core(value)
+    far = shifted(value, lambda d, f: (d ^ 4, f ^ 2))
+    both = shifted(value, lambda d, f: (d ^ 4, f ^ 3))
+    return [value, near, far, both]
 
 
 def call(body, out_shape, scratch=(), flops=0, moved=0, in_specs=None):
@@ -81,7 +85,9 @@
     filt = info[1]
     for j, part in enumerate((s0, s1, s2, s3)):
         start = pl.multiple_of((filt ^ j) * 32, 32)
-        weights[pl.ds(start, 32), :] = part[...]
+        for tap in range(0, 8, 2):
+            pair = jnp.concatenate([part[tap], part[tap + 1]], axis=1)
+            weights[pl.ds(start, 32), tap * 64 : tap * 64 + 128] = pair
     source = lax.broadcasted_iota(jnp.int32, (256, 256), 0)
     target = lax.broadcasted_iota(jnp.int32, (256, 256), 1)
     pick = source == 2 * (target % 128) + target // 128
@@ -101,11 +107,21 @@
             act_ref[p, r] = (pre * jax.nn.sigmoid(pre)).astype(jnp.bfloat16)
 
 
-def turn_body(cot_ref, out_ref):
-    for p in range(2):
-        for r in range(2):
-            block = jnp.concatenate([cot_ref[j, p, r] for j in range(4)], axis=0)
-            out_ref[p, r] = block.astype(jnp.float32).T.astype(jnp.bfloat16)
+def turn_body(info, own, near, far, both, cells_ref, own_ref, tiles):
+    filt, chip = info[1], info[3]
+    for p in range(6):
+        for r in range(6):
+            row = 2 * filt - 2 + r
+            valid = jnp.where((row >= 0) & (row <= 7), 1.0, 0.0)
+            wide = jnp.clip(row, 0, 7)
+            cut = jnp.clip(row - 2 * chip, 0, 5)
+            for j, (part, at) in enumerate(((own, wide), (near, wide), (far, cut), (both, cut))):
+                start = pl.multiple_of((filt ^ j) * 32, 32)
+                tiles[p * 6 + r, pl.ds(start, 32), :] = part[p, at]
+            tile = tiles[p * 6 + r]
+            cells_ref[p, r] = (tile.astype(jnp.float32).T * valid).astype(jnp.bfloat16)
+            if 2 <= p < 4 and 2 <= r < 4:
+                own_ref[p - 2, r - 2] = tile
 
 
 def fill_window(window, left, middle, right):
@@ -167,7 +183,7 @@
 def inside(info, p):
     depth, filt = info[0], info[1]
     row = lax.broadcasted_iota(jnp.int32, (4 * CELLS, 1), 0) // CELLS
-    bad = ((depth == 0) & (p == 0)) | ((depth == info[2] - 1) & (p == 3))
+    bad = ((depth == 0) & (p == 0)) | ((depth == lax.axis_size("depth") - 1) & (p == 3))
     low = jnp.where(filt == 0, 1, 0)
     high = jnp.where(filt == 3, 2, 3)
     low = jnp.where(bad, 4, low)
@@ -175,29 +191,39 @@
 
 
 def middle_body(
-    info, left, mid, right, m0, m1, m2, m3, l0, l1, l2, l3,
-    act_ref, pre_ref, result_ref, window, weights_m, weights_l,
+    info, left, mid, right, m0, m1, m2, m3, act_ref, pre_ref, window, weights
 ):
     filt = info[1]
     fill_window(window, left, mid, right)
-    fill_forward(weights_m, (m0, m1, m2, m3), filt)
-    fill_forward(weights_l, (l0, l1, l2, l3), filt)
+    fill_forward(weights, (m0, m1, m2, m3), filt)
 
     def plane(p, carry):
-        pre = conv_forward(window, p, 1, 0, 4, weights_m)
+        pre = conv_forward(window, p, 1, 0, 4, weights)
         act = jnp.where(inside(info, p), pre * jax.nn.sigmoid(pre), 0.0)
         pre_ref[pl.ds(p, 1)] = pre.reshape(1, 4, CELLS, 128)
         act_ref[pl.ds(p, 1)] = act.astype(jnp.bfloat16).reshape(1, 4, CELLS, 128)
         return carry
 
     lax.fori_loop(0, 4, plane, 0)
-    out = conv_forward(act_ref, 0, 2, 0, 2, weights_l)
+
+
+def result_body(info, act_ref, l0, l1, l2, l3, near_ref, far_ref, weights, turned):
+    filt = info[1]
+    fill_forward(weights, (l0, l1, l2, l3), filt)
+    out = conv_forward(act_ref, 0, 2, 0, 2, weights)
     for p in range(2):
         for r in range(2):
             at = (2 * p + r) * CELLS
-            block = out[at : at + CELLS].T.astype(jnp.bfloat16)
-            for f in range(4):
-                result_ref[f, p, r] = block[f * 32 : f * 32 + 32]
+            turned[...] = out[at : at + CELLS].T.astype(jnp.bfloat16)
+            for j, ref in enumerate((near_ref, far_ref, near_ref, far_ref)):
+                start = pl.multiple_of((filt ^ j) * 32, 32)
+                ref[j // 2, p, r] = turned[pl.ds(start, 32), :]
+
+
+def rows_body(info, own, near, far, out_ref):
+    filt = info[1]
+    for j, part in enumerate((own.at[0], near.at[0], far.at[0], far.at[1])):
+        out_ref[filt ^ j] = part[...]
 
 
 def shifts_of(value):
@@ -208,22 +234,30 @@
     return jnp.concatenate([after, value, before], axis=0).astype(jnp.bfloat16)
 
 
-def put_kernel_grad(grads_ref, first, grad):
+def in_order(ref, at, core):
+    rows = [ref[at + (pl.ds(pl.multiple_of((k ^ core) * 32, 32), 32),)] for k in range(4)]
+    return jnp.concatenate(rows, axis=0)
+
+
+def put_grad(refs, slot, block):
+    for k in range(4):
+        refs[k % 2][k // 2, slot] = block[k * 32 : k * 32 + 32].astype(jnp.bfloat16)
+
+
+def put_kernel_grad(refs, first, grad):
     for n, (a, b) in enumerate(TAPS):
         for c in range(3):
-            for f in range(4):
-                at = c * 128 + f * 32
-                piece = grad[at : at + 32, n * 128 : n * 128 + 128]
-                grads_ref[f, first + 9 * a + 3 * b + c] = piece.astype(jnp.bfloat16)
+            block = grad[c * 128 : c * 128 + 128, n * 128 : n * 128 + 128]
+            put_grad(refs, first + 9 * a + 3 * b + c, block)
 
 
 def back_body(
-    info, act_l, act_m, act_r, cot_l, cot_m, cot_r, m0, m1, m2, m3, l0, l1, l2, l3,
+    info, act_l, act_m, act_r, window, m0, m1, m2, m3, l0, l1, l2, l3,
     mid_act, mid_pre, level_pre, columns, cot_own,
-    grads_ref, window, act_window, weights_m, weights_l, delta,
+    keep_ref, send_ref, act_window, weights_m, weights_l, delta, turned,
 ):
-    filt = info[1]
-    fill_window(window, cot_l, cot_m, cot_r)
+    filt, core = info[1], info[4]
+    refs = (keep_ref, send_ref)
     fill_window(act_window, act_l, act_m, act_r)
     fill_backward(weights_l, (l0, l1, l2, l3), filt)
     fill_backward(weights_m, (m0, m1, m2, m3), filt)
@@ -237,31 +271,30 @@
 
     lax.fori_loop(0, 4, plane, 0)
 
-    own = [
-        jnp.concatenate([cot_own[j, p, r] for j in range(4)], axis=0).astype(jnp.float32)
-        for p in range(2)
-        for r in range(2)
-    ]
+    own = [in_order(cot_own, (p, r), core).astype(jnp.float32) for p in range(2) for r in range(2)]
     cot_rows = shifts_of(jnp.concatenate(own, axis=1))
     wide = jnp.concatenate([block_of(mid_act, a, 2, b, 2) for a, b in TAPS], axis=1)
-    put_kernel_grad(grads_ref, 0, dot(cot_rows, wide))
-
-    own = [delta[1 + p, 1 + r].astype(jnp.float32).T for p in range(2) for r in range(2)]
-    delta_rows = shifts_of(jnp.concatenate(own, axis=1))
+    put_kernel_grad(refs, 0, dot(cot_rows, wide))
+
+    for p in range(2):
+        for r in range(2):
+            at = (2 * p + r) * CELLS
+            turned[:, at : at + CELLS] = delta[1 + p, 1 + r].astype(jnp.float32).T
+    delta_rows = shifts_of(in_order(turned, (), core))
     wide = jnp.concatenate([block_of(act_window, 1 + a, 2, 1 + b, 2) for a, b in TAPS], axis=1)
-    put_kernel_grad(grads_ref, 27, dot(delta_rows, wide))
+    put_kernel_grad(refs, 27, dot(delta_rows, wide))
 
     back = conv_backward(delta, 0, 2, 0, 2, weights_m)
     pre = level_pre[...].reshape(4 * CELLS, 128)
     level_delta = (back * silu_slope(pre)).astype(jnp.bfloat16)
     grad = dot(columns[...], level_delta)
     for n in range(4):
-        block = grad[n * 128 : n * 128 + 128].T.astype(jnp.bfloat16)
-        for f in range(4):
-            grads_ref[f, 54 + n] = block[f * 32 : f * 32 + 32]
+        turned[:, n * 128 : n * 128 + 128] = grad[n * 128 : n * 128 + 128].T
+    ordered = in_order(turned, (), core)
+    for n in range(4):
+        put_grad(refs, 54 + n, ordered[:, n * 128 : n * 128 + 128])
     for n in range(58, 64):
-        for f in range(4):
-            grads_ref[f, n] = jnp.zeros((32, 128), jnp.bfloat16)
+        put_grad(refs, n, jnp.zeros((128, 128), jnp.float32))
 
 
 def neighbourhood(block):
@@ -273,17 +306,32 @@
     return left, column, right
 
 
-def per_device(upper_level, stride_weight, middle_weight, last_weight, cotangent):
+def cotangent_parts(cotangent, chip):
+    block = cotangent.transpose(1, 2, 0, 3)
+    low = shifted(block, lambda d, f: (d + 1, f))
+    high = shifted(block, lambda d, f: (d - 1, f))
+    column = jnp.concatenate([low, block, high], axis=0)
+    wanted = lax.dynamic_slice_in_dim(column, 2 * (1 - chip), 6, axis=1)
+    far = swap_chip(wanted)
+    return column, swap_core(column), far, swap_core(far)
+
+
+def whole(upper_level, stride_weight, middle_weight, last_weight, cotangent):
     depth = lax.axis_size("depth")
-    info = jnp.stack([lax.axis_index("depth"), lax.axis_index("filt"), jnp.int32(depth)])
-    stride_parts = four_parts(stride_weight.transpose(1, 0, 2).reshape(32, 512), swap_chip)
-    middle_parts = four_parts(middle_weight, swap_chip)
-    last_parts = four_parts(last_weight, swap_chip_across)
-
-    cot_own = cotangent.reshape(32, 2, 4, 2, 128).transpose(2, 1, 3, 0, 4)
-    cot_own = lax.all_to_all(cot_own, "filt", 0, 0, tiled=True)
-    cot_cells = call(turn_body, shape((2, 2, 128, 128)), in_specs=[VMEM])(cot_own)
-    cot_near = neighbourhood(cot_cells)
+    chip, core = lax.axis_index("chip"), lax.axis_index("core")
+    info = jnp.stack([lax.axis_index("depth"), 2 * chip + core, jnp.int32(depth), chip, core])
+    stride_parts = four_parts(stride_weight)
+    middle_parts = four_parts(middle_weight)
+    last_parts = four_parts_across(last_weight)
+    cot_parts = cotangent_parts(cotangent, chip)
+    cot_cells, cot_own = call(
+        turn_body,
+        [shape((6, 6, 128, 128)), shape((2, 2, 128, 128))],
+        [pltpu.VMEM((36, 128, 128), jnp.bfloat16)],
+        flops=1_000_000,
+        moved=3_000_000,
+        in_specs=[SMEM] + [VMEM] * 4,
+    )(info, *cot_parts)
 
     upper = upper_level.transpose(1, 2, 0, 3)
     level_act, level_pre, columns = call(
@@ -296,46 +344,55 @@
     )(info, upper, *stride_parts)
     act_near = neighbourhood(level_act)
 
-    mid_act, mid_pre, result = call(
+    mid_act, mid_pre = call(
         middle_body,
-        [
-            shape((4, 4, 128, 128)),
-            shape((4, 4, 128, 128), jnp.float32),
-            shape((4, 2, 2, 32, 128)),
-        ],
+        [shape((4, 4, 128, 128)), shape((4, 4, 128, 128), jnp.float32)],
         [
             pltpu.VMEM((6, 6, 128, 128), jnp.bfloat16),
             pltpu.VMEM((384, 1152), jnp.bfloat16),
-            pltpu.VMEM((384, 1152), jnp.bfloat16),
         ],
         flops=3_000_000_000,
-        moved=5_000_000,
-        in_specs=[SMEM] + [VMEM] * 11,
-    )(info, *act_near, *middle_parts, *last_parts)
-
-    grads = call(
+        moved=4_000_000,
+        in_specs=[SMEM] + [VMEM] * 7,
+    )(info, *act_near, *middle_parts)
+
+    stay, leave = call(
+        result_body,
+        [shape((2, 2, 2, 32, 128))] * 2,
+        [pltpu.VMEM((384, 1152), jnp.bfloat16), pltpu.VMEM((128, 128), jnp.bfloat16)],
+        flops=500_000_000,
+        moved=2_000_000,
+        in_specs=[SMEM] + [VMEM] * 5,
+    )(info, mid_act, *last_parts)
+    result_near = swap_core(leave)
+    result_far = swap_chip(jnp.stack([stay[1], result_near[1]]))
+
+    keep, send = call(
         back_body,
-        shape((4, 64, 32, 128)),
+        [shape((2, 64, 32, 128)), shape((2, 64, 32, 128))],
         [
-            pltpu.VMEM((6, 6, 128, 128), jnp.bfloat16),
             pltpu.VMEM((6, 6, 128, 128), jnp.bfloat16),
             pltpu.VMEM((1152, 384), jnp.bfloat16),
             pltpu.VMEM((1152, 384), jnp.bfloat16),
             pltpu.VMEM((4, 4, 128, 128), jnp.bfloat16),
+            pltpu.VMEM((128, 512), jnp.float32),
         ],
         flops=4_000_000_000,
         moved=8_000_000,
-        in_specs=[SMEM] + [VMEM] * 19,
+        in_specs=[SMEM] + [VMEM] * 17,
     )(
-        info, *act_near, *cot_near, *middle_parts, *last_parts,
+        info, *act_near, cot_cells, *middle_parts, *last_parts,
         mid_act, mid_pre, level_pre, columns, cot_own,
     )
 
-    result = lax.all_to_all(result, "filt", 0, 0, tiled=True)
+    result = call(
+        rows_body, shape((4, 2, 2, 32, 128)), in_specs=[SMEM] + [VMEM] * 3
+    )(info, stay, result_near, result_far)
     result = result.transpose(3, 1, 0, 2, 4).reshape(32, 2, 8, 128)
 
-    terms = grads.reshape(4 * depth, 64, 128)
-    terms = lax.all_to_all(terms, ("filt", "depth"), 0, 0, tiled=True)
+    other = swap_core(send)
+    terms = (keep.astype(jnp.float32) + other.astype(jnp.float32)).astype(jnp.bfloat16)
+    terms = lax.all_to_all(terms.reshape(2 * depth, 64, 128), ("chip", "depth"), 0, 0, tiled=True)
     mine = jnp.sum(terms.astype(jnp.float32), axis=0).astype(jnp.bfloat16)
     spread = jnp.broadcast_to(mine[None], (depth, 64, 128))
     full = lax.all_to_all(spread, "depth", 0, 0, tiled=True)
@@ -346,21 +403,22 @@
 
 def solution(mesh):
     placed = (
-        P(None, "depth", "filt", None),
-        P(None, "filt", None),
-        P(None, "filt", None),
-        P(None, "filt", None),
-        P("filt", "depth", None, None),
-    )
+        P(None, "depth", FILT, None),
+        P(None, FILT, None),
+        P(None, FILT, None),
+        P(None, FILT, None),
+        P(FILT, "depth", None, None),
+    )
+    fine = Mesh(mesh.devices.reshape(-1, 2, 2), AXES)
     return jax.shard_map(
-        per_device,
-        mesh=mesh,
+        whole,
+        mesh=fine,
         in_specs=placed,
         out_specs=(
-            P("filt", "depth", None, None),
-            P(None, "filt", None),
-            P(None, "filt", None),
-            P(None, "filt", None),
+            P(FILT, "depth", None, None),
+            P(None, FILT, None),
+            P(None, FILT, None),
+            P(None, FILT, None),
         ),
         check_vma=False,
     )

time: 146 us -> 141 us (0.966)
  blocking collectives: 48.7 us -> 35.9 us
  Pallas kernels: 22.7 us -> 27.6 us
  waiting for transfers between devices: 20.8 us -> 25.6 us
  starting transfers between devices: 37.1 us -> 34.3 us
    ppermute x17 -> x21, waiting for transfers between devices: 3.76 us -> 25.6 us  [shifted(): return lax.ppermute(value, AXES, pairs_of(move))]
    all_to_all x3 -> x1, waiting for transfers between devices: 17.1 us -> 0.01 us  [whole(): full = lax.all_to_all(spread, 'depth', 0, 0, tiled=True)]
    all_to_all x1, blocking collectives: 48.7 us -> 35.9 us  [whole(): lax.all_to_all(terms.reshape(2 * depth, 64, 128), ('chip', 'depth'), 0, 0...]
    all_to_all x3 -> x1, starting transfers between devices: 10.8 us -> 4.7 us  [whole(): full = lax.all_to_all(spread, 'depth', 0, 0, tiled=True)]
    pallas_call x4 -> x6, Pallas kernels: 22.7 us -> 27.6 us  [the longest x1 10.5 us: whole(): call(back_body, [shape((2, 64, 32, 128)), shape((2, 64, 32, 128))], [pltp...]
    ppermute x17 -> x21, starting transfers between devices: 26.4 us -> 29.6 us  [shifted(): return lax.ppermute(value, AXES, pairs_of(move))]
    convert_element_type x0 -> x1, other arithmetic: none -> 1.5 us  [whole(): (keep.astype(jnp.float32) + other.astype(jnp.float32)).astype(jnp.bfloat16)]
    unnamed x42 -> x41, local copies, waits for them, and re-layouts: 7.93 us -> 8.66 us
  transfers between devices with their start and end apart: 20 -> 22, of which waited for: 6 -> 7; matrix products, arithmetic and copies ran while one was open for 4% -> 4% of each run, Pallas kernels for 6% -> 12%
where the time goes in v1:
time: 141 us; the launch traced here: 140 us
  blocking collectives  35.9 us (25%)
  starting transfers between devices  34.3 us (24%)
  Pallas kernels  27.6 us (20%)
  waiting for transfers between devices  25.6 us (18%)
  local copies, waits for them, and re-layouts  13.1 us (9%)
  other arithmetic  2.4 us (2%)
    all_to_all x1, blocking collectives, whole(): lax.all_to_all(terms.reshape(2 * depth, 64, 128), ('chip', 'depth'), 0, 0...  35.9 us
    ppermute x21, starting transfers between devices, shifted(): return lax.ppermute(value, AXES, pairs_of(move))  29.6 us
    ppermute x21, waiting for transfers between devices, shifted(): return lax.ppermute(value, AXES, pairs_of(move))  25.6 us
    pallas_call x1, Pallas kernels, whole(): call(back_body, [shape((2, 64, 32, 128)), shape((2, 64, 32, 128))], [pltp...  10.5 us
    unnamed x41, local copies, waits for them, and re-layouts  8.66 us
    pallas_call x1, Pallas kernels, whole(): call(middle_body, [shape((4, 4, 128, 128)), shape((4, 4, 128, 128), jnp.f...  6.42 us
    all_to_all x1, starting transfers between devices, whole(): full = lax.all_to_all(spread, 'depth', 0, 0, tiled=True)  4.7 us
    pallas_call x1, Pallas kernels, whole(): call(stride_body, [shape((2, 2, 128, 128)), shape((2, 2, 128, 128), jnp.f...  3.14 us
  transfers between devices with their start and end apart: 22, of which 7 were waited for; matrix products, arithmetic and copies ran while one was open for 4% of the time, Pallas kernels for 12%

profile of v1, /device:TPU:0, one launch (start us, length us, event | category | flops | bytes accessed | tf_op | source)
XLA Modules:
  0.0 139.7 jit_solution(14835608014987267514)
XLA Ops:
  0.6 0.0 copy-start.12
  0.6 1.0 copy.18
  1.6 1.3 collective-permute-start.16
  2.9 4.6 %collective-permute-start.15 = (bf16[2,8,32,128]{3,2,1,0:T(8,128)(2,1)S(1)}, bf16[2,8,32,128]{3,2,1,0:T(8,128)(2,1)S(1)}, u32[]{:S(2)}, u32[]{:S(2)}) collective-permute-start(bf16[2,8,32,128]{3,2,1,0:T(8,128)(2,1)S(1)} %bitcast.23), channel_id=1, source_target_pairs={{0,4},{1,5},{2,6},{3,7},{4,8},{5,9},{6,10},{7,11},{8,12},{9,13},{1... | collective-permute-start | bytes 393224 | tf_op jit(solution)/shard_map/ppermute | solution.py:35
  7.5 2.1 %collective-permute-start.1 = (bf16[8,32,64]{2,1,0:T(8,128)(2,1)}, bf16[8,32,64]{2,1,0:T(8,128)(2,1)S(1)}, u32[]{:S(2)}, u32[]{:S(2)}) collective-permute-start(bf16[8,32,64]{2,1,0:T(8,128)(2,1)} %s0.1), channel_id=1, source_target_pairs={{0,2},{1,3},{2,0},{3,1},{4,6},{5,7},{6,4},{7,5},{8,10},{9,11},{10,... | collective-permute-start | bytes 98312 | tf_op jit(solution)/shard_map/ppermute | solution.py:35
  9.6 0.0 collective-permute-start
  9.6 2.5 %collective-permute-done.1.s2 = bf16[8,32,64]{2,1,0:T(8,128)(2,1)S(1)} collective-permute-done((bf16[8,32,64]{2,1,0:T(8,128)(2,1)}, bf16[8,32,64]{2,1,0:T(8,128)(2,1)S(1)}, u32[]{:S(2)}, u32[]{:S(2)}) %collective-permute-start.1) | collective-permute-done | bytes 32800 | tf_op jit(solution)/shard_map/ppermute | solution.py:35
  12.1 0.0 collective-permute-start.2
  12.1 2.0 %copy.17 = bf16[64,4,4,256]{3,0,2,1:T(8,128)(2,1)} copy(bf16[64,4,4,256]{3,2,1,0:T(4,128)(2,1)} %param.5) | data formatting | bytes 1048576 | tf_op args[0]
  14.1 0.7 stack.22.info
  14.8 0.0 copy-start.8
  14.8 0.6 copy-done.7
  15.4 0.0 copy-done.8
  15.4 3.1 %shard_map.84 = (bf16[2,2,128,128]{3,2,1,0:T(8,128)(2,1)}, f32[2,2,128,128]{3,2,1,0:T(8,128)}, bf16[512,512]{1,0:T(8,128)(2,1)}) custom-call(s32[5]{0:T(128)} %stack.22.info, bf16[4,4,64,256]{3,2,1,0:T(8,128)(2,1)} %bitcast.19, bf16[8,32,64]{2,1,0:T(8,128)(2,1)} %s0.1, bf16[8,32,64]{2,1,0:T(8,128)(2,1)} %copy-done.7, bf16[8,32,64]{2,1,0:T(8,128)(2,1)} %copy-done.6, ...), custom_call_target="tpu_custom_call" | custom-call | flops 200000000 | bytes 1500000 | tf_op jit(solution)/shard_map/pallas_call | solution.py:337
  18.5 3.7 %collective-permute-start.3 = (bf16[2,2,128,128]{3,2,1,0:T(8,128)(2,1)}, bf16[2,2,128,128]{3,2,1,0:T(8,128)(2,1)S(1)}, u32[]{:S(2)}, u32[]{:S(2)}) collective-permute-start(bf16[2,2,128,128]{3,2,1,0:T(8,128)(2,1)} %get-tuple-element.15), channel_id=1, source_target_pairs={{0,4},{1,5},{2,6},{3,7},{4,8},{5,9},{6,10},{7,11},{8,12},{9,13},{1... | collective-permute-start | bytes 393224 | tf_op jit(solution)/shard_map/ppermute | solution.py:35
  22.3 2.0 %collective-permute-start.8 = (bf16[27,32,128]{2,1,0:T(8,128)(2,1)S(1)}, bf16[27,32,128]{2,1,0:T(8,128)(2,1)S(1)}, u32[]{:S(2)}, u32[]{:S(2)}) collective-permute-start(bf16[27,32,128]{2,1,0:T(8,128)(2,1)S(1)} %copy-done.12), channel_id=1, source_target_pairs={{0,2},{1,3},{2,0},{3,1},{4,6},{5,7},{6,4},{7,5},{8,10},{9,11},{10,... | collective-permute-start | bytes 663560 | tf_op jit(solution)/shard_map/ppermute | solution.py:35
  24.3 0.0 collective-permute-start.7
  24.3 0.0 collective-permute-done.16
  24.3 1.3 collective-permute-start.4
  25.6 0.3 collective-permute-done.3
  26.0 0.9 constant_dynamic-update-slice_fusion.1
  26.9 5.4 %collective-permute-done.4 = bf16[2,2,128,128]{3,2,1,0:T(8,128)(2,1)S(1)} collective-permute-done((bf16[2,2,128,128]{3,2,1,0:T(8,128)(2,1)}, bf16[2,2,128,128]{3,2,1,0:T(8,128)(2,1)S(1)}, u32[]{:S(2)}, u32[]{:S(2)}) %collective-permute-start.4) | collective-permute-done | bytes 131104 | tf_op jit(solution)/shard_map/ppermute | solution.py:35
  32.3 0.0 copy-start.9
  32.3 1.3 collective-permute-start.6
  33.6 3.1 %collective-permute-start.5 = (bf16[6,2,128,128]{3,2,1,0:T(8,128)(2,1)S(1)}, bf16[6,2,128,128]{3,2,1,0:T(8,128)(2,1)S(1)}, u32[]{:S(2)}, u32[]{:S(2)}) collective-permute-start(bf16[6,2,128,128]{3,2,1,0:T(8,128)(2,1)S(1)} %constant_dynamic-update-slice_fusion.mid.act_m), channel_id=1, source_target_pairs={{0,1},{1,2},{2,3},{4,5},{5,6},{6,7},{8,9},{9,10},{10,11},{12,13},{... | collective-permute-start | bytes 1179656 | tf_op jit(solution)/shard_map/ppermute | solution.py:35
  36.7 0.8 collective-permute-start.18
  37.5 0.0 collective-permute-done.8.m2
  37.5 0.2 collective-permute-start.9
  37.8 0.3 collective-permute-start.17
  38.1 9.5 %collective-permute-done.18.far = bf16[6,6,32,128]{3,2,1,0:T(8,128)(2,1)S(1)} collective-permute-done((bf16[6,6,32,128]{3,2,1,0:T(8,128)(2,1)S(1)}, bf16[6,6,32,128]{3,2,1,0:T(8,128)(2,1)S(1)}, u32[]{:S(2)}, u32[]{:S(2)}) %collective-permute-start.18) | collective-permute-done | bytes 294944 | tf_op jit(solution)/shard_map/ppermute | solution.py:35
  47.5 1.0 collective-permute-start.19
  48.6 6.1 %collective-permute-start.12 = (bf16[27,32,128]{2,1,0:T(8,128)(2,1)S(1)}, bf16[27,32,128]{2,1,0:T(8,128)(2,1)S(1)}, u32[]{:S(2)}, u32[]{:S(2)}) collective-permute-start(bf16[27,32,128]{2,1,0:T(8,128)(2,1)S(1)} %copy-done.13), channel_id=1, source_target_pairs={{0,19},{1,18},{2,17},{3,16},{4,23},{5,22},{6,21},{7,20},{8,27},{9,... | collective-permute-start | bytes 663560 | tf_op jit(solution)/shard_map/ppermute | solution.py:35
  54.6 0.0 collective-permute-done.6.right.act_r
  54.6 0.5 collective-permute-start.11
  55.1 0.0 collective-permute-done.5.left.act_l
  55.1 0.1 collective-permute-start.10
  55.2 0.1 copy-done.10
  55.4 0.5 copy-done.11
  55.9 6.4 %shard_map.85 = (bf16[4,4,128,128]{3,2,1,0:T(8,128)(2,1)}, f32[4,4,128,128]{3,2,1,0:T(8,128)}) custom-call(s32[5]{0:T(128)} %stack.22.info, bf16[6,2,128,128]{3,2,1,0:T(8,128)(2,1)} %copy-done.11, bf16[6,2,128,128]{3,2,1,0:T(8,128)(2,1)} %copy-done.9, bf16[6,2,128,128]{3,2,1,0:T(8,128)(2,1)} %copy-done.10, bf16[27,32,128]{2,1,0:T(8,128)(2,1)} %m0.3, ...), custom_call_target="tpu_custom_call" | custom-call | flops 3000000000 | bytes 4000000 | tf_op jit(solution)/shard_map/pallas_call | solution.py:347
  62.3 0.0 collective-permute-done.19.both
  62.3 0.7 copy-done.1
  63.1 0.7 copy-done.3
  63.8 2.8 %shard_map.88 = (bf16[6,6,128,128]{3,2,1,0:T(8,128)(2,1)}, bf16[2,2,128,128]{3,2,1,0:T(8,128)(2,1)}) custom-call(s32[5]{0:T(128)} %stack.22.info, bf16[6,8,32,128]{3,2,1,0:T(8,128)(2,1)} %copy-done, bf16[6,8,32,128]{3,2,1,0:T(8,128)(2,1)} %copy-done.1, bf16[6,6,32,128]{3,2,1,0:T(8,128)(2,1)} %copy-done.2, bf16[6,6,32,128]{3,2,1,0:T(8,128)(2,1)} %copy-done.3), custom_call_target="tpu_custom_call" | custom-call | flops 1000000 | bytes 3000000 | tf_op jit(solution)/shard_map/pallas_call | solution.py:327
  66.6 0.7 copy-done.16
  67.3 10.5 %shard_map.89 = (bf16[2,64,32,128]{3,2,1,0:T(8,128)(2,1)}, bf16[2,64,32,128]{3,2,1,0:T(8,128)(2,1)}) custom-call(s32[5]{0:T(128)} %stack.22.info, bf16[6,2,128,128]{3,2,1,0:T(8,128)(2,1)} %copy-done.11, bf16[6,2,128,128]{3,2,1,0:T(8,128)(2,1)} %copy-done.9, bf16[6,2,128,128]{3,2,1,0:T(8,128)(2,1)} %copy-done.10, ...), custom_call_target="tpu_custom_call" | custom-call | flops 4000000000 | bytes 8000000 | tf_op jit(solution)/shard_map/pallas_call | solution.py:370
  77.8 0.1 collective-permute-start.20
  78.0 2.7 %collective-permute-done.20 = bf16[2,64,32,128]{3,2,1,0:T(8,128)(2,1)S(1)} collective-permute-done((bf16[2,64,32,128]{3,2,1,0:T(8,128)(2,1)}, bf16[2,64,32,128]{3,2,1,0:T(8,128)(2,1)S(1)}, u32[]{:S(2)}, u32[]{:S(2)}) %collective-permute-start.20) | collective-permute-done | bytes 1048608 | tf_op jit(solution)/shard_map/ppermute | solution.py:35
  80.7 1.5 %add_convert_fusion = bf16[2,64,32,128]{3,2,1,0:T(8,128)(2,1)S(1)} fusion(bf16[2,64,32,128]{3,2,1,0:T(8,128)(2,1)S(1)} %collective-permute-done.20, bf16[2,64,32,128]{3,2,1,0:T(8,128)(2,1)} %get-tuple-element.24), kind=kLoop, calls=%fused_computation | loop fusion | flops 2097152 | bytes 3145728 | tf_op jit(solution)/shard_map/convert_element_type | solution.py:394
  82.2 35.9 %all_to_all.10 = bf16[64,64,128]{2,1,0:T(8,128)(2,1)S(1)} all-to-all(bf16[64,64,128]{2,1,0:T(8,128)(2,1)S(1)} %bitcast.18), channel_id=1, replica_groups=mesh['depth'=32,'chip'=2,'core'=2] {'chip','depth'}, dimensions={0} | all-to-all | bytes 2097152 | tf_op jit(solution)/shard_map/all_to_all | solution.py:395
  118.1 0.2 reduce_sum.12
  118.3 0.9 broadcast_in_dim.2
  119.2 4.7 %all-to-all-start.1 = ((bf16[32,64,128]{2,1,0:T(8,128)(2,1)}), bf16[32,64,128]{2,1,0:T(8,128)(2,1)S(1)}, u32[]{:S(2)}, u32[]{:S(2)}) async-start(bf16[32,64,128]{2,1,0:T(8,128)(2,1)} %broadcast_in_dim.2), calls=%async_computation.1 | async-start | bytes 1048576 | tf_op jit(solution)/shard_map/all_to_all | solution.py:398
  123.9 3.1 %shard_map.86 = (bf16[2,2,2,32,128]{4,3,2,1,0:T(8,128)(2,1)}, bf16[2,2,2,32,128]{4,3,2,1,0:T(8,128)(2,1)}) custom-call(s32[5]{0:T(128)} %stack.22.info, bf16[4,4,128,128]{3,2,1,0:T(8,128)(2,1)} %get-tuple-element.16.act_ref.mid_act, bf16[27,32,128]{2,1,0:T(8,128)(2,1)} %l0.3, bf16[27,32,128]{2,1,0:T(8,128)(2,1)} %collective-permute-done.10.l1, ...), custom_call_target="tpu_custom_call" | custom-call | flops 500000000 | bytes 2000000 | tf_op jit(solution)/shard_map/pallas_call | solution.py:359
  127.0 0.8 slice.21
  127.8 0.7 collective-permute-done.13.near
  128.5 1.1 collective-permute-start.14
  129.6 4.5 %collective-permute-done.14.far = bf16[2,2,2,32,128]{4,3,2,1,0:T(8,128)(2,1)S(1)} collective-permute-done((bf16[2,2,2,32,128]{4,3,2,1,0:T(8,128)(2,1)S(1)}, bf16[2,2,2,32,128]{4,3,2,1,0:T(8,128)(2,1)S(1)}, u32[]{:S(2)}, u32[]{:S(2)}) %collective-permute-start.14) | collective-permute-done | bytes 65568 | tf_op jit(solution)/shard_map/ppermute | solution.py:35
  134.1 0.6 copy-done.5
  134.7 1.6 %shard_map.87 = bf16[4,2,2,32,128]{4,3,2,1,0:T(8,128)(2,1)} custom-call(s32[5]{0:T(128)} %stack.22.info, bf16[2,2,2,32,128]{4,3,2,1,0:T(8,128)(2,1)} %get-tuple-element.17.own, bf16[2,2,2,32,128]{4,3,2,1,0:T(8,128)(2,1)} %copy-done.4, bf16[2,2,2,32,128]{4,3,2,1,0:T(8,128)(2,1)} %copy-done.5), custom_call_target="tpu_custom_call" | custom-call | tf_op jit(solution)/shard_map/pallas_call | solution.py:388
  136.3 0.9 copy.12
  137.2 0.7 copy.14
  137.9 0.1 fusion.1
  138.0 1.0 fusion
  139.0 0.7 pad_maximum_fusion.1
  (42 shorter events, 0.2 us)
Async XLA Ops:
  0.6 21.6 %copy-start.12 = (bf16[27,32,128]{2,1,0:T(8,128)(2,1)S(1)}, bf16[27,32,128]{2,1,0:T(8,128)(2,1)}, u32[]{:S(2)}) copy-start(bf16[27,32,128]{2,1,0:T(8,128)(2,1)} %m0.3) | copy-start | bytes 663556
  1.6 22.6 %collective-permute-start.16 = (bf16[2,8,32,128]{3,2,1,0:T(8,128)(2,1)S(1)}, bf16[2,8,32,128]{3,2,1,0:T(8,128)(2,1)S(1)}, u32[]{:S(2)}, u32[]{:S(2)}) collective-permute-start(bf16[2,8,32,128]{3,2,1,0:T(8,128)(2,1)S(1)} %bitcast.22), channel_id=1, source_target_pairs={{4,0},{5,1},{6,2},{7,3},{8,4},{9,5},{10,6},{11,7},{12,8},{13,9},{1... | collective-permute-start | bytes 393224 | tf_op jit(solution)/shard_map/ppermute | solution.py:35
  2.9 22.6 %collective-permute-start.15 = (bf16[2,8,32,128]{3,2,1,0:T(8,128)(2,1)S(1)}, bf16[2,8,32,128]{3,2,1,0:T(8,128)(2,1)S(1)}, u32[]{:S(2)}, u32[]{:S(2)}) collective-permute-start(bf16[2,8,32,128]{3,2,1,0:T(8,128)(2,1)S(1)} %bitcast.23), channel_id=1, source_target_pairs={{0,4},{1,5},{2,6},{3,7},{4,8},{5,9},{6,10},{7,11},{8,12},{9,13},{1... | collective-permute-start | bytes 393224 | tf_op jit(solution)/shard_map/ppermute | solution.py:35
  7.5 4.6 %collective-permute-start.1 = (bf16[8,32,64]{2,1,0:T(8,128)(2,1)}, bf16[8,32,64]{2,1,0:T(8,128)(2,1)S(1)}, u32[]{:S(2)}, u32[]{:S(2)}) collective-permute-start(bf16[8,32,64]{2,1,0:T(8,128)(2,1)} %s0.1), channel_id=1, source_target_pairs={{0,2},{1,3},{2,0},{3,1},{4,6},{5,7},{6,4},{7,5},{8,10},{9,11},{10,... | collective-permute-start | bytes 98312 | tf_op jit(solution)/shard_map/ppermute | solution.py:35
  9.6 5.1 %collective-permute-start = (bf16[8,32,64]{2,1,0:T(8,128)(2,1)}, bf16[8,32,64]{2,1,0:T(8,128)(2,1)S(1)}, u32[]{:S(2)}, u32[]{:S(2)}) collective-permute-start(bf16[8,32,64]{2,1,0:T(8,128)(2,1)} %s0.1), channel_id=1, source_target_pairs={{0,1},{1,0},{2,3},{3,2},{4,5},{5,4},{6,7},{7,6},{8,9},{9,8},{10,11... | collective-permute-start | bytes 98312 | tf_op jit(solution)/shard_map/ppermute | solution.py:35
  12.1 2.7 %copy-start.6 = (bf16[8,32,64]{2,1,0:T(8,128)(2,1)}, bf16[8,32,64]{2,1,0:T(8,128)(2,1)S(1)}, u32[]{:S(2)}) copy-start(bf16[8,32,64]{2,1,0:T(8,128)(2,1)S(1)} %collective-permute-done.1.s2) | copy-start | bytes 98308
  12.1 2.7 %collective-permute-start.2 = (bf16[8,32,64]{2,1,0:T(8,128)(2,1)S(1)}, bf16[8,32,64]{2,1,0:T(8,128)(2,1)S(1)}, u32[]{:S(2)}, u32[]{:S(2)}) collective-permute-start(bf16[8,32,64]{2,1,0:T(8,128)(2,1)S(1)} %collective-permute-done.1.s2), channel_id=1, source_target_pairs={{0,1},{1,0},{2,3},{3,2},{4,5},{5,4},{6,7},{7,6},{8,9},{9,8},{10,11... | collective-permute-start | bytes 98312 | tf_op jit(solution)/shard_map/ppermute | solution.py:35
  14.7 0.6 copy-start.7
  14.8 0.6 copy-start.8
  18.5 30.0 %copy-start.13 = (bf16[27,32,128]{2,1,0:T(8,128)(2,1)S(1)}, bf16[27,32,128]{2,1,0:T(8,128)(2,1)}, u32[]{:S(2)}) copy-start(bf16[27,32,128]{2,1,0:T(8,128)(2,1)} %l0.3) | copy-start | bytes 663556
  18.5 7.4 %collective-permute-start.3 = (bf16[2,2,128,128]{3,2,1,0:T(8,128)(2,1)}, bf16[2,2,128,128]{3,2,1,0:T(8,128)(2,1)S(1)}, u32[]{:S(2)}, u32[]{:S(2)}) collective-permute-start(bf16[2,2,128,128]{3,2,1,0:T(8,128)(2,1)} %get-tuple-element.15), channel_id=1, source_target_pairs={{0,4},{1,5},{2,6},{3,7},{4,8},{5,9},{6,10},{7,11},{8,12},{9,13},{1... | collective-permute-start | bytes 393224 | tf_op jit(solution)/shard_map/ppermute | solution.py:35
  22.3 15.3 %collective-permute-start.8 = (bf16[27,32,128]{2,1,0:T(8,128)(2,1)S(1)}, bf16[27,32,128]{2,1,0:T(8,128)(2,1)S(1)}, u32[]{:S(2)}, u32[]{:S(2)}) collective-permute-start(bf16[27,32,128]{2,1,0:T(8,128)(2,1)S(1)} %copy-done.12), channel_id=1, source_target_pairs={{0,2},{1,3},{2,0},{3,1},{4,6},{5,7},{6,4},{7,5},{8,10},{9,11},{10,... | collective-permute-start | bytes 663560 | tf_op jit(solution)/shard_map/ppermute | solution.py:35
  24.3 13.5 %collective-permute-start.7 = (bf16[27,32,128]{2,1,0:T(8,128)(2,1)S(1)}, bf16[27,32,128]{2,1,0:T(8,128)(2,1)S(1)}, u32[]{:S(2)}, u32[]{:S(2)}) collective-permute-start(bf16[27,32,128]{2,1,0:T(8,128)(2,1)S(1)} %copy-done.12), channel_id=1, source_target_pairs={{0,1},{1,0},{2,3},{3,2},{4,5},{5,4},{6,7},{7,6},{8,9},{9,8},{10,11... | collective-permute-start | bytes 663560 | tf_op jit(solution)/shard_map/ppermute | solution.py:35
  24.3 8.0 %collective-permute-start.4 = (bf16[2,2,128,128]{3,2,1,0:T(8,128)(2,1)}, bf16[2,2,128,128]{3,2,1,0:T(8,128)(2,1)S(1)}, u32[]{:S(2)}, u32[]{:S(2)}) collective-permute-start(bf16[2,2,128,128]{3,2,1,0:T(8,128)(2,1)} %get-tuple-element.15), channel_id=1, source_target_pairs={{4,0},{5,1},{6,2},{7,3},{8,4},{9,5},{10,6},{11,7},{12,8},{13,9},{1... | collective-permute-start | bytes 393224 | tf_op jit(solution)/shard_map/ppermute | solution.py:35
  25.6 36.7 %copy-start = (bf16[6,8,32,128]{3,2,1,0:T(8,128)(2,1)}, bf16[6,8,32,128]{3,2,1,0:T(8,128)(2,1)S(1)}, u32[]{:S(2)}) copy-start(bf16[6,8,32,128]{3,2,1,0:T(8,128)(2,1)S(1)} %pad_maximum_fusion.own) | copy-start | bytes 1179652
  32.3 23.0 %copy-start.9 = (bf16[6,2,128,128]{3,2,1,0:T(8,128)(2,1)}, bf16[6,2,128,128]{3,2,1,0:T(8,128)(2,1)S(1)}, u32[]{:S(2)}) copy-start(bf16[6,2,128,128]{3,2,1,0:T(8,128)(2,1)S(1)} %constant_dynamic-update-slice_fusion.mid.act_m) | copy-start | bytes 1179652
  32.3 22.3 %collective-permute-start.6 = (bf16[6,2,128,128]{3,2,1,0:T(8,128)(2,1)S(1)}, bf16[6,2,128,128]{3,2,1,0:T(8,128)(2,1)S(1)}, u32[]{:S(2)}, u32[]{:S(2)}) collective-permute-start(bf16[6,2,128,128]{3,2,1,0:T(8,128)(2,1)S(1)} %constant_dynamic-update-slice_fusion.mid.act_m), channel_id=1, source_target_pairs={{1,0},{2,1},{3,2},{5,4},{6,5},{7,6},{9,8},{10,9},{11,10},{13,12},{... | collective-permute-start | bytes 1179656 | tf_op jit(solution)/shard_map/ppermute | solution.py:35
  33.6 21.5 %collective-permute-start.5 = (bf16[6,2,128,128]{3,2,1,0:T(8,128)(2,1)S(1)}, bf16[6,2,128,128]{3,2,1,0:T(8,128)(2,1)S(1)}, u32[]{:S(2)}, u32[]{:S(2)}) collective-permute-start(bf16[6,2,128,128]{3,2,1,0:T(8,128)(2,1)S(1)} %constant_dynamic-update-slice_fusion.mid.act_m), channel_id=1, source_target_pairs={{0,1},{1,2},{2,3},{4,5},{5,6},{6,7},{8,9},{9,10},{10,11},{12,13},{... | collective-permute-start | bytes 1179656 | tf_op jit(solution)/shard_map/ppermute | solution.py:35
  36.7 10.8 %collective-permute-start.18 = (bf16[6,6,32,128]{3,2,1,0:T(8,128)(2,1)S(1)}, bf16[6,6,32,128]{3,2,1,0:T(8,128)(2,1)S(1)}, u32[]{:S(2)}, u32[]{:S(2)}) collective-permute-start(bf16[6,6,32,128]{3,2,1,0:T(8,128)(2,1)S(1)} %constant_dynamic-slice_fusion), channel_id=1, source_target_pairs={{0,2},{1,3},{2,0},{3,1},{4,6},{5,7},{6,4},{7,5},{8,10},{9,11},{10,... | collective-permute-start | bytes 884744 | tf_op jit(solution)/shard_map/ppermute | solution.py:35
  37.5 17.7 %copy-start.14 = (bf16[27,32,128]{2,1,0:T(8,128)(2,1)}, bf16[27,32,128]{2,1,0:T(8,128)(2,1)S(1)}, u32[]{:S(2)}) copy-start(bf16[27,32,128]{2,1,0:T(8,128)(2,1)S(1)} %collective-permute-done.8.m2) | copy-start | bytes 663556
  37.5 11.0 %collective-permute-start.9 = (bf16[27,32,128]{2,1,0:T(8,128)(2,1)S(1)}, bf16[27,32,128]{2,1,0:T(8,128)(2,1)S(1)}, u32[]{:S(2)}, u32[]{:S(2)}) collective-permute-start(bf16[27,32,128]{2,1,0:T(8,128)(2,1)S(1)} %collective-permute-done.8.m2), channel_id=1, source_target_pairs={{0,1},{1,0},{2,3},{3,2},{4,5},{5,4},{6,7},{7,6},{8,9},{9,8},{10,11... | collective-permute-start | bytes 663560 | tf_op jit(solution)/shard_map/ppermute | solution.py:35
  37.8 17.5 %copy-start.15 = (bf16[27,32,128]{2,1,0:T(8,128)(2,1)}, bf16[27,32,128]{2,1,0:T(8,128)(2,1)S(1)}, u32[]{:S(2)}) copy-start(bf16[27,32,128]{2,1,0:T(8,128)(2,1)S(1)} %collective-permute-done.7.m1) | copy-start | bytes 663556
  37.8 24.5 %collective-permute-start.17 = (bf16[6,8,32,128]{3,2,1,0:T(8,128)(2,1)S(1)}, bf16[6,8,32,128]{3,2,1,0:T(8,128)(2,1)S(1)}, u32[]{:S(2)}, u32[]{:S(2)}) collective-permute-start(bf16[6,8,32,128]{3,2,1,0:T(8,128)(2,1)S(1)} %pad_maximum_fusion.own), channel_id=1, source_target_pairs={{0,1},{1,0},{2,3},{3,2},{4,5},{5,4},{6,7},{7,6},{8,9},{9,8},{10,11... | collective-permute-start | bytes 1179656 | tf_op jit(solution)/shard_map/ppermute | solution.py:35
  47.5 14.8 %copy-start.2 = (bf16[6,6,32,128]{3,2,1,0:T(8,128)(2,1)}, bf16[6,6,32,128]{3,2,1,0:T(8,128)(2,1)S(1)}, u32[]{:S(2)}) copy-start(bf16[6,6,32,128]{3,2,1,0:T(8,128)(2,1)S(1)} %collective-permute-done.18.far) | copy-start | bytes 884740
  47.5 14.8 %collective-permute-start.19 = (bf16[6,6,32,128]{3,2,1,0:T(8,128)(2,1)S(1)}, bf16[6,6,32,128]{3,2,1,0:T(8,128)(2,1)S(1)}, u32[]{:S(2)}, u32[]{:S(2)}) collective-permute-start(bf16[6,6,32,128]{3,2,1,0:T(8,128)(2,1)S(1)} %collective-permute-done.18.far), channel_id=1, source_target_pairs={{0,1},{1,0},{2,3},{3,2},{4,5},{5,4},{6,7},{7,6},{8,9},{9,8},{10,11... | collective-permute-start | bytes 884744 | tf_op jit(solution)/shard_map/ppermute | solution.py:35
  48.6 6.6 %copy-start.17 = (bf16[27,32,128]{2,1,0:T(8,128)(2,1)}, bf16[27,32,128]{2,1,0:T(8,128)(2,1)S(1)}, u32[]{:S(2)}) copy-start(bf16[27,32,128]{2,1,0:T(8,128)(2,1)S(1)} %collective-permute-done.9.m3) | copy-start | bytes 663556
  48.6 18.0 %collective-permute-start.12 = (bf16[27,32,128]{2,1,0:T(8,128)(2,1)S(1)}, bf16[27,32,128]{2,1,0:T(8,128)(2,1)S(1)}, u32[]{:S(2)}, u32[]{:S(2)}) collective-permute-start(bf16[27,32,128]{2,1,0:T(8,128)(2,1)S(1)} %copy-done.13), channel_id=1, source_target_pairs={{0,19},{1,18},{2,17},{3,16},{4,23},{5,22},{6,21},{7,20},{8,27},{9,... | collective-permute-start | bytes 663560 | tf_op jit(solution)/shard_map/ppermute | solution.py:35
  54.6 0.7 copy-start.10
  54.6 12.0 %collective-permute-start.11 = (bf16[27,32,128]{2,1,0:T(8,128)(2,1)S(1)}, bf16[27,32,128]{2,1,0:T(8,128)(2,1)}, u32[]{:S(2)}, u32[]{:S(2)}) collective-permute-start(bf16[27,32,128]{2,1,0:T(8,128)(2,1)S(1)} %copy-done.13), channel_id=1, source_target_pairs={{0,18},{1,19},{2,16},{3,17},{4,22},{5,23},{6,20},{7,21},{8,26},{9,... | collective-permute-start | bytes 663560 | tf_op jit(solution)/shard_map/ppermute | solution.py:35
  55.1 0.7 copy-start.11
  55.1 11.5 %collective-permute-start.10 = (bf16[27,32,128]{2,1,0:T(8,128)(2,1)S(1)}, bf16[27,32,128]{2,1,0:T(8,128)(2,1)}, u32[]{:S(2)}, u32[]{:S(2)}) collective-permute-start(bf16[27,32,128]{2,1,0:T(8,128)(2,1)S(1)} %copy-done.13), channel_id=1, source_target_pairs={{0,1},{1,0},{2,3},{3,2},{4,5},{5,4},{6,7},{7,6},{8,9},{9,8},{10,11... | collective-permute-start | bytes 663560 | tf_op jit(solution)/shard_map/ppermute | solution.py:35
  62.3 0.8 copy-start.1
  63.1 0.7 copy-start.3
  66.6 0.7 copy-start.16
  77.8 2.9 %collective-permute-start.20 = (bf16[2,64,32,128]{3,2,1,0:T(8,128)(2,1)}, bf16[2,64,32,128]{3,2,1,0:T(8,128)(2,1)S(1)}, u32[]{:S(2)}, u32[]{:S(2)}) collective-permute-start(bf16[2,64,32,128]{3,2,1,0:T(8,128)(2,1)} %get-tuple-element.25), channel_id=1, source_target_pairs={{0,1},{1,0},{2,3},{3,2},{4,5},{5,4},{6,7},{7,6},{8,9},{9,8},{10,11... | collective-permute-start | bytes 3145736 | tf_op jit(solution)/shard_map/ppermute | solution.py:35
  119.2 18.8 %all-to-all-start.1 = ((bf16[32,64,128]{2,1,0:T(8,128)(2,1)}), bf16[32,64,128]{2,1,0:T(8,128)(2,1)S(1)}, u32[]{:S(2)}, u32[]{:S(2)}) async-start(bf16[32,64,128]{2,1,0:T(8,128)(2,1)} %broadcast_in_dim.2), calls=%async_computation.1 | async-start | bytes 1048576 | tf_op jit(solution)/shard_map/all_to_all | solution.py:398
  127.0 1.5 %collective-permute-start.13 = (bf16[2,2,2,32,128]{4,3,2,1,0:T(8,128)(2,1)}, bf16[2,2,2,32,128]{4,3,2,1,0:T(8,128)(2,1)S(1)}, u32[]{:S(2)}, u32[]{:S(2)}) collective-permute-start(bf16[2,2,2,32,128]{4,3,2,1,0:T(8,128)(2,1)} %get-tuple-element.18), channel_id=1, source_target_pairs={{0,1},{1,0},{2,3},{3,2},{4,5},{5,4},{6,7},{7,6},{8,9},{9,8},{10,11... | collective-permute-start | bytes 196616 | tf_op jit(solution)/shard_map/ppermute | solution.py:35
  128.5 5.6 %copy-start.4 = (bf16[2,2,2,32,128]{4,3,2,1,0:T(8,128)(2,1)}, bf16[2,2,2,32,128]{4,3,2,1,0:T(8,128)(2,1)S(1)}, u32[]{:S(2)}) copy-start(bf16[2,2,2,32,128]{4,3,2,1,0:T(8,128)(2,1)S(1)} %collective-permute-done.13.near) | copy-start | bytes 196612
  128.5 5.6 %collective-permute-start.14 = (bf16[2,2,2,32,128]{4,3,2,1,0:T(8,128)(2,1)S(1)}, bf16[2,2,2,32,128]{4,3,2,1,0:T(8,128)(2,1)S(1)}, u32[]{:S(2)}, u32[]{:S(2)}) collective-permute-start(bf16[2,2,2,32,128]{4,3,2,1,0:T(8,128)(2,1)S(1)} %pad_maximum_fusion.2), channel_id=1, source_target_pairs={{0,2},{1,3},{2,0},{3,1},{4,6},{5,7},{6,4},{7,5},{8,10},{9,11},{10,... | collective-permute-start | bytes 196616 | tf_op jit(solution)/shard_map/ppermute | solution.py:35
  134.1 0.6 copy-start.5

commit v2 on v1

--- a/solution.py
+++ b/solution.py
@@ -43,16 +43,13 @@
     return shifted(value, lambda d, f: (d, f ^ 2))
 
 
-def four_parts(value):
-    far = swap_chip(value)
+def four_parts(value, turn):
+    far = shifted(value, lambda d, f: (d ^ turn, f ^ 2))
     return [value, swap_core(value), far, swap_core(far)]
 
 
-def four_parts_across(value):
-    near = swap_core(value)
-    far = shifted(value, lambda d, f: (d ^ 4, f ^ 2))
-    both = shifted(value, lambda d, f: (d ^ 4, f ^ 3))
-    return [value, near, far, both]
+def four_parts_direct(value):
+    return [value] + [shifted(value, lambda d, f, step=step: (d, f ^ step)) for step in (1, 2, 3)]
 
 
 def call(body, out_shape, scratch=(), flops=0, moved=0, in_specs=None):
@@ -81,7 +78,7 @@
     )
 
 
-def stride_body(info, u_ref, s0, s1, s2, s3, act_ref, pre_ref, columns_ref, weights):
+def stride_body(info, u_ref, s0, s1, s2, s3, cot_ref, pack_ref, pre_ref, columns_ref, weights):
     filt = info[1]
     for j, part in enumerate((s0, s1, s2, s3)):
         start = pl.multiple_of((filt ^ j) * 32, 32)
@@ -104,7 +101,8 @@
             columns_ref[:, cell * 128 : cell * 128 + 128] = block
             pre = dot(weights[...], block).T
             pre_ref[p, r] = pre
-            act_ref[p, r] = (pre * jax.nn.sigmoid(pre)).astype(jnp.bfloat16)
+            pack_ref[p, r] = (pre * jax.nn.sigmoid(pre)).astype(jnp.bfloat16)
+    pack_ref[:, 2:4] = cot_ref[...]
 
 
 def turn_body(info, own, near, far, both, cells_ref, own_ref, tiles):
@@ -297,20 +295,13 @@
         put_grad(refs, n, jnp.zeros((128, 128), jnp.float32))
 
 
-def neighbourhood(block):
-    low = shifted(block, lambda d, f: (d + 1, f))
-    high = shifted(block, lambda d, f: (d - 1, f))
-    column = jnp.concatenate([low, block, high], axis=0)
+def row_parts(column):
     left = shifted(column, lambda d, f: (d, f + 1))
     right = shifted(column, lambda d, f: (d, f - 1))
     return left, column, right
 
 
-def cotangent_parts(cotangent, chip):
-    block = cotangent.transpose(1, 2, 0, 3)
-    low = shifted(block, lambda d, f: (d + 1, f))
-    high = shifted(block, lambda d, f: (d - 1, f))
-    column = jnp.concatenate([low, block, high], axis=0)
+def cotangent_parts(column, chip):
     wanted = lax.dynamic_slice_in_dim(column, 2 * (1 - chip), 6, axis=1)
     far = swap_chip(wanted)
     return column, swap_core(column), far, swap_core(far)
@@ -320,10 +311,24 @@
     depth = lax.axis_size("depth")
     chip, core = lax.axis_index("chip"), lax.axis_index("core")
     info = jnp.stack([lax.axis_index("depth"), 2 * chip + core, jnp.int32(depth), chip, core])
-    stride_parts = four_parts(stride_weight)
-    middle_parts = four_parts(middle_weight)
-    last_parts = four_parts_across(last_weight)
-    cot_parts = cotangent_parts(cotangent, chip)
+    stride_parts = four_parts_direct(stride_weight)
+    middle_parts = four_parts(middle_weight, 0)
+    last_parts = four_parts(last_weight, 4)
+    upper = upper_level.transpose(1, 2, 0, 3)
+    cot_rows = cotangent.transpose(1, 2, 0, 3).reshape(2, 2, 128, 128)
+    pack, level_pre, columns = call(
+        stride_body,
+        [shape((2, 4, 128, 128)), shape((2, 2, 128, 128), jnp.float32), shape((512, 512))],
+        [pltpu.VMEM((128, 512), jnp.bfloat16)],
+        flops=200_000_000,
+        moved=1_500_000,
+        in_specs=[SMEM] + [VMEM] * 6,
+    )(info, upper, *stride_parts, cot_rows)
+    low = shifted(pack, lambda d, f: (d + 1, f))
+    high = shifted(pack, lambda d, f: (d - 1, f))
+    act_near = row_parts(jnp.concatenate([x[:, :2] for x in (low, pack, high)], axis=0))
+    cot_column = jnp.concatenate([x[:, 2:] for x in (low, pack, high)], axis=0)
+    cot_parts = cotangent_parts(cot_column.reshape(6, 8, 32, 128), chip)
     cot_cells, cot_own = call(
         turn_body,
         [shape((6, 6, 128, 128)), shape((2, 2, 128, 128))],
@@ -332,17 +337,6 @@
         moved=3_000_000,
         in_specs=[SMEM] + [VMEM] * 4,
     )(info, *cot_parts)
-
-    upper = upper_level.transpose(1, 2, 0, 3)
-    level_act, level_pre, columns = call(
-        stride_body,
-        [shape((2, 2, 128, 128)), shape((2, 2, 128, 128), jnp.float32), shape((512, 512))],
-        [pltpu.VMEM((128, 512), jnp.bfloat16)],
-        flops=200_000_000,
-        moved=1_500_000,
-        in_specs=[SMEM] + [VMEM] * 5,
-    )(info, upper, *stride_parts)
-    act_near = neighbourhood(level_act)
 
     mid_act, mid_pre = call(
         middle_body,

time: 141 us -> 130 us (0.922)
  starting transfers between devices: 34.3 us -> 26.9 us
  waiting for transfers between devices: 25.6 us -> 21.9 us
  blocking collectives: 35.9 us -> 34 us
    ppermute x21 -> x19, starting transfers between devices: 29.6 us -> 22.1 us  [shifted(): return lax.ppermute(value, AXES, pairs_of(move))]
    ppermute x21 -> x19, waiting for transfers between devices: 25.6 us -> 21.9 us  [shifted(): return lax.ppermute(value, AXES, pairs_of(move))]
    all_to_all x1, blocking collectives: 35.9 us -> 34 us  [whole(): lax.all_to_all(terms.reshape(2 * depth, 64, 128), ('chip', 'depth'), 0, 0...]
    transpose x0 -> x1, local copies, waits for them, and re-layouts: none -> 1.59 us  [whole(): cot_rows = cotangent.transpose(1, 2, 0, 3).reshape(2, 2, 128, 128)]
    unnamed x41 -> x38, local copies, waits for them, and re-layouts: 8.66 us -> 7.37 us
  transfers between devices with their start and end apart: 22 -> 20, of which waited for: 7 -> 5; matrix products, arithmetic and copies ran while one was open for 4% -> 6% of each run, Pallas kernels for 12% -> 11%
where the time goes in v2:
time: 130 us; the launch traced here: 128 us
  blocking collectives  34 us (26%)
  Pallas kernels  27.7 us (21%)
  starting transfers between devices  26.9 us (21%)
  waiting for transfers between devices  21.9 us (17%)
  local copies, waits for them, and re-layouts  14.3 us (11%)
  other arithmetic  2.44 us (2%)
    all_to_all x1, blocking collectives, whole(): lax.all_to_all(terms.reshape(2 * depth, 64, 128), ('chip', 'depth'), 0, 0...  34 us
    ppermute x19, starting transfers between devices, shifted(): return lax.ppermute(value, AXES, pairs_of(move))  22.1 us
    ppermute x19, waiting for transfers between devices, shifted(): return lax.ppermute(value, AXES, pairs_of(move))  21.9 us
    pallas_call x1, Pallas kernels, whole(): call(back_body, [shape((2, 64, 32, 128)), shape((2, 64, 32, 128))], [pltp...  10.5 us
    unnamed x38, local copies, waits for them, and re-layouts  7.37 us
    pallas_call x1, Pallas kernels, whole(): call(middle_body, [shape((4, 4, 128, 128)), shape((4, 4, 128, 128), jnp.f...  6.4 us
    all_to_all x1, starting transfers between devices, whole(): full = lax.all_to_all(spread, 'depth', 0, 0, tiled=True)  4.78 us
    pallas_call x1, Pallas kernels, whole(): call(stride_body, [shape((2, 4, 128, 128)), shape((2, 2, 128, 128), jnp.f...  3.24 us
  transfers between devices with their start and end apart: 20, of which 5 were waited for; matrix products, arithmetic and copies ran while one was open for 6% of the time, Pallas kernels for 11%

profile of v2, /device:TPU:0, one launch (start us, length us, event | category | flops | bytes accessed | tf_op | source)
XLA Modules:
  0.0 128.1 jit_solution(18206814715301131121)
XLA Ops:
  0.6 0.0 copy-start.12
  0.6 0.0 copy-start.13
  0.7 2.1 %collective-permute-start.1 = (bf16[8,32,64]{2,1,0:T(8,128)(2,1)}, bf16[8,32,64]{2,1,0:T(8,128)(2,1)S(1)}, u32[]{:S(2)}, u32[]{:S(2)}) collective-permute-start(bf16[8,32,64]{2,1,0:T(8,128)(2,1)} %s0.1), channel_id=1, source_target_pairs={{0,2},{1,3},{2,0},{3,1},{4,6},{5,7},{6,4},{7,5},{8,10},{9,11},{10,... | collective-permute-start | bytes 98312 | tf_op jit(solution)/shard_map/ppermute | solution.py:35
  2.8 0.2 collective-permute-start.2
  3.0 1.6 %copy.12 = bf16[2,8,32,128]{3,2,1,0:T(8,128)(2,1)} copy(bf16[2,8,32,128]{3,1,0,2:T(8,128)(2,1)} %bitcast.26) | data formatting | bytes 262144 | tf_op jit(solution)/shard_map/transpose | solution.py:318
  4.6 2.0 %copy.16 = bf16[64,4,4,256]{3,0,2,1:T(8,128)(2,1)} copy(bf16[64,4,4,256]{3,2,1,0:T(4,128)(2,1)} %param.5) | data formatting | bytes 1048576 | tf_op args[0]
  6.6 0.6 stack.22.info
  7.2 0.0 collective-permute-done.1.s2
  7.2 0.0 copy-start.7
  7.2 0.0 collective-permute-done.2.s3
  7.2 0.6 copy-done.6
  7.8 0.0 copy-done.7
  7.8 0.0 copy-done.8
  7.8 3.2 %shard_map.84 = (bf16[2,4,128,128]{3,2,1,0:T(8,128)(2,1)}, f32[2,2,128,128]{3,2,1,0:T(8,128)}, bf16[512,512]{1,0:T(8,128)(2,1)}) custom-call(s32[5]{0:T(128)} %stack.22.info, bf16[4,4,64,256]{3,2,1,0:T(8,128)(2,1)} %bitcast.22, bf16[8,32,64]{2,1,0:T(8,128)(2,1)} %s0.1, bf16[8,32,64]{2,1,0:T(8,128)(2,1)} %copy-done.7, bf16[8,32,64]{2,1,0:T(8,128)(2,1)} %copy-done.6, ...), custom_call_target="tpu_custom_call" | custom-call | flops 200000000 | bytes 1500000 | tf_op jit(solution)/shard_map/pallas_call | solution.py:319
  11.1 1.3 collective-permute-start.4
  12.4 2.0 %collective-permute-start.8 = (bf16[27,32,128]{2,1,0:T(8,128)(2,1)S(1)}, bf16[27,32,128]{2,1,0:T(8,128)(2,1)S(1)}, u32[]{:S(2)}, u32[]{:S(2)}) collective-permute-start(bf16[27,32,128]{2,1,0:T(8,128)(2,1)S(1)} %copy-done.12), channel_id=1, source_target_pairs={{0,2},{1,3},{2,0},{3,1},{4,6},{5,7},{6,4},{7,5},{8,10},{9,11},{10,... | collective-permute-start | bytes 663560 | tf_op jit(solution)/shard_map/ppermute | solution.py:35
  14.4 0.0 collective-permute-start.7
  14.4 5.9 %collective-permute-start.11 = (bf16[27,32,128]{2,1,0:T(8,128)(2,1)S(1)}, bf16[27,32,128]{2,1,0:T(8,128)(2,1)S(1)}, u32[]{:S(2)}, u32[]{:S(2)}) collective-permute-start(bf16[27,32,128]{2,1,0:T(8,128)(2,1)S(1)} %copy-done.13), channel_id=1, source_target_pairs={{0,18},{1,19},{2,16},{3,17},{4,22},{5,23},{6,20},{7,21},{8,26},{9,... | collective-permute-start | bytes 663560 | tf_op jit(solution)/shard_map/ppermute | solution.py:35
  20.3 1.3 %collective-permute-start.3 = (bf16[2,4,128,128]{3,2,1,0:T(8,128)(2,1)}, bf16[2,4,128,128]{3,2,1,0:T(8,128)(2,1)S(1)}, u32[]{:S(2)}, u32[]{:S(2)}) collective-permute-start(bf16[2,4,128,128]{3,2,1,0:T(8,128)(2,1)} %get-tuple-element.15), channel_id=1, source_target_pairs={{0,4},{1,5},{2,6},{3,7},{4,8},{5,9},{6,10},{7,11},{8,12},{9,13},{1... | collective-permute-start | bytes 786440 | tf_op jit(solution)/shard_map/ppermute | solution.py:35
  21.6 1.0 fusion.3
  22.7 5.4 %collective-permute-done.3 = bf16[2,4,128,128]{3,2,1,0:T(8,128)(2,1)S(1)} collective-permute-done((bf16[2,4,128,128]{3,2,1,0:T(8,128)(2,1)}, bf16[2,4,128,128]{3,2,1,0:T(8,128)(2,1)S(1)}, u32[]{:S(2)}, u32[]{:S(2)}) %collective-permute-start.3) | collective-permute-done | bytes 262176 | tf_op jit(solution)/shard_map/ppermute | solution.py:35
  28.1 0.0 copy-start.1
  28.1 1.3 %collective-permute-start.6 = (bf16[6,2,128,128]{3,2,1,0:T(8,128)(2,1)S(1)}, bf16[6,2,128,128]{3,2,1,0:T(8,128)(2,1)S(1)}, u32[]{:S(2)}, u32[]{:S(2)}) collective-permute-start(bf16[6,2,128,128]{3,2,1,0:T(8,128)(2,1)S(1)} %pad_maximum_fusion.mid.act_m), channel_id=1, source_target_pairs={{1,0},{2,1},{3,2},{5,4},{6,5},{7,6},{9,8},{10,9},{11,10},{13,12},{... | collective-permute-start | bytes 1179656 | tf_op jit(solution)/shard_map/ppermute | solution.py:35
  29.4 3.1 %collective-permute-start.5 = (bf16[6,2,128,128]{3,2,1,0:T(8,128)(2,1)S(1)}, bf16[6,2,128,128]{3,2,1,0:T(8,128)(2,1)S(1)}, u32[]{:S(2)}, u32[]{:S(2)}) collective-permute-start(bf16[6,2,128,128]{3,2,1,0:T(8,128)(2,1)S(1)} %pad_maximum_fusion.mid.act_m), channel_id=1, source_target_pairs={{0,1},{1,2},{2,3},{4,5},{5,6},{6,7},{8,9},{9,10},{10,11},{12,13},{... | collective-permute-start | bytes 1179656 | tf_op jit(solution)/shard_map/ppermute | solution.py:35
  32.6 1.4 %collective-permute-start.16 = (bf16[6,6,32,128]{3,2,1,0:T(8,128)(2,1)S(1)}, bf16[6,6,32,128]{3,2,1,0:T(8,128)(2,1)S(1)}, u32[]{:S(2)}, u32[]{:S(2)}) collective-permute-start(bf16[6,6,32,128]{3,2,1,0:T(8,128)(2,1)S(1)} %constant_dynamic-slice_fusion), channel_id=1, source_target_pairs={{0,2},{1,3},{2,0},{3,1},{4,6},{5,7},{6,4},{7,5},{8,10},{9,11},{10,... | collective-permute-start | bytes 884744 | tf_op jit(solution)/shard_map/ppermute | solution.py:35
  34.0 0.0 collective-permute-start.9
  34.1 0.5 collective-permute-start.15
  34.6 0.2 copy-done.16
  34.7 8.7 %collective-permute-done.16.far = bf16[6,6,32,128]{3,2,1,0:T(8,128)(2,1)S(1)} collective-permute-done((bf16[6,6,32,128]{3,2,1,0:T(8,128)(2,1)S(1)}, bf16[6,6,32,128]{3,2,1,0:T(8,128)(2,1)S(1)}, u32[]{:S(2)}, u32[]{:S(2)}) %collective-permute-start.16) | collective-permute-done | bytes 294944 | tf_op jit(solution)/shard_map/ppermute | solution.py:35
  43.4 1.0 collective-permute-start.17
  44.4 0.0 collective-permute-done.9.m3
  44.5 0.1 collective-permute-start.10
  44.5 0.4 collective-permute-start.12
  45.0 0.3 copy-done.10
  45.3 0.7 copy-done.11
  46.0 6.4 %shard_map.85 = (bf16[4,4,128,128]{3,2,1,0:T(8,128)(2,1)}, f32[4,4,128,128]{3,2,1,0:T(8,128)}) custom-call(s32[5]{0:T(128)} %stack.22.info, bf16[6,2,128,128]{3,2,1,0:T(8,128)(2,1)} %copy-done.11, bf16[6,2,128,128]{3,2,1,0:T(8,128)(2,1)} %copy-done.1, bf16[6,2,128,128]{3,2,1,0:T(8,128)(2,1)} %copy-done.10, bf16[27,32,128]{2,1,0:T(8,128)(2,1)} %m0.3, ...), custom_call_target="tpu_custom_call" | custom-call | flops 3000000000 | bytes 4000000 | tf_op jit(solution)/shard_map/pallas_call | solution.py:341
  52.5 0.0 collective-permute-done.15.near
  52.5 0.0 collective-permute-done.17.both
  52.5 0.7 copy-done.2
  53.2 0.7 copy-done.4
  53.9 2.8 %shard_map.88 = (bf16[6,6,128,128]{3,2,1,0:T(8,128)(2,1)}, bf16[2,2,128,128]{3,2,1,0:T(8,128)(2,1)}) custom-call(s32[5]{0:T(128)} %stack.22.info, bf16[6,8,32,128]{3,2,1,0:T(8,128)(2,1)} %bitcast.21, bf16[6,8,32,128]{3,2,1,0:T(8,128)(2,1)} %copy-done.2, bf16[6,6,32,128]{3,2,1,0:T(8,128)(2,1)} %copy-done.3, bf16[6,6,32,128]{3,2,1,0:T(8,128)(2,1)} %copy-done.4), custom_call_target="tpu_custom_call" | custom-call | flops 1000000 | bytes 3000000 | tf_op jit(solution)/shard_map/pallas_call | solution.py:332
  56.7 0.0 collective-permute-done.10.l1
  56.7 0.0 collective-permute-done.12.l3
  56.8 0.7 copy-done.17
  57.4 10.5 %shard_map.89 = (bf16[2,64,32,128]{3,2,1,0:T(8,128)(2,1)}, bf16[2,64,32,128]{3,2,1,0:T(8,128)(2,1)}) custom-call(s32[5]{0:T(128)} %stack.22.info, bf16[6,2,128,128]{3,2,1,0:T(8,128)(2,1)} %copy-done.11, bf16[6,2,128,128]{3,2,1,0:T(8,128)(2,1)} %copy-done.1, bf16[6,2,128,128]{3,2,1,0:T(8,128)(2,1)} %copy-done.10, ...), custom_call_target="tpu_custom_call" | custom-call | flops 4000000000 | bytes 8000000 | tf_op jit(solution)/shard_map/pallas_call | solution.py:364
  68.0 0.5 collective-permute-start.18
  68.4 2.5 %collective-permute-done.18 = bf16[2,64,32,128]{3,2,1,0:T(8,128)(2,1)S(1)} collective-permute-done((bf16[2,64,32,128]{3,2,1,0:T(8,128)(2,1)}, bf16[2,64,32,128]{3,2,1,0:T(8,128)(2,1)S(1)}, u32[]{:S(2)}, u32[]{:S(2)}) %collective-permute-start.18) | collective-permute-done | bytes 1048608 | tf_op jit(solution)/shard_map/ppermute | solution.py:35
  70.9 1.5 %add_convert_fusion = bf16[2,64,32,128]{3,2,1,0:T(8,128)(2,1)S(1)} fusion(bf16[2,64,32,128]{3,2,1,0:T(8,128)(2,1)S(1)} %collective-permute-done.18, bf16[2,64,32,128]{3,2,1,0:T(8,128)(2,1)} %get-tuple-element.24), kind=kLoop, calls=%fused_computation | loop fusion | flops 2097152 | bytes 3145728 | tf_op jit(solution)/shard_map/convert_element_type | solution.py:388
  72.4 34.0 %all_to_all.10 = bf16[64,64,128]{2,1,0:T(8,128)(2,1)S(1)} all-to-all(bf16[64,64,128]{2,1,0:T(8,128)(2,1)S(1)} %bitcast.18), channel_id=1, replica_groups=mesh['depth'=32,'chip'=2,'core'=2] {'chip','depth'}, dimensions={0} | all-to-all | bytes 2097152 | tf_op jit(solution)/shard_map/all_to_all | solution.py:389
  106.4 0.2 reduce_sum.12
  106.6 0.9 broadcast_in_dim.2
  107.5 4.8 %all-to-all-start.1 = ((bf16[32,64,128]{2,1,0:T(8,128)(2,1)}), bf16[32,64,128]{2,1,0:T(8,128)(2,1)S(1)}, u32[]{:S(2)}, u32[]{:S(2)}) async-start(bf16[32,64,128]{2,1,0:T(8,128)(2,1)} %broadcast_in_dim.2), calls=%async_computation.1 | async-start | bytes 1048576 | tf_op jit(solution)/shard_map/all_to_all | solution.py:392
  112.3 3.1 %shard_map.86 = (bf16[2,2,2,32,128]{4,3,2,1,0:T(8,128)(2,1)}, bf16[2,2,2,32,128]{4,3,2,1,0:T(8,128)(2,1)}) custom-call(s32[5]{0:T(128)} %stack.22.info, bf16[4,4,128,128]{3,2,1,0:T(8,128)(2,1)} %get-tuple-element.16.act_ref.mid_act, bf16[27,32,128]{2,1,0:T(8,128)(2,1)} %l0.3, bf16[27,32,128]{2,1,0:T(8,128)(2,1)} %copy-done.17, ...), custom_call_target="tpu_custom_call" | custom-call | flops 500000000 | bytes 2000000 | tf_op jit(solution)/shard_map/pallas_call | solution.py:353
  115.4 0.8 slice.42
  116.2 0.7 collective-permute-done.13.near
  116.9 1.0 collective-permute-start.14
  118.0 4.6 %collective-permute-done.14.far = bf16[2,2,2,32,128]{4,3,2,1,0:T(8,128)(2,1)S(1)} collective-permute-done((bf16[2,2,2,32,128]{4,3,2,1,0:T(8,128)(2,1)S(1)}, bf16[2,2,2,32,128]{4,3,2,1,0:T(8,128)(2,1)S(1)}, u32[]{:S(2)}, u32[]{:S(2)}) %collective-permute-start.14) | collective-permute-done | bytes 65568 | tf_op jit(solution)/shard_map/ppermute | solution.py:35
  122.5 0.6 copy-done.9
  123.2 1.6 %shard_map.87 = bf16[4,2,2,32,128]{4,3,2,1,0:T(8,128)(2,1)} custom-call(s32[5]{0:T(128)} %stack.22.info, bf16[2,2,2,32,128]{4,3,2,1,0:T(8,128)(2,1)} %get-tuple-element.17.own, bf16[2,2,2,32,128]{4,3,2,1,0:T(8,128)(2,1)} %copy-done.5, bf16[2,2,2,32,128]{4,3,2,1,0:T(8,128)(2,1)} %copy-done.9), custom_call_target="tpu_custom_call" | custom-call | tf_op jit(solution)/shard_map/pallas_call | solution.py:382
  124.8 0.9 copy.13
  125.7 0.7 copy.14
  126.4 0.1 fusion.1
  126.5 1.0 fusion
  127.5 0.7 pad_maximum_fusion.2
  (39 shorter events, 0.2 us)
Async XLA Ops:
  0.6 11.7 %copy-start.12 = (bf16[27,32,128]{2,1,0:T(8,128)(2,1)S(1)}, bf16[27,32,128]{2,1,0:T(8,128)(2,1)}, u32[]{:S(2)}) copy-start(bf16[27,32,128]{2,1,0:T(8,128)(2,1)} %m0.3) | copy-start | bytes 663556
  0.6 13.8 %copy-start.13 = (bf16[27,32,128]{2,1,0:T(8,128)(2,1)S(1)}, bf16[27,32,128]{2,1,0:T(8,128)(2,1)}, u32[]{:S(2)}) copy-start(bf16[27,32,128]{2,1,0:T(8,128)(2,1)} %l0.3) | copy-start | bytes 663556
  0.7 6.5 %collective-permute-start.1 = (bf16[8,32,64]{2,1,0:T(8,128)(2,1)}, bf16[8,32,64]{2,1,0:T(8,128)(2,1)S(1)}, u32[]{:S(2)}, u32[]{:S(2)}) collective-permute-start(bf16[8,32,64]{2,1,0:T(8,128)(2,1)} %s0.1), channel_id=1, source_target_pairs={{0,2},{1,3},{2,0},{3,1},{4,6},{5,7},{6,4},{7,5},{8,10},{9,11},{10,... | collective-permute-start | bytes 98312 | tf_op jit(solution)/shard_map/ppermute | solution.py:35
  2.8 4.4 %collective-permute-start = (bf16[8,32,64]{2,1,0:T(8,128)(2,1)}, bf16[8,32,64]{2,1,0:T(8,128)(2,1)S(1)}, u32[]{:S(2)}, u32[]{:S(2)}) collective-permute-start(bf16[8,32,64]{2,1,0:T(8,128)(2,1)} %s0.1), channel_id=1, source_target_pairs={{0,1},{1,0},{2,3},{3,2},{4,5},{5,4},{6,7},{7,6},{8,9},{9,8},{10,11... | collective-permute-start | bytes 98312 | tf_op jit(solution)/shard_map/ppermute | solution.py:35
  2.8 4.4 %collective-permute-start.2 = (bf16[8,32,64]{2,1,0:T(8,128)(2,1)}, bf16[8,32,64]{2,1,0:T(8,128)(2,1)S(1)}, u32[]{:S(2)}, u32[]{:S(2)}) collective-permute-start(bf16[8,32,64]{2,1,0:T(8,128)(2,1)} %s0.1), channel_id=1, source_target_pairs={{0,3},{1,2},{2,1},{3,0},{4,7},{5,6},{6,5},{7,4},{8,11},{9,10},{10,... | collective-permute-start | bytes 98312 | tf_op jit(solution)/shard_map/ppermute | solution.py:35
  7.2 0.6 copy-start.6
  7.2 0.6 copy-start.7
  7.2 0.6 copy-start.8
  11.1 11.5 %collective-permute-start.4 = (bf16[2,4,128,128]{3,2,1,0:T(8,128)(2,1)}, bf16[2,4,128,128]{3,2,1,0:T(8,128)(2,1)S(1)}, u32[]{:S(2)}, u32[]{:S(2)}) collective-permute-start(bf16[2,4,128,128]{3,2,1,0:T(8,128)(2,1)} %get-tuple-element.15), channel_id=1, source_target_pairs={{4,0},{5,1},{6,2},{7,3},{8,4},{9,5},{10,6},{11,7},{12,8},{13,9},{1... | collective-permute-start | bytes 786440 | tf_op jit(solution)/shard_map/ppermute | solution.py:35
  12.4 20.2 %collective-permute-start.8 = (bf16[27,32,128]{2,1,0:T(8,128)(2,1)S(1)}, bf16[27,32,128]{2,1,0:T(8,128)(2,1)S(1)}, u32[]{:S(2)}, u32[]{:S(2)}) collective-permute-start(bf16[27,32,128]{2,1,0:T(8,128)(2,1)S(1)} %copy-done.12), channel_id=1, source_target_pairs={{0,2},{1,3},{2,0},{3,1},{4,6},{5,7},{6,4},{7,5},{8,10},{9,11},{10,... | collective-permute-start | bytes 663560 | tf_op jit(solution)/shard_map/ppermute | solution.py:35
  14.4 19.6 %collective-permute-start.7 = (bf16[27,32,128]{2,1,0:T(8,128)(2,1)S(1)}, bf16[27,32,128]{2,1,0:T(8,128)(2,1)S(1)}, u32[]{:S(2)}, u32[]{:S(2)}) collective-permute-start(bf16[27,32,128]{2,1,0:T(8,128)(2,1)S(1)} %copy-done.12), channel_id=1, source_target_pairs={{0,1},{1,0},{2,3},{3,2},{4,5},{5,4},{6,7},{7,6},{8,9},{9,8},{10,11... | collective-permute-start | bytes 663560 | tf_op jit(solution)/shard_map/ppermute | solution.py:35
  14.4 19.6 %collective-permute-start.11 = (bf16[27,32,128]{2,1,0:T(8,128)(2,1)S(1)}, bf16[27,32,128]{2,1,0:T(8,128)(2,1)S(1)}, u32[]{:S(2)}, u32[]{:S(2)}) collective-permute-start(bf16[27,32,128]{2,1,0:T(8,128)(2,1)S(1)} %copy-done.13), channel_id=1, source_target_pairs={{0,18},{1,19},{2,16},{3,17},{4,22},{5,23},{6,20},{7,21},{8,26},{9,... | collective-permute-start | bytes 663560 | tf_op jit(solution)/shard_map/ppermute | solution.py:35
  20.3 7.7 %collective-permute-start.3 = (bf16[2,4,128,128]{3,2,1,0:T(8,128)(2,1)}, bf16[2,4,128,128]{3,2,1,0:T(8,128)(2,1)S(1)}, u32[]{:S(2)}, u32[]{:S(2)}) collective-permute-start(bf16[2,4,128,128]{3,2,1,0:T(8,128)(2,1)} %get-tuple-element.15), channel_id=1, source_target_pairs={{0,4},{1,5},{2,6},{3,7},{4,8},{5,9},{6,10},{7,11},{8,12},{9,13},{1... | collective-permute-start | bytes 786440 | tf_op jit(solution)/shard_map/ppermute | solution.py:35
  28.1 16.8 %copy-start.1 = (bf16[6,2,128,128]{3,2,1,0:T(8,128)(2,1)}, bf16[6,2,128,128]{3,2,1,0:T(8,128)(2,1)S(1)}, u32[]{:S(2)}) copy-start(bf16[6,2,128,128]{3,2,1,0:T(8,128)(2,1)S(1)} %pad_maximum_fusion.mid.act_m) | copy-start | bytes 1179652
  28.1 16.4 %collective-permute-start.6 = (bf16[6,2,128,128]{3,2,1,0:T(8,128)(2,1)S(1)}, bf16[6,2,128,128]{3,2,1,0:T(8,128)(2,1)S(1)}, u32[]{:S(2)}, u32[]{:S(2)}) collective-permute-start(bf16[6,2,128,128]{3,2,1,0:T(8,128)(2,1)S(1)} %pad_maximum_fusion.mid.act_m), channel_id=1, source_target_pairs={{1,0},{2,1},{3,2},{5,4},{6,5},{7,6},{9,8},{10,9},{11,10},{13,12},{... | collective-permute-start | bytes 1179656 | tf_op jit(solution)/shard_map/ppermute | solution.py:35
  29.4 15.5 %collective-permute-start.5 = (bf16[6,2,128,128]{3,2,1,0:T(8,128)(2,1)S(1)}, bf16[6,2,128,128]{3,2,1,0:T(8,128)(2,1)S(1)}, u32[]{:S(2)}, u32[]{:S(2)}) collective-permute-start(bf16[6,2,128,128]{3,2,1,0:T(8,128)(2,1)S(1)} %pad_maximum_fusion.mid.act_m), channel_id=1, source_target_pairs={{0,1},{1,2},{2,3},{4,5},{5,6},{6,7},{8,9},{9,10},{10,11},{12,13},{... | collective-permute-start | bytes 1179656 | tf_op jit(solution)/shard_map/ppermute | solution.py:35
  32.6 19.9 %copy-start = (bf16[6,2,128,128]{3,2,1,0:T(8,128)(2,1)}, bf16[6,2,128,128]{3,2,1,0:T(8,128)(2,1)S(1)}, u32[]{:S(2)}) copy-start(bf16[6,2,128,128]{3,2,1,0:T(8,128)(2,1)S(1)} %pad_maximum_fusion.1) | copy-start | bytes 1179652
  32.6 12.4 %copy-start.15 = (bf16[27,32,128]{2,1,0:T(8,128)(2,1)}, bf16[27,32,128]{2,1,0:T(8,128)(2,1)S(1)}, u32[]{:S(2)}) copy-start(bf16[27,32,128]{2,1,0:T(8,128)(2,1)S(1)} %collective-permute-done.8.m2) | copy-start | bytes 663556
  32.6 10.8 %collective-permute-start.16 = (bf16[6,6,32,128]{3,2,1,0:T(8,128)(2,1)S(1)}, bf16[6,6,32,128]{3,2,1,0:T(8,128)(2,1)S(1)}, u32[]{:S(2)}, u32[]{:S(2)}) collective-permute-start(bf16[6,6,32,128]{3,2,1,0:T(8,128)(2,1)S(1)} %constant_dynamic-slice_fusion), channel_id=1, source_target_pairs={{0,2},{1,3},{2,0},{3,1},{4,6},{5,7},{6,4},{7,5},{8,10},{9,11},{10,... | collective-permute-start | bytes 884744 | tf_op jit(solution)/shard_map/ppermute | solution.py:35
  34.0 0.7 copy-start.16
  34.0 10.4 %collective-permute-start.9 = (bf16[27,32,128]{2,1,0:T(8,128)(2,1)S(1)}, bf16[27,32,128]{2,1,0:T(8,128)(2,1)}, u32[]{:S(2)}, u32[]{:S(2)}) collective-permute-start(bf16[27,32,128]{2,1,0:T(8,128)(2,1)S(1)} %collective-permute-done.8.m2), channel_id=1, source_target_pairs={{0,1},{1,0},{2,3},{3,2},{4,5},{5,4},{6,7},{7,6},{8,9},{9,8},{10,11... | collective-permute-start | bytes 663560 | tf_op jit(solution)/shard_map/ppermute | solution.py:35
  34.0 18.4 %copy-start.14 = (bf16[27,32,128]{2,1,0:T(8,128)(2,1)}, bf16[27,32,128]{2,1,0:T(8,128)(2,1)S(1)}, u32[]{:S(2)}) copy-start(bf16[27,32,128]{2,1,0:T(8,128)(2,1)S(1)} %collective-permute-done.11.l2) | copy-start | bytes 663556
  34.1 18.4 %collective-permute-start.15 = (bf16[6,8,32,128]{3,2,1,0:T(8,128)(2,1)S(1)}, bf16[6,8,32,128]{3,2,1,0:T(8,128)(2,1)S(1)}, u32[]{:S(2)}, u32[]{:S(2)}) collective-permute-start(bf16[6,8,32,128]{3,2,1,0:T(8,128)(2,1)S(1)} %bitcast.20), channel_id=1, source_target_pairs={{0,1},{1,0},{2,3},{3,2},{4,5},{5,4},{6,7},{7,6},{8,9},{9,8},{10,11... | collective-permute-start | bytes 1179656 | tf_op jit(solution)/shard_map/ppermute | solution.py:35
  43.4 9.0 %copy-start.3 = (bf16[6,6,32,128]{3,2,1,0:T(8,128)(2,1)}, bf16[6,6,32,128]{3,2,1,0:T(8,128)(2,1)S(1)}, u32[]{:S(2)}) copy-start(bf16[6,6,32,128]{3,2,1,0:T(8,128)(2,1)S(1)} %collective-permute-done.16.far) | copy-start | bytes 884740
  43.4 9.0 %collective-permute-start.17 = (bf16[6,6,32,128]{3,2,1,0:T(8,128)(2,1)S(1)}, bf16[6,6,32,128]{3,2,1,0:T(8,128)(2,1)S(1)}, u32[]{:S(2)}, u32[]{:S(2)}) collective-permute-start(bf16[6,6,32,128]{3,2,1,0:T(8,128)(2,1)S(1)} %collective-permute-done.16.far), channel_id=1, source_target_pairs={{0,1},{1,0},{2,3},{3,2},{4,5},{5,4},{6,7},{7,6},{8,9},{9,8},{10,11... | collective-permute-start | bytes 884744 | tf_op jit(solution)/shard_map/ppermute | solution.py:35
  44.5 12.3 %collective-permute-start.10 = (bf16[27,32,128]{2,1,0:T(8,128)(2,1)S(1)}, bf16[27,32,128]{2,1,0:T(8,128)(2,1)S(1)}, u32[]{:S(2)}, u32[]{:S(2)}) collective-permute-start(bf16[27,32,128]{2,1,0:T(8,128)(2,1)S(1)} %copy-done.13), channel_id=1, source_target_pairs={{0,1},{1,0},{2,3},{3,2},{4,5},{5,4},{6,7},{7,6},{8,9},{9,8},{10,11... | collective-permute-start | bytes 663560 | tf_op jit(solution)/shard_map/ppermute | solution.py:35
  44.5 0.8 copy-start.10
  44.5 12.2 %collective-permute-start.12 = (bf16[27,32,128]{2,1,0:T(8,128)(2,1)S(1)}, bf16[27,32,128]{2,1,0:T(8,128)(2,1)}, u32[]{:S(2)}, u32[]{:S(2)}) collective-permute-start(bf16[27,32,128]{2,1,0:T(8,128)(2,1)S(1)} %collective-permute-done.11.l2), channel_id=1, source_target_pairs={{0,1},{1,0},{2,3},{3,2},{4,5},{5,4},{6,7},{7,6},{8,9},{9,8},{10,11... | collective-permute-start | bytes 663560 | tf_op jit(solution)/shard_map/ppermute | solution.py:35
  45.3 0.7 copy-start.11
  52.5 0.8 copy-start.2
  53.2 0.7 copy-start.4
  56.7 0.7 copy-start.17
  68.0 3.0 %collective-permute-start.18 = (bf16[2,64,32,128]{3,2,1,0:T(8,128)(2,1)}, bf16[2,64,32,128]{3,2,1,0:T(8,128)(2,1)S(1)}, u32[]{:S(2)}, u32[]{:S(2)}) collective-permute-start(bf16[2,64,32,128]{3,2,1,0:T(8,128)(2,1)} %get-tuple-element.25), channel_id=1, source_target_pairs={{0,1},{1,0},{2,3},{3,2},{4,5},{5,4},{6,7},{7,6},{8,9},{9,8},{10,11... | collective-permute-start | bytes 3145736 | tf_op jit(solution)/shard_map/ppermute | solution.py:35
  107.5 18.9 %all-to-all-start.1 = ((bf16[32,64,128]{2,1,0:T(8,128)(2,1)}), bf16[32,64,128]{2,1,0:T(8,128)(2,1)S(1)}, u32[]{:S(2)}, u32[]{:S(2)}) async-start(bf16[32,64,128]{2,1,0:T(8,128)(2,1)} %broadcast_in_dim.2), calls=%async_computation.1 | async-start | bytes 1048576 | tf_op jit(solution)/shard_map/all_to_all | solution.py:392
  115.4 1.5 %collective-permute-start.13 = (bf16[2,2,2,32,128]{4,3,2,1,0:T(8,128)(2,1)}, bf16[2,2,2,32,128]{4,3,2,1,0:T(8,128)(2,1)S(1)}, u32[]{:S(2)}, u32[]{:S(2)}) collective-permute-start(bf16[2,2,2,32,128]{4,3,2,1,0:T(8,128)(2,1)} %get-tuple-element.18), channel_id=1, source_target_pairs={{0,1},{1,0},{2,3},{3,2},{4,5},{5,4},{6,7},{7,6},{8,9},{9,8},{10,11... | collective-permute-start | bytes 196616 | tf_op jit(solution)/shard_map/ppermute | solution.py:35
  116.9 5.7 %copy-start.5 = (bf16[2,2,2,32,128]{4,3,2,1,0:T(8,128)(2,1)}, bf16[2,2,2,32,128]{4,3,2,1,0:T(8,128)(2,1)S(1)}, u32[]{:S(2)}) copy-start(bf16[2,2,2,32,128]{4,3,2,1,0:T(8,128)(2,1)S(1)} %collective-permute-done.13.near) | copy-start | bytes 196612
  116.9 5.6 %collective-permute-start.14 = (bf16[2,2,2,32,128]{4,3,2,1,0:T(8,128)(2,1)S(1)}, bf16[2,2,2,32,128]{4,3,2,1,0:T(8,128)(2,1)S(1)}, u32[]{:S(2)}, u32[]{:S(2)}) collective-permute-start(bf16[2,2,2,32,128]{4,3,2,1,0:T(8,128)(2,1)S(1)} %pad_maximum_fusion.3), channel_id=1, source_target_pairs={{0,2},{1,3},{2,0},{3,1},{4,6},{5,7},{6,4},{7,5},{8,10},{9,11},{10,... | collective-permute-start | bytes 196616 | tf_op jit(solution)/shard_map/ppermute | solution.py:35
  122.5 0.6 copy-start.9

commit v3 on v2

--- a/solution.py
+++ b/solution.py
@@ -10,6 +10,7 @@
 AXES = ("depth", "chip", "core")
 FILT = ("chip", "core")
 CELLS = 128
+LIMITS = {"stride": 8, "turn": 8, "middle": 14, "result": 8, "back": 24, "rows": 2}
 VMEM = pl.BlockSpec(memory_space=pltpu.VMEM)
 SMEM = pl.BlockSpec(memory_space=pltpu.SMEM)
 TAPS = [(a, b) for a in range(3) for b in range(3)]
@@ -52,7 +53,7 @@
     return [value] + [shifted(value, lambda d, f, step=step: (d, f ^ step)) for step in (1, 2, 3)]
 
 
-def call(body, out_shape, scratch=(), flops=0, moved=0, in_specs=None):
+def call(name, body, out_shape, scratch=(), flops=0, moved=0, in_specs=None):
     many = isinstance(out_shape, (list, tuple))
     return pl.pallas_call(
         body,
@@ -60,6 +61,7 @@
         in_specs=in_specs,
         out_specs=[VMEM] * len(out_shape) if many else VMEM,
         scratch_shapes=list(scratch),
+        compiler_params=pltpu.CompilerParams(vmem_limit_bytes=LIMITS[name] << 20),
         cost_estimate=pl.CostEstimate(flops=flops, bytes_accessed=moved, transcendentals=0),
     )
 
@@ -317,6 +319,7 @@
     upper = upper_level.transpose(1, 2, 0, 3)
     cot_rows = cotangent.transpose(1, 2, 0, 3).reshape(2, 2, 128, 128)
     pack, level_pre, columns = call(
+        "stride",
         stride_body,
         [shape((2, 4, 128, 128)), shape((2, 2, 128, 128), jnp.float32), shape((512, 512))],
         [pltpu.VMEM((128, 512), jnp.bfloat16)],
@@ -330,6 +333,7 @@
     cot_column = jnp.concatenate([x[:, 2:] for x in (low, pack, high)], axis=0)
     cot_parts = cotangent_parts(cot_column.reshape(6, 8, 32, 128), chip)
     cot_cells, cot_own = call(
+        "turn",
         turn_body,
         [shape((6, 6, 128, 128)), shape((2, 2, 128, 128))],
         [pltpu.VMEM((36, 128, 128), jnp.bfloat16)],
@@ -339,6 +343,7 @@
     )(info, *cot_parts)
 
     mid_act, mid_pre = call(
+        "middle",
         middle_body,
         [shape((4, 4, 128, 128)), shape((4, 4, 128, 128), jnp.float32)],
         [
@@ -351,6 +356,7 @@
     )(info, *act_near, *middle_parts)
 
     stay, leave = call(
+        "result",
         result_body,
         [shape((2, 2, 2, 32, 128))] * 2,
         [pltpu.VMEM((384, 1152), jnp.bfloat16), pltpu.VMEM((128, 128), jnp.bfloat16)],
@@ -362,6 +368,7 @@
     result_far = swap_chip(jnp.stack([stay[1], result_near[1]]))
 
     keep, send = call(
+        "back",
         back_body,
         [shape((2, 64, 32, 128)), shape((2, 64, 32, 128))],
         [
@@ -380,7 +387,7 @@
     )
 
     result = call(
-        rows_body, shape((4, 2, 2, 32, 128)), in_specs=[SMEM] + [VMEM] * 3
+        "rows", rows_body, shape((4, 2, 2, 32, 128)), in_specs=[SMEM] + [VMEM] * 3
     )(info, stay, result_near, result_far)
     result = result.transpose(3, 1, 0, 2, 4).reshape(32, 2, 8, 128)
 

time: 130 us -> 112 us (0.86); the launches traced: 128 us -> 112 us
  Pallas kernels: 27.7 us -> 16 us
  local copies, waits for them, and re-layouts: 14.3 us -> 5.08 us
  waiting for transfers between devices: 21.9 us -> 27.4 us
    pallas_call x6, Pallas kernels: 27.7 us -> 16 us  [the longest x1 6.94 us: whole(): call('back', back_body, [shape((2, 64, 32, 128)), shape((2, 64, 32, 128))...]
    unnamed x38 -> x8, local copies, waits for them, and re-layouts: 7.37 us -> 1.92 us
    ppermute x19, waiting for transfers between devices: 21.9 us -> 26.2 us  [shifted(): return lax.ppermute(value, AXES, pairs_of(move))]
  transfers between devices with their start and end apart: 20 -> 20, of which waited for: 5 -> 9; matrix products, arithmetic and copies ran while one was open for 6% -> 3% of each run, Pallas kernels for 11% -> 7%
where the time goes in v3:
time: 112 us
  blocking collectives  34 us (30%)
  waiting for transfers between devices  27.4 us (24%)
  starting transfers between devices  26 us (23%)
  Pallas kernels  16 us (14%)
  local copies, waits for them, and re-layouts  5.08 us (5%)
  other arithmetic  2.44 us (2%)
    all_to_all x1, blocking collectives, whole(): lax.all_to_all(terms.reshape(2 * depth, 64, 128), ('chip', 'depth'), 0, 0...  34 us
    ppermute x19, waiting for transfers between devices, shifted(): return lax.ppermute(value, AXES, pairs_of(move))  26.2 us
    ppermute x19, starting transfers between devices, shifted(): return lax.ppermute(value, AXES, pairs_of(move))  21.5 us
    pallas_call x1, Pallas kernels, whole(): call('back', back_body, [shape((2, 64, 32, 128)), shape((2, 64, 32, 128))...  6.94 us
    all_to_all x1, starting transfers between devices, whole(): full = lax.all_to_all(spread, 'depth', 0, 0, tiled=True)  4.55 us
    pallas_call x1, Pallas kernels, whole(): call('middle', middle_body, [shape((4, 4, 128, 128)), shape((4, 4, 128, 1...  4.26 us
  transfers between devices with their start and end apart: 20, of which 9 were waited for; matrix products, arithmetic and copies ran while one was open for 3% of the time, Pallas kernels for 7%

profile of v3, /device:TPU:0, one launch (start us, length us, event | category | flops | bytes accessed | tf_op | source)
XLA Modules:
  0.0 111.9 jit_solution(17878883333526419120)
XLA Ops:
  0.6 0.0 copy-start
  0.6 0.0 copy-start.1
  0.7 0.0 copy-start.2
  0.7 2.1 %collective-permute-start.1 = (bf16[8,32,64]{2,1,0:T(8,128)(2,1)}, bf16[8,32,64]{2,1,0:T(8,128)(2,1)S(1)}, u32[]{:S(2)}, u32[]{:S(2)}) collective-permute-start(bf16[8,32,64]{2,1,0:T(8,128)(2,1)} %s0.1), channel_id=1, source_target_pairs={{0,2},{1,3},{2,0},{3,1},{4,6},{5,7},{6,4},{7,5},{8,10},{9,11},{10,... | collective-permute-start | bytes 98312 | tf_op jit(solution)/shard_map/ppermute | solution.py:36
  2.8 0.0 collective-permute-start
  2.8 0.2 collective-permute-start.2
  3.0 0.9 copy.12
  3.9 1.2 %copy.16 = bf16[64,4,4,256]{3,0,2,1:T(8,128)(2,1)S(1)} copy(bf16[64,4,4,256]{3,2,1,0:T(4,128)(2,1)} %param.5) | data formatting | bytes 1048576 | tf_op args[0]
  5.1 0.1 stack.22.info
  5.2 0.2 collective-permute-done.1.s2
  5.4 0.0 collective-permute-done.s1
  5.4 1.3 %collective-permute-done.2.s3 = bf16[8,32,64]{2,1,0:T(8,128)(2,1)S(1)} collective-permute-done((bf16[8,32,64]{2,1,0:T(8,128)(2,1)}, bf16[8,32,64]{2,1,0:T(8,128)(2,1)S(1)}, u32[]{:S(2)}, u32[]{:S(2)}) %collective-permute-start.2) | collective-permute-done | bytes 32800 | tf_op jit(solution)/shard_map/ppermute | solution.py:36
  6.7 0.0 copy-done
  6.7 1.6 %shard_map.84 = (bf16[2,4,128,128]{3,2,1,0:T(8,128)(2,1)S(1)}, f32[2,2,128,128]{3,2,1,0:T(8,128)S(1)}, bf16[512,512]{1,0:T(8,128)(2,1)S(1)}) custom-call(s32[5]{0:T(128)S(1)} %stack.22.info, bf16[4,4,64,256]{3,2,1,0:T(8,128)(2,1)S(1)} %bitcast.19, bf16[8,32,64]{2,1,0:T(8,128)(2,1)S(1)} %copy-done, bf16[8,32,64]{2,1,0:T(8,128)(2,1)S(1)} %collective-permute-done.s1, ...), custom_call_target="tpu_custom_call" | custom-call | flops 200000000 | bytes 1500000 | tf_op jit(solution)/shard_map/pallas_call | solution.py:321
  8.3 1.3 %collective-permute-start.4 = (bf16[2,4,128,128]{3,2,1,0:T(8,128)(2,1)S(1)}, bf16[2,4,128,128]{3,2,1,0:T(8,128)(2,1)S(1)}, u32[]{:S(2)}, u32[]{:S(2)}) collective-permute-start(bf16[2,4,128,128]{3,2,1,0:T(8,128)(2,1)S(1)} %get-tuple-element.15), channel_id=1, source_target_pairs={{4,0},{5,1},{6,2},{7,3},{8,4},{9,5},{10,6},{11,7},{12,8},{13,9},{1... | collective-permute-start | bytes 786440 | tf_op jit(solution)/shard_map/ppermute | solution.py:36
  9.6 0.0 copy-done.1
  9.7 1.2 %collective-permute-start.8 = (bf16[27,32,128]{2,1,0:T(8,128)(2,1)S(1)}, bf16[27,32,128]{2,1,0:T(8,128)(2,1)S(1)}, u32[]{:S(2)}, u32[]{:S(2)}) collective-permute-start(bf16[27,32,128]{2,1,0:T(8,128)(2,1)S(1)} %copy-done.1), channel_id=1, source_target_pairs={{0,2},{1,3},{2,0},{3,1},{4,6},{5,7},{6,4},{7,5},{8,10},{9,11},{10,... | collective-permute-start | bytes 663560 | tf_op jit(solution)/shard_map/ppermute | solution.py:36
  10.8 0.2 collective-permute-start.7
  11.1 0.0 copy-done.2
  11.1 5.8 %collective-permute-start.11 = (bf16[27,32,128]{2,1,0:T(8,128)(2,1)S(1)}, bf16[27,32,128]{2,1,0:T(8,128)(2,1)S(1)}, u32[]{:S(2)}, u32[]{:S(2)}) collective-permute-start(bf16[27,32,128]{2,1,0:T(8,128)(2,1)S(1)} %copy-done.2), channel_id=1, source_target_pairs={{0,18},{1,19},{2,16},{3,17},{4,22},{5,23},{6,20},{7,21},{8,26},{9,... | collective-permute-start | bytes 663560 | tf_op jit(solution)/shard_map/ppermute | solution.py:36
  16.9 1.5 %collective-permute-start.3 = (bf16[2,4,128,128]{3,2,1,0:T(8,128)(2,1)S(1)}, bf16[2,4,128,128]{3,2,1,0:T(8,128)(2,1)S(1)}, u32[]{:S(2)}, u32[]{:S(2)}) collective-permute-start(bf16[2,4,128,128]{3,2,1,0:T(8,128)(2,1)S(1)} %get-tuple-element.15), channel_id=1, source_target_pairs={{0,4},{1,5},{2,6},{3,7},{4,8},{5,9},{6,10},{7,11},{8,12},{9,13},{1... | collective-permute-start | bytes 786440 | tf_op jit(solution)/shard_map/ppermute | solution.py:36
  18.5 0.5 collective-permute-done.4
  19.0 5.4 %collective-permute-done.3 = bf16[2,4,128,128]{3,2,1,0:T(8,128)(2,1)S(1)} collective-permute-done((bf16[2,4,128,128]{3,2,1,0:T(8,128)(2,1)S(1)}, bf16[2,4,128,128]{3,2,1,0:T(8,128)(2,1)S(1)}, u32[]{:S(2)}, u32[]{:S(2)}) %collective-permute-start.3) | collective-permute-done | bytes 262176 | tf_op jit(solution)/shard_map/ppermute | solution.py:36
  24.5 1.3 %collective-permute-start.6 = (bf16[6,2,128,128]{3,2,1,0:T(8,128)(2,1)S(1)}, bf16[6,2,128,128]{3,2,1,0:T(8,128)(2,1)S(1)}, u32[]{:S(2)}, u32[]{:S(2)}) collective-permute-start(bf16[6,2,128,128]{3,2,1,0:T(8,128)(2,1)S(1)} %pad_maximum_fusion.mid.act_m), channel_id=1, source_target_pairs={{1,0},{2,1},{3,2},{5,4},{6,5},{7,6},{9,8},{10,9},{11,10},{13,12},{... | collective-permute-start | bytes 1179656 | tf_op jit(solution)/shard_map/ppermute | solution.py:36
  25.8 3.1 %collective-permute-start.5 = (bf16[6,2,128,128]{3,2,1,0:T(8,128)(2,1)S(1)}, bf16[6,2,128,128]{3,2,1,0:T(8,128)(2,1)S(1)}, u32[]{:S(2)}, u32[]{:S(2)}) collective-permute-start(bf16[6,2,128,128]{3,2,1,0:T(8,128)(2,1)S(1)} %pad_maximum_fusion.mid.act_m), channel_id=1, source_target_pairs={{0,1},{1,2},{2,3},{4,5},{5,6},{6,7},{8,9},{9,10},{10,11},{12,13},{... | collective-permute-start | bytes 1179656 | tf_op jit(solution)/shard_map/ppermute | solution.py:36
  28.9 0.0 collective-permute-done.8.m2
  28.9 1.2 %collective-permute-start.16 = (bf16[6,6,32,128]{3,2,1,0:T(8,128)(2,1)S(1)}, bf16[6,6,32,128]{3,2,1,0:T(8,128)(2,1)S(1)}, u32[]{:S(2)}, u32[]{:S(2)}) collective-permute-start(bf16[6,6,32,128]{3,2,1,0:T(8,128)(2,1)S(1)} %constant_dynamic-slice_fusion), channel_id=1, source_target_pairs={{0,2},{1,3},{2,0},{3,1},{4,6},{5,7},{6,4},{7,5},{8,10},{9,11},{10,... | collective-permute-start | bytes 884744 | tf_op jit(solution)/shard_map/ppermute | solution.py:36
  30.1 0.0 collective-permute-done.7.m1
  30.1 0.0 collective-permute-start.9
  30.1 0.0 collective-permute-done.11.l2
  30.1 0.5 collective-permute-start.15
  30.6 8.9 %collective-permute-done.16.far = bf16[6,6,32,128]{3,2,1,0:T(8,128)(2,1)S(1)} collective-permute-done((bf16[6,6,32,128]{3,2,1,0:T(8,128)(2,1)S(1)}, bf16[6,6,32,128]{3,2,1,0:T(8,128)(2,1)S(1)}, u32[]{:S(2)}, u32[]{:S(2)}) %collective-permute-start.16) | collective-permute-done | bytes 294944 | tf_op jit(solution)/shard_map/ppermute | solution.py:36
  39.6 1.0 collective-permute-start.17
  40.6 0.0 collective-permute-done.9.m3
  40.6 0.0 collective-permute-start.10
  40.6 0.0 collective-permute-done.6.right.act_r
  40.6 0.5 collective-permute-start.12
  41.1 0.0 collective-permute-done.5.left.act_l
  41.1 4.3 %shard_map.85 = (bf16[4,4,128,128]{3,2,1,0:T(8,128)(2,1)S(1)}, f32[4,4,128,128]{3,2,1,0:T(8,128)S(1)}) custom-call(s32[5]{0:T(128)S(1)} %stack.22.info, bf16[6,2,128,128]{3,2,1,0:T(8,128)(2,1)S(1)} %collective-permute-done.5.left.act_l, bf16[6,2,128,128]{3,2,1,0:T(8,128)(2,1)S(1)} %pad_maximum_fusion.mid.act_m, ...), custom_call_target="tpu_custom_call" | custom-call | flops 3000000000 | bytes 4000000 | tf_op jit(solution)/shard_map/pallas_call | solution.py:345
  45.3 0.0 collective-permute-done.15.near
  45.4 0.0 collective-permute-done.17.both
  45.4 1.0 shard_map.88
  46.4 0.0 collective-permute-done.10.l1
  46.4 0.0 collective-permute-done.12.l3
  46.4 6.9 %shard_map.89 = (bf16[2,64,32,128]{3,2,1,0:T(8,128)(2,1)S(1)}, bf16[2,64,32,128]{3,2,1,0:T(8,128)(2,1)S(1)}) custom-call(s32[5]{0:T(128)S(1)} %stack.22.info, bf16[6,2,128,128]{3,2,1,0:T(8,128)(2,1)S(1)} %collective-permute-done.5.left.act_l, bf16[6,2,128,128]{3,2,1,0:T(8,128)(2,1)S(1)} %pad_maximum_fusion.mid.act_m, ...), custom_call_target="tpu_custom_call" | custom-call | flops 4000000000 | bytes 8000000 | tf_op jit(solution)/shard_map/pallas_call | solution.py:370
  53.4 0.2 collective-permute-start.18
  53.6 2.6 %collective-permute-done.18 = bf16[2,64,32,128]{3,2,1,0:T(8,128)(2,1)S(1)} collective-permute-done((bf16[2,64,32,128]{3,2,1,0:T(8,128)(2,1)S(1)}, bf16[2,64,32,128]{3,2,1,0:T(8,128)(2,1)S(1)}, u32[]{:S(2)}, u32[]{:S(2)}) %collective-permute-start.18) | collective-permute-done | bytes 1048608 | tf_op jit(solution)/shard_map/ppermute | solution.py:36
  56.1 0.3 add_convert_fusion
  56.4 34.0 %all_to_all.10 = bf16[64,64,128]{2,1,0:T(8,128)(2,1)} all-to-all(bf16[64,64,128]{2,1,0:T(8,128)(2,1)S(1)} %bitcast.24), channel_id=1, replica_groups=mesh['depth'=32,'chip'=2,'core'=2] {'chip','depth'}, dimensions={0} | all-to-all | bytes 2097152 | tf_op jit(solution)/shard_map/all_to_all | solution.py:396
  90.4 1.4 %reduce_sum.12 = bf16[64,128]{1,0:T(8,128)(2,1)S(1)} reduce(bf16[64,64,128]{2,1,0:T(8,128)(2,1)} %all_to_all.10, bf16[]{:T(256)} %constant.24.clone.1), dimensions={0}, to_apply=%region_0.0 | reduce | flops 516096 | bytes 1064962 | tf_op jit(solution)/shard_map/reduce_sum | solution.py:397
  91.8 0.9 broadcast_in_dim.2
  92.7 4.5 %all-to-all-start.1 = ((bf16[32,64,128]{2,1,0:T(8,128)(2,1)}), bf16[32,64,128]{2,1,0:T(8,128)(2,1)S(1)}, u32[]{:S(2)}, u32[]{:S(2)}) async-start(bf16[32,64,128]{2,1,0:T(8,128)(2,1)} %broadcast_in_dim.2), calls=%async_computation.1 | async-start | bytes 1048576 | tf_op jit(solution)/shard_map/all_to_all | solution.py:399
  97.2 1.6 %shard_map.86 = (bf16[2,2,2,32,128]{4,3,2,1,0:T(8,128)(2,1)S(1)}, bf16[2,2,2,32,128]{4,3,2,1,0:T(8,128)(2,1)S(1)}) custom-call(s32[5]{0:T(128)S(1)} %stack.22.info, bf16[4,4,128,128]{3,2,1,0:T(8,128)(2,1)S(1)} %get-tuple-element.16.act_ref.mid_act, bf16[27,32,128]{2,1,0:T(8,128)(2,1)S(1)} %copy-done.2, bf16[27,32,128]{2,1,0:T(8,128)(2,1)S(1)} %collective-permute-done.10.l1, ...), custom_call_target="tpu_custom_call" | custom-call | flops 500000000 | bytes 2000000 | tf_op jit(solution)/shard_map/pallas_call | solution.py:358
  98.9 0.1 collective-permute-start.13
  99.0 1.2 %collective-permute-done.13.near = bf16[2,2,2,32,128]{4,3,2,1,0:T(8,128)(2,1)S(1)} collective-permute-done((bf16[2,2,2,32,128]{4,3,2,1,0:T(8,128)(2,1)S(1)}, bf16[2,2,2,32,128]{4,3,2,1,0:T(8,128)(2,1)S(1)}, u32[]{:S(2)}, u32[]{:S(2)}) %collective-permute-start.13) | collective-permute-done | bytes 65568 | tf_op jit(solution)/shard_map/ppermute | solution.py:36
  100.2 1.3 %collective-permute-start.14 = (bf16[2,2,2,32,128]{4,3,2,1,0:T(8,128)(2,1)S(1)}, bf16[2,2,2,32,128]{4,3,2,1,0:T(8,128)(2,1)S(1)}, u32[]{:S(2)}, u32[]{:S(2)}) collective-permute-start(bf16[2,2,2,32,128]{4,3,2,1,0:T(8,128)(2,1)S(1)} %pad_maximum_fusion.3), channel_id=1, source_target_pairs={{0,2},{1,3},{2,0},{3,1},{4,6},{5,7},{6,4},{7,5},{8,10},{9,11},{10,... | collective-permute-start | bytes 196616 | tf_op jit(solution)/shard_map/ppermute | solution.py:36
  101.5 6.1 %collective-permute-done.14.far = bf16[2,2,2,32,128]{4,3,2,1,0:T(8,128)(2,1)S(1)} collective-permute-done((bf16[2,2,2,32,128]{4,3,2,1,0:T(8,128)(2,1)S(1)}, bf16[2,2,2,32,128]{4,3,2,1,0:T(8,128)(2,1)S(1)}, u32[]{:S(2)}, u32[]{:S(2)}) %collective-permute-start.14) | collective-permute-done | bytes 65568 | tf_op jit(solution)/shard_map/ppermute | solution.py:36
  107.6 0.6 shard_map.87
  108.2 0.7 copy.14
  108.9 1.2 %all-to-all-done.1 = bf16[32,64,128]{2,1,0:T(8,128)(2,1)S(1)} async-done(((bf16[32,64,128]{2,1,0:T(8,128)(2,1)}), bf16[32,64,128]{2,1,0:T(8,128)(2,1)S(1)}, u32[]{:S(2)}, u32[]{:S(2)}) %all-to-all-start.1) | async-done | bytes 524320 | tf_op jit(solution)/shard_map/all_to_all | solution.py:399
  110.1 0.1 fusion.1
  110.2 1.0 fusion
  111.2 0.7 pad_maximum_fusion.2
  (10 shorter events, 0.2 us)
Async XLA Ops:
  0.6 6.1 %copy-start = (bf16[8,32,64]{2,1,0:T(8,128)(2,1)S(1)}, bf16[8,32,64]{2,1,0:T(8,128)(2,1)}, u32[]{:S(2)}) copy-start(bf16[8,32,64]{2,1,0:T(8,128)(2,1)} %s0.1) | copy-start | bytes 98308
  0.6 9.0 %copy-start.1 = (bf16[27,32,128]{2,1,0:T(8,128)(2,1)S(1)}, bf16[27,32,128]{2,1,0:T(8,128)(2,1)}, u32[]{:S(2)}) copy-start(bf16[27,32,128]{2,1,0:T(8,128)(2,1)} %m0.3) | copy-start | bytes 663556
  0.7 10.4 %copy-start.2 = (bf16[27,32,128]{2,1,0:T(8,128)(2,1)S(1)}, bf16[27,32,128]{2,1,0:T(8,128)(2,1)}, u32[]{:S(2)}) copy-start(bf16[27,32,128]{2,1,0:T(8,128)(2,1)} %l0.3) | copy-start | bytes 663556
  0.7 4.7 %collective-permute-start.1 = (bf16[8,32,64]{2,1,0:T(8,128)(2,1)}, bf16[8,32,64]{2,1,0:T(8,128)(2,1)S(1)}, u32[]{:S(2)}, u32[]{:S(2)}) collective-permute-start(bf16[8,32,64]{2,1,0:T(8,128)(2,1)} %s0.1), channel_id=1, source_target_pairs={{0,2},{1,3},{2,0},{3,1},{4,6},{5,7},{6,4},{7,5},{8,10},{9,11},{10,... | collective-permute-start | bytes 98312 | tf_op jit(solution)/shard_map/ppermute | solution.py:36
  2.8 2.6 %collective-permute-start = (bf16[8,32,64]{2,1,0:T(8,128)(2,1)}, bf16[8,32,64]{2,1,0:T(8,128)(2,1)S(1)}, u32[]{:S(2)}, u32[]{:S(2)}) collective-permute-start(bf16[8,32,64]{2,1,0:T(8,128)(2,1)} %s0.1), channel_id=1, source_target_pairs={{0,1},{1,0},{2,3},{3,2},{4,5},{5,4},{6,7},{7,6},{8,9},{9,8},{10,11... | collective-permute-start | bytes 98312 | tf_op jit(solution)/shard_map/ppermute | solution.py:36
  2.8 3.9 %collective-permute-start.2 = (bf16[8,32,64]{2,1,0:T(8,128)(2,1)}, bf16[8,32,64]{2,1,0:T(8,128)(2,1)S(1)}, u32[]{:S(2)}, u32[]{:S(2)}) collective-permute-start(bf16[8,32,64]{2,1,0:T(8,128)(2,1)} %s0.1), channel_id=1, source_target_pairs={{0,3},{1,2},{2,1},{3,0},{4,7},{5,6},{6,5},{7,4},{8,11},{9,10},{10,... | collective-permute-start | bytes 98312 | tf_op jit(solution)/shard_map/ppermute | solution.py:36
  8.3 10.6 %collective-permute-start.4 = (bf16[2,4,128,128]{3,2,1,0:T(8,128)(2,1)S(1)}, bf16[2,4,128,128]{3,2,1,0:T(8,128)(2,1)S(1)}, u32[]{:S(2)}, u32[]{:S(2)}) collective-permute-start(bf16[2,4,128,128]{3,2,1,0:T(8,128)(2,1)S(1)} %get-tuple-element.15), channel_id=1, source_target_pairs={{4,0},{5,1},{6,2},{7,3},{8,4},{9,5},{10,6},{11,7},{12,8},{13,9},{1... | collective-permute-start | bytes 786440 | tf_op jit(solution)/shard_map/ppermute | solution.py:36
  9.7 19.3 %collective-permute-start.8 = (bf16[27,32,128]{2,1,0:T(8,128)(2,1)S(1)}, bf16[27,32,128]{2,1,0:T(8,128)(2,1)S(1)}, u32[]{:S(2)}, u32[]{:S(2)}) collective-permute-start(bf16[27,32,128]{2,1,0:T(8,128)(2,1)S(1)} %copy-done.1), channel_id=1, source_target_pairs={{0,2},{1,3},{2,0},{3,1},{4,6},{5,7},{6,4},{7,5},{8,10},{9,11},{10,... | collective-permute-start | bytes 663560 | tf_op jit(solution)/shard_map/ppermute | solution.py:36
  10.8 19.3 %collective-permute-start.7 = (bf16[27,32,128]{2,1,0:T(8,128)(2,1)S(1)}, bf16[27,32,128]{2,1,0:T(8,128)(2,1)S(1)}, u32[]{:S(2)}, u32[]{:S(2)}) collective-permute-start(bf16[27,32,128]{2,1,0:T(8,128)(2,1)S(1)} %copy-done.1), channel_id=1, source_target_pairs={{0,1},{1,0},{2,3},{3,2},{4,5},{5,4},{6,7},{7,6},{8,9},{9,8},{10,11... | collective-permute-start | bytes 663560 | tf_op jit(solution)/shard_map/ppermute | solution.py:36
  11.1 19.1 %collective-permute-start.11 = (bf16[27,32,128]{2,1,0:T(8,128)(2,1)S(1)}, bf16[27,32,128]{2,1,0:T(8,128)(2,1)S(1)}, u32[]{:S(2)}, u32[]{:S(2)}) collective-permute-start(bf16[27,32,128]{2,1,0:T(8,128)(2,1)S(1)} %copy-done.2), channel_id=1, source_target_pairs={{0,18},{1,19},{2,16},{3,17},{4,22},{5,23},{6,20},{7,21},{8,26},{9,... | collective-permute-start | bytes 663560 | tf_op jit(solution)/shard_map/ppermute | solution.py:36
  16.9 7.5 %collective-permute-start.3 = (bf16[2,4,128,128]{3,2,1,0:T(8,128)(2,1)S(1)}, bf16[2,4,128,128]{3,2,1,0:T(8,128)(2,1)S(1)}, u32[]{:S(2)}, u32[]{:S(2)}) collective-permute-start(bf16[2,4,128,128]{3,2,1,0:T(8,128)(2,1)S(1)} %get-tuple-element.15), channel_id=1, source_target_pairs={{0,4},{1,5},{2,6},{3,7},{4,8},{5,9},{6,10},{7,11},{8,12},{9,13},{1... | collective-permute-start | bytes 786440 | tf_op jit(solution)/shard_map/ppermute | solution.py:36
  24.5 16.1 %collective-permute-start.6 = (bf16[6,2,128,128]{3,2,1,0:T(8,128)(2,1)S(1)}, bf16[6,2,128,128]{3,2,1,0:T(8,128)(2,1)S(1)}, u32[]{:S(2)}, u32[]{:S(2)}) collective-permute-start(bf16[6,2,128,128]{3,2,1,0:T(8,128)(2,1)S(1)} %pad_maximum_fusion.mid.act_m), channel_id=1, source_target_pairs={{1,0},{2,1},{3,2},{5,4},{6,5},{7,6},{9,8},{10,9},{11,10},{13,12},{... | collective-permute-start | bytes 1179656 | tf_op jit(solution)/shard_map/ppermute | solution.py:36
  25.8 15.3 %collective-permute-start.5 = (bf16[6,2,128,128]{3,2,1,0:T(8,128)(2,1)S(1)}, bf16[6,2,128,128]{3,2,1,0:T(8,128)(2,1)S(1)}, u32[]{:S(2)}, u32[]{:S(2)}) collective-permute-start(bf16[6,2,128,128]{3,2,1,0:T(8,128)(2,1)S(1)} %pad_maximum_fusion.mid.act_m), channel_id=1, source_target_pairs={{0,1},{1,2},{2,3},{4,5},{5,6},{6,7},{8,9},{9,10},{10,11},{12,13},{... | collective-permute-start | bytes 1179656 | tf_op jit(solution)/shard_map/ppermute | solution.py:36
  28.9 10.6 %collective-permute-start.16 = (bf16[6,6,32,128]{3,2,1,0:T(8,128)(2,1)S(1)}, bf16[6,6,32,128]{3,2,1,0:T(8,128)(2,1)S(1)}, u32[]{:S(2)}, u32[]{:S(2)}) collective-permute-start(bf16[6,6,32,128]{3,2,1,0:T(8,128)(2,1)S(1)} %constant_dynamic-slice_fusion), channel_id=1, source_target_pairs={{0,2},{1,3},{2,0},{3,1},{4,6},{5,7},{6,4},{7,5},{8,10},{9,11},{10,... | collective-permute-start | bytes 884744 | tf_op jit(solution)/shard_map/ppermute | solution.py:36
  30.1 10.4 %collective-permute-start.9 = (bf16[27,32,128]{2,1,0:T(8,128)(2,1)S(1)}, bf16[27,32,128]{2,1,0:T(8,128)(2,1)S(1)}, u32[]{:S(2)}, u32[]{:S(2)}) collective-permute-start(bf16[27,32,128]{2,1,0:T(8,128)(2,1)S(1)} %collective-permute-done.8.m2), channel_id=1, source_target_pairs={{0,1},{1,0},{2,3},{3,2},{4,5},{5,4},{6,7},{7,6},{8,9},{9,8},{10,11... | collective-permute-start | bytes 663560 | tf_op jit(solution)/shard_map/ppermute | solution.py:36
  30.1 15.2 %collective-permute-start.15 = (bf16[6,8,32,128]{3,2,1,0:T(8,128)(2,1)S(1)}, bf16[6,8,32,128]{3,2,1,0:T(8,128)(2,1)S(1)}, u32[]{:S(2)}, u32[]{:S(2)}) collective-permute-start(bf16[6,8,32,128]{3,2,1,0:T(8,128)(2,1)S(1)} %bitcast.17), channel_id=1, source_target_pairs={{0,1},{1,0},{2,3},{3,2},{4,5},{5,4},{6,7},{7,6},{8,9},{9,8},{10,11... | collective-permute-start | bytes 1179656 | tf_op jit(solution)/shard_map/ppermute | solution.py:36
  39.6 5.8 %collective-permute-start.17 = (bf16[6,6,32,128]{3,2,1,0:T(8,128)(2,1)S(1)}, bf16[6,6,32,128]{3,2,1,0:T(8,128)(2,1)S(1)}, u32[]{:S(2)}, u32[]{:S(2)}) collective-permute-start(bf16[6,6,32,128]{3,2,1,0:T(8,128)(2,1)S(1)} %collective-permute-done.16.far), channel_id=1, source_target_pairs={{0,1},{1,0},{2,3},{3,2},{4,5},{5,4},{6,7},{7,6},{8,9},{9,8},{10,11... | collective-permute-start | bytes 884744 | tf_op jit(solution)/shard_map/ppermute | solution.py:36
  40.6 5.8 %collective-permute-start.10 = (bf16[27,32,128]{2,1,0:T(8,128)(2,1)S(1)}, bf16[27,32,128]{2,1,0:T(8,128)(2,1)S(1)}, u32[]{:S(2)}, u32[]{:S(2)}) collective-permute-start(bf16[27,32,128]{2,1,0:T(8,128)(2,1)S(1)} %copy-done.2), channel_id=1, source_target_pairs={{0,1},{1,0},{2,3},{3,2},{4,5},{5,4},{6,7},{7,6},{8,9},{9,8},{10,11... | collective-permute-start | bytes 663560 | tf_op jit(solution)/shard_map/ppermute | solution.py:36
  40.6 5.8 %collective-permute-start.12 = (bf16[27,32,128]{2,1,0:T(8,128)(2,1)S(1)}, bf16[27,32,128]{2,1,0:T(8,128)(2,1)S(1)}, u32[]{:S(2)}, u32[]{:S(2)}) collective-permute-start(bf16[27,32,128]{2,1,0:T(8,128)(2,1)S(1)} %collective-permute-done.11.l2), channel_id=1, source_target_pairs={{0,1},{1,0},{2,3},{3,2},{4,5},{5,4},{6,7},{7,6},{8,9},{9,8},{10,11... | collective-permute-start | bytes 663560 | tf_op jit(solution)/shard_map/ppermute | solution.py:36
  53.4 2.7 %collective-permute-start.18 = (bf16[2,64,32,128]{3,2,1,0:T(8,128)(2,1)S(1)}, bf16[2,64,32,128]{3,2,1,0:T(8,128)(2,1)S(1)}, u32[]{:S(2)}, u32[]{:S(2)}) collective-permute-start(bf16[2,64,32,128]{3,2,1,0:T(8,128)(2,1)S(1)} %get-tuple-element.25), channel_id=1, source_target_pairs={{0,1},{1,0},{2,3},{3,2},{4,5},{5,4},{6,7},{7,6},{8,9},{9,8},{10,11... | collective-permute-start | bytes 3145736 | tf_op jit(solution)/shard_map/ppermute | solution.py:36
  92.7 17.4 %all-to-all-start.1 = ((bf16[32,64,128]{2,1,0:T(8,128)(2,1)}), bf16[32,64,128]{2,1,0:T(8,128)(2,1)S(1)}, u32[]{:S(2)}, u32[]{:S(2)}) async-start(bf16[32,64,128]{2,1,0:T(8,128)(2,1)} %broadcast_in_dim.2), calls=%async_computation.1 | async-start | bytes 1048576 | tf_op jit(solution)/shard_map/all_to_all | solution.py:399
  98.9 1.3 %collective-permute-start.13 = (bf16[2,2,2,32,128]{4,3,2,1,0:T(8,128)(2,1)S(1)}, bf16[2,2,2,32,128]{4,3,2,1,0:T(8,128)(2,1)S(1)}, u32[]{:S(2)}, u32[]{:S(2)}) collective-permute-start(bf16[2,2,2,32,128]{4,3,2,1,0:T(8,128)(2,1)S(1)} %get-tuple-element.18), channel_id=1, source_target_pairs={{0,1},{1,0},{2,3},{3,2},{4,5},{5,4},{6,7},{7,6},{8,9},{9,8},{10,11... | collective-permute-start | bytes 196616 | tf_op jit(solution)/shard_map/ppermute | solution.py:36
  100.2 7.4 %collective-permute-start.14 = (bf16[2,2,2,32,128]{4,3,2,1,0:T(8,128)(2,1)S(1)}, bf16[2,2,2,32,128]{4,3,2,1,0:T(8,128)(2,1)S(1)}, u32[]{:S(2)}, u32[]{:S(2)}) collective-permute-start(bf16[2,2,2,32,128]{4,3,2,1,0:T(8,128)(2,1)S(1)} %pad_maximum_fusion.3), channel_id=1, source_target_pairs={{0,2},{1,3},{2,0},{3,1},{4,6},{5,7},{6,4},{7,5},{8,10},{9,11},{10,... | collective-permute-start | bytes 196616 | tf_op jit(solution)/shard_map/ppermute | solution.py:36

commit v4 on v3

--- a/solution.py
+++ b/solution.py
@@ -10,7 +10,9 @@
 AXES = ("depth", "chip", "core")
 FILT = ("chip", "core")
 CELLS = 128
-LIMITS = {"stride": 8, "turn": 8, "middle": 14, "result": 8, "back": 24, "rows": 2}
+LIMITS = {
+    "stride": 8, "turn": 8, "weights": 10, "middle": 14, "result": 8, "back": 20, "rows": 2, "sum": 6
+}
 VMEM = pl.BlockSpec(memory_space=pltpu.VMEM)
 SMEM = pl.BlockSpec(memory_space=pltpu.SMEM)
 TAPS = [(a, b) for a in range(3) for b in range(3)]
@@ -124,10 +126,10 @@
                 own_ref[p - 2, r - 2] = tile
 
 
-def fill_window(window, left, middle, right):
-    window[:, 0:2] = left[...]
+def fill_window(window, middle, near, cross, core):
     window[:, 2:4] = middle[...]
-    window[:, 4:6] = right[...]
+    window[:, pl.ds(4 - 4 * core, 2)] = near[...]
+    window[:, pl.ds(4 * core, 2)] = cross[...]
 
 
 def fill_forward(weights, parts, filt):
@@ -146,6 +148,14 @@
             at = pl.multiple_of(start + n * 128, 32)
             for c in range(3):
                 weights[pl.ds(at, 32), c * 128 : c * 128 + 128] = part[9 * a + 3 * b + c]
+
+
+def weights_body(info, m0, m1, m2, m3, l0, l1, l2, l3, fm_ref, fl_ref, bl_ref, bm_ref):
+    filt = info[1]
+    fill_forward(fm_ref, (m0, m1, m2, m3), filt)
+    fill_forward(fl_ref, (l0, l1, l2, l3), filt)
+    fill_backward(bl_ref, (l0, l1, l2, l3), filt)
+    fill_backward(bm_ref, (m0, m1, m2, m3), filt)
 
 
 def column_of(size):
@@ -190,12 +200,8 @@
     return (row >= low) & (row <= high)
 
 
-def middle_body(
-    info, left, mid, right, m0, m1, m2, m3, act_ref, pre_ref, window, weights
-):
-    filt = info[1]
-    fill_window(window, left, mid, right)
-    fill_forward(weights, (m0, m1, m2, m3), filt)
+def middle_body(info, mid, near, cross, weights, act_ref, pre_ref, window):
+    fill_window(window, mid, near, cross, info[4])
 
     def plane(p, carry):
         pre = conv_forward(window, p, 1, 0, 4, weights)
@@ -207,9 +213,8 @@
     lax.fori_loop(0, 4, plane, 0)
 
 
-def result_body(info, act_ref, l0, l1, l2, l3, near_ref, far_ref, weights, turned):
+def result_body(info, act_ref, weights, near_ref, far_ref, turned):
     filt = info[1]
-    fill_forward(weights, (l0, l1, l2, l3), filt)
     out = conv_forward(act_ref, 0, 2, 0, 2, weights)
     for p in range(2):
         for r in range(2):
@@ -252,15 +257,11 @@
 
 
 def back_body(
-    info, act_l, act_m, act_r, window, m0, m1, m2, m3, l0, l1, l2, l3,
-    mid_act, mid_pre, level_pre, columns, cot_own,
-    keep_ref, send_ref, act_window, weights_m, weights_l, delta, turned,
+    info, act_window, window, weights_l, weights_m, mid_act, mid_pre, level_pre, columns, cot_own,
+    keep_ref, send_ref, delta, turned,
 ):
-    filt, core = info[1], info[4]
+    core = info[4]
     refs = (keep_ref, send_ref)
-    fill_window(act_window, act_l, act_m, act_r)
-    fill_backward(weights_l, (l0, l1, l2, l3), filt)
-    fill_backward(weights_m, (m0, m1, m2, m3), filt)
 
     def plane(p, carry):
         back = conv_backward(window, p, 1, 0, 4, weights_l)
@@ -297,10 +298,9 @@
         put_grad(refs, n, jnp.zeros((128, 128), jnp.float32))
 
 
-def row_parts(column):
-    left = shifted(column, lambda d, f: (d, f + 1))
-    right = shifted(column, lambda d, f: (d, f - 1))
-    return left, column, right
+def sum_body(terms_ref, out_ref):
+    total = jnp.sum(terms_ref[...].astype(jnp.float32), axis=0).astype(jnp.bfloat16)
+    out_ref[...] = jnp.broadcast_to(total[None], out_ref.shape)
 
 
 def cotangent_parts(column, chip):
@@ -327,10 +327,22 @@
         moved=1_500_000,
         in_specs=[SMEM] + [VMEM] * 6,
     )(info, upper, *stride_parts, cot_rows)
-    low = shifted(pack, lambda d, f: (d + 1, f))
-    high = shifted(pack, lambda d, f: (d - 1, f))
-    act_near = row_parts(jnp.concatenate([x[:, :2] for x in (low, pack, high)], axis=0))
-    cot_column = jnp.concatenate([x[:, 2:] for x in (low, pack, high)], axis=0)
+    odd = lax.axis_index("depth") % 2 == 1
+    pair = shifted(pack, lambda d, f: (d ^ 1, f))
+    next_pair = shifted(pack, lambda d, f: (d + 1 if d % 2 else d - 1, f))
+    act_column, cot_column = [
+        jnp.concatenate(
+            [
+                jnp.where(odd, pair[:, at], next_pair[:, at]),
+                pack[:, at],
+                jnp.where(odd, next_pair[:, at], pair[:, at]),
+            ],
+            axis=0,
+        )
+        for at in (slice(0, 2), slice(2, 4))
+    ]
+    act_near = swap_core(act_column)
+    act_cross = shifted(act_column, lambda d, f: (d, 3 - f) if f in (1, 2) else (-1, f))
     cot_parts = cotangent_parts(cot_column.reshape(6, 8, 32, 128), chip)
     cot_cells, cot_own = call(
         "turn",
@@ -342,28 +354,33 @@
         in_specs=[SMEM] + [VMEM] * 4,
     )(info, *cot_parts)
 
-    mid_act, mid_pre = call(
+    forward_m, forward_l, backward_l, backward_m = call(
+        "weights",
+        weights_body,
+        [shape((384, 1152))] * 2 + [shape((1152, 384))] * 2,
+        flops=1_000_000,
+        moved=6_000_000,
+        in_specs=[SMEM] + [VMEM] * 8,
+    )(info, *middle_parts, *last_parts)
+
+    mid_act, mid_pre, act_window = call(
         "middle",
         middle_body,
-        [shape((4, 4, 128, 128)), shape((4, 4, 128, 128), jnp.float32)],
-        [
-            pltpu.VMEM((6, 6, 128, 128), jnp.bfloat16),
-            pltpu.VMEM((384, 1152), jnp.bfloat16),
-        ],
+        [shape((4, 4, 128, 128)), shape((4, 4, 128, 128), jnp.float32), shape((6, 6, 128, 128))],
         flops=3_000_000_000,
         moved=4_000_000,
-        in_specs=[SMEM] + [VMEM] * 7,
-    )(info, *act_near, *middle_parts)
+        in_specs=[SMEM] + [VMEM] * 4,
+    )(info, act_column, act_near, act_cross, forward_m)
 
     stay, leave = call(
         "result",
         result_body,
         [shape((2, 2, 2, 32, 128))] * 2,
-        [pltpu.VMEM((384, 1152), jnp.bfloat16), pltpu.VMEM((128, 128), jnp.bfloat16)],
+        [pltpu.VMEM((128, 128), jnp.bfloat16)],
         flops=500_000_000,
         moved=2_000_000,
-        in_specs=[SMEM] + [VMEM] * 5,
-    )(info, mid_act, *last_parts)
+        in_specs=[SMEM] + [VMEM] * 2,
+    )(info, mid_act, forward_l)
     result_near = swap_core(leave)
     result_far = swap_chip(jnp.stack([stay[1], result_near[1]]))
 
@@ -371,18 +388,12 @@
         "back",
         back_body,
         [shape((2, 64, 32, 128)), shape((2, 64, 32, 128))],
-        [
-            pltpu.VMEM((6, 6, 128, 128), jnp.bfloat16),
-            pltpu.VMEM((1152, 384), jnp.bfloat16),
-            pltpu.VMEM((1152, 384), jnp.bfloat16),
-            pltpu.VMEM((4, 4, 128, 128), jnp.bfloat16),
-            pltpu.VMEM((128, 512), jnp.float32),
-        ],
+        [pltpu.VMEM((4, 4, 128, 128), jnp.bfloat16), pltpu.VMEM((128, 512), jnp.float32)],
         flops=4_000_000_000,
         moved=8_000_000,
-        in_specs=[SMEM] + [VMEM] * 17,
+        in_specs=[SMEM] + [VMEM] * 9,
     )(
-        info, *act_near, cot_cells, *middle_parts, *last_parts,
+        info, act_window, cot_cells, backward_l, backward_m,
         mid_act, mid_pre, level_pre, columns, cot_own,
     )
 
@@ -394,8 +405,7 @@
     other = swap_core(send)
     terms = (keep.astype(jnp.float32) + other.astype(jnp.float32)).astype(jnp.bfloat16)
     terms = lax.all_to_all(terms.reshape(2 * depth, 64, 128), ("chip", "depth"), 0, 0, tiled=True)
-    mine = jnp.sum(terms.astype(jnp.float32), axis=0).astype(jnp.bfloat16)
-    spread = jnp.broadcast_to(mine[None], (depth, 64, 128))
+    spread = call("sum", sum_body, shape((depth, 64, 128)), in_specs=[VMEM])(terms)
     full = lax.all_to_all(spread, "depth", 0, 0, tiled=True)
     full = full.reshape(64, 32, 128).astype(jnp.float32)
     grad_stride = full[54:58].reshape(4, 32, 2, 64).transpose(0, 2, 1, 3).reshape(8, 32, 64)

time: 112 us -> 111 us (level)
  waiting for transfers between devices: 27.4 us -> 36.8 us
  starting transfers between devices: 26 us -> 20 us
  blocking collectives: 34 us -> 29 us
  Pallas kernels: 16 us -> 17.4 us
    ppermute x19, waiting for transfers between devices: 26.2 us -> 35.3 us  [shifted(): return lax.ppermute(value, AXES, pairs_of(move))]
    ppermute x19, starting transfers between devices: 21.5 us -> 15.3 us  [shifted(): return lax.ppermute(value, AXES, pairs_of(move))]
    all_to_all x1, blocking collectives: 34 us -> 29 us  [whole(): lax.all_to_all(terms.reshape(2 * depth, 64, 128), ('chip', 'depth'), 0, 0...]
    pallas_call x0 -> x2, Pallas kernels: none -> 2.15 us  [the longest x1 1.16 us: whole(): call('weights', weights_body, [shape((384, 1152))] * 2 + [shape((1152, 38...]
    reduce_sum x1 -> x0, other arithmetic: 1.4 us -> none  [whole(): mine = jnp.sum(terms.astype(jnp.float32), axis=0).astype(jnp.bfloat16)]
  transfers between devices with their start and end apart: 20 -> 20, of which waited for: 9 -> 9; matrix products, arithmetic and copies ran while one was open for 3% -> 4% of each run, Pallas kernels for 7% -> 7%
where the time goes in v4:
time: 111 us; the launch traced here: 110 us
  waiting for transfers between devices  36.8 us (33%)
  blocking collectives  29 us (26%)
  starting transfers between devices  20 us (18%)
  Pallas kernels  17.4 us (16%)
  local copies, waits for them, and re-layouts  4.11 us (4%)
  other arithmetic  2.06 us (2%)
    ppermute x19, waiting for transfers between devices, shifted(): return lax.ppermute(value, AXES, pairs_of(move))  35.3 us
    all_to_all x1, blocking collectives, whole(): lax.all_to_all(terms.reshape(2 * depth, 64, 128), ('chip', 'depth'), 0, 0...  29 us
    ppermute x19, starting transfers between devices, shifted(): return lax.ppermute(value, AXES, pairs_of(move))  15.3 us
    pallas_call x1, Pallas kernels, whole(): call('back', back_body, [shape((2, 64, 32, 128)), shape((2, 64, 32, 128))...  6.52 us
    all_to_all x1, starting transfers between devices, whole(): full = lax.all_to_all(spread, 'depth', 0, 0, tiled=True)  4.78 us
    pallas_call x1, Pallas kernels, whole(): call('middle', middle_body, [shape((4, 4, 128, 128)), shape((4, 4, 128, 1...  4.09 us
  transfers between devices with their start and end apart: 20, of which 9 were waited for; matrix products, arithmetic and copies ran while one was open for 4% of the time, Pallas kernels for 7%

profile of v4, /device:TPU:0, one launch (start us, length us, event | category | flops | bytes accessed | tf_op | source)
XLA Modules:
  0.0 110.4 jit_solution(9453389019824085849)
XLA Ops:
  0.6 0.0 copy-start.2
  0.6 0.0 copy-start
  0.7 0.0 copy-start.1
  0.7 0.1 collective-permute-start
  0.8 2.1 %collective-permute-start.1 = (bf16[8,32,64]{2,1,0:T(8,128)(2,1)}, bf16[8,32,64]{2,1,0:T(8,128)(2,1)S(1)}, u32[]{:S(2)}, u32[]{:S(2)}) collective-permute-start(bf16[8,32,64]{2,1,0:T(8,128)(2,1)} %s0.1), channel_id=1, source_target_pairs={{0,2},{1,3},{2,0},{3,1},{4,6},{5,7},{6,4},{7,5},{8,10},{9,11},{10,... | collective-permute-start | bytes 98312 | tf_op jit(solution)/shard_map/ppermute | solution.py:38
  2.9 0.0 collective-permute-start.2
  2.9 1.2 %copy.16 = bf16[64,4,4,256]{3,0,2,1:T(8,128)(2,1)S(1)} copy(bf16[64,4,4,256]{3,2,1,0:T(4,128)(2,1)} %param.5) | data formatting | bytes 1048576 | tf_op args[0]
  4.1 0.9 copy.12
  5.0 0.1 stack.22.info
  5.1 0.0 collective-permute-done.s1
  5.1 0.6 collective-permute-done.1.s2
  5.7 1.4 %collective-permute-done.2.s3 = bf16[8,32,64]{2,1,0:T(8,128)(2,1)S(1)} collective-permute-done((bf16[8,32,64]{2,1,0:T(8,128)(2,1)}, bf16[8,32,64]{2,1,0:T(8,128)(2,1)S(1)}, u32[]{:S(2)}, u32[]{:S(2)}) %collective-permute-start.2) | collective-permute-done | bytes 32800 | tf_op jit(solution)/shard_map/ppermute | solution.py:38
  7.1 0.0 copy-done.2
  7.2 1.6 %shard_map.84 = (bf16[2,4,128,128]{3,2,1,0:T(8,128)(2,1)S(1)}, f32[2,2,128,128]{3,2,1,0:T(8,128)S(1)}, bf16[512,512]{1,0:T(8,128)(2,1)S(1)}) custom-call(s32[5]{0:T(128)S(1)} %stack.22.info, bf16[4,4,64,256]{3,2,1,0:T(8,128)(2,1)S(1)} %bitcast.19, bf16[8,32,64]{2,1,0:T(8,128)(2,1)S(1)} %copy-done.2, bf16[8,32,64]{2,1,0:T(8,128)(2,1)S(1)} %collective-permute-done.s1, ...), custom_call_target="tpu_custom_call" | custom-call | flops 200000000 | bytes 1500000 | tf_op jit(solution)/shard_map/pallas_call | solution.py:321
  8.8 0.7 collective-permute-start.4
  9.5 4.5 %collective-permute-start.3 = (bf16[2,4,128,128]{3,2,1,0:T(8,128)(2,1)S(1)}, bf16[2,4,128,128]{3,2,1,0:T(8,128)(2,1)}, u32[]{:S(2)}, u32[]{:S(2)}) collective-permute-start(bf16[2,4,128,128]{3,2,1,0:T(8,128)(2,1)S(1)} %get-tuple-element.20), channel_id=1, source_target_pairs={{0,4},{1,5},{2,6},{3,7},{4,0},{5,1},{6,2},{7,3},{8,12},{9,13},{10,... | collective-permute-start | bytes 786440 | tf_op jit(solution)/shard_map/ppermute | solution.py:38
  13.9 0.0 copy-done
  13.9 0.0 collective-permute-start.7
  13.9 1.2 %collective-permute-start.8 = (bf16[27,32,128]{2,1,0:T(8,128)(2,1)S(1)}, bf16[27,32,128]{2,1,0:T(8,128)(2,1)S(1)}, u32[]{:S(2)}, u32[]{:S(2)}) collective-permute-start(bf16[27,32,128]{2,1,0:T(8,128)(2,1)S(1)} %copy-done), channel_id=1, source_target_pairs={{0,2},{1,3},{2,0},{3,1},{4,6},{5,7},{6,4},{7,5},{8,10},{9,11},{10,... | collective-permute-start | bytes 663560 | tf_op jit(solution)/shard_map/ppermute | solution.py:38
  15.1 0.0 copy-done.1
  15.1 0.2 collective-permute-start.10
  15.4 12.0 %collective-permute-done.8.m2 = bf16[27,32,128]{2,1,0:T(8,128)(2,1)S(1)} collective-permute-done((bf16[27,32,128]{2,1,0:T(8,128)(2,1)S(1)}, bf16[27,32,128]{2,1,0:T(8,128)(2,1)S(1)}, u32[]{:S(2)}, u32[]{:S(2)}) %collective-permute-start.8) | collective-permute-done | bytes 221216 | tf_op jit(solution)/shard_map/ppermute | solution.py:38
  27.4 0.0 collective-permute-start.11
  27.4 0.0 collective-permute-done.4
  27.4 0.0 collective-permute-start.9
  27.4 0.0 collective-permute-done.3
  27.4 1.0 broadcast_select_fusion.1
  28.5 0.6 collective-permute-start.5
  29.1 0.0 collective-permute-done.7.m1
  29.1 0.7 collective-permute-start.6
  29.9 0.0 collective-permute-done.10.l1
  29.9 3.0 %collective-permute-start.16 = (bf16[6,6,32,128]{3,2,1,0:T(8,128)(2,1)S(1)}, bf16[6,6,32,128]{3,2,1,0:T(8,128)(2,1)S(1)}, u32[]{:S(2)}, u32[]{:S(2)}) collective-permute-start(bf16[6,6,32,128]{3,2,1,0:T(8,128)(2,1)S(1)} %constant_dynamic-slice_fusion), channel_id=1, source_target_pairs={{0,2},{1,3},{2,0},{3,1},{4,6},{5,7},{6,4},{7,5},{8,10},{9,11},{10,... | collective-permute-start | bytes 884744 | tf_op jit(solution)/shard_map/ppermute | solution.py:38
  32.8 2.8 %collective-permute-done.11.l2 = bf16[27,32,128]{2,1,0:T(8,128)(2,1)S(1)} collective-permute-done((bf16[27,32,128]{2,1,0:T(8,128)(2,1)S(1)}, bf16[27,32,128]{2,1,0:T(8,128)(2,1)S(1)}, u32[]{:S(2)}, u32[]{:S(2)}) %collective-permute-start.11) | collective-permute-done | bytes 221216 | tf_op jit(solution)/shard_map/ppermute | solution.py:38
  35.6 0.0 collective-permute-start.12
  35.6 0.0 collective-permute-done.9.m3
  35.6 0.5 collective-permute-start.15
  36.1 8.6 %collective-permute-done.16.far = bf16[6,6,32,128]{3,2,1,0:T(8,128)(2,1)S(1)} collective-permute-done((bf16[6,6,32,128]{3,2,1,0:T(8,128)(2,1)S(1)}, bf16[6,6,32,128]{3,2,1,0:T(8,128)(2,1)S(1)}, u32[]{:S(2)}, u32[]{:S(2)}) %collective-permute-start.16) | collective-permute-done | bytes 294944 | tf_op jit(solution)/shard_map/ppermute | solution.py:38
  44.8 0.0 collective-permute-start.17
  44.8 0.0 collective-permute-done.12.l3
  44.8 1.2 %shard_map.85 = (bf16[384,1152]{1,0:T(8,128)(2,1)S(1)}, bf16[384,1152]{1,0:T(8,128)(2,1)S(1)}, bf16[1152,384]{1,0:T(8,128)(2,1)S(1)}, bf16[1152,384]{1,0:T(8,128)(2,1)S(1)}) custom-call(s32[5]{0:T(128)S(1)} %stack.22.info, bf16[27,32,128]{2,1,0:T(8,128)(2,1)S(1)} %copy-done, bf16[27,32,128]{2,1,0:T(8,128)(2,1)S(1)} %collective-permute-done.7.m1, ...), custom_call_target="tpu_custom_call" | custom-call | flops 1000000 | bytes 6000000 | tf_op jit(solution)/shard_map/pallas_call | solution.py:357
  45.9 0.0 collective-permute-done.5.near
  45.9 0.0 collective-permute-done.6.cross
  46.0 4.1 %shard_map.86 = (bf16[4,4,128,128]{3,2,1,0:T(8,128)(2,1)S(1)}, f32[4,4,128,128]{3,2,1,0:T(8,128)S(1)}, bf16[6,6,128,128]{3,2,1,0:T(8,128)(2,1)S(1)}) custom-call(s32[5]{0:T(128)S(1)} %stack.22.info, bf16[6,2,128,128]{3,2,1,0:T(8,128)(2,1)S(1)} %pad_maximum_fusion.mid, bf16[6,2,128,128]{3,2,1,0:T(8,128)(2,1)S(1)} %collective-permute-done.5.near, ...), custom_call_target="tpu_custom_call" | custom-call | flops 3000000000 | bytes 4000000 | tf_op jit(solution)/shard_map/pallas_call | solution.py:366
  50.0 0.0 collective-permute-done.15.near
  50.1 0.0 collective-permute-done.17.both
  50.1 1.0 shard_map.89
  51.1 6.5 %shard_map.90 = (bf16[2,64,32,128]{3,2,1,0:T(8,128)(2,1)S(1)}, bf16[2,64,32,128]{3,2,1,0:T(8,128)(2,1)S(1)}) custom-call(s32[5]{0:T(128)S(1)} %stack.22.info, bf16[6,6,128,128]{3,2,1,0:T(8,128)(2,1)S(1)} %get-tuple-element.26.act_window, bf16[6,6,128,128]{3,2,1,0:T(8,128)(2,1)S(1)} %get-tuple-element.27.window, ...), custom_call_target="tpu_custom_call" | custom-call | flops 4000000000 | bytes 8000000 | tf_op jit(solution)/shard_map/pallas_call | solution.py:387
  57.6 0.6 collective-permute-start.18
  58.3 2.3 %collective-permute-done.18 = bf16[2,64,32,128]{3,2,1,0:T(8,128)(2,1)S(1)} collective-permute-done((bf16[2,64,32,128]{3,2,1,0:T(8,128)(2,1)S(1)}, bf16[2,64,32,128]{3,2,1,0:T(8,128)(2,1)S(1)}, u32[]{:S(2)}, u32[]{:S(2)}) %collective-permute-start.18) | collective-permute-done | bytes 1048608 | tf_op jit(solution)/shard_map/ppermute | solution.py:38
  60.5 0.3 add_convert_fusion
  60.8 29.0 %all_to_all.10.terms_ref = bf16[64,64,128]{2,1,0:T(8,128)(2,1)S(1)} all-to-all(bf16[64,64,128]{2,1,0:T(8,128)(2,1)S(1)} %bitcast.24), channel_id=1, replica_groups=mesh['depth'=32,'chip'=2,'core'=2] {'chip','depth'}, dimensions={0} | all-to-all | bytes 2097152 | tf_op jit(solution)/shard_map/all_to_all | solution.py:407
  89.8 1.0 shard_map.91
  90.8 4.8 %all-to-all-start.1 = ((bf16[32,64,128]{2,1,0:T(8,128)(2,1)}), bf16[32,64,128]{2,1,0:T(8,128)(2,1)S(1)}, u32[]{:S(2)}, u32[]{:S(2)}) async-start(bf16[32,64,128]{2,1,0:T(8,128)(2,1)} %shard_map.91), calls=%async_computation.1 | async-start | bytes 1048576 | tf_op jit(solution)/shard_map/all_to_all | solution.py:409
  95.6 1.5 %shard_map.87 = (bf16[2,2,2,32,128]{4,3,2,1,0:T(8,128)(2,1)S(1)}, bf16[2,2,2,32,128]{4,3,2,1,0:T(8,128)(2,1)S(1)}) custom-call(s32[5]{0:T(128)S(1)} %stack.22.info, bf16[4,4,128,128]{3,2,1,0:T(8,128)(2,1)S(1)} %get-tuple-element.22.act_ref.mid_act, bf16[384,1152]{1,0:T(8,128)(2,1)S(1)} %get-tuple-element.23.weights), custom_call_target="tpu_custom_call" | custom-call | flops 500000000 | bytes 2000000 | tf_op jit(solution)/shard_map/pallas_call | solution.py:375
  97.1 0.1 collective-permute-start.13
  97.2 1.2 %collective-permute-done.13.near = bf16[2,2,2,32,128]{4,3,2,1,0:T(8,128)(2,1)S(1)} collective-permute-done((bf16[2,2,2,32,128]{4,3,2,1,0:T(8,128)(2,1)S(1)}, bf16[2,2,2,32,128]{4,3,2,1,0:T(8,128)(2,1)S(1)}, u32[]{:S(2)}, u32[]{:S(2)}) %collective-permute-start.13) | collective-permute-done | bytes 65568 | tf_op jit(solution)/shard_map/ppermute | solution.py:38
  98.4 1.1 collective-permute-start.14
  99.5 6.3 %collective-permute-done.14.far = bf16[2,2,2,32,128]{4,3,2,1,0:T(8,128)(2,1)S(1)} collective-permute-done((bf16[2,2,2,32,128]{4,3,2,1,0:T(8,128)(2,1)S(1)}, bf16[2,2,2,32,128]{4,3,2,1,0:T(8,128)(2,1)S(1)}, u32[]{:S(2)}, u32[]{:S(2)}) %collective-permute-start.14) | collective-permute-done | bytes 65568 | tf_op jit(solution)/shard_map/ppermute | solution.py:38
  105.8 0.6 shard_map.88
  106.4 0.7 copy.14
  107.1 1.6 %all-to-all-done.1 = bf16[32,64,128]{2,1,0:T(8,128)(2,1)S(1)} async-done(((bf16[32,64,128]{2,1,0:T(8,128)(2,1)}), bf16[32,64,128]{2,1,0:T(8,128)(2,1)S(1)}, u32[]{:S(2)}, u32[]{:S(2)}) %all-to-all-start.1) | async-done | bytes 524320 | tf_op jit(solution)/shard_map/all_to_all | solution.py:409
  108.6 0.1 fusion.1
  108.7 1.0 fusion
  109.7 0.7 pad_maximum_fusion.2
  (8 shorter events, 0.2 us)
Async XLA Ops:
  0.6 6.5 %copy-start.2 = (bf16[8,32,64]{2,1,0:T(8,128)(2,1)S(1)}, bf16[8,32,64]{2,1,0:T(8,128)(2,1)}, u32[]{:S(2)}) copy-start(bf16[8,32,64]{2,1,0:T(8,128)(2,1)} %s0.1) | copy-start | bytes 98308
  0.6 13.3 %copy-start = (bf16[27,32,128]{2,1,0:T(8,128)(2,1)S(1)}, bf16[27,32,128]{2,1,0:T(8,128)(2,1)}, u32[]{:S(2)}) copy-start(bf16[27,32,128]{2,1,0:T(8,128)(2,1)} %m0.1) | copy-start | bytes 663556
  0.7 14.5 %copy-start.1 = (bf16[27,32,128]{2,1,0:T(8,128)(2,1)S(1)}, bf16[27,32,128]{2,1,0:T(8,128)(2,1)}, u32[]{:S(2)}) copy-start(bf16[27,32,128]{2,1,0:T(8,128)(2,1)} %l0.1) | copy-start | bytes 663556
  0.7 4.5 %collective-permute-start = (bf16[8,32,64]{2,1,0:T(8,128)(2,1)}, bf16[8,32,64]{2,1,0:T(8,128)(2,1)S(1)}, u32[]{:S(2)}, u32[]{:S(2)}) collective-permute-start(bf16[8,32,64]{2,1,0:T(8,128)(2,1)} %s0.1), channel_id=1, source_target_pairs={{0,1},{1,0},{2,3},{3,2},{4,5},{5,4},{6,7},{7,6},{8,9},{9,8},{10,11... | collective-permute-start | bytes 98312 | tf_op jit(solution)/shard_map/ppermute | solution.py:38
  0.8 5.0 %collective-permute-start.1 = (bf16[8,32,64]{2,1,0:T(8,128)(2,1)}, bf16[8,32,64]{2,1,0:T(8,128)(2,1)S(1)}, u32[]{:S(2)}, u32[]{:S(2)}) collective-permute-start(bf16[8,32,64]{2,1,0:T(8,128)(2,1)} %s0.1), channel_id=1, source_target_pairs={{0,2},{1,3},{2,0},{3,1},{4,6},{5,7},{6,4},{7,5},{8,10},{9,11},{10,... | collective-permute-start | bytes 98312 | tf_op jit(solution)/shard_map/ppermute | solution.py:38
  2.9 4.3 %collective-permute-start.2 = (bf16[8,32,64]{2,1,0:T(8,128)(2,1)}, bf16[8,32,64]{2,1,0:T(8,128)(2,1)S(1)}, u32[]{:S(2)}, u32[]{:S(2)}) collective-permute-start(bf16[8,32,64]{2,1,0:T(8,128)(2,1)} %s0.1), channel_id=1, source_target_pairs={{0,3},{1,2},{2,1},{3,0},{4,7},{5,6},{6,5},{7,4},{8,11},{9,10},{10,... | collective-permute-start | bytes 98312 | tf_op jit(solution)/shard_map/ppermute | solution.py:38
  8.8 18.6 %collective-permute-start.4 = (bf16[2,4,128,128]{3,2,1,0:T(8,128)(2,1)S(1)}, bf16[2,4,128,128]{3,2,1,0:T(8,128)(2,1)S(1)}, u32[]{:S(2)}, u32[]{:S(2)}) collective-permute-start(bf16[2,4,128,128]{3,2,1,0:T(8,128)(2,1)S(1)} %get-tuple-element.20), channel_id=1, source_target_pairs={{4,8},{5,9},{6,10},{7,11},{8,4},{9,5},{10,6},{11,7},{12,16},{13,17... | collective-permute-start | bytes 786440 | tf_op jit(solution)/shard_map/ppermute | solution.py:38
  9.5 17.9 %collective-permute-start.3 = (bf16[2,4,128,128]{3,2,1,0:T(8,128)(2,1)S(1)}, bf16[2,4,128,128]{3,2,1,0:T(8,128)(2,1)}, u32[]{:S(2)}, u32[]{:S(2)}) collective-permute-start(bf16[2,4,128,128]{3,2,1,0:T(8,128)(2,1)S(1)} %get-tuple-element.20), channel_id=1, source_target_pairs={{0,4},{1,5},{2,6},{3,7},{4,0},{5,1},{6,2},{7,3},{8,12},{9,13},{10,... | collective-permute-start | bytes 786440 | tf_op jit(solution)/shard_map/ppermute | solution.py:38
  13.9 15.2 %collective-permute-start.7 = (bf16[27,32,128]{2,1,0:T(8,128)(2,1)S(1)}, bf16[27,32,128]{2,1,0:T(8,128)(2,1)S(1)}, u32[]{:S(2)}, u32[]{:S(2)}) collective-permute-start(bf16[27,32,128]{2,1,0:T(8,128)(2,1)S(1)} %copy-done), channel_id=1, source_target_pairs={{0,1},{1,0},{2,3},{3,2},{4,5},{5,4},{6,7},{7,6},{8,9},{9,8},{10,11... | collective-permute-start | bytes 663560 | tf_op jit(solution)/shard_map/ppermute | solution.py:38
  13.9 13.5 %collective-permute-start.8 = (bf16[27,32,128]{2,1,0:T(8,128)(2,1)S(1)}, bf16[27,32,128]{2,1,0:T(8,128)(2,1)S(1)}, u32[]{:S(2)}, u32[]{:S(2)}) collective-permute-start(bf16[27,32,128]{2,1,0:T(8,128)(2,1)S(1)} %copy-done), channel_id=1, source_target_pairs={{0,2},{1,3},{2,0},{3,1},{4,6},{5,7},{6,4},{7,5},{8,10},{9,11},{10,... | collective-permute-start | bytes 663560 | tf_op jit(solution)/shard_map/ppermute | solution.py:38
  15.1 14.7 %collective-permute-start.10 = (bf16[27,32,128]{2,1,0:T(8,128)(2,1)S(1)}, bf16[27,32,128]{2,1,0:T(8,128)(2,1)S(1)}, u32[]{:S(2)}, u32[]{:S(2)}) collective-permute-start(bf16[27,32,128]{2,1,0:T(8,128)(2,1)S(1)} %copy-done.1), channel_id=1, source_target_pairs={{0,1},{1,0},{2,3},{3,2},{4,5},{5,4},{6,7},{7,6},{8,9},{9,8},{10,11... | collective-permute-start | bytes 663560 | tf_op jit(solution)/shard_map/ppermute | solution.py:38
  27.4 8.2 %collective-permute-start.11 = (bf16[27,32,128]{2,1,0:T(8,128)(2,1)S(1)}, bf16[27,32,128]{2,1,0:T(8,128)(2,1)S(1)}, u32[]{:S(2)}, u32[]{:S(2)}) collective-permute-start(bf16[27,32,128]{2,1,0:T(8,128)(2,1)S(1)} %copy-done.1), channel_id=1, source_target_pairs={{0,18},{1,19},{2,16},{3,17},{4,22},{5,23},{6,20},{7,21},{8,26},{9,... | collective-permute-start | bytes 663560 | tf_op jit(solution)/shard_map/ppermute | solution.py:38
  27.4 8.2 %collective-permute-start.9 = (bf16[27,32,128]{2,1,0:T(8,128)(2,1)S(1)}, bf16[27,32,128]{2,1,0:T(8,128)(2,1)S(1)}, u32[]{:S(2)}, u32[]{:S(2)}) collective-permute-start(bf16[27,32,128]{2,1,0:T(8,128)(2,1)S(1)} %collective-permute-done.8.m2), channel_id=1, source_target_pairs={{0,1},{1,0},{2,3},{3,2},{4,5},{5,4},{6,7},{7,6},{8,9},{9,8},{10,11... | collective-permute-start | bytes 663560 | tf_op jit(solution)/shard_map/ppermute | solution.py:38
  28.5 17.4 %collective-permute-start.5 = (bf16[6,2,128,128]{3,2,1,0:T(8,128)(2,1)S(1)}, bf16[6,2,128,128]{3,2,1,0:T(8,128)(2,1)S(1)}, u32[]{:S(2)}, u32[]{:S(2)}) collective-permute-start(bf16[6,2,128,128]{3,2,1,0:T(8,128)(2,1)S(1)} %pad_maximum_fusion.mid), channel_id=1, source_target_pairs={{0,1},{1,0},{2,3},{3,2},{4,5},{5,4},{6,7},{7,6},{8,9},{9,8},{10,11... | collective-permute-start | bytes 1179656 | tf_op jit(solution)/shard_map/ppermute | solution.py:38
  29.1 16.8 %collective-permute-start.6 = (bf16[6,2,128,128]{3,2,1,0:T(8,128)(2,1)S(1)}, bf16[6,2,128,128]{3,2,1,0:T(8,128)(2,1)S(1)}, u32[]{:S(2)}, u32[]{:S(2)}) collective-permute-start(bf16[6,2,128,128]{3,2,1,0:T(8,128)(2,1)S(1)} %pad_maximum_fusion.mid), channel_id=1, source_target_pairs={{1,2},{2,1},{5,6},{6,5},{9,10},{10,9},{13,14},{14,13},{17,18},{18,... | collective-permute-start | bytes 1179656 | tf_op jit(solution)/shard_map/ppermute | solution.py:38
  29.9 14.9 %collective-permute-start.16 = (bf16[6,6,32,128]{3,2,1,0:T(8,128)(2,1)S(1)}, bf16[6,6,32,128]{3,2,1,0:T(8,128)(2,1)S(1)}, u32[]{:S(2)}, u32[]{:S(2)}) collective-permute-start(bf16[6,6,32,128]{3,2,1,0:T(8,128)(2,1)S(1)} %constant_dynamic-slice_fusion), channel_id=1, source_target_pairs={{0,2},{1,3},{2,0},{3,1},{4,6},{5,7},{6,4},{7,5},{8,10},{9,11},{10,... | collective-permute-start | bytes 884744 | tf_op jit(solution)/shard_map/ppermute | solution.py:38
  35.6 9.2 %collective-permute-start.12 = (bf16[27,32,128]{2,1,0:T(8,128)(2,1)S(1)}, bf16[27,32,128]{2,1,0:T(8,128)(2,1)S(1)}, u32[]{:S(2)}, u32[]{:S(2)}) collective-permute-start(bf16[27,32,128]{2,1,0:T(8,128)(2,1)S(1)} %collective-permute-done.11.l2), channel_id=1, source_target_pairs={{0,1},{1,0},{2,3},{3,2},{4,5},{5,4},{6,7},{7,6},{8,9},{9,8},{10,11... | collective-permute-start | bytes 663560 | tf_op jit(solution)/shard_map/ppermute | solution.py:38
  35.6 14.4 %collective-permute-start.15 = (bf16[6,8,32,128]{3,2,1,0:T(8,128)(2,1)S(1)}, bf16[6,8,32,128]{3,2,1,0:T(8,128)(2,1)S(1)}, u32[]{:S(2)}, u32[]{:S(2)}) collective-permute-start(bf16[6,8,32,128]{3,2,1,0:T(8,128)(2,1)S(1)} %bitcast.17), channel_id=1, source_target_pairs={{0,1},{1,0},{2,3},{3,2},{4,5},{5,4},{6,7},{7,6},{8,9},{9,8},{10,11... | collective-permute-start | bytes 1179656 | tf_op jit(solution)/shard_map/ppermute | solution.py:38
  44.8 5.3 %collective-permute-start.17 = (bf16[6,6,32,128]{3,2,1,0:T(8,128)(2,1)S(1)}, bf16[6,6,32,128]{3,2,1,0:T(8,128)(2,1)S(1)}, u32[]{:S(2)}, u32[]{:S(2)}) collective-permute-start(bf16[6,6,32,128]{3,2,1,0:T(8,128)(2,1)S(1)} %collective-permute-done.16.far), channel_id=1, source_target_pairs={{0,1},{1,0},{2,3},{3,2},{4,5},{5,4},{6,7},{7,6},{8,9},{9,8},{10,11... | collective-permute-start | bytes 884744 | tf_op jit(solution)/shard_map/ppermute | solution.py:38
  57.6 2.9 %collective-permute-start.18 = (bf16[2,64,32,128]{3,2,1,0:T(8,128)(2,1)S(1)}, bf16[2,64,32,128]{3,2,1,0:T(8,128)(2,1)S(1)}, u32[]{:S(2)}, u32[]{:S(2)}) collective-permute-start(bf16[2,64,32,128]{3,2,1,0:T(8,128)(2,1)S(1)} %get-tuple-element.35), channel_id=1, source_target_pairs={{0,1},{1,0},{2,3},{3,2},{4,5},{5,4},{6,7},{7,6},{8,9},{9,8},{10,11... | collective-permute-start | bytes 3145736 | tf_op jit(solution)/shard_map/ppermute | solution.py:38
  90.8 17.8 %all-to-all-start.1 = ((bf16[32,64,128]{2,1,0:T(8,128)(2,1)}), bf16[32,64,128]{2,1,0:T(8,128)(2,1)S(1)}, u32[]{:S(2)}, u32[]{:S(2)}) async-start(bf16[32,64,128]{2,1,0:T(8,128)(2,1)} %shard_map.91), calls=%async_computation.1 | async-start | bytes 1048576 | tf_op jit(solution)/shard_map/all_to_all | solution.py:409
  97.1 1.3 %collective-permute-start.13 = (bf16[2,2,2,32,128]{4,3,2,1,0:T(8,128)(2,1)S(1)}, bf16[2,2,2,32,128]{4,3,2,1,0:T(8,128)(2,1)S(1)}, u32[]{:S(2)}, u32[]{:S(2)}) collective-permute-start(bf16[2,2,2,32,128]{4,3,2,1,0:T(8,128)(2,1)S(1)} %get-tuple-element.25), channel_id=1, source_target_pairs={{0,1},{1,0},{2,3},{3,2},{4,5},{5,4},{6,7},{7,6},{8,9},{9,8},{10,11... | collective-permute-start | bytes 196616 | tf_op jit(solution)/shard_map/ppermute | solution.py:38
  98.4 7.4 %collective-permute-start.14 = (bf16[2,2,2,32,128]{4,3,2,1,0:T(8,128)(2,1)S(1)}, bf16[2,2,2,32,128]{4,3,2,1,0:T(8,128)(2,1)S(1)}, u32[]{:S(2)}, u32[]{:S(2)}) collective-permute-start(bf16[2,2,2,32,128]{4,3,2,1,0:T(8,128)(2,1)S(1)} %pad_maximum_fusion.3), channel_id=1, source_target_pairs={{0,2},{1,3},{2,0},{3,1},{4,6},{5,7},{6,4},{7,5},{8,10},{9,11},{10,... | collective-permute-start | bytes 196616 | tf_op jit(solution)/shard_map/ppermute | solution.py:38

commit v5 on v4

--- a/solution.py
+++ b/solution.py
@@ -11,7 +11,8 @@
 FILT = ("chip", "core")
 CELLS = 128
 LIMITS = {
-    "stride": 8, "turn": 8, "weights": 10, "middle": 14, "result": 8, "back": 20, "rows": 2, "sum": 6
+    "stride": 8, "act_join": 4, "cot_join": 4, "turn": 8, "weights": 10, "middle": 20, "result": 8,
+    "back": 28, "rows": 2, "sum": 6, "finish": 4,
 }
 VMEM = pl.BlockSpec(memory_space=pltpu.VMEM)
 SMEM = pl.BlockSpec(memory_space=pltpu.SMEM)
@@ -49,10 +50,6 @@
 def four_parts(value, turn):
     far = shifted(value, lambda d, f: (d ^ turn, f ^ 2))
     return [value, swap_core(value), far, swap_core(far)]
-
-
-def four_parts_direct(value):
-    return [value] + [shifted(value, lambda d, f, step=step: (d, f ^ step)) for step in (1, 2, 3)]
 
 
 def call(name, body, out_shape, scratch=(), flops=0, moved=0, in_specs=None):
@@ -105,8 +102,24 @@
             columns_ref[:, cell * 128 : cell * 128 + 128] = block
             pre = dot(weights[...], block).T
             pre_ref[p, r] = pre
-            pack_ref[p, r] = (pre * jax.nn.sigmoid(pre)).astype(jnp.bfloat16)
-    pack_ref[:, 2:4] = cot_ref[...]
+            act = (pre * jax.nn.sigmoid(pre)).astype(jnp.bfloat16)
+            pack_ref[p, r * 128 : r * 128 + 128] = act
+    pack_ref[:, 256:512] = cot_ref[...]
+
+
+def act_body(info, pack, pair, beyond, column_ref):
+    odd = info[0] & 1
+    column_ref[2:4] = pack[:, :256]
+    column_ref[pl.ds(4 - 4 * odd, 2)] = pair[:, :256]
+    column_ref[pl.ds(4 * odd, 2)] = beyond[:, :256]
+
+
+def cot_body(info, pack, pair, beyond, column_ref, wanted_ref):
+    odd, chip = info[0] & 1, info[3]
+    start = pl.multiple_of(256 + 64 * (1 - chip), 64)
+    for at, part in ((2, pack), (4 - 4 * odd, pair), (4 * odd, beyond)):
+        column_ref[pl.ds(at, 2)] = part[:, 256:512]
+        wanted_ref[pl.ds(at, 2)] = part[:, pl.ds(start, 192)]
 
 
 def turn_body(info, own, near, far, both, cells_ref, own_ref, tiles):
@@ -190,27 +203,22 @@
     return from_after(out[:, :128]) + out[:, 128:256] + from_before(out[:, 256:])
 
 
-def inside(info, p):
+def inside(info):
     depth, filt = info[0], info[1]
-    row = lax.broadcasted_iota(jnp.int32, (4 * CELLS, 1), 0) // CELLS
-    bad = ((depth == 0) & (p == 0)) | ((depth == lax.axis_size("depth") - 1) & (p == 3))
-    low = jnp.where(filt == 0, 1, 0)
-    high = jnp.where(filt == 3, 2, 3)
-    low = jnp.where(bad, 4, low)
-    return (row >= low) & (row <= high)
+    cell = lax.broadcasted_iota(jnp.int32, (16 * CELLS, 1), 0) // CELLS
+    plane, row = cell // 4, cell % 4
+    valid = (plane >= jnp.where(depth == 0, 1, 0)) & (row >= jnp.where(filt == 0, 1, 0))
+    last = jnp.where(depth == lax.axis_size("depth") - 1, 2, 3)
+    return valid & (plane <= last) & (row <= jnp.where(filt == 3, 2, 3))
 
 
 def middle_body(info, mid, near, cross, weights, act_ref, pre_ref, window):
     fill_window(window, mid, near, cross, info[4])
 
-    def plane(p, carry):
-        pre = conv_forward(window, p, 1, 0, 4, weights)
-        act = jnp.where(inside(info, p), pre * jax.nn.sigmoid(pre), 0.0)
-        pre_ref[pl.ds(p, 1)] = pre.reshape(1, 4, CELLS, 128)
-        act_ref[pl.ds(p, 1)] = act.astype(jnp.bfloat16).reshape(1, 4, CELLS, 128)
-        return carry
-
-    lax.fori_loop(0, 4, plane, 0)
+    pre = conv_forward(window, 0, 4, 0, 4, weights)
+    act = jnp.where(inside(info), pre * jax.nn.sigmoid(pre), 0.0)
+    pre_ref[...] = pre.reshape(4, 4, CELLS, 128)
+    act_ref[...] = act.astype(jnp.bfloat16).reshape(4, 4, CELLS, 128)
 
 
 def result_body(info, act_ref, weights, near_ref, far_ref, turned):
@@ -263,14 +271,9 @@
     core = info[4]
     refs = (keep_ref, send_ref)
 
-    def plane(p, carry):
-        back = conv_backward(window, p, 1, 0, 4, weights_l)
-        pre = mid_pre[pl.ds(p, 1)].reshape(4 * CELLS, 128)
-        here = jnp.where(inside(info, p), back * silu_slope(pre), 0.0)
-        delta[pl.ds(p, 1)] = here.astype(jnp.bfloat16).reshape(1, 4, CELLS, 128)
-        return carry
-
-    lax.fori_loop(0, 4, plane, 0)
+    back = conv_backward(window, 0, 4, 0, 4, weights_l)
+    here = jnp.where(inside(info), back * silu_slope(mid_pre[...].reshape(16 * CELLS, 128)), 0.0)
+    delta[...] = here.astype(jnp.bfloat16).reshape(4, 4, CELLS, 128)
 
     own = [in_order(cot_own, (p, r), core).astype(jnp.float32) for p in range(2) for r in range(2)]
     cot_rows = shifts_of(jnp.concatenate(own, axis=1))
@@ -298,52 +301,56 @@
         put_grad(refs, n, jnp.zeros((128, 128), jnp.float32))
 
 
+def finish_body(full_ref, stride_ref, middle_ref, last_ref):
+    last_ref[...] = full_ref[0:27].astype(jnp.float32)
+    middle_ref[...] = full_ref[27:54].astype(jnp.float32)
+    for n in range(4):
+        block = full_ref[54 + n].astype(jnp.float32)
+        stride_ref[2 * n] = block[:, :64]
+        stride_ref[2 * n + 1] = block[:, 64:]
+
+
 def sum_body(terms_ref, out_ref):
     total = jnp.sum(terms_ref[...].astype(jnp.float32), axis=0).astype(jnp.bfloat16)
     out_ref[...] = jnp.broadcast_to(total[None], out_ref.shape)
-
-
-def cotangent_parts(column, chip):
-    wanted = lax.dynamic_slice_in_dim(column, 2 * (1 - chip), 6, axis=1)
-    far = swap_chip(wanted)
-    return column, swap_core(column), far, swap_core(far)
 
 
 def whole(upper_level, stride_weight, middle_weight, last_weight, cotangent):
     depth = lax.axis_size("depth")
     chip, core = lax.axis_index("chip"), lax.axis_index("core")
     info = jnp.stack([lax.axis_index("depth"), 2 * chip + core, jnp.int32(depth), chip, core])
-    stride_parts = four_parts_direct(stride_weight)
+    stride_parts = four_parts(stride_weight, 0)
     middle_parts = four_parts(middle_weight, 0)
     last_parts = four_parts(last_weight, 4)
     upper = upper_level.transpose(1, 2, 0, 3)
-    cot_rows = cotangent.transpose(1, 2, 0, 3).reshape(2, 2, 128, 128)
+    cot_rows = cotangent.transpose(1, 2, 0, 3).reshape(2, 256, 128)
     pack, level_pre, columns = call(
         "stride",
         stride_body,
-        [shape((2, 4, 128, 128)), shape((2, 2, 128, 128), jnp.float32), shape((512, 512))],
+        [shape((2, 512, 128)), shape((2, 2, 128, 128), jnp.float32), shape((512, 512))],
         [pltpu.VMEM((128, 512), jnp.bfloat16)],
         flops=200_000_000,
         moved=1_500_000,
         in_specs=[SMEM] + [VMEM] * 6,
     )(info, upper, *stride_parts, cot_rows)
-    odd = lax.axis_index("depth") % 2 == 1
+    beyond = shifted(pack, lambda d, f: (d + 1 if d % 2 else d - 1, f))
     pair = shifted(pack, lambda d, f: (d ^ 1, f))
-    next_pair = shifted(pack, lambda d, f: (d + 1 if d % 2 else d - 1, f))
-    act_column, cot_column = [
-        jnp.concatenate(
-            [
-                jnp.where(odd, pair[:, at], next_pair[:, at]),
-                pack[:, at],
-                jnp.where(odd, next_pair[:, at], pair[:, at]),
-            ],
-            axis=0,
-        )
-        for at in (slice(0, 2), slice(2, 4))
-    ]
+    act_column = call(
+        "act_join", act_body, shape((6, 256, 128)), in_specs=[SMEM] + [VMEM] * 3
+    )(info, pack, pair, beyond)
+    act_cross = shifted(act_column, lambda d, f: (d, 3 - f) if f in (1, 2) else (-1, f))
     act_near = swap_core(act_column)
-    act_cross = shifted(act_column, lambda d, f: (d, 3 - f) if f in (1, 2) else (-1, f))
-    cot_parts = cotangent_parts(cot_column.reshape(6, 8, 32, 128), chip)
+    act_parts = [x.reshape(6, 2, 128, 128) for x in (act_column, act_near, act_cross)]
+    cot_column, cot_wanted = call(
+        "cot_join",
+        cot_body,
+        [shape((6, 256, 128)), shape((6, 192, 128))],
+        in_specs=[SMEM] + [VMEM] * 3,
+    )(info, pack, pair, beyond)
+    cot_near = swap_core(cot_column)
+    cot_far = swap_chip(cot_wanted)
+    cot_both = swap_core(cot_far)
+    cot_parts = [x.reshape(6, -1, 32, 128) for x in (cot_column, cot_near, cot_far, cot_both)]
     cot_cells, cot_own = call(
         "turn",
         turn_body,
@@ -370,7 +377,7 @@
         flops=3_000_000_000,
         moved=4_000_000,
         in_specs=[SMEM] + [VMEM] * 4,
-    )(info, act_column, act_near, act_cross, forward_m)
+    )(info, *act_parts, forward_m)
 
     stay, leave = call(
         "result",
@@ -407,9 +414,17 @@
     terms = lax.all_to_all(terms.reshape(2 * depth, 64, 128), ("chip", "depth"), 0, 0, tiled=True)
     spread = call("sum", sum_body, shape((depth, 64, 128)), in_specs=[VMEM])(terms)
     full = lax.all_to_all(spread, "depth", 0, 0, tiled=True)
-    full = full.reshape(64, 32, 128).astype(jnp.float32)
-    grad_stride = full[54:58].reshape(4, 32, 2, 64).transpose(0, 2, 1, 3).reshape(8, 32, 64)
-    return (result, grad_stride, full[27:54], full[:27])
+    grads = call(
+        "finish",
+        finish_body,
+        [
+            shape((8, 32, 64), jnp.float32),
+            shape((27, 32, 128), jnp.float32),
+            shape((27, 32, 128), jnp.float32),
+        ],
+        in_specs=[VMEM],
+    )(full.reshape(64, 32, 128))
+    return (result, *grads)
 
 
 def solution(mesh):

time: 111 us -> 107 us (0.964)
  waiting for transfers between devices: 36.8 us -> 28.7 us
  blocking collectives: 29 us -> 32.7 us
  starting transfers between devices: 20 us -> 22.2 us
  Pallas kernels: 17.4 us -> 19.2 us
  other arithmetic: 2.06 us -> 0.28 us
  local copies, waits for them, and re-layouts: 4.11 us -> 2.97 us
    ppermute x19, waiting for transfers between devices: 35.3 us -> 27.2 us  [shifted(): return lax.ppermute(value, AXES, pairs_of(move))]
    all_to_all x1, blocking collectives: 29 us -> 32.7 us  [whole(): lax.all_to_all(terms.reshape(2 * depth, 64, 128), ('chip', 'depth'), 0, 0...]
    ppermute x19, starting transfers between devices: 15.3 us -> 17.4 us  [shifted(): return lax.ppermute(value, AXES, pairs_of(move))]
    pallas_call x1 -> x4, Pallas kernels: 1.64 us -> 3.78 us  [the longest x1 1.64 us: whole(): call('stride', stride_body, [shape((2, 512, 128)), shape((2, 2, 128, 128)...]
    slice x3 -> x0, local copies, waits for them, and re-layouts: 1.11 us -> none  [the longest x1 1.02 us: whole(): return (result, grad_stride, full[27:54], full[:27])]
  transfers between devices with their start and end apart: 20 -> 20, of which waited for: 9 -> 8; matrix products, arithmetic and copies ran while one was open for 4% -> 3% of each run, Pallas kernels for 7% -> 8%
where the time goes in v5:
time: 107 us
  blocking collectives  32.7 us (31%)
  waiting for transfers between devices  28.7 us (27%)
  starting transfers between devices  22.2 us (21%)
  Pallas kernels  19.2 us (18%)
  local copies, waits for them, and re-layouts  2.97 us (3%)
    all_to_all x1, blocking collectives, whole(): lax.all_to_all(terms.reshape(2 * depth, 64, 128), ('chip', 'depth'), 0, 0...  32.7 us
    ppermute x19, waiting for transfers between devices, shifted(): return lax.ppermute(value, AXES, pairs_of(move))  27.2 us
    ppermute x19, starting transfers between devices, shifted(): return lax.ppermute(value, AXES, pairs_of(move))  17.4 us
    pallas_call x1, Pallas kernels, whole(): call('back', back_body, [shape((2, 64, 32, 128)), shape((2, 64, 32, 128))...  6.17 us
    all_to_all x1, starting transfers between devices, whole(): full = lax.all_to_all(spread, 'depth', 0, 0, tiled=True)  4.78 us
    pallas_call x1, Pallas kernels, whole(): call('middle', middle_body, [shape((4, 4, 128, 128)), shape((4, 4, 128, 1...  3.98 us
  transfers between devices with their start and end apart: 20, of which 8 were waited for; matrix products, arithmetic and copies ran while one was open for 3% of the time, Pallas kernels for 8%

profile of v5, /device:TPU:0, one launch (start us, length us, event | category | flops | bytes accessed | tf_op | source)
XLA Modules:
  0.0 106.9 jit_solution(3287609866580441411)
XLA Ops:
  0.6 0.0 copy-start.2
  0.6 0.0 copy-start
  0.7 0.0 copy-start.1
  0.7 2.1 %collective-permute-start.1 = (bf16[8,32,64]{2,1,0:T(8,128)(2,1)}, bf16[8,32,64]{2,1,0:T(8,128)(2,1)S(1)}, u32[]{:S(2)}, u32[]{:S(2)}) collective-permute-start(bf16[8,32,64]{2,1,0:T(8,128)(2,1)} %s0.1), channel_id=1, source_target_pairs={{0,2},{1,3},{2,0},{3,1},{4,6},{5,7},{6,4},{7,5},{8,10},{9,11},{10,... | collective-permute-start | bytes 98312 | tf_op jit(solution)/shard_map/ppermute | solution.py:39
  2.8 0.0 collective-permute-start
  2.8 2.5 %collective-permute-done.1.s2 = bf16[8,32,64]{2,1,0:T(8,128)(2,1)S(1)} collective-permute-done((bf16[8,32,64]{2,1,0:T(8,128)(2,1)}, bf16[8,32,64]{2,1,0:T(8,128)(2,1)S(1)}, u32[]{:S(2)}, u32[]{:S(2)}) %collective-permute-start.1) | collective-permute-done | bytes 32800 | tf_op jit(solution)/shard_map/ppermute | solution.py:39
  5.2 0.0 collective-permute-start.2
  5.2 1.2 %copy.16 = bf16[64,4,4,256]{3,0,2,1:T(8,128)(2,1)S(1)} copy(bf16[64,4,4,256]{3,2,1,0:T(4,128)(2,1)} %param.5) | data formatting | bytes 1048576 | tf_op args[0]
  6.4 0.9 copy.12
  7.4 0.1 stack.22.info
  7.5 0.0 collective-permute-done.s1
  7.5 0.0 collective-permute-done.2.s3
  7.5 0.0 copy-done.2
  7.5 1.6 %shard_map.84 = (bf16[2,512,128]{2,1,0:T(8,128)(2,1)S(1)}, f32[2,2,128,128]{3,2,1,0:T(8,128)S(1)}, bf16[512,512]{1,0:T(8,128)(2,1)S(1)}) custom-call(s32[5]{0:T(128)S(1)} %stack.22.info, bf16[4,4,64,256]{3,2,1,0:T(8,128)(2,1)S(1)} %bitcast.21, bf16[8,32,64]{2,1,0:T(8,128)(2,1)S(1)} %copy-done.2, bf16[8,32,64]{2,1,0:T(8,128)(2,1)S(1)} %collective-permute-done.s1, ...), custom_call_target="tpu_custom_call" | custom-call | flops 200000000 | bytes 1500000 | tf_op jit(solution)/shard_map/pallas_call | solution.py:327
  9.1 1.8 %collective-permute-start.3 = (bf16[2,512,128]{2,1,0:T(8,128)(2,1)S(1)}, bf16[2,512,128]{2,1,0:T(8,128)(2,1)S(1)}, u32[]{:S(2)}, u32[]{:S(2)}) collective-permute-start(bf16[2,512,128]{2,1,0:T(8,128)(2,1)S(1)} %get-tuple-element.25.pack), channel_id=1, source_target_pairs={{0,4},{1,5},{2,6},{3,7},{4,0},{5,1},{6,2},{7,3},{8,12},{9,13},{10,... | collective-permute-start | bytes 786440 | tf_op jit(solution)/shard_map/ppermute | solution.py:39
  10.9 0.7 collective-permute-start.4
  11.6 0.0 copy-done
  11.6 0.3 collective-permute-start.7
  11.9 1.9 %collective-permute-start.8 = (bf16[27,32,128]{2,1,0:T(8,128)(2,1)S(1)}, bf16[27,32,128]{2,1,0:T(8,128)(2,1)S(1)}, u32[]{:S(2)}, u32[]{:S(2)}) collective-permute-start(bf16[27,32,128]{2,1,0:T(8,128)(2,1)S(1)} %copy-done), channel_id=1, source_target_pairs={{0,2},{1,3},{2,0},{3,1},{4,6},{5,7},{6,4},{7,5},{8,10},{9,11},{10,... | collective-permute-start | bytes 663560 | tf_op jit(solution)/shard_map/ppermute | solution.py:39
  13.8 0.0 copy-done.1
  13.8 0.0 collective-permute-start.10
  13.8 4.1 %collective-permute-done.3.pair = bf16[2,512,128]{2,1,0:T(8,128)(2,1)S(1)} collective-permute-done((bf16[2,512,128]{2,1,0:T(8,128)(2,1)S(1)}, bf16[2,512,128]{2,1,0:T(8,128)(2,1)S(1)}, u32[]{:S(2)}, u32[]{:S(2)}) %collective-permute-start.3) | collective-permute-done | bytes 262176 | tf_op jit(solution)/shard_map/ppermute | solution.py:39
  17.9 4.1 %collective-permute-start.11 = (bf16[27,32,128]{2,1,0:T(8,128)(2,1)S(1)}, bf16[27,32,128]{2,1,0:T(8,128)(2,1)S(1)}, u32[]{:S(2)}, u32[]{:S(2)}) collective-permute-start(bf16[27,32,128]{2,1,0:T(8,128)(2,1)S(1)} %copy-done.1), channel_id=1, source_target_pairs={{0,18},{1,19},{2,16},{3,17},{4,22},{5,23},{6,20},{7,21},{8,26},{9,... | collective-permute-start | bytes 663560 | tf_op jit(solution)/shard_map/ppermute | solution.py:39
  22.1 0.0 collective-permute-done.4.beyond
  22.1 0.6 shard_map.85
  22.7 0.1 collective-permute-start.5
  22.7 0.0 collective-permute-done.7.m1
  22.8 0.7 collective-permute-start.6
  23.4 0.0 collective-permute-done.8.m2
  23.5 1.8 %collective-permute-start.9 = (bf16[27,32,128]{2,1,0:T(8,128)(2,1)S(1)}, bf16[27,32,128]{2,1,0:T(8,128)(2,1)S(1)}, u32[]{:S(2)}, u32[]{:S(2)}) collective-permute-start(bf16[27,32,128]{2,1,0:T(8,128)(2,1)S(1)} %collective-permute-done.8.m2), channel_id=1, source_target_pairs={{0,1},{1,0},{2,3},{3,2},{4,5},{5,4},{6,7},{7,6},{8,9},{9,8},{10,11... | collective-permute-start | bytes 663560 | tf_op jit(solution)/shard_map/ppermute | solution.py:39
  25.3 0.6 shard_map.90
  25.9 0.0 collective-permute-done.10.l1
  25.9 1.7 %collective-permute-start.16 = (bf16[6,192,128]{2,1,0:T(8,128)(2,1)S(1)}, bf16[6,192,128]{2,1,0:T(8,128)(2,1)S(1)}, u32[]{:S(2)}, u32[]{:S(2)}) collective-permute-start(bf16[6,192,128]{2,1,0:T(8,128)(2,1)S(1)} %get-tuple-element.33), channel_id=1, source_target_pairs={{0,2},{1,3},{2,0},{3,1},{4,6},{5,7},{6,4},{7,5},{8,10},{9,11},{10,... | collective-permute-start | bytes 884744 | tf_op jit(solution)/shard_map/ppermute | solution.py:39
  27.6 2.3 %collective-permute-done.11.l2 = bf16[27,32,128]{2,1,0:T(8,128)(2,1)S(1)} collective-permute-done((bf16[27,32,128]{2,1,0:T(8,128)(2,1)S(1)}, bf16[27,32,128]{2,1,0:T(8,128)(2,1)S(1)}, u32[]{:S(2)}, u32[]{:S(2)}) %collective-permute-start.11) | collective-permute-done | bytes 221216 | tf_op jit(solution)/shard_map/ppermute | solution.py:39
  29.9 0.0 collective-permute-start.12
  29.9 0.0 collective-permute-done.9.m3
  29.9 0.5 collective-permute-start.15
  30.4 8.4 %collective-permute-done.16 = bf16[6,192,128]{2,1,0:T(8,128)(2,1)S(1)} collective-permute-done((bf16[6,192,128]{2,1,0:T(8,128)(2,1)S(1)}, bf16[6,192,128]{2,1,0:T(8,128)(2,1)S(1)}, u32[]{:S(2)}, u32[]{:S(2)}) %collective-permute-start.16) | collective-permute-done | bytes 294944 | tf_op jit(solution)/shard_map/ppermute | solution.py:39
  38.8 0.0 collective-permute-start.17
  38.8 0.0 collective-permute-done.12.l3
  38.8 1.2 %shard_map.86 = (bf16[384,1152]{1,0:T(8,128)(2,1)S(1)}, bf16[384,1152]{1,0:T(8,128)(2,1)S(1)}, bf16[1152,384]{1,0:T(8,128)(2,1)S(1)}, bf16[1152,384]{1,0:T(8,128)(2,1)S(1)}) custom-call(s32[5]{0:T(128)S(1)} %stack.22.info, bf16[27,32,128]{2,1,0:T(8,128)(2,1)S(1)} %copy-done, bf16[27,32,128]{2,1,0:T(8,128)(2,1)S(1)} %collective-permute-done.7.m1, ...), custom_call_target="tpu_custom_call" | custom-call | flops 1000000 | bytes 6000000 | tf_op jit(solution)/shard_map/pallas_call | solution.py:364
  40.0 0.0 collective-permute-done.5
  40.0 0.0 collective-permute-done.6
  40.0 4.0 %shard_map.87 = (bf16[4,4,128,128]{3,2,1,0:T(8,128)(2,1)S(1)}, f32[4,4,128,128]{3,2,1,0:T(8,128)S(1)}, bf16[6,6,128,128]{3,2,1,0:T(8,128)(2,1)S(1)}) custom-call(s32[5]{0:T(128)S(1)} %stack.22.info, bf16[6,2,128,128]{3,2,1,0:T(8,128)(2,1)S(1)} %bitcast.24, bf16[6,2,128,128]{3,2,1,0:T(8,128)(2,1)S(1)} %bitcast.29, bf16[6,2,128,128]{3,2,1,0:T(8,128)(2,1)S(1)} %bitcast.30, ...), custom_call_target="tpu_custom_call" | custom-call | flops 3000000000 | bytes 4000000 | tf_op jit(solution)/shard_map/pallas_call | solution.py:373
  44.0 0.0 collective-permute-done.15
  44.0 0.0 collective-permute-done.17
  44.0 1.0 shard_map.91
  45.1 6.2 %shard_map.92 = (bf16[2,64,32,128]{3,2,1,0:T(8,128)(2,1)S(1)}, bf16[2,64,32,128]{3,2,1,0:T(8,128)(2,1)S(1)}) custom-call(s32[5]{0:T(128)S(1)} %stack.22.info, bf16[6,6,128,128]{3,2,1,0:T(8,128)(2,1)S(1)} %get-tuple-element.31.act_window, bf16[6,6,128,128]{3,2,1,0:T(8,128)(2,1)S(1)} %get-tuple-element.34.window, ...), custom_call_target="tpu_custom_call" | custom-call | flops 4000000000 | bytes 8000000 | tf_op jit(solution)/shard_map/pallas_call | solution.py:394
  51.3 0.6 collective-permute-start.18
  51.8 2.3 %collective-permute-done.18 = bf16[2,64,32,128]{3,2,1,0:T(8,128)(2,1)S(1)} collective-permute-done((bf16[2,64,32,128]{3,2,1,0:T(8,128)(2,1)S(1)}, bf16[2,64,32,128]{3,2,1,0:T(8,128)(2,1)S(1)}, u32[]{:S(2)}, u32[]{:S(2)}) %collective-permute-start.18) | collective-permute-done | bytes 1048608 | tf_op jit(solution)/shard_map/ppermute | solution.py:39
  54.1 0.3 add_convert_fusion
  54.4 32.7 %all_to_all.10.terms_ref = bf16[64,64,128]{2,1,0:T(8,128)(2,1)S(1)} all-to-all(bf16[64,64,128]{2,1,0:T(8,128)(2,1)S(1)} %bitcast.31), channel_id=1, replica_groups=mesh['depth'=32,'chip'=2,'core'=2] {'chip','depth'}, dimensions={0} | all-to-all | bytes 2097152 | tf_op jit(solution)/shard_map/all_to_all | solution.py:414
  87.1 1.0 shard_map.93
  88.1 4.8 %all-to-all-start.1 = ((bf16[32,64,128]{2,1,0:T(8,128)(2,1)}), bf16[32,64,128]{2,1,0:T(8,128)(2,1)S(1)}, u32[]{:S(2)}, u32[]{:S(2)}) async-start(bf16[32,64,128]{2,1,0:T(8,128)(2,1)} %shard_map.93), calls=%async_computation.1 | async-start | bytes 1048576 | tf_op jit(solution)/shard_map/all_to_all | solution.py:416
  92.9 1.5 %shard_map.88 = (bf16[2,2,2,32,128]{4,3,2,1,0:T(8,128)(2,1)S(1)}, bf16[2,2,2,32,128]{4,3,2,1,0:T(8,128)(2,1)S(1)}) custom-call(s32[5]{0:T(128)S(1)} %stack.22.info, bf16[4,4,128,128]{3,2,1,0:T(8,128)(2,1)S(1)} %get-tuple-element.27.act_ref.mid_act, bf16[384,1152]{1,0:T(8,128)(2,1)S(1)} %get-tuple-element.28.weights), custom_call_target="tpu_custom_call" | custom-call | flops 500000000 | bytes 2000000 | tf_op jit(solution)/shard_map/pallas_call | solution.py:382
  94.3 0.1 collective-permute-start.13
  94.5 1.2 %collective-permute-done.13.near = bf16[2,2,2,32,128]{4,3,2,1,0:T(8,128)(2,1)S(1)} collective-permute-done((bf16[2,2,2,32,128]{4,3,2,1,0:T(8,128)(2,1)S(1)}, bf16[2,2,2,32,128]{4,3,2,1,0:T(8,128)(2,1)S(1)}, u32[]{:S(2)}, u32[]{:S(2)}) %collective-permute-start.13) | collective-permute-done | bytes 65568 | tf_op jit(solution)/shard_map/ppermute | solution.py:39
  95.7 1.0 collective-permute-start.14
  96.7 6.3 %collective-permute-done.14.far = bf16[2,2,2,32,128]{4,3,2,1,0:T(8,128)(2,1)S(1)} collective-permute-done((bf16[2,2,2,32,128]{4,3,2,1,0:T(8,128)(2,1)S(1)}, bf16[2,2,2,32,128]{4,3,2,1,0:T(8,128)(2,1)S(1)}, u32[]{:S(2)}, u32[]{:S(2)}) %collective-permute-start.14) | collective-permute-done | bytes 65568 | tf_op jit(solution)/shard_map/ppermute | solution.py:39
  103.1 0.6 shard_map.89
  103.6 0.7 copy.14
  104.3 1.6 %all-to-all-done.1 = bf16[32,64,128]{2,1,0:T(8,128)(2,1)S(1)} async-done(((bf16[32,64,128]{2,1,0:T(8,128)(2,1)}), bf16[32,64,128]{2,1,0:T(8,128)(2,1)S(1)}, u32[]{:S(2)}, u32[]{:S(2)}) %all-to-all-start.1) | async-done | bytes 524320 | tf_op jit(solution)/shard_map/all_to_all | solution.py:416
  105.9 1.0 shard_map.94
  (4 shorter events, 0.0 us)
Async XLA Ops:
  0.6 6.8 %copy-start.2 = (bf16[8,32,64]{2,1,0:T(8,128)(2,1)S(1)}, bf16[8,32,64]{2,1,0:T(8,128)(2,1)}, u32[]{:S(2)}) copy-start(bf16[8,32,64]{2,1,0:T(8,128)(2,1)} %s0.1) | copy-start | bytes 98308
  0.6 10.9 %copy-start = (bf16[27,32,128]{2,1,0:T(8,128)(2,1)S(1)}, bf16[27,32,128]{2,1,0:T(8,128)(2,1)}, u32[]{:S(2)}) copy-start(bf16[27,32,128]{2,1,0:T(8,128)(2,1)} %m0.1) | copy-start | bytes 663556
  0.7 13.1 %copy-start.1 = (bf16[27,32,128]{2,1,0:T(8,128)(2,1)S(1)}, bf16[27,32,128]{2,1,0:T(8,128)(2,1)}, u32[]{:S(2)}) copy-start(bf16[27,32,128]{2,1,0:T(8,128)(2,1)} %l0.1) | copy-start | bytes 663556
  0.7 4.6 %collective-permute-start.1 = (bf16[8,32,64]{2,1,0:T(8,128)(2,1)}, bf16[8,32,64]{2,1,0:T(8,128)(2,1)S(1)}, u32[]{:S(2)}, u32[]{:S(2)}) collective-permute-start(bf16[8,32,64]{2,1,0:T(8,128)(2,1)} %s0.1), channel_id=1, source_target_pairs={{0,2},{1,3},{2,0},{3,1},{4,6},{5,7},{6,4},{7,5},{8,10},{9,11},{10,... | collective-permute-start | bytes 98312 | tf_op jit(solution)/shard_map/ppermute | solution.py:39
  2.8 4.7 %collective-permute-start = (bf16[8,32,64]{2,1,0:T(8,128)(2,1)}, bf16[8,32,64]{2,1,0:T(8,128)(2,1)S(1)}, u32[]{:S(2)}, u32[]{:S(2)}) collective-permute-start(bf16[8,32,64]{2,1,0:T(8,128)(2,1)} %s0.1), channel_id=1, source_target_pairs={{0,1},{1,0},{2,3},{3,2},{4,5},{5,4},{6,7},{7,6},{8,9},{9,8},{10,11... | collective-permute-start | bytes 98312 | tf_op jit(solution)/shard_map/ppermute | solution.py:39
  5.2 2.3 %collective-permute-start.2 = (bf16[8,32,64]{2,1,0:T(8,128)(2,1)S(1)}, bf16[8,32,64]{2,1,0:T(8,128)(2,1)S(1)}, u32[]{:S(2)}, u32[]{:S(2)}) collective-permute-start(bf16[8,32,64]{2,1,0:T(8,128)(2,1)S(1)} %collective-permute-done.1.s2), channel_id=1, source_target_pairs={{0,1},{1,0},{2,3},{3,2},{4,5},{5,4},{6,7},{7,6},{8,9},{9,8},{10,11... | collective-permute-start | bytes 98312 | tf_op jit(solution)/shard_map/ppermute | solution.py:39
  9.1 8.8 %collective-permute-start.3 = (bf16[2,512,128]{2,1,0:T(8,128)(2,1)S(1)}, bf16[2,512,128]{2,1,0:T(8,128)(2,1)S(1)}, u32[]{:S(2)}, u32[]{:S(2)}) collective-permute-start(bf16[2,512,128]{2,1,0:T(8,128)(2,1)S(1)} %get-tuple-element.25.pack), channel_id=1, source_target_pairs={{0,4},{1,5},{2,6},{3,7},{4,0},{5,1},{6,2},{7,3},{8,12},{9,13},{10,... | collective-permute-start | bytes 786440 | tf_op jit(solution)/shard_map/ppermute | solution.py:39
  10.9 11.2 %collective-permute-start.4 = (bf16[2,512,128]{2,1,0:T(8,128)(2,1)S(1)}, bf16[2,512,128]{2,1,0:T(8,128)(2,1)S(1)}, u32[]{:S(2)}, u32[]{:S(2)}) collective-permute-start(bf16[2,512,128]{2,1,0:T(8,128)(2,1)S(1)} %get-tuple-element.25.pack), channel_id=1, source_target_pairs={{4,8},{5,9},{6,10},{7,11},{8,4},{9,5},{10,6},{11,7},{12,16},{13,17... | collective-permute-start | bytes 786440 | tf_op jit(solution)/shard_map/ppermute | solution.py:39
  11.6 11.2 %collective-permute-start.7 = (bf16[27,32,128]{2,1,0:T(8,128)(2,1)S(1)}, bf16[27,32,128]{2,1,0:T(8,128)(2,1)S(1)}, u32[]{:S(2)}, u32[]{:S(2)}) collective-permute-start(bf16[27,32,128]{2,1,0:T(8,128)(2,1)S(1)} %copy-done), channel_id=1, source_target_pairs={{0,1},{1,0},{2,3},{3,2},{4,5},{5,4},{6,7},{7,6},{8,9},{9,8},{10,11... | collective-permute-start | bytes 663560 | tf_op jit(solution)/shard_map/ppermute | solution.py:39
  11.9 11.6 %collective-permute-start.8 = (bf16[27,32,128]{2,1,0:T(8,128)(2,1)S(1)}, bf16[27,32,128]{2,1,0:T(8,128)(2,1)S(1)}, u32[]{:S(2)}, u32[]{:S(2)}) collective-permute-start(bf16[27,32,128]{2,1,0:T(8,128)(2,1)S(1)} %copy-done), channel_id=1, source_target_pairs={{0,2},{1,3},{2,0},{3,1},{4,6},{5,7},{6,4},{7,5},{8,10},{9,11},{10,... | collective-permute-start | bytes 663560 | tf_op jit(solution)/shard_map/ppermute | solution.py:39
  13.8 12.1 %collective-permute-start.10 = (bf16[27,32,128]{2,1,0:T(8,128)(2,1)S(1)}, bf16[27,32,128]{2,1,0:T(8,128)(2,1)S(1)}, u32[]{:S(2)}, u32[]{:S(2)}) collective-permute-start(bf16[27,32,128]{2,1,0:T(8,128)(2,1)S(1)} %copy-done.1), channel_id=1, source_target_pairs={{0,1},{1,0},{2,3},{3,2},{4,5},{5,4},{6,7},{7,6},{8,9},{9,8},{10,11... | collective-permute-start | bytes 663560 | tf_op jit(solution)/shard_map/ppermute | solution.py:39
  17.9 12.0 %collective-permute-start.11 = (bf16[27,32,128]{2,1,0:T(8,128)(2,1)S(1)}, bf16[27,32,128]{2,1,0:T(8,128)(2,1)S(1)}, u32[]{:S(2)}, u32[]{:S(2)}) collective-permute-start(bf16[27,32,128]{2,1,0:T(8,128)(2,1)S(1)} %copy-done.1), channel_id=1, source_target_pairs={{0,18},{1,19},{2,16},{3,17},{4,22},{5,23},{6,20},{7,21},{8,26},{9,... | collective-permute-start | bytes 663560 | tf_op jit(solution)/shard_map/ppermute | solution.py:39
  22.7 17.4 %collective-permute-start.5 = (bf16[6,256,128]{2,1,0:T(8,128)(2,1)S(1)}, bf16[6,256,128]{2,1,0:T(8,128)(2,1)S(1)}, u32[]{:S(2)}, u32[]{:S(2)}) collective-permute-start(bf16[6,256,128]{2,1,0:T(8,128)(2,1)S(1)} %shard_map.85), channel_id=1, source_target_pairs={{0,1},{1,0},{2,3},{3,2},{4,5},{5,4},{6,7},{7,6},{8,9},{9,8},{10,11... | collective-permute-start | bytes 1179656 | tf_op jit(solution)/shard_map/ppermute | solution.py:39
  22.8 17.3 %collective-permute-start.6 = (bf16[6,256,128]{2,1,0:T(8,128)(2,1)S(1)}, bf16[6,256,128]{2,1,0:T(8,128)(2,1)S(1)}, u32[]{:S(2)}, u32[]{:S(2)}) collective-permute-start(bf16[6,256,128]{2,1,0:T(8,128)(2,1)S(1)} %shard_map.85), channel_id=1, source_target_pairs={{1,2},{2,1},{5,6},{6,5},{9,10},{10,9},{13,14},{14,13},{17,18},{18,... | collective-permute-start | bytes 1179656 | tf_op jit(solution)/shard_map/ppermute | solution.py:39
  23.5 6.5 %collective-permute-start.9 = (bf16[27,32,128]{2,1,0:T(8,128)(2,1)S(1)}, bf16[27,32,128]{2,1,0:T(8,128)(2,1)S(1)}, u32[]{:S(2)}, u32[]{:S(2)}) collective-permute-start(bf16[27,32,128]{2,1,0:T(8,128)(2,1)S(1)} %collective-permute-done.8.m2), channel_id=1, source_target_pairs={{0,1},{1,0},{2,3},{3,2},{4,5},{5,4},{6,7},{7,6},{8,9},{9,8},{10,11... | collective-permute-start | bytes 663560 | tf_op jit(solution)/shard_map/ppermute | solution.py:39
  25.9 13.0 %collective-permute-start.16 = (bf16[6,192,128]{2,1,0:T(8,128)(2,1)S(1)}, bf16[6,192,128]{2,1,0:T(8,128)(2,1)S(1)}, u32[]{:S(2)}, u32[]{:S(2)}) collective-permute-start(bf16[6,192,128]{2,1,0:T(8,128)(2,1)S(1)} %get-tuple-element.33), channel_id=1, source_target_pairs={{0,2},{1,3},{2,0},{3,1},{4,6},{5,7},{6,4},{7,5},{8,10},{9,11},{10,... | collective-permute-start | bytes 884744 | tf_op jit(solution)/shard_map/ppermute | solution.py:39
  29.9 8.9 %collective-permute-start.12 = (bf16[27,32,128]{2,1,0:T(8,128)(2,1)S(1)}, bf16[27,32,128]{2,1,0:T(8,128)(2,1)S(1)}, u32[]{:S(2)}, u32[]{:S(2)}) collective-permute-start(bf16[27,32,128]{2,1,0:T(8,128)(2,1)S(1)} %collective-permute-done.11.l2), channel_id=1, source_target_pairs={{0,1},{1,0},{2,3},{3,2},{4,5},{5,4},{6,7},{7,6},{8,9},{9,8},{10,11... | collective-permute-start | bytes 663560 | tf_op jit(solution)/shard_map/ppermute | solution.py:39
  29.9 14.1 %collective-permute-start.15 = (bf16[6,256,128]{2,1,0:T(8,128)(2,1)S(1)}, bf16[6,256,128]{2,1,0:T(8,128)(2,1)S(1)}, u32[]{:S(2)}, u32[]{:S(2)}) collective-permute-start(bf16[6,256,128]{2,1,0:T(8,128)(2,1)S(1)} %get-tuple-element.32), channel_id=1, source_target_pairs={{0,1},{1,0},{2,3},{3,2},{4,5},{5,4},{6,7},{7,6},{8,9},{9,8},{10,11... | collective-permute-start | bytes 1179656 | tf_op jit(solution)/shard_map/ppermute | solution.py:39
  38.8 5.2 %collective-permute-start.17 = (bf16[6,192,128]{2,1,0:T(8,128)(2,1)S(1)}, bf16[6,192,128]{2,1,0:T(8,128)(2,1)S(1)}, u32[]{:S(2)}, u32[]{:S(2)}) collective-permute-start(bf16[6,192,128]{2,1,0:T(8,128)(2,1)S(1)} %collective-permute-done.16), channel_id=1, source_target_pairs={{0,1},{1,0},{2,3},{3,2},{4,5},{5,4},{6,7},{7,6},{8,9},{9,8},{10,11... | collective-permute-start | bytes 884744 | tf_op jit(solution)/shard_map/ppermute | solution.py:39
  51.3 2.9 %collective-permute-start.18 = (bf16[2,64,32,128]{3,2,1,0:T(8,128)(2,1)S(1)}, bf16[2,64,32,128]{3,2,1,0:T(8,128)(2,1)S(1)}, u32[]{:S(2)}, u32[]{:S(2)}) collective-permute-start(bf16[2,64,32,128]{3,2,1,0:T(8,128)(2,1)S(1)} %get-tuple-element.42), channel_id=1, source_target_pairs={{0,1},{1,0},{2,3},{3,2},{4,5},{5,4},{6,7},{7,6},{8,9},{9,8},{10,11... | collective-permute-start | bytes 3145736 | tf_op jit(solution)/shard_map/ppermute | solution.py:39
  88.1 17.8 %all-to-all-start.1 = ((bf16[32,64,128]{2,1,0:T(8,128)(2,1)}), bf16[32,64,128]{2,1,0:T(8,128)(2,1)S(1)}, u32[]{:S(2)}, u32[]{:S(2)}) async-start(bf16[32,64,128]{2,1,0:T(8,128)(2,1)} %shard_map.93), calls=%async_computation.1 | async-start | bytes 1048576 | tf_op jit(solution)/shard_map/all_to_all | solution.py:416
  94.3 1.3 %collective-permute-start.13 = (bf16[2,2,2,32,128]{4,3,2,1,0:T(8,128)(2,1)S(1)}, bf16[2,2,2,32,128]{4,3,2,1,0:T(8,128)(2,1)S(1)}, u32[]{:S(2)}, u32[]{:S(2)}) collective-permute-start(bf16[2,2,2,32,128]{4,3,2,1,0:T(8,128)(2,1)S(1)} %get-tuple-element.30), channel_id=1, source_target_pairs={{0,1},{1,0},{2,3},{3,2},{4,5},{5,4},{6,7},{7,6},{8,9},{9,8},{10,11... | collective-permute-start | bytes 196616 | tf_op jit(solution)/shard_map/ppermute | solution.py:39
  95.7 7.4 %collective-permute-start.14 = (bf16[2,2,2,32,128]{4,3,2,1,0:T(8,128)(2,1)S(1)}, bf16[2,2,2,32,128]{4,3,2,1,0:T(8,128)(2,1)S(1)}, u32[]{:S(2)}, u32[]{:S(2)}) collective-permute-start(bf16[2,2,2,32,128]{4,3,2,1,0:T(8,128)(2,1)S(1)} %pad_maximum_fusion), channel_id=1, source_target_pairs={{0,2},{1,3},{2,0},{3,1},{4,6},{5,7},{6,4},{7,5},{8,10},{9,11},{10,... | collective-permute-start | bytes 196616 | tf_op jit(solution)/shard_map/ppermute | solution.py:39

commit v6 on v5

--- a/solution.py
+++ b/solution.py
@@ -11,8 +11,8 @@
 FILT = ("chip", "core")
 CELLS = 128
 LIMITS = {
-    "stride": 8, "act_join": 4, "cot_join": 4, "turn": 8, "weights": 10, "middle": 20, "result": 8,
-    "back": 28, "rows": 2, "sum": 6, "finish": 4,
+    "stride": 8, "join": 6, "weights": 10, "middle": 20, "result": 8, "grad_l": 10, "back": 26,
+    "rows": 2, "sum": 6, "finish": 4,
 }
 VMEM = pl.BlockSpec(memory_space=pltpu.VMEM)
 SMEM = pl.BlockSpec(memory_space=pltpu.SMEM)
@@ -79,7 +79,10 @@
     )
 
 
-def stride_body(info, u_ref, s0, s1, s2, s3, cot_ref, pack_ref, pre_ref, columns_ref, weights):
+def stride_body(
+    info, u_ref, s0, s1, s2, s3, c0, c1, c2, c3,
+    pack_ref, pre_ref, columns_ref, cot_ref, weights,
+):
     filt = info[1]
     for j, part in enumerate((s0, s1, s2, s3)):
         start = pl.multiple_of((filt ^ j) * 32, 32)
@@ -104,39 +107,18 @@
             pre_ref[p, r] = pre
             act = (pre * jax.nn.sigmoid(pre)).astype(jnp.bfloat16)
             pack_ref[p, r * 128 : r * 128 + 128] = act
-    pack_ref[:, 256:512] = cot_ref[...]
-
-
-def act_body(info, pack, pair, beyond, column_ref):
+            for j, part in enumerate((c0, c1, c2, c3)):
+                start = pl.multiple_of((filt ^ j) * 32, 32)
+                cot_ref[p, r, pl.ds(start, 32), :] = part[filt, r, p]
+            cot = cot_ref[p, r].astype(jnp.float32).T.astype(jnp.bfloat16)
+            pack_ref[p, 256 + r * 128 : 384 + r * 128] = cot
+
+
+def join_body(info, pack, pair, beyond, act_ref, cot_ref):
     odd = info[0] & 1
-    column_ref[2:4] = pack[:, :256]
-    column_ref[pl.ds(4 - 4 * odd, 2)] = pair[:, :256]
-    column_ref[pl.ds(4 * odd, 2)] = beyond[:, :256]
-
-
-def cot_body(info, pack, pair, beyond, column_ref, wanted_ref):
-    odd, chip = info[0] & 1, info[3]
-    start = pl.multiple_of(256 + 64 * (1 - chip), 64)
     for at, part in ((2, pack), (4 - 4 * odd, pair), (4 * odd, beyond)):
-        column_ref[pl.ds(at, 2)] = part[:, 256:512]
-        wanted_ref[pl.ds(at, 2)] = part[:, pl.ds(start, 192)]
-
-
-def turn_body(info, own, near, far, both, cells_ref, own_ref, tiles):
-    filt, chip = info[1], info[3]
-    for p in range(6):
-        for r in range(6):
-            row = 2 * filt - 2 + r
-            valid = jnp.where((row >= 0) & (row <= 7), 1.0, 0.0)
-            wide = jnp.clip(row, 0, 7)
-            cut = jnp.clip(row - 2 * chip, 0, 5)
-            for j, (part, at) in enumerate(((own, wide), (near, wide), (far, cut), (both, cut))):
-                start = pl.multiple_of((filt ^ j) * 32, 32)
-                tiles[p * 6 + r, pl.ds(start, 32), :] = part[p, at]
-            tile = tiles[p * 6 + r]
-            cells_ref[p, r] = (tile.astype(jnp.float32).T * valid).astype(jnp.bfloat16)
-            if 2 <= p < 4 and 2 <= r < 4:
-                own_ref[p - 2, r - 2] = tile
+        act_ref[pl.ds(at, 2)] = part[:, :256]
+        cot_ref[pl.ds(at, 2)] = part[:, 256:]
 
 
 def fill_window(window, middle, near, cross, core):
@@ -264,21 +246,25 @@
             put_grad(refs, first + 9 * a + 3 * b + c, block)
 
 
+def last_body(info, mid_act, cot_own, keep_ref, send_ref):
+    core = info[4]
+    own = [in_order(cot_own, (p, r), core).astype(jnp.float32) for p in range(2) for r in range(2)]
+    cot_rows = shifts_of(jnp.concatenate(own, axis=1))
+    wide = jnp.concatenate([block_of(mid_act, a, 2, b, 2) for a, b in TAPS], axis=1)
+    put_kernel_grad((keep_ref, send_ref), 0, dot(cot_rows, wide))
+
+
 def back_body(
-    info, act_window, window, weights_l, weights_m, mid_act, mid_pre, level_pre, columns, cot_own,
-    keep_ref, send_ref, delta, turned,
+    info, act_window, mid, near, cross, weights_l, weights_m, mid_pre, level_pre, columns,
+    keep_ref, send_ref, window, delta, turned,
 ):
     core = info[4]
     refs = (keep_ref, send_ref)
+    fill_window(window, mid, near, cross, core)
 
     back = conv_backward(window, 0, 4, 0, 4, weights_l)
     here = jnp.where(inside(info), back * silu_slope(mid_pre[...].reshape(16 * CELLS, 128)), 0.0)
     delta[...] = here.astype(jnp.bfloat16).reshape(4, 4, CELLS, 128)
-
-    own = [in_order(cot_own, (p, r), core).astype(jnp.float32) for p in range(2) for r in range(2)]
-    cot_rows = shifts_of(jnp.concatenate(own, axis=1))
-    wide = jnp.concatenate([block_of(mid_act, a, 2, b, 2) for a, b in TAPS], axis=1)
-    put_kernel_grad(refs, 0, dot(cot_rows, wide))
 
     for p in range(2):
         for r in range(2):
@@ -286,7 +272,7 @@
             turned[:, at : at + CELLS] = delta[1 + p, 1 + r].astype(jnp.float32).T
     delta_rows = shifts_of(in_order(turned, (), core))
     wide = jnp.concatenate([block_of(act_window, 1 + a, 2, 1 + b, 2) for a, b in TAPS], axis=1)
-    put_kernel_grad(refs, 27, dot(delta_rows, wide))
+    put_kernel_grad(refs, 0, dot(delta_rows, wide))
 
     back = conv_backward(delta, 0, 2, 0, 2, weights_m)
     pre = level_pre[...].reshape(4 * CELLS, 128)
@@ -296,8 +282,8 @@
         turned[:, n * 128 : n * 128 + 128] = grad[n * 128 : n * 128 + 128].T
     ordered = in_order(turned, (), core)
     for n in range(4):
-        put_grad(refs, 54 + n, ordered[:, n * 128 : n * 128 + 128])
-    for n in range(58, 64):
+        put_grad(refs, 27 + n, ordered[:, n * 128 : n * 128 + 128])
+    for n in range(31, 37):
         put_grad(refs, n, jnp.zeros((128, 128), jnp.float32))
 
 
@@ -315,51 +301,48 @@
     out_ref[...] = jnp.broadcast_to(total[None], out_ref.shape)
 
 
+def row_parts(column):
+    def inner(d, f):
+        return (d, 3 - f) if f in (1, 2) else (-1, f)
+
+    cross = shifted(column, inner)
+    return column, swap_core(column), cross
+
+
 def whole(upper_level, stride_weight, middle_weight, last_weight, cotangent):
     depth = lax.axis_size("depth")
     chip, core = lax.axis_index("chip"), lax.axis_index("core")
     info = jnp.stack([lax.axis_index("depth"), 2 * chip + core, jnp.int32(depth), chip, core])
+    cot_rows = cotangent.reshape(32, 2, 4, 2, 128).transpose(2, 3, 1, 0, 4)
+    cot_parts = four_parts(cot_rows, 0)
     stride_parts = four_parts(stride_weight, 0)
     middle_parts = four_parts(middle_weight, 0)
     last_parts = four_parts(last_weight, 4)
     upper = upper_level.transpose(1, 2, 0, 3)
-    cot_rows = cotangent.transpose(1, 2, 0, 3).reshape(2, 256, 128)
-    pack, level_pre, columns = call(
+
+    pack, level_pre, columns, cot_own = call(
         "stride",
         stride_body,
-        [shape((2, 512, 128)), shape((2, 2, 128, 128), jnp.float32), shape((512, 512))],
+        [
+            shape((2, 512, 128)),
+            shape((2, 2, 128, 128), jnp.float32),
+            shape((512, 512)),
+            shape((2, 2, 128, 128)),
+        ],
         [pltpu.VMEM((128, 512), jnp.bfloat16)],
         flops=200_000_000,
         moved=1_500_000,
-        in_specs=[SMEM] + [VMEM] * 6,
-    )(info, upper, *stride_parts, cot_rows)
+        in_specs=[SMEM] + [VMEM] * 9,
+    )(info, upper, *stride_parts, *cot_parts)
     beyond = shifted(pack, lambda d, f: (d + 1 if d % 2 else d - 1, f))
     pair = shifted(pack, lambda d, f: (d ^ 1, f))
-    act_column = call(
-        "act_join", act_body, shape((6, 256, 128)), in_specs=[SMEM] + [VMEM] * 3
+    columns_joined = call(
+        "join", join_body, [shape((6, 256, 128))] * 2, in_specs=[SMEM] + [VMEM] * 3
     )(info, pack, pair, beyond)
-    act_cross = shifted(act_column, lambda d, f: (d, 3 - f) if f in (1, 2) else (-1, f))
-    act_near = swap_core(act_column)
-    act_parts = [x.reshape(6, 2, 128, 128) for x in (act_column, act_near, act_cross)]
-    cot_column, cot_wanted = call(
-        "cot_join",
-        cot_body,
-        [shape((6, 256, 128)), shape((6, 192, 128))],
-        in_specs=[SMEM] + [VMEM] * 3,
-    )(info, pack, pair, beyond)
-    cot_near = swap_core(cot_column)
-    cot_far = swap_chip(cot_wanted)
-    cot_both = swap_core(cot_far)
-    cot_parts = [x.reshape(6, -1, 32, 128) for x in (cot_column, cot_near, cot_far, cot_both)]
-    cot_cells, cot_own = call(
-        "turn",
-        turn_body,
-        [shape((6, 6, 128, 128)), shape((2, 2, 128, 128))],
-        [pltpu.VMEM((36, 128, 128), jnp.bfloat16)],
-        flops=1_000_000,
-        moved=3_000_000,
-        in_specs=[SMEM] + [VMEM] * 4,
-    )(info, *cot_parts)
+    act_parts, back_parts = [
+        [x.reshape(6, 2, 128, 128) for x in (column, near, cross)]
+        for column, near, cross in (row_parts(columns_joined[0]), row_parts(columns_joined[1]))
+    ]
 
     forward_m, forward_l, backward_l, backward_m = call(
         "weights",
@@ -391,17 +374,30 @@
     result_near = swap_core(leave)
     result_far = swap_chip(jnp.stack([stay[1], result_near[1]]))
 
+    keep_l, send_l = call(
+        "grad_l",
+        last_body,
+        [shape((2, 27, 32, 128))] * 2,
+        flops=500_000_000,
+        moved=3_000_000,
+        in_specs=[SMEM] + [VMEM] * 2,
+    )(info, mid_act, cot_own)
+    other_l = swap_core(send_l)
+
     keep, send = call(
         "back",
         back_body,
-        [shape((2, 64, 32, 128)), shape((2, 64, 32, 128))],
-        [pltpu.VMEM((4, 4, 128, 128), jnp.bfloat16), pltpu.VMEM((128, 512), jnp.float32)],
+        [shape((2, 37, 32, 128))] * 2,
+        [
+            pltpu.VMEM((6, 6, 128, 128), jnp.bfloat16),
+            pltpu.VMEM((4, 4, 128, 128), jnp.bfloat16),
+            pltpu.VMEM((128, 512), jnp.float32),
+        ],
         flops=4_000_000_000,
         moved=8_000_000,
         in_specs=[SMEM] + [VMEM] * 9,
     )(
-        info, act_window, cot_cells, backward_l, backward_m,
-        mid_act, mid_pre, level_pre, columns, cot_own,
+        info, act_window, *back_parts, backward_l, backward_m, mid_pre, level_pre, columns
     )
 
     result = call(
@@ -410,7 +406,13 @@
     result = result.transpose(3, 1, 0, 2, 4).reshape(32, 2, 8, 128)
 
     other = swap_core(send)
-    terms = (keep.astype(jnp.float32) + other.astype(jnp.float32)).astype(jnp.bfloat16)
+    terms = jnp.concatenate(
+        [
+            (x.astype(jnp.float32) + y.astype(jnp.float32)).astype(jnp.bfloat16)
+            for x, y in ((keep_l, other_l), (keep, other))
+        ],
+        axis=1,
+    )
     terms = lax.all_to_all(terms.reshape(2 * depth, 64, 128), ("chip", "depth"), 0, 0, tiled=True)
     spread = call("sum", sum_body, shape((depth, 64, 128)), in_specs=[VMEM])(terms)
     full = lax.all_to_all(spread, "depth", 0, 0, tiled=True)

time: 107 us -> 104 us (0.972)
  waiting for transfers between devices: 28.7 us -> 23.6 us
  starting transfers between devices: 22.2 us -> 27.1 us
  blocking collectives: 32.7 us -> 30.1 us
    ppermute x19 -> x22, starting transfers between devices: 17.4 us -> 22.4 us  [shifted(): return lax.ppermute(value, AXES, pairs_of(move))]
    ppermute x19 -> x22, waiting for transfers between devices: 27.2 us -> 22.3 us  [shifted(): return lax.ppermute(value, AXES, pairs_of(move))]
    all_to_all x1, blocking collectives: 32.7 us -> 30.1 us  [whole(): lax.all_to_all(terms.reshape(2 * depth, 64, 128), ('chip', 'depth'), 0, 0...]
    unnamed x8 -> x9, local copies, waits for them, and re-layouts: 1.92 us -> 2.95 us
    pallas_call x4 -> x3, Pallas kernels: 8.36 us -> 7.93 us  [the longest x1 6.06 us: whole(): call('back', back_body, [shape((2, 37, 32, 128))] * 2, [pltpu.VMEM((6, 6,...]
  transfers between devices with their start and end apart: 20 -> 23, of which waited for: 8 -> 8; matrix products, arithmetic and copies ran while one was open for 3% -> 2% of each run, Pallas kernels for 8% -> 15%
where the time goes in v6:
time: 104 us
  blocking collectives  30.1 us (29%)
  starting transfers between devices  27.1 us (26%)
  waiting for transfers between devices  23.6 us (23%)
  Pallas kernels  18.7 us (18%)
  local copies, waits for them, and re-layouts  3.05 us (3%)
    all_to_all x1, blocking collectives, whole(): lax.all_to_all(terms.reshape(2 * depth, 64, 128), ('chip', 'depth'), 0, 0...  30.1 us
    ppermute x22, starting transfers between devices, shifted(): return lax.ppermute(value, AXES, pairs_of(move))  22.4 us
    ppermute x22, waiting for transfers between devices, shifted(): return lax.ppermute(value, AXES, pairs_of(move))  22.3 us
    pallas_call x1, Pallas kernels, whole(): call('back', back_body, [shape((2, 37, 32, 128))] * 2, [pltpu.VMEM((6, 6,...  6.06 us
    all_to_all x1, starting transfers between devices, whole(): full = lax.all_to_all(spread, 'depth', 0, 0, tiled=True)  4.69 us
    pallas_call x1, Pallas kernels, whole(): call('middle', middle_body, [shape((4, 4, 128, 128)), shape((4, 4, 128, 1...  3.98 us
    unnamed x9, local copies, waits for them, and re-layouts  2.95 us
  transfers between devices with their start and end apart: 23, of which 8 were waited for; matrix products, arithmetic and copies ran while one was open for 2% of the time, Pallas kernels for 15%

profile of v6, /device:TPU:0, one launch (start us, length us, event | category | flops | bytes accessed | tf_op | source)
XLA Modules:
  0.0 103.8 jit_solution(12781263517528930270)
XLA Ops:
  0.6 0.0 copy-start.2
  0.6 1.0 copy.12
  1.6 2.1 %collective-permute-start.4 = (bf16[4,2,2,32,128]{4,3,2,1,0:T(8,128)(2,1)S(1)}, bf16[4,2,2,32,128]{4,3,2,1,0:T(8,128)(2,1)S(1)}, u32[]{:S(2)}, u32[]{:S(2)}) collective-permute-start(bf16[4,2,2,32,128]{4,3,2,1,0:T(8,128)(2,1)S(1)} %bitcast.22), channel_id=1, source_target_pairs={{0,2},{1,3},{2,0},{3,1},{4,6},{5,7},{6,4},{7,5},{8,10},{9,11},{10,... | collective-permute-start | bytes 393224 | tf_op jit(solution)/shard_map/ppermute | solution.py:39
  3.7 0.0 collective-permute-start.3
  3.7 3.5 %collective-permute-done.4.c2 = bf16[4,2,2,32,128]{4,3,2,1,0:T(8,128)(2,1)S(1)} collective-permute-done((bf16[4,2,2,32,128]{4,3,2,1,0:T(8,128)(2,1)S(1)}, bf16[4,2,2,32,128]{4,3,2,1,0:T(8,128)(2,1)S(1)}, u32[]{:S(2)}, u32[]{:S(2)}) %collective-permute-start.4) | collective-permute-done | bytes 131104 | tf_op jit(solution)/shard_map/ppermute | solution.py:39
  7.2 0.0 collective-permute-start.5
  7.2 1.7 %collective-permute-start.1 = (bf16[8,32,64]{2,1,0:T(8,128)(2,1)}, bf16[8,32,64]{2,1,0:T(8,128)(2,1)S(1)}, u32[]{:S(2)}, u32[]{:S(2)}) collective-permute-start(bf16[8,32,64]{2,1,0:T(8,128)(2,1)} %s0.1), channel_id=1, source_target_pairs={{0,2},{1,3},{2,0},{3,1},{4,6},{5,7},{6,4},{7,5},{8,10},{9,11},{10,... | collective-permute-start | bytes 98312 | tf_op jit(solution)/shard_map/ppermute | solution.py:39
  9.0 0.2 collective-permute-start
  9.2 2.7 %collective-permute-done.1.s2 = bf16[8,32,64]{2,1,0:T(8,128)(2,1)S(1)} collective-permute-done((bf16[8,32,64]{2,1,0:T(8,128)(2,1)}, bf16[8,32,64]{2,1,0:T(8,128)(2,1)S(1)}, u32[]{:S(2)}, u32[]{:S(2)}) %collective-permute-start.1) | collective-permute-done | bytes 32800 | tf_op jit(solution)/shard_map/ppermute | solution.py:39
  11.9 0.0 collective-permute-start.2
  11.9 1.3 %copy.16 = bf16[64,4,4,256]{3,0,2,1:T(8,128)(2,1)S(1)} copy(bf16[64,4,4,256]{3,2,1,0:T(4,128)(2,1)} %param.5) | data formatting | bytes 1048576 | tf_op args[0]
  13.2 0.1 stack.22.info
  13.3 0.0 collective-permute-done.s1
  13.3 0.0 collective-permute-done.2.s3
  13.3 0.0 collective-permute-done.3.c1
  13.3 0.0 collective-permute-done.5.c3
  13.3 1.6 %shard_map.84 = (bf16[2,512,128]{2,1,0:T(8,128)(2,1)S(1)}, f32[2,2,128,128]{3,2,1,0:T(8,128)S(1)}, bf16[512,512]{1,0:T(8,128)(2,1)S(1)}, bf16[2,2,128,128]{3,2,1,0:T(8,128)(2,1)S(1)}) custom-call(s32[5]{0:T(128)S(1)} %stack.22.info, bf16[4,4,64,256]{3,2,1,0:T(8,128)(2,1)S(1)} %bitcast.20, bf16[8,32,64]{2,1,0:T(8,128)(2,1)S(1)} %copy-done.2, ...), custom_call_target="tpu_custom_call" | custom-call | flops 200000000 | bytes 1500000 | tf_op jit(solution)/shard_map/pallas_call | solution.py:323
  15.0 1.7 %collective-permute-start.6 = (bf16[2,512,128]{2,1,0:T(8,128)(2,1)S(1)}, bf16[2,512,128]{2,1,0:T(8,128)(2,1)S(1)}, u32[]{:S(2)}, u32[]{:S(2)}) collective-permute-start(bf16[2,512,128]{2,1,0:T(8,128)(2,1)S(1)} %get-tuple-element.26.pack), channel_id=1, source_target_pairs={{0,4},{1,5},{2,6},{3,7},{4,0},{5,1},{6,2},{7,3},{8,12},{9,13},{10,... | collective-permute-start | bytes 786440 | tf_op jit(solution)/shard_map/ppermute | solution.py:39
  16.6 0.7 collective-permute-start.7
  17.3 0.3 collective-permute-start.10
  17.6 1.7 %collective-permute-start.11 = (bf16[27,32,128]{2,1,0:T(8,128)(2,1)S(1)}, bf16[27,32,128]{2,1,0:T(8,128)(2,1)S(1)}, u32[]{:S(2)}, u32[]{:S(2)}) collective-permute-start(bf16[27,32,128]{2,1,0:T(8,128)(2,1)S(1)} %copy-done), channel_id=1, source_target_pairs={{0,2},{1,3},{2,0},{3,1},{4,6},{5,7},{6,4},{7,5},{8,10},{9,11},{10,... | collective-permute-start | bytes 663560 | tf_op jit(solution)/shard_map/ppermute | solution.py:39
  19.4 5.5 %collective-permute-start.14 = (bf16[27,32,128]{2,1,0:T(8,128)(2,1)S(1)}, bf16[27,32,128]{2,1,0:T(8,128)(2,1)S(1)}, u32[]{:S(2)}, u32[]{:S(2)}) collective-permute-start(bf16[27,32,128]{2,1,0:T(8,128)(2,1)S(1)} %copy-done.1), channel_id=1, source_target_pairs={{0,18},{1,19},{2,16},{3,17},{4,22},{5,23},{6,20},{7,21},{8,26},{9,... | collective-permute-start | bytes 663560 | tf_op jit(solution)/shard_map/ppermute | solution.py:39
  24.9 0.0 collective-permute-done.6.pair
  24.9 0.0 collective-permute-done.7.beyond
  24.9 0.6 shard_map.85
  25.5 0.1 collective-permute-start.8
  25.6 0.7 collective-permute-start.9
  26.3 0.0 collective-permute-done.10.m1
  26.3 2.7 %collective-permute-start.13 = (bf16[27,32,128]{2,1,0:T(8,128)(2,1)S(1)}, bf16[27,32,128]{2,1,0:T(8,128)(2,1)S(1)}, u32[]{:S(2)}, u32[]{:S(2)}) collective-permute-start(bf16[27,32,128]{2,1,0:T(8,128)(2,1)S(1)} %copy-done.1), channel_id=1, source_target_pairs={{0,1},{1,0},{2,3},{3,2},{4,5},{5,4},{6,7},{7,6},{8,9},{9,8},{10,11... | collective-permute-start | bytes 663560 | tf_op jit(solution)/shard_map/ppermute | solution.py:39
  29.0 0.0 collective-permute-done.11.m2
  29.0 0.1 collective-permute-start.12
  29.1 6.4 %collective-permute-done.14.l2 = bf16[27,32,128]{2,1,0:T(8,128)(2,1)S(1)} collective-permute-done((bf16[27,32,128]{2,1,0:T(8,128)(2,1)S(1)}, bf16[27,32,128]{2,1,0:T(8,128)(2,1)S(1)}, u32[]{:S(2)}, u32[]{:S(2)}) %collective-permute-start.14) | collective-permute-done | bytes 221216 | tf_op jit(solution)/shard_map/ppermute | solution.py:39
  35.5 0.0 collective-permute-start.15
  35.5 0.0 collective-permute-done.13.l1
  35.5 0.5 collective-permute-start.19
  36.0 0.0 collective-permute-done.12.m3
  36.0 0.7 collective-permute-start.20
  36.7 0.3 collective-permute-done.15.l3
  37.0 1.2 %shard_map.86 = (bf16[384,1152]{1,0:T(8,128)(2,1)S(1)}, bf16[384,1152]{1,0:T(8,128)(2,1)S(1)}, bf16[1152,384]{1,0:T(8,128)(2,1)S(1)}, bf16[1152,384]{1,0:T(8,128)(2,1)S(1)}) custom-call(s32[5]{0:T(128)S(1)} %stack.22.info, bf16[27,32,128]{2,1,0:T(8,128)(2,1)S(1)} %copy-done, bf16[27,32,128]{2,1,0:T(8,128)(2,1)S(1)} %collective-permute-done.10.m1, ...), custom_call_target="tpu_custom_call" | custom-call | flops 1000000 | bytes 6000000 | tf_op jit(solution)/shard_map/pallas_call | solution.py:347
  38.2 0.0 collective-permute-done.8
  38.2 0.0 collective-permute-done.9
  38.2 4.0 %shard_map.87 = (bf16[4,4,128,128]{3,2,1,0:T(8,128)(2,1)S(1)}, f32[4,4,128,128]{3,2,1,0:T(8,128)S(1)}, bf16[6,6,128,128]{3,2,1,0:T(8,128)(2,1)S(1)}) custom-call(s32[5]{0:T(128)S(1)} %stack.22.info, bf16[6,2,128,128]{3,2,1,0:T(8,128)(2,1)S(1)} %bitcast.27, bf16[6,2,128,128]{3,2,1,0:T(8,128)(2,1)S(1)} %bitcast.28, bf16[6,2,128,128]{3,2,1,0:T(8,128)(2,1)S(1)} %bitcast.29, ...), custom_call_target="tpu_custom_call" | custom-call | flops 3000000000 | bytes 4000000 | tf_op jit(solution)/shard_map/pallas_call | solution.py:356
  42.2 1.3 %shard_map.90 = (bf16[2,27,32,128]{3,2,1,0:T(8,128)(2,1)S(1)}, bf16[2,27,32,128]{3,2,1,0:T(8,128)(2,1)S(1)}) custom-call(s32[5]{0:T(128)S(1)} %stack.22.info, bf16[4,4,128,128]{3,2,1,0:T(8,128)(2,1)S(1)} %get-tuple-element.29.act_ref.mid_act, bf16[2,2,128,128]{3,2,1,0:T(8,128)(2,1)S(1)} %get-tuple-element.33.cot_own), custom_call_target="tpu_custom_call" | custom-call | flops 500000000 | bytes 3000000 | tf_op jit(solution)/shard_map/pallas_call | solution.py:377
  43.4 2.3 %collective-permute-start.18 = (bf16[2,27,32,128]{3,2,1,0:T(8,128)(2,1)S(1)}, bf16[2,27,32,128]{3,2,1,0:T(8,128)(2,1)S(1)}, u32[]{:S(2)}, u32[]{:S(2)}) collective-permute-start(bf16[2,27,32,128]{3,2,1,0:T(8,128)(2,1)S(1)} %get-tuple-element.35), channel_id=1, source_target_pairs={{0,1},{1,0},{2,3},{3,2},{4,5},{5,4},{6,7},{7,6},{8,9},{9,8},{10,11... | collective-permute-start | bytes 1327112 | tf_op jit(solution)/shard_map/ppermute | solution.py:39
  45.8 0.0 collective-permute-done.19
  45.8 6.1 %shard_map.91 = (bf16[2,37,32,128]{3,2,1,0:T(8,128)(2,1)S(1)}, bf16[2,37,32,128]{3,2,1,0:T(8,128)(2,1)S(1)}) custom-call(s32[5]{0:T(128)S(1)} %stack.22.info, bf16[6,6,128,128]{3,2,1,0:T(8,128)(2,1)S(1)} %get-tuple-element.36.act_window, bf16[6,2,128,128]{3,2,1,0:T(8,128)(2,1)S(1)} %bitcast.26, bf16[6,2,128,128]{3,2,1,0:T(8,128)(2,1)S(1)} %bitcast.30, ...), custom_call_target="tpu_custom_call" | custom-call | flops 4000000000 | bytes 8000000 | tf_op jit(solution)/shard_map/pallas_call | solution.py:387
  51.8 0.1 collective-permute-start.21
  51.9 0.0 collective-permute-done.18
  51.9 0.1 add_convert_fusion.1
  52.1 1.9 %collective-permute-done.21 = bf16[2,37,32,128]{3,2,1,0:T(8,128)(2,1)S(1)} collective-permute-done((bf16[2,37,32,128]{3,2,1,0:T(8,128)(2,1)S(1)}, bf16[2,37,32,128]{3,2,1,0:T(8,128)(2,1)S(1)}, u32[]{:S(2)}, u32[]{:S(2)}) %collective-permute-start.21) | collective-permute-done | bytes 606240 | tf_op jit(solution)/shard_map/ppermute | solution.py:39
  53.9 0.2 add_convert_fusion
  54.1 0.1 pad_maximum_fusion
  54.2 30.1 %all_to_all.10.terms_ref = bf16[64,64,128]{2,1,0:T(8,128)(2,1)S(1)} all-to-all(bf16[64,64,128]{2,1,0:T(8,128)(2,1)S(1)} %bitcast.32), channel_id=1, replica_groups=mesh['depth'=32,'chip'=2,'core'=2] {'chip','depth'}, dimensions={0} | all-to-all | bytes 2097152 | tf_op jit(solution)/shard_map/all_to_all | solution.py:416
  84.3 1.0 shard_map.92
  85.3 4.7 %all-to-all-start.1 = ((bf16[32,64,128]{2,1,0:T(8,128)(2,1)}), bf16[32,64,128]{2,1,0:T(8,128)(2,1)S(1)}, u32[]{:S(2)}, u32[]{:S(2)}) async-start(bf16[32,64,128]{2,1,0:T(8,128)(2,1)} %shard_map.92), calls=%async_computation.1 | async-start | bytes 1048576 | tf_op jit(solution)/shard_map/all_to_all | solution.py:418
  90.0 1.5 %shard_map.88 = (bf16[2,2,2,32,128]{4,3,2,1,0:T(8,128)(2,1)S(1)}, bf16[2,2,2,32,128]{4,3,2,1,0:T(8,128)(2,1)S(1)}) custom-call(s32[5]{0:T(128)S(1)} %stack.22.info, bf16[4,4,128,128]{3,2,1,0:T(8,128)(2,1)S(1)} %get-tuple-element.29.act_ref.mid_act, bf16[384,1152]{1,0:T(8,128)(2,1)S(1)} %get-tuple-element.30.weights), custom_call_target="tpu_custom_call" | custom-call | flops 500000000 | bytes 2000000 | tf_op jit(solution)/shard_map/pallas_call | solution.py:365
  91.5 0.1 collective-permute-start.16
  91.6 1.2 %collective-permute-done.16.near = bf16[2,2,2,32,128]{4,3,2,1,0:T(8,128)(2,1)S(1)} collective-permute-done((bf16[2,2,2,32,128]{4,3,2,1,0:T(8,128)(2,1)S(1)}, bf16[2,2,2,32,128]{4,3,2,1,0:T(8,128)(2,1)S(1)}, u32[]{:S(2)}, u32[]{:S(2)}) %collective-permute-start.16) | collective-permute-done | bytes 65568 | tf_op jit(solution)/shard_map/ppermute | solution.py:39
  92.8 1.1 %collective-permute-start.17 = (bf16[2,2,2,32,128]{4,3,2,1,0:T(8,128)(2,1)S(1)}, bf16[2,2,2,32,128]{4,3,2,1,0:T(8,128)(2,1)S(1)}, u32[]{:S(2)}, u32[]{:S(2)}) collective-permute-start(bf16[2,2,2,32,128]{4,3,2,1,0:T(8,128)(2,1)S(1)} %pad_maximum_fusion.1), channel_id=1, source_target_pairs={{0,2},{1,3},{2,0},{3,1},{4,6},{5,7},{6,4},{7,5},{8,10},{9,11},{10,... | collective-permute-start | bytes 196616 | tf_op jit(solution)/shard_map/ppermute | solution.py:39
  94.0 6.2 %collective-permute-done.17.far = bf16[2,2,2,32,128]{4,3,2,1,0:T(8,128)(2,1)S(1)} collective-permute-done((bf16[2,2,2,32,128]{4,3,2,1,0:T(8,128)(2,1)S(1)}, bf16[2,2,2,32,128]{4,3,2,1,0:T(8,128)(2,1)S(1)}, u32[]{:S(2)}, u32[]{:S(2)}) %collective-permute-start.17) | collective-permute-done | bytes 65568 | tf_op jit(solution)/shard_map/ppermute | solution.py:39
  100.2 0.6 shard_map.89
  100.7 0.7 copy.14
  101.4 1.4 %all-to-all-done.1 = bf16[32,64,128]{2,1,0:T(8,128)(2,1)S(1)} async-done(((bf16[32,64,128]{2,1,0:T(8,128)(2,1)}), bf16[32,64,128]{2,1,0:T(8,128)(2,1)S(1)}, u32[]{:S(2)}, u32[]{:S(2)}) %all-to-all-start.1) | async-done | bytes 524320 | tf_op jit(solution)/shard_map/all_to_all | solution.py:418
  102.8 1.0 shard_map.93
  (10 shorter events, 0.0 us)
Async XLA Ops:
  0.6 12.7 %copy-start.2 = (bf16[8,32,64]{2,1,0:T(8,128)(2,1)S(1)}, bf16[8,32,64]{2,1,0:T(8,128)(2,1)}, u32[]{:S(2)}) copy-start(bf16[8,32,64]{2,1,0:T(8,128)(2,1)} %s0.1) | copy-start | bytes 98308
  1.6 5.6 %collective-permute-start.4 = (bf16[4,2,2,32,128]{4,3,2,1,0:T(8,128)(2,1)S(1)}, bf16[4,2,2,32,128]{4,3,2,1,0:T(8,128)(2,1)S(1)}, u32[]{:S(2)}, u32[]{:S(2)}) collective-permute-start(bf16[4,2,2,32,128]{4,3,2,1,0:T(8,128)(2,1)S(1)} %bitcast.22), channel_id=1, source_target_pairs={{0,2},{1,3},{2,0},{3,1},{4,6},{5,7},{6,4},{7,5},{8,10},{9,11},{10,... | collective-permute-start | bytes 393224 | tf_op jit(solution)/shard_map/ppermute | solution.py:39
  3.7 9.6 %collective-permute-start.3 = (bf16[4,2,2,32,128]{4,3,2,1,0:T(8,128)(2,1)S(1)}, bf16[4,2,2,32,128]{4,3,2,1,0:T(8,128)(2,1)S(1)}, u32[]{:S(2)}, u32[]{:S(2)}) collective-permute-start(bf16[4,2,2,32,128]{4,3,2,1,0:T(8,128)(2,1)S(1)} %bitcast.23), channel_id=1, source_target_pairs={{0,1},{1,0},{2,3},{3,2},{4,5},{5,4},{6,7},{7,6},{8,9},{9,8},{10,11... | collective-permute-start | bytes 393224 | tf_op jit(solution)/shard_map/ppermute | solution.py:39
  7.2 6.1 %collective-permute-start.5 = (bf16[4,2,2,32,128]{4,3,2,1,0:T(8,128)(2,1)S(1)}, bf16[4,2,2,32,128]{4,3,2,1,0:T(8,128)(2,1)S(1)}, u32[]{:S(2)}, u32[]{:S(2)}) collective-permute-start(bf16[4,2,2,32,128]{4,3,2,1,0:T(8,128)(2,1)S(1)} %collective-permute-done.4.c2), channel_id=1, source_target_pairs={{0,1},{1,0},{2,3},{3,2},{4,5},{5,4},{6,7},{7,6},{8,9},{9,8},{10,11... | collective-permute-start | bytes 393224 | tf_op jit(solution)/shard_map/ppermute | solution.py:39
  7.2 4.7 %collective-permute-start.1 = (bf16[8,32,64]{2,1,0:T(8,128)(2,1)}, bf16[8,32,64]{2,1,0:T(8,128)(2,1)S(1)}, u32[]{:S(2)}, u32[]{:S(2)}) collective-permute-start(bf16[8,32,64]{2,1,0:T(8,128)(2,1)} %s0.1), channel_id=1, source_target_pairs={{0,2},{1,3},{2,0},{3,1},{4,6},{5,7},{6,4},{7,5},{8,10},{9,11},{10,... | collective-permute-start | bytes 98312 | tf_op jit(solution)/shard_map/ppermute | solution.py:39
  9.0 4.3 %collective-permute-start = (bf16[8,32,64]{2,1,0:T(8,128)(2,1)}, bf16[8,32,64]{2,1,0:T(8,128)(2,1)S(1)}, u32[]{:S(2)}, u32[]{:S(2)}) collective-permute-start(bf16[8,32,64]{2,1,0:T(8,128)(2,1)} %s0.1), channel_id=1, source_target_pairs={{0,1},{1,0},{2,3},{3,2},{4,5},{5,4},{6,7},{7,6},{8,9},{9,8},{10,11... | collective-permute-start | bytes 98312 | tf_op jit(solution)/shard_map/ppermute | solution.py:39
  11.9 1.4 %collective-permute-start.2 = (bf16[8,32,64]{2,1,0:T(8,128)(2,1)S(1)}, bf16[8,32,64]{2,1,0:T(8,128)(2,1)S(1)}, u32[]{:S(2)}, u32[]{:S(2)}) collective-permute-start(bf16[8,32,64]{2,1,0:T(8,128)(2,1)S(1)} %collective-permute-done.1.s2), channel_id=1, source_target_pairs={{0,1},{1,0},{2,3},{3,2},{4,5},{5,4},{6,7},{7,6},{8,9},{9,8},{10,11... | collective-permute-start | bytes 98312 | tf_op jit(solution)/shard_map/ppermute | solution.py:39
  11.9 5.4 %copy-start = (bf16[27,32,128]{2,1,0:T(8,128)(2,1)S(1)}, bf16[27,32,128]{2,1,0:T(8,128)(2,1)}, u32[]{:S(2)}) copy-start(bf16[27,32,128]{2,1,0:T(8,128)(2,1)} %m0.1) | copy-start | bytes 663556
  11.9 7.4 %copy-start.1 = (bf16[27,32,128]{2,1,0:T(8,128)(2,1)S(1)}, bf16[27,32,128]{2,1,0:T(8,128)(2,1)}, u32[]{:S(2)}) copy-start(bf16[27,32,128]{2,1,0:T(8,128)(2,1)} %l0.1) | copy-start | bytes 663556
  15.0 9.9 %collective-permute-start.6 = (bf16[2,512,128]{2,1,0:T(8,128)(2,1)S(1)}, bf16[2,512,128]{2,1,0:T(8,128)(2,1)S(1)}, u32[]{:S(2)}, u32[]{:S(2)}) collective-permute-start(bf16[2,512,128]{2,1,0:T(8,128)(2,1)S(1)} %get-tuple-element.26.pack), channel_id=1, source_target_pairs={{0,4},{1,5},{2,6},{3,7},{4,0},{5,1},{6,2},{7,3},{8,12},{9,13},{10,... | collective-permute-start | bytes 786440 | tf_op jit(solution)/shard_map/ppermute | solution.py:39
  16.6 8.2 %collective-permute-start.7 = (bf16[2,512,128]{2,1,0:T(8,128)(2,1)S(1)}, bf16[2,512,128]{2,1,0:T(8,128)(2,1)S(1)}, u32[]{:S(2)}, u32[]{:S(2)}) collective-permute-start(bf16[2,512,128]{2,1,0:T(8,128)(2,1)S(1)} %get-tuple-element.26.pack), channel_id=1, source_target_pairs={{4,8},{5,9},{6,10},{7,11},{8,4},{9,5},{10,6},{11,7},{12,16},{13,17... | collective-permute-start | bytes 786440 | tf_op jit(solution)/shard_map/ppermute | solution.py:39
  17.3 9.0 %collective-permute-start.10 = (bf16[27,32,128]{2,1,0:T(8,128)(2,1)S(1)}, bf16[27,32,128]{2,1,0:T(8,128)(2,1)S(1)}, u32[]{:S(2)}, u32[]{:S(2)}) collective-permute-start(bf16[27,32,128]{2,1,0:T(8,128)(2,1)S(1)} %copy-done), channel_id=1, source_target_pairs={{0,1},{1,0},{2,3},{3,2},{4,5},{5,4},{6,7},{7,6},{8,9},{9,8},{10,11... | collective-permute-start | bytes 663560 | tf_op jit(solution)/shard_map/ppermute | solution.py:39
  17.6 11.4 %collective-permute-start.11 = (bf16[27,32,128]{2,1,0:T(8,128)(2,1)S(1)}, bf16[27,32,128]{2,1,0:T(8,128)(2,1)S(1)}, u32[]{:S(2)}, u32[]{:S(2)}) collective-permute-start(bf16[27,32,128]{2,1,0:T(8,128)(2,1)S(1)} %copy-done), channel_id=1, source_target_pairs={{0,2},{1,3},{2,0},{3,1},{4,6},{5,7},{6,4},{7,5},{8,10},{9,11},{10,... | collective-permute-start | bytes 663560 | tf_op jit(solution)/shard_map/ppermute | solution.py:39
  19.4 16.1 %collective-permute-start.14 = (bf16[27,32,128]{2,1,0:T(8,128)(2,1)S(1)}, bf16[27,32,128]{2,1,0:T(8,128)(2,1)S(1)}, u32[]{:S(2)}, u32[]{:S(2)}) collective-permute-start(bf16[27,32,128]{2,1,0:T(8,128)(2,1)S(1)} %copy-done.1), channel_id=1, source_target_pairs={{0,18},{1,19},{2,16},{3,17},{4,22},{5,23},{6,20},{7,21},{8,26},{9,... | collective-permute-start | bytes 663560 | tf_op jit(solution)/shard_map/ppermute | solution.py:39
  25.5 12.7 %collective-permute-start.8 = (bf16[6,256,128]{2,1,0:T(8,128)(2,1)S(1)}, bf16[6,256,128]{2,1,0:T(8,128)(2,1)S(1)}, u32[]{:S(2)}, u32[]{:S(2)}) collective-permute-start(bf16[6,256,128]{2,1,0:T(8,128)(2,1)S(1)} %get-tuple-element.27), channel_id=1, source_target_pairs={{0,1},{1,0},{2,3},{3,2},{4,5},{5,4},{6,7},{7,6},{8,9},{9,8},{10,11... | collective-permute-start | bytes 1179656 | tf_op jit(solution)/shard_map/ppermute | solution.py:39
  25.6 12.6 %collective-permute-start.9 = (bf16[6,256,128]{2,1,0:T(8,128)(2,1)S(1)}, bf16[6,256,128]{2,1,0:T(8,128)(2,1)S(1)}, u32[]{:S(2)}, u32[]{:S(2)}) collective-permute-start(bf16[6,256,128]{2,1,0:T(8,128)(2,1)S(1)} %get-tuple-element.27), channel_id=1, source_target_pairs={{1,2},{2,1},{5,6},{6,5},{9,10},{10,9},{13,14},{14,13},{17,18},{18,... | collective-permute-start | bytes 1179656 | tf_op jit(solution)/shard_map/ppermute | solution.py:39
  26.3 9.3 %collective-permute-start.13 = (bf16[27,32,128]{2,1,0:T(8,128)(2,1)S(1)}, bf16[27,32,128]{2,1,0:T(8,128)(2,1)S(1)}, u32[]{:S(2)}, u32[]{:S(2)}) collective-permute-start(bf16[27,32,128]{2,1,0:T(8,128)(2,1)S(1)} %copy-done.1), channel_id=1, source_target_pairs={{0,1},{1,0},{2,3},{3,2},{4,5},{5,4},{6,7},{7,6},{8,9},{9,8},{10,11... | collective-permute-start | bytes 663560 | tf_op jit(solution)/shard_map/ppermute | solution.py:39
  29.0 7.0 %collective-permute-start.12 = (bf16[27,32,128]{2,1,0:T(8,128)(2,1)S(1)}, bf16[27,32,128]{2,1,0:T(8,128)(2,1)S(1)}, u32[]{:S(2)}, u32[]{:S(2)}) collective-permute-start(bf16[27,32,128]{2,1,0:T(8,128)(2,1)S(1)} %collective-permute-done.11.m2), channel_id=1, source_target_pairs={{0,1},{1,0},{2,3},{3,2},{4,5},{5,4},{6,7},{7,6},{8,9},{9,8},{10,11... | collective-permute-start | bytes 663560 | tf_op jit(solution)/shard_map/ppermute | solution.py:39
  35.5 1.5 %collective-permute-start.15 = (bf16[27,32,128]{2,1,0:T(8,128)(2,1)S(1)}, bf16[27,32,128]{2,1,0:T(8,128)(2,1)S(1)}, u32[]{:S(2)}, u32[]{:S(2)}) collective-permute-start(bf16[27,32,128]{2,1,0:T(8,128)(2,1)S(1)} %collective-permute-done.14.l2), channel_id=1, source_target_pairs={{0,1},{1,0},{2,3},{3,2},{4,5},{5,4},{6,7},{7,6},{8,9},{9,8},{10,11... | collective-permute-start | bytes 663560 | tf_op jit(solution)/shard_map/ppermute | solution.py:39
  35.5 10.2 %collective-permute-start.19 = (bf16[6,256,128]{2,1,0:T(8,128)(2,1)S(1)}, bf16[6,256,128]{2,1,0:T(8,128)(2,1)S(1)}, u32[]{:S(2)}, u32[]{:S(2)}) collective-permute-start(bf16[6,256,128]{2,1,0:T(8,128)(2,1)S(1)} %get-tuple-element.37), channel_id=1, source_target_pairs={{0,1},{1,0},{2,3},{3,2},{4,5},{5,4},{6,7},{7,6},{8,9},{9,8},{10,11... | collective-permute-start | bytes 1179656 | tf_op jit(solution)/shard_map/ppermute | solution.py:39
  36.0 9.7 %collective-permute-start.20 = (bf16[6,256,128]{2,1,0:T(8,128)(2,1)S(1)}, bf16[6,256,128]{2,1,0:T(8,128)(2,1)S(1)}, u32[]{:S(2)}, u32[]{:S(2)}) collective-permute-start(bf16[6,256,128]{2,1,0:T(8,128)(2,1)S(1)} %get-tuple-element.37), channel_id=1, source_target_pairs={{1,2},{2,1},{5,6},{6,5},{9,10},{10,9},{13,14},{14,13},{17,18},{18,... | collective-permute-start | bytes 1179656 | tf_op jit(solution)/shard_map/ppermute | solution.py:39
  43.4 8.5 %collective-permute-start.18 = (bf16[2,27,32,128]{3,2,1,0:T(8,128)(2,1)S(1)}, bf16[2,27,32,128]{3,2,1,0:T(8,128)(2,1)S(1)}, u32[]{:S(2)}, u32[]{:S(2)}) collective-permute-start(bf16[2,27,32,128]{3,2,1,0:T(8,128)(2,1)S(1)} %get-tuple-element.35), channel_id=1, source_target_pairs={{0,1},{1,0},{2,3},{3,2},{4,5},{5,4},{6,7},{7,6},{8,9},{9,8},{10,11... | collective-permute-start | bytes 1327112 | tf_op jit(solution)/shard_map/ppermute | solution.py:39
  51.8 2.1 %collective-permute-start.21 = (bf16[2,37,32,128]{3,2,1,0:T(8,128)(2,1)S(1)}, bf16[2,37,32,128]{3,2,1,0:T(8,128)(2,1)S(1)}, u32[]{:S(2)}, u32[]{:S(2)}) collective-permute-start(bf16[2,37,32,128]{3,2,1,0:T(8,128)(2,1)S(1)} %get-tuple-element.44), channel_id=1, source_target_pairs={{0,1},{1,0},{2,3},{3,2},{4,5},{5,4},{6,7},{7,6},{8,9},{9,8},{10,11... | collective-permute-start | bytes 1818632 | tf_op jit(solution)/shard_map/ppermute | solution.py:39
  85.3 17.5 %all-to-all-start.1 = ((bf16[32,64,128]{2,1,0:T(8,128)(2,1)}), bf16[32,64,128]{2,1,0:T(8,128)(2,1)S(1)}, u32[]{:S(2)}, u32[]{:S(2)}) async-start(bf16[32,64,128]{2,1,0:T(8,128)(2,1)} %shard_map.92), calls=%async_computation.1 | async-start | bytes 1048576 | tf_op jit(solution)/shard_map/all_to_all | solution.py:418
  91.5 1.3 %collective-permute-start.16 = (bf16[2,2,2,32,128]{4,3,2,1,0:T(8,128)(2,1)S(1)}, bf16[2,2,2,32,128]{4,3,2,1,0:T(8,128)(2,1)S(1)}, u32[]{:S(2)}, u32[]{:S(2)}) collective-permute-start(bf16[2,2,2,32,128]{4,3,2,1,0:T(8,128)(2,1)S(1)} %get-tuple-element.32), channel_id=1, source_target_pairs={{0,1},{1,0},{2,3},{3,2},{4,5},{5,4},{6,7},{7,6},{8,9},{9,8},{10,11... | collective-permute-start | bytes 196616 | tf_op jit(solution)/shard_map/ppermute | solution.py:39
  92.8 7.4 %collective-permute-start.17 = (bf16[2,2,2,32,128]{4,3,2,1,0:T(8,128)(2,1)S(1)}, bf16[2,2,2,32,128]{4,3,2,1,0:T(8,128)(2,1)S(1)}, u32[]{:S(2)}, u32[]{:S(2)}) collective-permute-start(bf16[2,2,2,32,128]{4,3,2,1,0:T(8,128)(2,1)S(1)} %pad_maximum_fusion.1), channel_id=1, source_target_pairs={{0,2},{1,3},{2,0},{3,1},{4,6},{5,7},{6,4},{7,5},{8,10},{9,11},{10,... | collective-permute-start | bytes 196616 | tf_op jit(solution)/shard_map/ppermute | solution.py:39

commit v7 on v6

--- a/solution.py
+++ b/solution.py
@@ -11,7 +11,7 @@
 FILT = ("chip", "core")
 CELLS = 128
 LIMITS = {
-    "stride": 8, "join": 6, "weights": 10, "middle": 20, "result": 8, "grad_l": 10, "back": 26,
+    "stride": 8, "cells": 4, "join": 6, "weights": 10, "middle": 20, "result": 8, "grad_l": 10, "back": 26,
     "rows": 2, "sum": 6, "finish": 4,
 }
 VMEM = pl.BlockSpec(memory_space=pltpu.VMEM)
@@ -79,10 +79,7 @@
     )
 
 
-def stride_body(
-    info, u_ref, s0, s1, s2, s3, c0, c1, c2, c3,
-    pack_ref, pre_ref, columns_ref, cot_ref, weights,
-):
+def stride_body(info, u_ref, s0, s1, s2, s3, act_ref, pre_ref, columns_ref, weights):
     filt = info[1]
     for j, part in enumerate((s0, s1, s2, s3)):
         start = pl.multiple_of((filt ^ j) * 32, 32)
@@ -106,19 +103,24 @@
             pre = dot(weights[...], block).T
             pre_ref[p, r] = pre
             act = (pre * jax.nn.sigmoid(pre)).astype(jnp.bfloat16)
-            pack_ref[p, r * 128 : r * 128 + 128] = act
+            act_ref[p, r * 128 : r * 128 + 128] = act
+
+
+def cells_body(info, c0, c1, c2, c3, own_ref, cells_ref):
+    filt = info[1]
+    for p in range(2):
+        for r in range(2):
             for j, part in enumerate((c0, c1, c2, c3)):
                 start = pl.multiple_of((filt ^ j) * 32, 32)
-                cot_ref[p, r, pl.ds(start, 32), :] = part[filt, r, p]
-            cot = cot_ref[p, r].astype(jnp.float32).T.astype(jnp.bfloat16)
-            pack_ref[p, 256 + r * 128 : 384 + r * 128] = cot
-
-
-def join_body(info, pack, pair, beyond, act_ref, cot_ref):
+                own_ref[p, r, pl.ds(start, 32), :] = part[filt, r, p]
+            cot = own_ref[p, r].astype(jnp.float32).T.astype(jnp.bfloat16)
+            cells_ref[p, r * 128 : r * 128 + 128] = cot
+
+
+def join_body(info, own, pair, beyond, column_ref):
     odd = info[0] & 1
-    for at, part in ((2, pack), (4 - 4 * odd, pair), (4 * odd, beyond)):
-        act_ref[pl.ds(at, 2)] = part[:, :256]
-        cot_ref[pl.ds(at, 2)] = part[:, 256:]
+    for at, part in ((2, own), (4 - 4 * odd, pair), (4 * odd, beyond)):
+        column_ref[pl.ds(at, 2)] = part[...]
 
 
 def fill_window(window, middle, near, cross, core):
@@ -301,12 +303,18 @@
     out_ref[...] = jnp.broadcast_to(total[None], out_ref.shape)
 
 
-def row_parts(column):
+def neighbourhood(info, own):
     def inner(d, f):
         return (d, 3 - f) if f in (1, 2) else (-1, f)
 
+    beyond = shifted(own, lambda d, f: (d + 1 if d % 2 else d - 1, f))
+    pair = shifted(own, lambda d, f: (d ^ 1, f))
+    column = call(
+        "join", join_body, shape((6, 256, 128)), in_specs=[SMEM] + [VMEM] * 3
+    )(info, own, pair, beyond)
     cross = shifted(column, inner)
-    return column, swap_core(column), cross
+    near = swap_core(column)
+    return [x.reshape(6, 2, 128, 128) for x in (column, near, cross)]
 
 
 def whole(upper_level, stride_weight, middle_weight, last_weight, cotangent):
@@ -320,29 +328,27 @@
     last_parts = four_parts(last_weight, 4)
     upper = upper_level.transpose(1, 2, 0, 3)
 
-    pack, level_pre, columns, cot_own = call(
+    level_act, level_pre, columns = call(
         "stride",
         stride_body,
         [
-            shape((2, 512, 128)),
+            shape((2, 256, 128)),
             shape((2, 2, 128, 128), jnp.float32),
             shape((512, 512)),
-            shape((2, 2, 128, 128)),
         ],
         [pltpu.VMEM((128, 512), jnp.bfloat16)],
         flops=200_000_000,
         moved=1_500_000,
-        in_specs=[SMEM] + [VMEM] * 9,
-    )(info, upper, *stride_parts, *cot_parts)
-    beyond = shifted(pack, lambda d, f: (d + 1 if d % 2 else d - 1, f))
-    pair = shifted(pack, lambda d, f: (d ^ 1, f))
-    columns_joined = call(
-        "join", join_body, [shape((6, 256, 128))] * 2, in_specs=[SMEM] + [VMEM] * 3
-    )(info, pack, pair, beyond)
-    act_parts, back_parts = [
-        [x.reshape(6, 2, 128, 128) for x in (column, near, cross)]
-        for column, near, cross in (row_parts(columns_joined[0]), row_parts(columns_joined[1]))
-    ]
+        in_specs=[SMEM] + [VMEM] * 5,
+    )(info, upper, *stride_parts)
+    act_parts = neighbourhood(info, level_act)
+    cot_own, cot_cells = call(
+        "cells",
+        cells_body,
+        [shape((2, 2, 128, 128)), shape((2, 256, 128))],
+        in_specs=[SMEM] + [VMEM] * 4,
+    )(info, *cot_parts)
+    back_parts = neighbourhood(info, cot_cells)
 
     forward_m, forward_l, backward_l, backward_m = call(
         "weights",

time: 104 us -> 113 us (1.087)
  blocking collectives: 30.1 us -> 38.9 us
  waiting for transfers between devices: 23.6 us -> 20.3 us
  starting transfers between devices: 27.1 us -> 28.9 us
  Pallas kernels: 18.7 us -> 19.9 us
    all_to_all x1, blocking collectives: 30.1 us -> 38.9 us  [whole(): lax.all_to_all(terms.reshape(2 * depth, 64, 128), ('chip', 'depth'), 0, 0...]
    ppermute x22 -> x24, waiting for transfers between devices: 22.3 us -> 18.9 us  [shifted(): return lax.ppermute(value, AXES, pairs_of(move))]
    ppermute x22 -> x24, starting transfers between devices: 22.4 us -> 24.3 us  [shifted(): return lax.ppermute(value, AXES, pairs_of(move))]
    pallas_call x2 -> x4, Pallas kernels: 2.24 us -> 3.46 us  [the longest x1 1.64 us: whole(): call('stride', stride_body, [shape((2, 256, 128)), shape((2, 2, 128, 128)...]
  transfers between devices with their start and end apart: 23 -> 25, of which waited for: 8 -> 9; matrix products, arithmetic and copies ran while one was open for 2% -> 2% of each run, Pallas kernels for 15% -> 16%
where the time goes in v7:
time: 113 us; the launch traced here: 112 us
  blocking collectives  38.9 us (34%)
  starting transfers between devices  28.9 us (26%)
  waiting for transfers between devices  20.3 us (18%)
  Pallas kernels  19.9 us (18%)
  local copies, waits for them, and re-layouts  3.01 us (3%)
    all_to_all x1, blocking collectives, whole(): lax.all_to_all(terms.reshape(2 * depth, 64, 128), ('chip', 'depth'), 0, 0...  38.9 us
    ppermute x24, starting transfers between devices, shifted(): return lax.ppermute(value, AXES, pairs_of(move))  24.3 us
    ppermute x24, waiting for transfers between devices, shifted(): return lax.ppermute(value, AXES, pairs_of(move))  18.9 us
    pallas_call x1, Pallas kernels, whole(): call('back', back_body, [shape((2, 37, 32, 128))] * 2, [pltpu.VMEM((6, 6,...  6.06 us
    all_to_all x1, starting transfers between devices, whole(): full = lax.all_to_all(spread, 'depth', 0, 0, tiled=True)  4.54 us
    pallas_call x1, Pallas kernels, whole(): call('middle', middle_body, [shape((4, 4, 128, 128)), shape((4, 4, 128, 1...  3.98 us
    unnamed x9, local copies, waits for them, and re-layouts  2.91 us
  transfers between devices with their start and end apart: 25, of which 9 were waited for; matrix products, arithmetic and copies ran while one was open for 2% of the time, Pallas kernels for 16%

profile of v7, /device:TPU:0, one launch (start us, length us, event | category | flops | bytes accessed | tf_op | source)
XLA Modules:
  0.0 112.3 jit_solution(5079975470028613413)
XLA Ops:
  0.6 0.0 copy-start.2
  0.7 1.0 copy.13
  1.6 2.1 %collective-permute-start.16 = (bf16[4,2,2,32,128]{4,3,2,1,0:T(8,128)(2,1)S(1)}, bf16[4,2,2,32,128]{4,3,2,1,0:T(8,128)(2,1)S(1)}, u32[]{:S(2)}, u32[]{:S(2)}) collective-permute-start(bf16[4,2,2,32,128]{4,3,2,1,0:T(8,128)(2,1)S(1)} %bitcast.22), channel_id=1, source_target_pairs={{0,2},{1,3},{2,0},{3,1},{4,6},{5,7},{6,4},{7,5},{8,10},{9,11},{10,... | collective-permute-start | bytes 393224 | tf_op jit(solution)/shard_map/ppermute | solution.py:39
  3.7 0.0 collective-permute-start.15
  3.8 3.5 %collective-permute-done.16.c2 = bf16[4,2,2,32,128]{4,3,2,1,0:T(8,128)(2,1)S(1)} collective-permute-done((bf16[4,2,2,32,128]{4,3,2,1,0:T(8,128)(2,1)S(1)}, bf16[4,2,2,32,128]{4,3,2,1,0:T(8,128)(2,1)S(1)}, u32[]{:S(2)}, u32[]{:S(2)}) %collective-permute-start.16) | collective-permute-done | bytes 131104 | tf_op jit(solution)/shard_map/ppermute | solution.py:39
  7.2 0.0 collective-permute-start.17
  7.2 1.7 %collective-permute-start.1 = (bf16[8,32,64]{2,1,0:T(8,128)(2,1)}, bf16[8,32,64]{2,1,0:T(8,128)(2,1)S(1)}, u32[]{:S(2)}, u32[]{:S(2)}) collective-permute-start(bf16[8,32,64]{2,1,0:T(8,128)(2,1)} %s0.1), channel_id=1, source_target_pairs={{0,2},{1,3},{2,0},{3,1},{4,6},{5,7},{6,4},{7,5},{8,10},{9,11},{10,... | collective-permute-start | bytes 98312 | tf_op jit(solution)/shard_map/ppermute | solution.py:39
  9.0 0.2 collective-permute-start.7
  9.2 0.3 collective-permute-start
  9.5 2.5 %collective-permute-done.1.s2 = bf16[8,32,64]{2,1,0:T(8,128)(2,1)S(1)} collective-permute-done((bf16[8,32,64]{2,1,0:T(8,128)(2,1)}, bf16[8,32,64]{2,1,0:T(8,128)(2,1)S(1)}, u32[]{:S(2)}, u32[]{:S(2)}) %collective-permute-start.1) | collective-permute-done | bytes 32800 | tf_op jit(solution)/shard_map/ppermute | solution.py:39
  12.0 0.0 collective-permute-start.2
  12.0 0.0 collective-permute-done.s1
  12.0 1.7 %collective-permute-start.8 = (bf16[27,32,128]{2,1,0:T(8,128)(2,1)}, bf16[27,32,128]{2,1,0:T(8,128)(2,1)S(1)}, u32[]{:S(2)}, u32[]{:S(2)}) collective-permute-start(bf16[27,32,128]{2,1,0:T(8,128)(2,1)} %m0.1), channel_id=1, source_target_pairs={{0,2},{1,3},{2,0},{3,1},{4,6},{5,7},{6,4},{7,5},{8,10},{9,11},{10,... | collective-permute-start | bytes 663560 | tf_op jit(solution)/shard_map/ppermute | solution.py:39
  13.7 1.2 %copy.16 = bf16[64,4,4,256]{3,0,2,1:T(8,128)(2,1)S(1)} copy(bf16[64,4,4,256]{3,2,1,0:T(4,128)(2,1)} %param.5) | data formatting | bytes 1048576 | tf_op args[0]
  14.9 0.1 stack.22.info
  15.0 0.0 collective-permute-done.2.s3
  15.0 1.6 %shard_map.84 = (bf16[2,256,128]{2,1,0:T(8,128)(2,1)S(1)}, f32[2,2,128,128]{3,2,1,0:T(8,128)S(1)}, bf16[512,512]{1,0:T(8,128)(2,1)S(1)}) custom-call(s32[5]{0:T(128)S(1)} %stack.22.info, bf16[4,4,64,256]{3,2,1,0:T(8,128)(2,1)S(1)} %bitcast.21, bf16[8,32,64]{2,1,0:T(8,128)(2,1)S(1)} %copy-done.2, bf16[8,32,64]{2,1,0:T(8,128)(2,1)S(1)} %collective-permute-done.s1, ...), custom_call_target="tpu_custom_call" | custom-call | flops 200000000 | bytes 1500000 | tf_op jit(solution)/shard_map/pallas_call | solution.py:331
  16.7 0.0 copy-start
  16.7 1.7 %collective-permute-start.3 = (bf16[2,256,128]{2,1,0:T(8,128)(2,1)S(1)}, bf16[2,256,128]{2,1,0:T(8,128)(2,1)S(1)}, u32[]{:S(2)}, u32[]{:S(2)}) collective-permute-start(bf16[2,256,128]{2,1,0:T(8,128)(2,1)S(1)} %get-tuple-element.25.own), channel_id=1, source_target_pairs={{0,4},{1,5},{2,6},{3,7},{4,0},{5,1},{6,2},{7,3},{8,12},{9,13},{10,... | collective-permute-start | bytes 393224 | tf_op jit(solution)/shard_map/ppermute | solution.py:39
  18.3 0.0 collective-permute-done.15.c1
  18.3 0.7 collective-permute-start.4
  19.0 5.9 %collective-permute-start.11 = (bf16[27,32,128]{2,1,0:T(8,128)(2,1)S(1)}, bf16[27,32,128]{2,1,0:T(8,128)(2,1)S(1)}, u32[]{:S(2)}, u32[]{:S(2)}) collective-permute-start(bf16[27,32,128]{2,1,0:T(8,128)(2,1)S(1)} %copy-done.1), channel_id=1, source_target_pairs={{0,18},{1,19},{2,16},{3,17},{4,22},{5,23},{6,20},{7,21},{8,26},{9,... | collective-permute-start | bytes 663560 | tf_op jit(solution)/shard_map/ppermute | solution.py:39
  24.9 0.7 shard_map.90
  25.6 0.0 collective-permute-done.3.pair
  25.6 0.9 collective-permute-start.19
  26.5 0.0 collective-permute-done.4.beyond
  26.5 0.6 shard_map.85
  27.1 0.1 collective-permute-start.5
  27.2 0.7 collective-permute-start.6
  27.9 0.0 collective-permute-done.8.m2
  27.9 0.7 collective-permute-start.20
  28.6 3.7 %collective-permute-done.11.l2 = bf16[27,32,128]{2,1,0:T(8,128)(2,1)S(1)} collective-permute-done((bf16[27,32,128]{2,1,0:T(8,128)(2,1)S(1)}, bf16[27,32,128]{2,1,0:T(8,128)(2,1)S(1)}, u32[]{:S(2)}, u32[]{:S(2)}) %collective-permute-start.11) | collective-permute-done | bytes 221216 | tf_op jit(solution)/shard_map/ppermute | solution.py:39
  32.2 0.5 collective-permute-start.9
  32.8 0.0 collective-permute-done.20.beyond
  32.8 0.1 collective-permute-start.12
  32.8 0.6 shard_map.92
  33.4 0.3 collective-permute-done.10.l1
  33.7 0.2 collective-permute-start.21
  33.9 0.1 collective-permute-done.9.m3
  34.0 0.7 collective-permute-start.22
  34.7 0.0 collective-permute-done.12.l3
  34.7 1.2 %shard_map.86 = (bf16[384,1152]{1,0:T(8,128)(2,1)S(1)}, bf16[384,1152]{1,0:T(8,128)(2,1)S(1)}, bf16[1152,384]{1,0:T(8,128)(2,1)S(1)}, bf16[1152,384]{1,0:T(8,128)(2,1)S(1)}) custom-call(s32[5]{0:T(128)S(1)} %stack.22.info, bf16[27,32,128]{2,1,0:T(8,128)(2,1)S(1)} %copy-done, bf16[27,32,128]{2,1,0:T(8,128)(2,1)S(1)} %collective-permute-done.7.m1, ...), custom_call_target="tpu_custom_call" | custom-call | flops 1000000 | bytes 6000000 | tf_op jit(solution)/shard_map/pallas_call | solution.py:353
  35.9 0.0 collective-permute-done.6
  35.9 4.0 %shard_map.87 = (bf16[4,4,128,128]{3,2,1,0:T(8,128)(2,1)S(1)}, f32[4,4,128,128]{3,2,1,0:T(8,128)S(1)}, bf16[6,6,128,128]{3,2,1,0:T(8,128)(2,1)S(1)}) custom-call(s32[5]{0:T(128)S(1)} %stack.22.info, bf16[6,2,128,128]{3,2,1,0:T(8,128)(2,1)S(1)} %bitcast.26, bf16[6,2,128,128]{3,2,1,0:T(8,128)(2,1)S(1)} %bitcast.28, bf16[6,2,128,128]{3,2,1,0:T(8,128)(2,1)S(1)} %bitcast.29, ...), custom_call_target="tpu_custom_call" | custom-call | flops 3000000000 | bytes 4000000 | tf_op jit(solution)/shard_map/pallas_call | solution.py:362
  39.9 1.3 %shard_map.91 = (bf16[2,27,32,128]{3,2,1,0:T(8,128)(2,1)S(1)}, bf16[2,27,32,128]{3,2,1,0:T(8,128)(2,1)S(1)}) custom-call(s32[5]{0:T(128)S(1)} %stack.22.info, bf16[4,4,128,128]{3,2,1,0:T(8,128)(2,1)S(1)} %get-tuple-element.27.act_ref.mid_act, bf16[2,2,128,128]{3,2,1,0:T(8,128)(2,1)S(1)} %get-tuple-element.31.cot_own), custom_call_target="tpu_custom_call" | custom-call | flops 500000000 | bytes 3000000 | tf_op jit(solution)/shard_map/pallas_call | solution.py:383
  41.2 2.1 %collective-permute-start.18 = (bf16[2,27,32,128]{3,2,1,0:T(8,128)(2,1)S(1)}, bf16[2,27,32,128]{3,2,1,0:T(8,128)(2,1)S(1)}, u32[]{:S(2)}, u32[]{:S(2)}) collective-permute-start(bf16[2,27,32,128]{3,2,1,0:T(8,128)(2,1)S(1)} %get-tuple-element.33), channel_id=1, source_target_pairs={{0,1},{1,0},{2,3},{3,2},{4,5},{5,4},{6,7},{7,6},{8,9},{9,8},{10,11... | collective-permute-start | bytes 1327112 | tf_op jit(solution)/shard_map/ppermute | solution.py:39
  43.3 6.1 %shard_map.93 = (bf16[2,37,32,128]{3,2,1,0:T(8,128)(2,1)S(1)}, bf16[2,37,32,128]{3,2,1,0:T(8,128)(2,1)S(1)}) custom-call(s32[5]{0:T(128)S(1)} %stack.22.info, bf16[6,6,128,128]{3,2,1,0:T(8,128)(2,1)S(1)} %get-tuple-element.34.act_window, bf16[6,2,128,128]{3,2,1,0:T(8,128)(2,1)S(1)} %bitcast.27, bf16[6,2,128,128]{3,2,1,0:T(8,128)(2,1)S(1)} %bitcast.30, ...), custom_call_target="tpu_custom_call" | custom-call | flops 4000000000 | bytes 8000000 | tf_op jit(solution)/shard_map/pallas_call | solution.py:393
  49.4 2.7 %collective-permute-start.23 = (bf16[2,37,32,128]{3,2,1,0:T(8,128)(2,1)S(1)}, bf16[2,37,32,128]{3,2,1,0:T(8,128)(2,1)S(1)}, u32[]{:S(2)}, u32[]{:S(2)}) collective-permute-start(bf16[2,37,32,128]{3,2,1,0:T(8,128)(2,1)S(1)} %get-tuple-element.42), channel_id=1, source_target_pairs={{0,1},{1,0},{2,3},{3,2},{4,5},{5,4},{6,7},{7,6},{8,9},{9,8},{10,11... | collective-permute-start | bytes 1818632 | tf_op jit(solution)/shard_map/ppermute | solution.py:39
  52.1 0.1 add_convert_fusion.1
  52.2 1.5 %collective-permute-done.23 = bf16[2,37,32,128]{3,2,1,0:T(8,128)(2,1)S(1)} collective-permute-done((bf16[2,37,32,128]{3,2,1,0:T(8,128)(2,1)S(1)}, bf16[2,37,32,128]{3,2,1,0:T(8,128)(2,1)S(1)}, u32[]{:S(2)}, u32[]{:S(2)}) %collective-permute-start.23) | collective-permute-done | bytes 606240 | tf_op jit(solution)/shard_map/ppermute | solution.py:39
  53.7 0.2 add_convert_fusion
  53.9 0.1 pad_maximum_fusion
  54.0 38.9 %all_to_all.10.terms_ref = bf16[64,64,128]{2,1,0:T(8,128)(2,1)S(1)} all-to-all(bf16[64,64,128]{2,1,0:T(8,128)(2,1)S(1)} %bitcast.32), channel_id=1, replica_groups=mesh['depth'=32,'chip'=2,'core'=2] {'chip','depth'}, dimensions={0} | all-to-all | bytes 2097152 | tf_op jit(solution)/shard_map/all_to_all | solution.py:422
  93.0 1.0 shard_map.94
  94.0 4.5 %all-to-all-start.1 = ((bf16[32,64,128]{2,1,0:T(8,128)(2,1)}), bf16[32,64,128]{2,1,0:T(8,128)(2,1)S(1)}, u32[]{:S(2)}, u32[]{:S(2)}) async-start(bf16[32,64,128]{2,1,0:T(8,128)(2,1)} %shard_map.94), calls=%async_computation.1 | async-start | bytes 1048576 | tf_op jit(solution)/shard_map/all_to_all | solution.py:424
  98.5 1.5 %shard_map.88 = (bf16[2,2,2,32,128]{4,3,2,1,0:T(8,128)(2,1)S(1)}, bf16[2,2,2,32,128]{4,3,2,1,0:T(8,128)(2,1)S(1)}) custom-call(s32[5]{0:T(128)S(1)} %stack.22.info, bf16[4,4,128,128]{3,2,1,0:T(8,128)(2,1)S(1)} %get-tuple-element.27.act_ref.mid_act, bf16[384,1152]{1,0:T(8,128)(2,1)S(1)} %get-tuple-element.28.weights), custom_call_target="tpu_custom_call" | custom-call | flops 500000000 | bytes 2000000 | tf_op jit(solution)/shard_map/pallas_call | solution.py:371
  100.0 0.1 collective-permute-start.13
  100.1 1.2 %collective-permute-done.13.near = bf16[2,2,2,32,128]{4,3,2,1,0:T(8,128)(2,1)S(1)} collective-permute-done((bf16[2,2,2,32,128]{4,3,2,1,0:T(8,128)(2,1)S(1)}, bf16[2,2,2,32,128]{4,3,2,1,0:T(8,128)(2,1)S(1)}, u32[]{:S(2)}, u32[]{:S(2)}) %collective-permute-start.13) | collective-permute-done | bytes 65568 | tf_op jit(solution)/shard_map/ppermute | solution.py:39
  101.3 1.3 %collective-permute-start.14 = (bf16[2,2,2,32,128]{4,3,2,1,0:T(8,128)(2,1)S(1)}, bf16[2,2,2,32,128]{4,3,2,1,0:T(8,128)(2,1)S(1)}, u32[]{:S(2)}, u32[]{:S(2)}) collective-permute-start(bf16[2,2,2,32,128]{4,3,2,1,0:T(8,128)(2,1)S(1)} %pad_maximum_fusion.1), channel_id=1, source_target_pairs={{0,2},{1,3},{2,0},{3,1},{4,6},{5,7},{6,4},{7,5},{8,10},{9,11},{10,... | collective-permute-start | bytes 196616 | tf_op jit(solution)/shard_map/ppermute | solution.py:39
  102.6 6.1 %collective-permute-done.14.far = bf16[2,2,2,32,128]{4,3,2,1,0:T(8,128)(2,1)S(1)} collective-permute-done((bf16[2,2,2,32,128]{4,3,2,1,0:T(8,128)(2,1)S(1)}, bf16[2,2,2,32,128]{4,3,2,1,0:T(8,128)(2,1)S(1)}, u32[]{:S(2)}, u32[]{:S(2)}) %collective-permute-start.14) | collective-permute-done | bytes 65568 | tf_op jit(solution)/shard_map/ppermute | solution.py:39
  108.7 0.6 shard_map.89
  109.3 0.7 copy.14
  110.0 1.4 %all-to-all-done.1 = bf16[32,64,128]{2,1,0:T(8,128)(2,1)S(1)} async-done(((bf16[32,64,128]{2,1,0:T(8,128)(2,1)}), bf16[32,64,128]{2,1,0:T(8,128)(2,1)S(1)}, u32[]{:S(2)}, u32[]{:S(2)}) %all-to-all-start.1) | async-done | bytes 524320 | tf_op jit(solution)/shard_map/all_to_all | solution.py:424
  111.4 1.0 shard_map.95
  (16 shorter events, 0.1 us)
Async XLA Ops:
  0.6 14.4 %copy-start.2 = (bf16[8,32,64]{2,1,0:T(8,128)(2,1)S(1)}, bf16[8,32,64]{2,1,0:T(8,128)(2,1)}, u32[]{:S(2)}) copy-start(bf16[8,32,64]{2,1,0:T(8,128)(2,1)} %s0.1) | copy-start | bytes 98308
  0.6 18.4 %copy-start.1 = (bf16[27,32,128]{2,1,0:T(8,128)(2,1)S(1)}, bf16[27,32,128]{2,1,0:T(8,128)(2,1)}, u32[]{:S(2)}) copy-start(bf16[27,32,128]{2,1,0:T(8,128)(2,1)} %l0.1) | copy-start | bytes 663556
  1.6 5.6 %collective-permute-start.16 = (bf16[4,2,2,32,128]{4,3,2,1,0:T(8,128)(2,1)S(1)}, bf16[4,2,2,32,128]{4,3,2,1,0:T(8,128)(2,1)S(1)}, u32[]{:S(2)}, u32[]{:S(2)}) collective-permute-start(bf16[4,2,2,32,128]{4,3,2,1,0:T(8,128)(2,1)S(1)} %bitcast.22), channel_id=1, source_target_pairs={{0,2},{1,3},{2,0},{3,1},{4,6},{5,7},{6,4},{7,5},{8,10},{9,11},{10,... | collective-permute-start | bytes 393224 | tf_op jit(solution)/shard_map/ppermute | solution.py:39
  3.7 14.6 %collective-permute-start.15 = (bf16[4,2,2,32,128]{4,3,2,1,0:T(8,128)(2,1)S(1)}, bf16[4,2,2,32,128]{4,3,2,1,0:T(8,128)(2,1)S(1)}, u32[]{:S(2)}, u32[]{:S(2)}) collective-permute-start(bf16[4,2,2,32,128]{4,3,2,1,0:T(8,128)(2,1)S(1)} %bitcast.23), channel_id=1, source_target_pairs={{0,1},{1,0},{2,3},{3,2},{4,5},{5,4},{6,7},{7,6},{8,9},{9,8},{10,11... | collective-permute-start | bytes 393224 | tf_op jit(solution)/shard_map/ppermute | solution.py:39
  7.2 11.8 %collective-permute-start.17 = (bf16[4,2,2,32,128]{4,3,2,1,0:T(8,128)(2,1)S(1)}, bf16[4,2,2,32,128]{4,3,2,1,0:T(8,128)(2,1)S(1)}, u32[]{:S(2)}, u32[]{:S(2)}) collective-permute-start(bf16[4,2,2,32,128]{4,3,2,1,0:T(8,128)(2,1)S(1)} %collective-permute-done.16.c2), channel_id=1, source_target_pairs={{0,1},{1,0},{2,3},{3,2},{4,5},{5,4},{6,7},{7,6},{8,9},{9,8},{10,11... | collective-permute-start | bytes 393224 | tf_op jit(solution)/shard_map/ppermute | solution.py:39
  7.2 4.7 %collective-permute-start.1 = (bf16[8,32,64]{2,1,0:T(8,128)(2,1)}, bf16[8,32,64]{2,1,0:T(8,128)(2,1)S(1)}, u32[]{:S(2)}, u32[]{:S(2)}) collective-permute-start(bf16[8,32,64]{2,1,0:T(8,128)(2,1)} %s0.1), channel_id=1, source_target_pairs={{0,2},{1,3},{2,0},{3,1},{4,6},{5,7},{6,4},{7,5},{8,10},{9,11},{10,... | collective-permute-start | bytes 98312 | tf_op jit(solution)/shard_map/ppermute | solution.py:39
  9.0 18.2 %collective-permute-start.7 = (bf16[27,32,128]{2,1,0:T(8,128)(2,1)}, bf16[27,32,128]{2,1,0:T(8,128)(2,1)S(1)}, u32[]{:S(2)}, u32[]{:S(2)}) collective-permute-start(bf16[27,32,128]{2,1,0:T(8,128)(2,1)} %m0.1), channel_id=1, source_target_pairs={{0,1},{1,0},{2,3},{3,2},{4,5},{5,4},{6,7},{7,6},{8,9},{9,8},{10,11... | collective-permute-start | bytes 663560 | tf_op jit(solution)/shard_map/ppermute | solution.py:39
  9.2 2.8 %collective-permute-start = (bf16[8,32,64]{2,1,0:T(8,128)(2,1)}, bf16[8,32,64]{2,1,0:T(8,128)(2,1)S(1)}, u32[]{:S(2)}, u32[]{:S(2)}) collective-permute-start(bf16[8,32,64]{2,1,0:T(8,128)(2,1)} %s0.1), channel_id=1, source_target_pairs={{0,1},{1,0},{2,3},{3,2},{4,5},{5,4},{6,7},{7,6},{8,9},{9,8},{10,11... | collective-permute-start | bytes 98312 | tf_op jit(solution)/shard_map/ppermute | solution.py:39
  12.0 3.0 %collective-permute-start.2 = (bf16[8,32,64]{2,1,0:T(8,128)(2,1)S(1)}, bf16[8,32,64]{2,1,0:T(8,128)(2,1)S(1)}, u32[]{:S(2)}, u32[]{:S(2)}) collective-permute-start(bf16[8,32,64]{2,1,0:T(8,128)(2,1)S(1)} %collective-permute-done.1.s2), channel_id=1, source_target_pairs={{0,1},{1,0},{2,3},{3,2},{4,5},{5,4},{6,7},{7,6},{8,9},{9,8},{10,11... | collective-permute-start | bytes 98312 | tf_op jit(solution)/shard_map/ppermute | solution.py:39
  12.0 15.9 %collective-permute-start.8 = (bf16[27,32,128]{2,1,0:T(8,128)(2,1)}, bf16[27,32,128]{2,1,0:T(8,128)(2,1)S(1)}, u32[]{:S(2)}, u32[]{:S(2)}) collective-permute-start(bf16[27,32,128]{2,1,0:T(8,128)(2,1)} %m0.1), channel_id=1, source_target_pairs={{0,2},{1,3},{2,0},{3,1},{4,6},{5,7},{6,4},{7,5},{8,10},{9,11},{10,... | collective-permute-start | bytes 663560 | tf_op jit(solution)/shard_map/ppermute | solution.py:39
  16.7 18.1 %copy-start = (bf16[27,32,128]{2,1,0:T(8,128)(2,1)S(1)}, bf16[27,32,128]{2,1,0:T(8,128)(2,1)}, u32[]{:S(2)}) copy-start(bf16[27,32,128]{2,1,0:T(8,128)(2,1)} %m0.1) | copy-start | bytes 663556
  16.7 8.9 %collective-permute-start.3 = (bf16[2,256,128]{2,1,0:T(8,128)(2,1)S(1)}, bf16[2,256,128]{2,1,0:T(8,128)(2,1)S(1)}, u32[]{:S(2)}, u32[]{:S(2)}) collective-permute-start(bf16[2,256,128]{2,1,0:T(8,128)(2,1)S(1)} %get-tuple-element.25.own), channel_id=1, source_target_pairs={{0,4},{1,5},{2,6},{3,7},{4,0},{5,1},{6,2},{7,3},{8,12},{9,13},{10,... | collective-permute-start | bytes 393224 | tf_op jit(solution)/shard_map/ppermute | solution.py:39
  18.3 8.2 %collective-permute-start.4 = (bf16[2,256,128]{2,1,0:T(8,128)(2,1)S(1)}, bf16[2,256,128]{2,1,0:T(8,128)(2,1)S(1)}, u32[]{:S(2)}, u32[]{:S(2)}) collective-permute-start(bf16[2,256,128]{2,1,0:T(8,128)(2,1)S(1)} %get-tuple-element.25.own), channel_id=1, source_target_pairs={{4,8},{5,9},{6,10},{7,11},{8,4},{9,5},{10,6},{11,7},{12,16},{13,17... | collective-permute-start | bytes 393224 | tf_op jit(solution)/shard_map/ppermute | solution.py:39
  19.0 13.2 %collective-permute-start.11 = (bf16[27,32,128]{2,1,0:T(8,128)(2,1)S(1)}, bf16[27,32,128]{2,1,0:T(8,128)(2,1)S(1)}, u32[]{:S(2)}, u32[]{:S(2)}) collective-permute-start(bf16[27,32,128]{2,1,0:T(8,128)(2,1)S(1)} %copy-done.1), channel_id=1, source_target_pairs={{0,18},{1,19},{2,16},{3,17},{4,22},{5,23},{6,20},{7,21},{8,26},{9,... | collective-permute-start | bytes 663560 | tf_op jit(solution)/shard_map/ppermute | solution.py:39
  25.6 6.6 %collective-permute-start.19 = (bf16[2,256,128]{2,1,0:T(8,128)(2,1)S(1)}, bf16[2,256,128]{2,1,0:T(8,128)(2,1)S(1)}, u32[]{:S(2)}, u32[]{:S(2)}) collective-permute-start(bf16[2,256,128]{2,1,0:T(8,128)(2,1)S(1)} %get-tuple-element.35.own), channel_id=1, source_target_pairs={{0,4},{1,5},{2,6},{3,7},{4,0},{5,1},{6,2},{7,3},{8,12},{9,13},{10,... | collective-permute-start | bytes 393224 | tf_op jit(solution)/shard_map/ppermute | solution.py:39
  27.1 8.8 %collective-permute-start.5 = (bf16[6,256,128]{2,1,0:T(8,128)(2,1)S(1)}, bf16[6,256,128]{2,1,0:T(8,128)(2,1)S(1)}, u32[]{:S(2)}, u32[]{:S(2)}) collective-permute-start(bf16[6,256,128]{2,1,0:T(8,128)(2,1)S(1)} %shard_map.85), channel_id=1, source_target_pairs={{0,1},{1,0},{2,3},{3,2},{4,5},{5,4},{6,7},{7,6},{8,9},{9,8},{10,11... | collective-permute-start | bytes 1179656 | tf_op jit(solution)/shard_map/ppermute | solution.py:39
  27.2 8.8 %collective-permute-start.6 = (bf16[6,256,128]{2,1,0:T(8,128)(2,1)S(1)}, bf16[6,256,128]{2,1,0:T(8,128)(2,1)S(1)}, u32[]{:S(2)}, u32[]{:S(2)}) collective-permute-start(bf16[6,256,128]{2,1,0:T(8,128)(2,1)S(1)} %shard_map.85), channel_id=1, source_target_pairs={{1,2},{2,1},{5,6},{6,5},{9,10},{10,9},{13,14},{14,13},{17,18},{18,... | collective-permute-start | bytes 1179656 | tf_op jit(solution)/shard_map/ppermute | solution.py:39
  27.9 4.9 %collective-permute-start.20 = (bf16[2,256,128]{2,1,0:T(8,128)(2,1)S(1)}, bf16[2,256,128]{2,1,0:T(8,128)(2,1)S(1)}, u32[]{:S(2)}, u32[]{:S(2)}) collective-permute-start(bf16[2,256,128]{2,1,0:T(8,128)(2,1)S(1)} %get-tuple-element.35.own), channel_id=1, source_target_pairs={{4,8},{5,9},{6,10},{7,11},{8,4},{9,5},{10,6},{11,7},{12,16},{13,17... | collective-permute-start | bytes 393224 | tf_op jit(solution)/shard_map/ppermute | solution.py:39
  32.2 1.5 %collective-permute-start.10 = (bf16[27,32,128]{2,1,0:T(8,128)(2,1)S(1)}, bf16[27,32,128]{2,1,0:T(8,128)(2,1)S(1)}, u32[]{:S(2)}, u32[]{:S(2)}) collective-permute-start(bf16[27,32,128]{2,1,0:T(8,128)(2,1)S(1)} %copy-done.1), channel_id=1, source_target_pairs={{0,1},{1,0},{2,3},{3,2},{4,5},{5,4},{6,7},{7,6},{8,9},{9,8},{10,11... | collective-permute-start | bytes 663560 | tf_op jit(solution)/shard_map/ppermute | solution.py:39
  32.2 1.8 %collective-permute-start.9 = (bf16[27,32,128]{2,1,0:T(8,128)(2,1)S(1)}, bf16[27,32,128]{2,1,0:T(8,128)(2,1)S(1)}, u32[]{:S(2)}, u32[]{:S(2)}) collective-permute-start(bf16[27,32,128]{2,1,0:T(8,128)(2,1)S(1)} %collective-permute-done.8.m2), channel_id=1, source_target_pairs={{0,1},{1,0},{2,3},{3,2},{4,5},{5,4},{6,7},{7,6},{8,9},{9,8},{10,11... | collective-permute-start | bytes 663560 | tf_op jit(solution)/shard_map/ppermute | solution.py:39
  32.8 2.0 %collective-permute-start.12 = (bf16[27,32,128]{2,1,0:T(8,128)(2,1)S(1)}, bf16[27,32,128]{2,1,0:T(8,128)(2,1)S(1)}, u32[]{:S(2)}, u32[]{:S(2)}) collective-permute-start(bf16[27,32,128]{2,1,0:T(8,128)(2,1)S(1)} %collective-permute-done.11.l2), channel_id=1, source_target_pairs={{0,1},{1,0},{2,3},{3,2},{4,5},{5,4},{6,7},{7,6},{8,9},{9,8},{10,11... | collective-permute-start | bytes 663560 | tf_op jit(solution)/shard_map/ppermute | solution.py:39
  33.7 9.6 %collective-permute-start.21 = (bf16[6,256,128]{2,1,0:T(8,128)(2,1)S(1)}, bf16[6,256,128]{2,1,0:T(8,128)(2,1)S(1)}, u32[]{:S(2)}, u32[]{:S(2)}) collective-permute-start(bf16[6,256,128]{2,1,0:T(8,128)(2,1)S(1)} %shard_map.92), channel_id=1, source_target_pairs={{0,1},{1,0},{2,3},{3,2},{4,5},{5,4},{6,7},{7,6},{8,9},{9,8},{10,11... | collective-permute-start | bytes 1179656 | tf_op jit(solution)/shard_map/ppermute | solution.py:39
  34.0 9.3 %collective-permute-start.22 = (bf16[6,256,128]{2,1,0:T(8,128)(2,1)S(1)}, bf16[6,256,128]{2,1,0:T(8,128)(2,1)S(1)}, u32[]{:S(2)}, u32[]{:S(2)}) collective-permute-start(bf16[6,256,128]{2,1,0:T(8,128)(2,1)S(1)} %shard_map.92), channel_id=1, source_target_pairs={{1,2},{2,1},{5,6},{6,5},{9,10},{10,9},{13,14},{14,13},{17,18},{18,... | collective-permute-start | bytes 1179656 | tf_op jit(solution)/shard_map/ppermute | solution.py:39
  41.2 10.9 %collective-permute-start.18 = (bf16[2,27,32,128]{3,2,1,0:T(8,128)(2,1)S(1)}, bf16[2,27,32,128]{3,2,1,0:T(8,128)(2,1)S(1)}, u32[]{:S(2)}, u32[]{:S(2)}) collective-permute-start(bf16[2,27,32,128]{3,2,1,0:T(8,128)(2,1)S(1)} %get-tuple-element.33), channel_id=1, source_target_pairs={{0,1},{1,0},{2,3},{3,2},{4,5},{5,4},{6,7},{7,6},{8,9},{9,8},{10,11... | collective-permute-start | bytes 1327112 | tf_op jit(solution)/shard_map/ppermute | solution.py:39
  49.4 4.3 %collective-permute-start.23 = (bf16[2,37,32,128]{3,2,1,0:T(8,128)(2,1)S(1)}, bf16[2,37,32,128]{3,2,1,0:T(8,128)(2,1)S(1)}, u32[]{:S(2)}, u32[]{:S(2)}) collective-permute-start(bf16[2,37,32,128]{3,2,1,0:T(8,128)(2,1)S(1)} %get-tuple-element.42), channel_id=1, source_target_pairs={{0,1},{1,0},{2,3},{3,2},{4,5},{5,4},{6,7},{7,6},{8,9},{9,8},{10,11... | collective-permute-start | bytes 1818632 | tf_op jit(solution)/shard_map/ppermute | solution.py:39
  94.0 17.4 %all-to-all-start.1 = ((bf16[32,64,128]{2,1,0:T(8,128)(2,1)}), bf16[32,64,128]{2,1,0:T(8,128)(2,1)S(1)}, u32[]{:S(2)}, u32[]{:S(2)}) async-start(bf16[32,64,128]{2,1,0:T(8,128)(2,1)} %shard_map.94), calls=%async_computation.1 | async-start | bytes 1048576 | tf_op jit(solution)/shard_map/all_to_all | solution.py:424
  100.0 1.3 %collective-permute-start.13 = (bf16[2,2,2,32,128]{4,3,2,1,0:T(8,128)(2,1)S(1)}, bf16[2,2,2,32,128]{4,3,2,1,0:T(8,128)(2,1)S(1)}, u32[]{:S(2)}, u32[]{:S(2)}) collective-permute-start(bf16[2,2,2,32,128]{4,3,2,1,0:T(8,128)(2,1)S(1)} %get-tuple-element.30), channel_id=1, source_target_pairs={{0,1},{1,0},{2,3},{3,2},{4,5},{5,4},{6,7},{7,6},{8,9},{9,8},{10,11... | collective-permute-start | bytes 196616 | tf_op jit(solution)/shard_map/ppermute | solution.py:39
  101.3 7.4 %collective-permute-start.14 = (bf16[2,2,2,32,128]{4,3,2,1,0:T(8,128)(2,1)S(1)}, bf16[2,2,2,32,128]{4,3,2,1,0:T(8,128)(2,1)S(1)}, u32[]{:S(2)}, u32[]{:S(2)}) collective-permute-start(bf16[2,2,2,32,128]{4,3,2,1,0:T(8,128)(2,1)S(1)} %pad_maximum_fusion.1), channel_id=1, source_target_pairs={{0,2},{1,3},{2,0},{3,1},{4,6},{5,7},{6,4},{7,5},{8,10},{9,11},{10,... | collective-permute-start | bytes 196616 | tf_op jit(solution)/shard_map/ppermute | solution.py:39

commit v8 on v7

--- a/solution.py
+++ b/solution.py
@@ -11,7 +11,7 @@
 FILT = ("chip", "core")
 CELLS = 128
 LIMITS = {
-    "stride": 8, "cells": 4, "join": 6, "weights": 10, "middle": 20, "result": 8, "grad_l": 10, "back": 26,
+    "stride": 8, "join": 6, "weights": 10, "middle": 20, "result": 8, "grad_l": 10, "back": 26,
     "rows": 2, "sum": 6, "finish": 4,
 }
 VMEM = pl.BlockSpec(memory_space=pltpu.VMEM)
@@ -79,7 +79,10 @@
     )
 
 
-def stride_body(info, u_ref, s0, s1, s2, s3, act_ref, pre_ref, columns_ref, weights):
+def stride_body(
+    info, u_ref, s0, s1, s2, s3, c0, c1, c2, c3,
+    act_ref, pre_ref, columns_ref, cot_ref, cells_ref, weights,
+):
     filt = info[1]
     for j, part in enumerate((s0, s1, s2, s3)):
         start = pl.multiple_of((filt ^ j) * 32, 32)
@@ -104,16 +107,10 @@
             pre_ref[p, r] = pre
             act = (pre * jax.nn.sigmoid(pre)).astype(jnp.bfloat16)
             act_ref[p, r * 128 : r * 128 + 128] = act
-
-
-def cells_body(info, c0, c1, c2, c3, own_ref, cells_ref):
-    filt = info[1]
-    for p in range(2):
-        for r in range(2):
             for j, part in enumerate((c0, c1, c2, c3)):
                 start = pl.multiple_of((filt ^ j) * 32, 32)
-                own_ref[p, r, pl.ds(start, 32), :] = part[filt, r, p]
-            cot = own_ref[p, r].astype(jnp.float32).T.astype(jnp.bfloat16)
+                cot_ref[p, r, pl.ds(start, 32), :] = part[filt, r, p]
+            cot = cot_ref[p, r].astype(jnp.float32).T.astype(jnp.bfloat16)
             cells_ref[p, r * 128 : r * 128 + 128] = cot
 
 
@@ -328,26 +325,22 @@
     last_parts = four_parts(last_weight, 4)
     upper = upper_level.transpose(1, 2, 0, 3)
 
-    level_act, level_pre, columns = call(
+    level_act, level_pre, columns, cot_own, cot_cells = call(
         "stride",
         stride_body,
         [
             shape((2, 256, 128)),
             shape((2, 2, 128, 128), jnp.float32),
             shape((512, 512)),
+            shape((2, 2, 128, 128)),
+            shape((2, 256, 128)),
         ],
         [pltpu.VMEM((128, 512), jnp.bfloat16)],
         flops=200_000_000,
         moved=1_500_000,
-        in_specs=[SMEM] + [VMEM] * 5,
-    )(info, upper, *stride_parts)
+        in_specs=[SMEM] + [VMEM] * 9,
+    )(info, upper, *stride_parts, *cot_parts)
     act_parts = neighbourhood(info, level_act)
-    cot_own, cot_cells = call(
-        "cells",
-        cells_body,
-        [shape((2, 2, 128, 128)), shape((2, 256, 128))],
-        in_specs=[SMEM] + [VMEM] * 4,
-    )(info, *cot_parts)
     back_parts = neighbourhood(info, cot_cells)
 
     forward_m, forward_l, backward_l, backward_m = call(

time: 113 us -> 113 us (level)
  transfers between devices with their start and end apart: 25 -> 25, of which waited for: 9 -> 9; matrix products, arithmetic and copies ran while one was open for 2% -> 2% of each run, Pallas kernels for 16% -> 15%
where the time goes in v8:
time: 113 us; the launch traced here: 112 us
  blocking collectives  38.9 us (34%)
  starting transfers between devices  28.8 us (25%)
  waiting for transfers between devices  21.1 us (19%)
  Pallas kernels  19.2 us (17%)
  local copies, waits for them, and re-layouts  3.04 us (3%)
    all_to_all x1, blocking collectives, whole(): lax.all_to_all(terms.reshape(2 * depth, 64, 128), ('chip', 'depth'), 0, 0...  38.9 us
    ppermute x24, starting transfers between devices, shifted(): return lax.ppermute(value, AXES, pairs_of(move))  24.2 us
    ppermute x24, waiting for transfers between devices, shifted(): return lax.ppermute(value, AXES, pairs_of(move))  19.7 us
    pallas_call x1, Pallas kernels, whole(): call('back', back_body, [shape((2, 37, 32, 128))] * 2, [pltpu.VMEM((6, 6,...  6.06 us
    all_to_all x1, starting transfers between devices, whole(): full = lax.all_to_all(spread, 'depth', 0, 0, tiled=True)  4.54 us
    pallas_call x1, Pallas kernels, whole(): call('middle', middle_body, [shape((4, 4, 128, 128)), shape((4, 4, 128, 1...  3.98 us
    unnamed x9, local copies, waits for them, and re-layouts  2.94 us
  transfers between devices with their start and end apart: 25, of which 9 were waited for; matrix products, arithmetic and copies ran while one was open for 2% of the time, Pallas kernels for 15%

profile of v8, /device:TPU:0, one launch (start us, length us, event | category | flops | bytes accessed | tf_op | source)
XLA Modules:
  0.0 112.4 jit_solution(13336974775416483068)
XLA Ops:
  0.6 0.0 copy-start.2
  0.6 1.0 copy.12
  1.6 2.1 %collective-permute-start.4 = (bf16[4,2,2,32,128]{4,3,2,1,0:T(8,128)(2,1)S(1)}, bf16[4,2,2,32,128]{4,3,2,1,0:T(8,128)(2,1)S(1)}, u32[]{:S(2)}, u32[]{:S(2)}) collective-permute-start(bf16[4,2,2,32,128]{4,3,2,1,0:T(8,128)(2,1)S(1)} %bitcast.22), channel_id=1, source_target_pairs={{0,2},{1,3},{2,0},{3,1},{4,6},{5,7},{6,4},{7,5},{8,10},{9,11},{10,... | collective-permute-start | bytes 393224 | tf_op jit(solution)/shard_map/ppermute | solution.py:39
  3.7 0.0 collective-permute-start.3
  3.7 3.5 %collective-permute-done.4.c2 = bf16[4,2,2,32,128]{4,3,2,1,0:T(8,128)(2,1)S(1)} collective-permute-done((bf16[4,2,2,32,128]{4,3,2,1,0:T(8,128)(2,1)S(1)}, bf16[4,2,2,32,128]{4,3,2,1,0:T(8,128)(2,1)S(1)}, u32[]{:S(2)}, u32[]{:S(2)}) %collective-permute-start.4) | collective-permute-done | bytes 131104 | tf_op jit(solution)/shard_map/ppermute | solution.py:39
  7.2 0.0 collective-permute-start.5
  7.2 1.7 %collective-permute-start.1 = (bf16[8,32,64]{2,1,0:T(8,128)(2,1)}, bf16[8,32,64]{2,1,0:T(8,128)(2,1)S(1)}, u32[]{:S(2)}, u32[]{:S(2)}) collective-permute-start(bf16[8,32,64]{2,1,0:T(8,128)(2,1)} %s0.1), channel_id=1, source_target_pairs={{0,2},{1,3},{2,0},{3,1},{4,6},{5,7},{6,4},{7,5},{8,10},{9,11},{10,... | collective-permute-start | bytes 98312 | tf_op jit(solution)/shard_map/ppermute | solution.py:39
  9.0 0.2 collective-permute-start.10
  9.2 0.3 collective-permute-start
  9.5 2.5 %collective-permute-done.1.s2 = bf16[8,32,64]{2,1,0:T(8,128)(2,1)S(1)} collective-permute-done((bf16[8,32,64]{2,1,0:T(8,128)(2,1)}, bf16[8,32,64]{2,1,0:T(8,128)(2,1)S(1)}, u32[]{:S(2)}, u32[]{:S(2)}) %collective-permute-start.1) | collective-permute-done | bytes 32800 | tf_op jit(solution)/shard_map/ppermute | solution.py:39
  11.9 0.0 collective-permute-start.2
  11.9 0.0 collective-permute-done.s1
  11.9 1.7 %collective-permute-start.11 = (bf16[27,32,128]{2,1,0:T(8,128)(2,1)}, bf16[27,32,128]{2,1,0:T(8,128)(2,1)S(1)}, u32[]{:S(2)}, u32[]{:S(2)}) collective-permute-start(bf16[27,32,128]{2,1,0:T(8,128)(2,1)} %m0.1), channel_id=1, source_target_pairs={{0,2},{1,3},{2,0},{3,1},{4,6},{5,7},{6,4},{7,5},{8,10},{9,11},{10,... | collective-permute-start | bytes 663560 | tf_op jit(solution)/shard_map/ppermute | solution.py:39
  13.7 1.2 %copy.16 = bf16[64,4,4,256]{3,0,2,1:T(8,128)(2,1)S(1)} copy(bf16[64,4,4,256]{3,2,1,0:T(4,128)(2,1)} %param.5) | data formatting | bytes 1048576 | tf_op args[0]
  14.9 0.1 stack.22.info
  15.0 0.0 collective-permute-done.2.s3
  15.0 0.0 collective-permute-done.3.c1
  15.0 0.0 collective-permute-done.5.c3
  15.1 0.0 copy-start
  15.1 1.6 %shard_map.84 = (bf16[2,256,128]{2,1,0:T(8,128)(2,1)S(1)}, f32[2,2,128,128]{3,2,1,0:T(8,128)S(1)}, bf16[512,512]{1,0:T(8,128)(2,1)S(1)}, bf16[2,2,128,128]{3,2,1,0:T(8,128)(2,1)S(1)}, bf16[2,256,128]{2,1,0:T(8,128)(2,1)S(1)}) custom-call(s32[5]{0:T(128)S(1)} %stack.22.info, bf16[4,4,64,256]{3,2,1,0:T(8,128)(2,1)S(1)} %bitcast.20, ...), custom_call_target="tpu_custom_call" | custom-call | flops 200000000 | bytes 1500000 | tf_op jit(solution)/shard_map/pallas_call | solution.py:328
  16.7 1.7 %collective-permute-start.6 = (bf16[2,256,128]{2,1,0:T(8,128)(2,1)S(1)}, bf16[2,256,128]{2,1,0:T(8,128)(2,1)S(1)}, u32[]{:S(2)}, u32[]{:S(2)}) collective-permute-start(bf16[2,256,128]{2,1,0:T(8,128)(2,1)S(1)} %get-tuple-element.25.own), channel_id=1, source_target_pairs={{0,4},{1,5},{2,6},{3,7},{4,0},{5,1},{6,2},{7,3},{8,12},{9,13},{10,... | collective-permute-start | bytes 393224 | tf_op jit(solution)/shard_map/ppermute | solution.py:39
  18.4 0.7 collective-permute-start.7
  19.1 5.9 %collective-permute-start.14 = (bf16[27,32,128]{2,1,0:T(8,128)(2,1)S(1)}, bf16[27,32,128]{2,1,0:T(8,128)(2,1)S(1)}, u32[]{:S(2)}, u32[]{:S(2)}) collective-permute-start(bf16[27,32,128]{2,1,0:T(8,128)(2,1)S(1)} %copy-done.1), channel_id=1, source_target_pairs={{0,18},{1,19},{2,16},{3,17},{4,22},{5,23},{6,20},{7,21},{8,26},{9,... | collective-permute-start | bytes 663560 | tf_op jit(solution)/shard_map/ppermute | solution.py:39
  24.9 0.0 collective-permute-done.6.pair
  24.9 0.8 collective-permute-start.19
  25.8 0.0 collective-permute-done.7.beyond
  25.8 0.6 shard_map.85
  26.3 0.1 collective-permute-start.8
  26.4 0.7 collective-permute-start.9
  27.1 0.0 collective-permute-done.11.m2
  27.1 0.7 collective-permute-start.20
  27.8 4.5 %collective-permute-done.14.l2 = bf16[27,32,128]{2,1,0:T(8,128)(2,1)S(1)} collective-permute-done((bf16[27,32,128]{2,1,0:T(8,128)(2,1)S(1)}, bf16[27,32,128]{2,1,0:T(8,128)(2,1)S(1)}, u32[]{:S(2)}, u32[]{:S(2)}) %collective-permute-start.14) | collective-permute-done | bytes 221216 | tf_op jit(solution)/shard_map/ppermute | solution.py:39
  32.3 0.5 collective-permute-start.12
  32.8 0.1 collective-permute-start.15
  32.9 0.6 shard_map.91
  33.5 0.3 collective-permute-done.13.l1
  33.8 0.2 collective-permute-start.21
  34.0 0.1 collective-permute-done.12.m3
  34.1 0.7 collective-permute-start.22
  34.8 1.2 %shard_map.86 = (bf16[384,1152]{1,0:T(8,128)(2,1)S(1)}, bf16[384,1152]{1,0:T(8,128)(2,1)S(1)}, bf16[1152,384]{1,0:T(8,128)(2,1)S(1)}, bf16[1152,384]{1,0:T(8,128)(2,1)S(1)}) custom-call(s32[5]{0:T(128)S(1)} %stack.22.info, bf16[27,32,128]{2,1,0:T(8,128)(2,1)S(1)} %copy-done, bf16[27,32,128]{2,1,0:T(8,128)(2,1)S(1)} %collective-permute-done.10.m1, ...), custom_call_target="tpu_custom_call" | custom-call | flops 1000000 | bytes 6000000 | tf_op jit(solution)/shard_map/pallas_call | solution.py:346
  36.0 0.0 collective-permute-done.9
  36.0 4.0 %shard_map.87 = (bf16[4,4,128,128]{3,2,1,0:T(8,128)(2,1)S(1)}, f32[4,4,128,128]{3,2,1,0:T(8,128)S(1)}, bf16[6,6,128,128]{3,2,1,0:T(8,128)(2,1)S(1)}) custom-call(s32[5]{0:T(128)S(1)} %stack.22.info, bf16[6,2,128,128]{3,2,1,0:T(8,128)(2,1)S(1)} %bitcast.26, bf16[6,2,128,128]{3,2,1,0:T(8,128)(2,1)S(1)} %bitcast.28, bf16[6,2,128,128]{3,2,1,0:T(8,128)(2,1)S(1)} %bitcast.29, ...), custom_call_target="tpu_custom_call" | custom-call | flops 3000000000 | bytes 4000000 | tf_op jit(solution)/shard_map/pallas_call | solution.py:355
  40.0 1.3 %shard_map.90 = (bf16[2,27,32,128]{3,2,1,0:T(8,128)(2,1)S(1)}, bf16[2,27,32,128]{3,2,1,0:T(8,128)(2,1)S(1)}) custom-call(s32[5]{0:T(128)S(1)} %stack.22.info, bf16[4,4,128,128]{3,2,1,0:T(8,128)(2,1)S(1)} %get-tuple-element.27.act_ref.mid_act, bf16[2,2,128,128]{3,2,1,0:T(8,128)(2,1)S(1)} %get-tuple-element.31.cot_own), custom_call_target="tpu_custom_call" | custom-call | flops 500000000 | bytes 3000000 | tf_op jit(solution)/shard_map/pallas_call | solution.py:376
  41.2 2.1 %collective-permute-start.18 = (bf16[2,27,32,128]{3,2,1,0:T(8,128)(2,1)S(1)}, bf16[2,27,32,128]{3,2,1,0:T(8,128)(2,1)S(1)}, u32[]{:S(2)}, u32[]{:S(2)}) collective-permute-start(bf16[2,27,32,128]{3,2,1,0:T(8,128)(2,1)S(1)} %get-tuple-element.33), channel_id=1, source_target_pairs={{0,1},{1,0},{2,3},{3,2},{4,5},{5,4},{6,7},{7,6},{8,9},{9,8},{10,11... | collective-permute-start | bytes 1327112 | tf_op jit(solution)/shard_map/ppermute | solution.py:39
  43.4 0.0 collective-permute-done.21
  43.4 6.1 %shard_map.92 = (bf16[2,37,32,128]{3,2,1,0:T(8,128)(2,1)S(1)}, bf16[2,37,32,128]{3,2,1,0:T(8,128)(2,1)S(1)}) custom-call(s32[5]{0:T(128)S(1)} %stack.22.info, bf16[6,6,128,128]{3,2,1,0:T(8,128)(2,1)S(1)} %get-tuple-element.34.act_window, bf16[6,2,128,128]{3,2,1,0:T(8,128)(2,1)S(1)} %bitcast.27, bf16[6,2,128,128]{3,2,1,0:T(8,128)(2,1)S(1)} %bitcast.30, ...), custom_call_target="tpu_custom_call" | custom-call | flops 4000000000 | bytes 8000000 | tf_op jit(solution)/shard_map/pallas_call | solution.py:386
  49.4 2.7 %collective-permute-start.23 = (bf16[2,37,32,128]{3,2,1,0:T(8,128)(2,1)S(1)}, bf16[2,37,32,128]{3,2,1,0:T(8,128)(2,1)S(1)}, u32[]{:S(2)}, u32[]{:S(2)}) collective-permute-start(bf16[2,37,32,128]{3,2,1,0:T(8,128)(2,1)S(1)} %get-tuple-element.42), channel_id=1, source_target_pairs={{0,1},{1,0},{2,3},{3,2},{4,5},{5,4},{6,7},{7,6},{8,9},{9,8},{10,11... | collective-permute-start | bytes 1818632 | tf_op jit(solution)/shard_map/ppermute | solution.py:39
  52.1 0.0 collective-permute-done.18
  52.1 0.1 add_convert_fusion.1
  52.3 1.5 %collective-permute-done.23 = bf16[2,37,32,128]{3,2,1,0:T(8,128)(2,1)S(1)} collective-permute-done((bf16[2,37,32,128]{3,2,1,0:T(8,128)(2,1)S(1)}, bf16[2,37,32,128]{3,2,1,0:T(8,128)(2,1)S(1)}, u32[]{:S(2)}, u32[]{:S(2)}) %collective-permute-start.23) | collective-permute-done | bytes 606240 | tf_op jit(solution)/shard_map/ppermute | solution.py:39
  53.8 0.2 add_convert_fusion
  54.0 0.1 pad_maximum_fusion
  54.1 38.9 %all_to_all.10.terms_ref = bf16[64,64,128]{2,1,0:T(8,128)(2,1)S(1)} all-to-all(bf16[64,64,128]{2,1,0:T(8,128)(2,1)S(1)} %bitcast.32), channel_id=1, replica_groups=mesh['depth'=32,'chip'=2,'core'=2] {'chip','depth'}, dimensions={0} | all-to-all | bytes 2097152 | tf_op jit(solution)/shard_map/all_to_all | solution.py:415
  93.0 1.0 shard_map.93
  94.0 4.5 %all-to-all-start.1 = ((bf16[32,64,128]{2,1,0:T(8,128)(2,1)}), bf16[32,64,128]{2,1,0:T(8,128)(2,1)S(1)}, u32[]{:S(2)}, u32[]{:S(2)}) async-start(bf16[32,64,128]{2,1,0:T(8,128)(2,1)} %shard_map.93), calls=%async_computation.1 | async-start | bytes 1048576 | tf_op jit(solution)/shard_map/all_to_all | solution.py:417
  98.5 1.5 %shard_map.88 = (bf16[2,2,2,32,128]{4,3,2,1,0:T(8,128)(2,1)S(1)}, bf16[2,2,2,32,128]{4,3,2,1,0:T(8,128)(2,1)S(1)}) custom-call(s32[5]{0:T(128)S(1)} %stack.22.info, bf16[4,4,128,128]{3,2,1,0:T(8,128)(2,1)S(1)} %get-tuple-element.27.act_ref.mid_act, bf16[384,1152]{1,0:T(8,128)(2,1)S(1)} %get-tuple-element.28.weights), custom_call_target="tpu_custom_call" | custom-call | flops 500000000 | bytes 2000000 | tf_op jit(solution)/shard_map/pallas_call | solution.py:364
  100.0 0.1 collective-permute-start.16
  100.1 1.2 %collective-permute-done.16.near = bf16[2,2,2,32,128]{4,3,2,1,0:T(8,128)(2,1)S(1)} collective-permute-done((bf16[2,2,2,32,128]{4,3,2,1,0:T(8,128)(2,1)S(1)}, bf16[2,2,2,32,128]{4,3,2,1,0:T(8,128)(2,1)S(1)}, u32[]{:S(2)}, u32[]{:S(2)}) %collective-permute-start.16) | collective-permute-done | bytes 65568 | tf_op jit(solution)/shard_map/ppermute | solution.py:39
  101.3 1.3 %collective-permute-start.17 = (bf16[2,2,2,32,128]{4,3,2,1,0:T(8,128)(2,1)S(1)}, bf16[2,2,2,32,128]{4,3,2,1,0:T(8,128)(2,1)S(1)}, u32[]{:S(2)}, u32[]{:S(2)}) collective-permute-start(bf16[2,2,2,32,128]{4,3,2,1,0:T(8,128)(2,1)S(1)} %pad_maximum_fusion.1), channel_id=1, source_target_pairs={{0,2},{1,3},{2,0},{3,1},{4,6},{5,7},{6,4},{7,5},{8,10},{9,11},{10,... | collective-permute-start | bytes 196616 | tf_op jit(solution)/shard_map/ppermute | solution.py:39
  102.6 6.1 %collective-permute-done.17.far = bf16[2,2,2,32,128]{4,3,2,1,0:T(8,128)(2,1)S(1)} collective-permute-done((bf16[2,2,2,32,128]{4,3,2,1,0:T(8,128)(2,1)S(1)}, bf16[2,2,2,32,128]{4,3,2,1,0:T(8,128)(2,1)S(1)}, u32[]{:S(2)}, u32[]{:S(2)}) %collective-permute-start.17) | collective-permute-done | bytes 65568 | tf_op jit(solution)/shard_map/ppermute | solution.py:39
  108.7 0.6 shard_map.89
  109.3 0.7 copy.14
  110.0 1.3 %all-to-all-done.1 = bf16[32,64,128]{2,1,0:T(8,128)(2,1)S(1)} async-done(((bf16[32,64,128]{2,1,0:T(8,128)(2,1)}), bf16[32,64,128]{2,1,0:T(8,128)(2,1)S(1)}, u32[]{:S(2)}, u32[]{:S(2)}) %all-to-all-start.1) | async-done | bytes 524320 | tf_op jit(solution)/shard_map/all_to_all | solution.py:417
  111.4 1.0 shard_map.94
  (15 shorter events, 0.1 us)
Async XLA Ops:
  0.6 14.4 %copy-start.2 = (bf16[8,32,64]{2,1,0:T(8,128)(2,1)S(1)}, bf16[8,32,64]{2,1,0:T(8,128)(2,1)}, u32[]{:S(2)}) copy-start(bf16[8,32,64]{2,1,0:T(8,128)(2,1)} %s0.1) | copy-start | bytes 98308
  1.6 5.6 %collective-permute-start.4 = (bf16[4,2,2,32,128]{4,3,2,1,0:T(8,128)(2,1)S(1)}, bf16[4,2,2,32,128]{4,3,2,1,0:T(8,128)(2,1)S(1)}, u32[]{:S(2)}, u32[]{:S(2)}) collective-permute-start(bf16[4,2,2,32,128]{4,3,2,1,0:T(8,128)(2,1)S(1)} %bitcast.22), channel_id=1, source_target_pairs={{0,2},{1,3},{2,0},{3,1},{4,6},{5,7},{6,4},{7,5},{8,10},{9,11},{10,... | collective-permute-start | bytes 393224 | tf_op jit(solution)/shard_map/ppermute | solution.py:39
  3.7 11.3 %collective-permute-start.3 = (bf16[4,2,2,32,128]{4,3,2,1,0:T(8,128)(2,1)S(1)}, bf16[4,2,2,32,128]{4,3,2,1,0:T(8,128)(2,1)S(1)}, u32[]{:S(2)}, u32[]{:S(2)}) collective-permute-start(bf16[4,2,2,32,128]{4,3,2,1,0:T(8,128)(2,1)S(1)} %bitcast.23), channel_id=1, source_target_pairs={{0,1},{1,0},{2,3},{3,2},{4,5},{5,4},{6,7},{7,6},{8,9},{9,8},{10,11... | collective-permute-start | bytes 393224 | tf_op jit(solution)/shard_map/ppermute | solution.py:39
  7.2 7.8 %collective-permute-start.5 = (bf16[4,2,2,32,128]{4,3,2,1,0:T(8,128)(2,1)S(1)}, bf16[4,2,2,32,128]{4,3,2,1,0:T(8,128)(2,1)S(1)}, u32[]{:S(2)}, u32[]{:S(2)}) collective-permute-start(bf16[4,2,2,32,128]{4,3,2,1,0:T(8,128)(2,1)S(1)} %collective-permute-done.4.c2), channel_id=1, source_target_pairs={{0,1},{1,0},{2,3},{3,2},{4,5},{5,4},{6,7},{7,6},{8,9},{9,8},{10,11... | collective-permute-start | bytes 393224 | tf_op jit(solution)/shard_map/ppermute | solution.py:39
  7.2 4.7 %collective-permute-start.1 = (bf16[8,32,64]{2,1,0:T(8,128)(2,1)}, bf16[8,32,64]{2,1,0:T(8,128)(2,1)S(1)}, u32[]{:S(2)}, u32[]{:S(2)}) collective-permute-start(bf16[8,32,64]{2,1,0:T(8,128)(2,1)} %s0.1), channel_id=1, source_target_pairs={{0,2},{1,3},{2,0},{3,1},{4,6},{5,7},{6,4},{7,5},{8,10},{9,11},{10,... | collective-permute-start | bytes 98312 | tf_op jit(solution)/shard_map/ppermute | solution.py:39
  9.0 17.5 %collective-permute-start.10 = (bf16[27,32,128]{2,1,0:T(8,128)(2,1)}, bf16[27,32,128]{2,1,0:T(8,128)(2,1)S(1)}, u32[]{:S(2)}, u32[]{:S(2)}) collective-permute-start(bf16[27,32,128]{2,1,0:T(8,128)(2,1)} %m0.1), channel_id=1, source_target_pairs={{0,1},{1,0},{2,3},{3,2},{4,5},{5,4},{6,7},{7,6},{8,9},{9,8},{10,11... | collective-permute-start | bytes 663560 | tf_op jit(solution)/shard_map/ppermute | solution.py:39
  9.2 2.8 %collective-permute-start = (bf16[8,32,64]{2,1,0:T(8,128)(2,1)}, bf16[8,32,64]{2,1,0:T(8,128)(2,1)S(1)}, u32[]{:S(2)}, u32[]{:S(2)}) collective-permute-start(bf16[8,32,64]{2,1,0:T(8,128)(2,1)} %s0.1), channel_id=1, source_target_pairs={{0,1},{1,0},{2,3},{3,2},{4,5},{5,4},{6,7},{7,6},{8,9},{9,8},{10,11... | collective-permute-start | bytes 98312 | tf_op jit(solution)/shard_map/ppermute | solution.py:39
  11.9 3.1 %collective-permute-start.2 = (bf16[8,32,64]{2,1,0:T(8,128)(2,1)S(1)}, bf16[8,32,64]{2,1,0:T(8,128)(2,1)S(1)}, u32[]{:S(2)}, u32[]{:S(2)}) collective-permute-start(bf16[8,32,64]{2,1,0:T(8,128)(2,1)S(1)} %collective-permute-done.1.s2), channel_id=1, source_target_pairs={{0,1},{1,0},{2,3},{3,2},{4,5},{5,4},{6,7},{7,6},{8,9},{9,8},{10,11... | collective-permute-start | bytes 98312 | tf_op jit(solution)/shard_map/ppermute | solution.py:39
  11.9 15.2 %collective-permute-start.11 = (bf16[27,32,128]{2,1,0:T(8,128)(2,1)}, bf16[27,32,128]{2,1,0:T(8,128)(2,1)S(1)}, u32[]{:S(2)}, u32[]{:S(2)}) collective-permute-start(bf16[27,32,128]{2,1,0:T(8,128)(2,1)} %m0.1), channel_id=1, source_target_pairs={{0,2},{1,3},{2,0},{3,1},{4,6},{5,7},{6,4},{7,5},{8,10},{9,11},{10,... | collective-permute-start | bytes 663560 | tf_op jit(solution)/shard_map/ppermute | solution.py:39
  13.7 5.4 %copy-start.1 = (bf16[27,32,128]{2,1,0:T(8,128)(2,1)S(1)}, bf16[27,32,128]{2,1,0:T(8,128)(2,1)}, u32[]{:S(2)}) copy-start(bf16[27,32,128]{2,1,0:T(8,128)(2,1)} %l0.1) | copy-start | bytes 663556
  15.1 19.7 %copy-start = (bf16[27,32,128]{2,1,0:T(8,128)(2,1)S(1)}, bf16[27,32,128]{2,1,0:T(8,128)(2,1)}, u32[]{:S(2)}) copy-start(bf16[27,32,128]{2,1,0:T(8,128)(2,1)} %m0.1) | copy-start | bytes 663556
  16.7 8.2 %collective-permute-start.6 = (bf16[2,256,128]{2,1,0:T(8,128)(2,1)S(1)}, bf16[2,256,128]{2,1,0:T(8,128)(2,1)S(1)}, u32[]{:S(2)}, u32[]{:S(2)}) collective-permute-start(bf16[2,256,128]{2,1,0:T(8,128)(2,1)S(1)} %get-tuple-element.25.own), channel_id=1, source_target_pairs={{0,4},{1,5},{2,6},{3,7},{4,0},{5,1},{6,2},{7,3},{8,12},{9,13},{10,... | collective-permute-start | bytes 393224 | tf_op jit(solution)/shard_map/ppermute | solution.py:39
  18.4 7.4 %collective-permute-start.7 = (bf16[2,256,128]{2,1,0:T(8,128)(2,1)S(1)}, bf16[2,256,128]{2,1,0:T(8,128)(2,1)S(1)}, u32[]{:S(2)}, u32[]{:S(2)}) collective-permute-start(bf16[2,256,128]{2,1,0:T(8,128)(2,1)S(1)} %get-tuple-element.25.own), channel_id=1, source_target_pairs={{4,8},{5,9},{6,10},{7,11},{8,4},{9,5},{10,6},{11,7},{12,16},{13,17... | collective-permute-start | bytes 393224 | tf_op jit(solution)/shard_map/ppermute | solution.py:39
  19.1 13.2 %collective-permute-start.14 = (bf16[27,32,128]{2,1,0:T(8,128)(2,1)S(1)}, bf16[27,32,128]{2,1,0:T(8,128)(2,1)S(1)}, u32[]{:S(2)}, u32[]{:S(2)}) collective-permute-start(bf16[27,32,128]{2,1,0:T(8,128)(2,1)S(1)} %copy-done.1), channel_id=1, source_target_pairs={{0,18},{1,19},{2,16},{3,17},{4,22},{5,23},{6,20},{7,21},{8,26},{9,... | collective-permute-start | bytes 663560 | tf_op jit(solution)/shard_map/ppermute | solution.py:39
  24.9 7.3 %collective-permute-start.19 = (bf16[2,256,128]{2,1,0:T(8,128)(2,1)S(1)}, bf16[2,256,128]{2,1,0:T(8,128)(2,1)S(1)}, u32[]{:S(2)}, u32[]{:S(2)}) collective-permute-start(bf16[2,256,128]{2,1,0:T(8,128)(2,1)S(1)} %get-tuple-element.35.own), channel_id=1, source_target_pairs={{0,4},{1,5},{2,6},{3,7},{4,0},{5,1},{6,2},{7,3},{8,12},{9,13},{10,... | collective-permute-start | bytes 393224 | tf_op jit(solution)/shard_map/ppermute | solution.py:39
  26.3 9.6 %collective-permute-start.8 = (bf16[6,256,128]{2,1,0:T(8,128)(2,1)S(1)}, bf16[6,256,128]{2,1,0:T(8,128)(2,1)S(1)}, u32[]{:S(2)}, u32[]{:S(2)}) collective-permute-start(bf16[6,256,128]{2,1,0:T(8,128)(2,1)S(1)} %shard_map.85), channel_id=1, source_target_pairs={{0,1},{1,0},{2,3},{3,2},{4,5},{5,4},{6,7},{7,6},{8,9},{9,8},{10,11... | collective-permute-start | bytes 1179656 | tf_op jit(solution)/shard_map/ppermute | solution.py:39
  26.4 9.5 %collective-permute-start.9 = (bf16[6,256,128]{2,1,0:T(8,128)(2,1)S(1)}, bf16[6,256,128]{2,1,0:T(8,128)(2,1)S(1)}, u32[]{:S(2)}, u32[]{:S(2)}) collective-permute-start(bf16[6,256,128]{2,1,0:T(8,128)(2,1)S(1)} %shard_map.85), channel_id=1, source_target_pairs={{1,2},{2,1},{5,6},{6,5},{9,10},{10,9},{13,14},{14,13},{17,18},{18,... | collective-permute-start | bytes 1179656 | tf_op jit(solution)/shard_map/ppermute | solution.py:39
  27.1 5.6 %collective-permute-start.20 = (bf16[2,256,128]{2,1,0:T(8,128)(2,1)S(1)}, bf16[2,256,128]{2,1,0:T(8,128)(2,1)S(1)}, u32[]{:S(2)}, u32[]{:S(2)}) collective-permute-start(bf16[2,256,128]{2,1,0:T(8,128)(2,1)S(1)} %get-tuple-element.35.own), channel_id=1, source_target_pairs={{4,8},{5,9},{6,10},{7,11},{8,4},{9,5},{10,6},{11,7},{12,16},{13,17... | collective-permute-start | bytes 393224 | tf_op jit(solution)/shard_map/ppermute | solution.py:39
  32.3 1.5 %collective-permute-start.13 = (bf16[27,32,128]{2,1,0:T(8,128)(2,1)S(1)}, bf16[27,32,128]{2,1,0:T(8,128)(2,1)S(1)}, u32[]{:S(2)}, u32[]{:S(2)}) collective-permute-start(bf16[27,32,128]{2,1,0:T(8,128)(2,1)S(1)} %copy-done.1), channel_id=1, source_target_pairs={{0,1},{1,0},{2,3},{3,2},{4,5},{5,4},{6,7},{7,6},{8,9},{9,8},{10,11... | collective-permute-start | bytes 663560 | tf_op jit(solution)/shard_map/ppermute | solution.py:39
  32.3 1.8 %collective-permute-start.12 = (bf16[27,32,128]{2,1,0:T(8,128)(2,1)S(1)}, bf16[27,32,128]{2,1,0:T(8,128)(2,1)S(1)}, u32[]{:S(2)}, u32[]{:S(2)}) collective-permute-start(bf16[27,32,128]{2,1,0:T(8,128)(2,1)S(1)} %collective-permute-done.11.m2), channel_id=1, source_target_pairs={{0,1},{1,0},{2,3},{3,2},{4,5},{5,4},{6,7},{7,6},{8,9},{9,8},{10,11... | collective-permute-start | bytes 663560 | tf_op jit(solution)/shard_map/ppermute | solution.py:39
  32.8 2.0 %collective-permute-start.15 = (bf16[27,32,128]{2,1,0:T(8,128)(2,1)S(1)}, bf16[27,32,128]{2,1,0:T(8,128)(2,1)S(1)}, u32[]{:S(2)}, u32[]{:S(2)}) collective-permute-start(bf16[27,32,128]{2,1,0:T(8,128)(2,1)S(1)} %collective-permute-done.14.l2), channel_id=1, source_target_pairs={{0,1},{1,0},{2,3},{3,2},{4,5},{5,4},{6,7},{7,6},{8,9},{9,8},{10,11... | collective-permute-start | bytes 663560 | tf_op jit(solution)/shard_map/ppermute | solution.py:39
  33.8 9.6 %collective-permute-start.21 = (bf16[6,256,128]{2,1,0:T(8,128)(2,1)S(1)}, bf16[6,256,128]{2,1,0:T(8,128)(2,1)S(1)}, u32[]{:S(2)}, u32[]{:S(2)}) collective-permute-start(bf16[6,256,128]{2,1,0:T(8,128)(2,1)S(1)} %shard_map.91), channel_id=1, source_target_pairs={{0,1},{1,0},{2,3},{3,2},{4,5},{5,4},{6,7},{7,6},{8,9},{9,8},{10,11... | collective-permute-start | bytes 1179656 | tf_op jit(solution)/shard_map/ppermute | solution.py:39
  34.1 9.3 %collective-permute-start.22 = (bf16[6,256,128]{2,1,0:T(8,128)(2,1)S(1)}, bf16[6,256,128]{2,1,0:T(8,128)(2,1)S(1)}, u32[]{:S(2)}, u32[]{:S(2)}) collective-permute-start(bf16[6,256,128]{2,1,0:T(8,128)(2,1)S(1)} %shard_map.91), channel_id=1, source_target_pairs={{1,2},{2,1},{5,6},{6,5},{9,10},{10,9},{13,14},{14,13},{17,18},{18,... | collective-permute-start | bytes 1179656 | tf_op jit(solution)/shard_map/ppermute | solution.py:39
  41.2 10.9 %collective-permute-start.18 = (bf16[2,27,32,128]{3,2,1,0:T(8,128)(2,1)S(1)}, bf16[2,27,32,128]{3,2,1,0:T(8,128)(2,1)S(1)}, u32[]{:S(2)}, u32[]{:S(2)}) collective-permute-start(bf16[2,27,32,128]{3,2,1,0:T(8,128)(2,1)S(1)} %get-tuple-element.33), channel_id=1, source_target_pairs={{0,1},{1,0},{2,3},{3,2},{4,5},{5,4},{6,7},{7,6},{8,9},{9,8},{10,11... | collective-permute-start | bytes 1327112 | tf_op jit(solution)/shard_map/ppermute | solution.py:39
  49.4 4.4 %collective-permute-start.23 = (bf16[2,37,32,128]{3,2,1,0:T(8,128)(2,1)S(1)}, bf16[2,37,32,128]{3,2,1,0:T(8,128)(2,1)S(1)}, u32[]{:S(2)}, u32[]{:S(2)}) collective-permute-start(bf16[2,37,32,128]{3,2,1,0:T(8,128)(2,1)S(1)} %get-tuple-element.42), channel_id=1, source_target_pairs={{0,1},{1,0},{2,3},{3,2},{4,5},{5,4},{6,7},{7,6},{8,9},{9,8},{10,11... | collective-permute-start | bytes 1818632 | tf_op jit(solution)/shard_map/ppermute | solution.py:39
  94.0 17.4 %all-to-all-start.1 = ((bf16[32,64,128]{2,1,0:T(8,128)(2,1)}), bf16[32,64,128]{2,1,0:T(8,128)(2,1)S(1)}, u32[]{:S(2)}, u32[]{:S(2)}) async-start(bf16[32,64,128]{2,1,0:T(8,128)(2,1)} %shard_map.93), calls=%async_computation.1 | async-start | bytes 1048576 | tf_op jit(solution)/shard_map/all_to_all | solution.py:417
  100.0 1.3 %collective-permute-start.16 = (bf16[2,2,2,32,128]{4,3,2,1,0:T(8,128)(2,1)S(1)}, bf16[2,2,2,32,128]{4,3,2,1,0:T(8,128)(2,1)S(1)}, u32[]{:S(2)}, u32[]{:S(2)}) collective-permute-start(bf16[2,2,2,32,128]{4,3,2,1,0:T(8,128)(2,1)S(1)} %get-tuple-element.30), channel_id=1, source_target_pairs={{0,1},{1,0},{2,3},{3,2},{4,5},{5,4},{6,7},{7,6},{8,9},{9,8},{10,11... | collective-permute-start | bytes 196616 | tf_op jit(solution)/shard_map/ppermute | solution.py:39
  101.3 7.4 %collective-permute-start.17 = (bf16[2,2,2,32,128]{4,3,2,1,0:T(8,128)(2,1)S(1)}, bf16[2,2,2,32,128]{4,3,2,1,0:T(8,128)(2,1)S(1)}, u32[]{:S(2)}, u32[]{:S(2)}) collective-permute-start(bf16[2,2,2,32,128]{4,3,2,1,0:T(8,128)(2,1)S(1)} %pad_maximum_fusion.1), channel_id=1, source_target_pairs={{0,2},{1,3},{2,0},{3,1},{4,6},{5,7},{6,4},{7,5},{8,10},{9,11},{10,... | collective-permute-start | bytes 196616 | tf_op jit(solution)/shard_map/ppermute | solution.py:39

commit v9 on v8

--- a/solution.py
+++ b/solution.py
@@ -296,8 +296,14 @@
 
 
 def sum_body(terms_ref, out_ref):
-    total = jnp.sum(terms_ref[...].astype(jnp.float32), axis=0).astype(jnp.bfloat16)
-    out_ref[...] = jnp.broadcast_to(total[None], out_ref.shape)
+    count, rows = terms_ref.shape[0], terms_ref.shape[1]
+    for at in range(0, rows, 16):
+        sums = [terms_ref[k, at : at + 16].astype(jnp.float32) for k in range(4)]
+        for k in range(4, count):
+            sums[k % 4] = sums[k % 4] + terms_ref[k, at : at + 16].astype(jnp.float32)
+        total = ((sums[0] + sums[1]) + (sums[2] + sums[3])).astype(jnp.bfloat16)
+        for d in range(out_ref.shape[0]):
+            out_ref[d, at : at + 16] = total
 
 
 def neighbourhood(info, own):

time: 113 us -> 113 us (level)
  no operation moved by 1% of the time
where the time goes in v9:
time: 113 us; the launch traced here: 112 us
  blocking collectives  38.9 us (34%)
  starting transfers between devices  28.8 us (25%)
  waiting for transfers between devices  21.1 us (19%)
  Pallas kernels  19.2 us (17%)
  local copies, waits for them, and re-layouts  3.04 us (3%)
    all_to_all x1, blocking collectives, whole(): lax.all_to_all(terms.reshape(2 * depth, 64, 128), ('chip', 'depth'), 0, 0...  38.9 us
    ppermute x24, starting transfers between devices, shifted(): return lax.ppermute(value, AXES, pairs_of(move))  24.3 us
    ppermute x24, waiting for transfers between devices, shifted(): return lax.ppermute(value, AXES, pairs_of(move))  19.7 us
    pallas_call x1, Pallas kernels, whole(): call('back', back_body, [shape((2, 37, 32, 128))] * 2, [pltpu.VMEM((6, 6,...  6.06 us
    all_to_all x1, starting transfers between devices, whole(): full = lax.all_to_all(spread, 'depth', 0, 0, tiled=True)  4.54 us
    pallas_call x1, Pallas kernels, whole(): call('middle', middle_body, [shape((4, 4, 128, 128)), shape((4, 4, 128, 1...  3.98 us
    unnamed x9, local copies, waits for them, and re-layouts  2.94 us
  transfers between devices with their start and end apart: 25, of which 9 were waited for; matrix products, arithmetic and copies ran while one was open for 2% of the time, Pallas kernels for 15%

profile of v9, /device:TPU:0, one launch (start us, length us, event | category | flops | bytes accessed | tf_op | source)
XLA Modules:
  0.0 112.3 jit_solution(7235604355427984400)
XLA Ops:
  0.6 0.0 copy-start.2
  0.6 1.0 copy.12
  1.6 2.1 %collective-permute-start.4 = (bf16[4,2,2,32,128]{4,3,2,1,0:T(8,128)(2,1)S(1)}, bf16[4,2,2,32,128]{4,3,2,1,0:T(8,128)(2,1)S(1)}, u32[]{:S(2)}, u32[]{:S(2)}) collective-permute-start(bf16[4,2,2,32,128]{4,3,2,1,0:T(8,128)(2,1)S(1)} %bitcast.22), channel_id=1, source_target_pairs={{0,2},{1,3},{2,0},{3,1},{4,6},{5,7},{6,4},{7,5},{8,10},{9,11},{10,... | collective-permute-start | bytes 393224 | tf_op jit(solution)/shard_map/ppermute | solution.py:39
  3.7 0.0 collective-permute-start.3
  3.7 3.5 %collective-permute-done.4.c2 = bf16[4,2,2,32,128]{4,3,2,1,0:T(8,128)(2,1)S(1)} collective-permute-done((bf16[4,2,2,32,128]{4,3,2,1,0:T(8,128)(2,1)S(1)}, bf16[4,2,2,32,128]{4,3,2,1,0:T(8,128)(2,1)S(1)}, u32[]{:S(2)}, u32[]{:S(2)}) %collective-permute-start.4) | collective-permute-done | bytes 131104 | tf_op jit(solution)/shard_map/ppermute | solution.py:39
  7.2 0.0 collective-permute-start.5
  7.2 1.7 %collective-permute-start.1 = (bf16[8,32,64]{2,1,0:T(8,128)(2,1)}, bf16[8,32,64]{2,1,0:T(8,128)(2,1)S(1)}, u32[]{:S(2)}, u32[]{:S(2)}) collective-permute-start(bf16[8,32,64]{2,1,0:T(8,128)(2,1)} %s0.1), channel_id=1, source_target_pairs={{0,2},{1,3},{2,0},{3,1},{4,6},{5,7},{6,4},{7,5},{8,10},{9,11},{10,... | collective-permute-start | bytes 98312 | tf_op jit(solution)/shard_map/ppermute | solution.py:39
  9.0 0.2 collective-permute-start.10
  9.2 0.3 collective-permute-start
  9.5 2.5 %collective-permute-done.1.s2 = bf16[8,32,64]{2,1,0:T(8,128)(2,1)S(1)} collective-permute-done((bf16[8,32,64]{2,1,0:T(8,128)(2,1)}, bf16[8,32,64]{2,1,0:T(8,128)(2,1)S(1)}, u32[]{:S(2)}, u32[]{:S(2)}) %collective-permute-start.1) | collective-permute-done | bytes 32800 | tf_op jit(solution)/shard_map/ppermute | solution.py:39
  11.9 0.0 collective-permute-start.2
  11.9 0.0 collective-permute-done.s1
  11.9 1.7 %collective-permute-start.11 = (bf16[27,32,128]{2,1,0:T(8,128)(2,1)}, bf16[27,32,128]{2,1,0:T(8,128)(2,1)S(1)}, u32[]{:S(2)}, u32[]{:S(2)}) collective-permute-start(bf16[27,32,128]{2,1,0:T(8,128)(2,1)} %m0.1), channel_id=1, source_target_pairs={{0,2},{1,3},{2,0},{3,1},{4,6},{5,7},{6,4},{7,5},{8,10},{9,11},{10,... | collective-permute-start | bytes 663560 | tf_op jit(solution)/shard_map/ppermute | solution.py:39
  13.7 1.2 %copy.16 = bf16[64,4,4,256]{3,0,2,1:T(8,128)(2,1)S(1)} copy(bf16[64,4,4,256]{3,2,1,0:T(4,128)(2,1)} %param.5) | data formatting | bytes 1048576 | tf_op args[0]
  14.9 0.1 stack.22.info
  15.0 0.0 collective-permute-done.2.s3
  15.0 0.0 collective-permute-done.3.c1
  15.0 0.0 collective-permute-done.5.c3
  15.1 0.0 copy-start
  15.1 1.6 %shard_map.84 = (bf16[2,256,128]{2,1,0:T(8,128)(2,1)S(1)}, f32[2,2,128,128]{3,2,1,0:T(8,128)S(1)}, bf16[512,512]{1,0:T(8,128)(2,1)S(1)}, bf16[2,2,128,128]{3,2,1,0:T(8,128)(2,1)S(1)}, bf16[2,256,128]{2,1,0:T(8,128)(2,1)S(1)}) custom-call(s32[5]{0:T(128)S(1)} %stack.22.info, bf16[4,4,64,256]{3,2,1,0:T(8,128)(2,1)S(1)} %bitcast.20, ...), custom_call_target="tpu_custom_call" | custom-call | flops 200000000 | bytes 1500000 | tf_op jit(solution)/shard_map/pallas_call | solution.py:334
  16.7 1.7 %collective-permute-start.6 = (bf16[2,256,128]{2,1,0:T(8,128)(2,1)S(1)}, bf16[2,256,128]{2,1,0:T(8,128)(2,1)S(1)}, u32[]{:S(2)}, u32[]{:S(2)}) collective-permute-start(bf16[2,256,128]{2,1,0:T(8,128)(2,1)S(1)} %get-tuple-element.25.own), channel_id=1, source_target_pairs={{0,4},{1,5},{2,6},{3,7},{4,0},{5,1},{6,2},{7,3},{8,12},{9,13},{10,... | collective-permute-start | bytes 393224 | tf_op jit(solution)/shard_map/ppermute | solution.py:39
  18.4 0.7 collective-permute-start.7
  19.1 5.9 %collective-permute-start.14 = (bf16[27,32,128]{2,1,0:T(8,128)(2,1)S(1)}, bf16[27,32,128]{2,1,0:T(8,128)(2,1)S(1)}, u32[]{:S(2)}, u32[]{:S(2)}) collective-permute-start(bf16[27,32,128]{2,1,0:T(8,128)(2,1)S(1)} %copy-done.1), channel_id=1, source_target_pairs={{0,18},{1,19},{2,16},{3,17},{4,22},{5,23},{6,20},{7,21},{8,26},{9,... | collective-permute-start | bytes 663560 | tf_op jit(solution)/shard_map/ppermute | solution.py:39
  24.9 0.0 collective-permute-done.6.pair
  24.9 0.8 collective-permute-start.19
  25.8 0.0 collective-permute-done.7.beyond
  25.8 0.6 shard_map.85
  26.3 0.1 collective-permute-start.8
  26.4 0.7 collective-permute-start.9
  27.1 0.0 collective-permute-done.11.m2
  27.1 0.7 collective-permute-start.20
  27.8 4.5 %collective-permute-done.14.l2 = bf16[27,32,128]{2,1,0:T(8,128)(2,1)S(1)} collective-permute-done((bf16[27,32,128]{2,1,0:T(8,128)(2,1)S(1)}, bf16[27,32,128]{2,1,0:T(8,128)(2,1)S(1)}, u32[]{:S(2)}, u32[]{:S(2)}) %collective-permute-start.14) | collective-permute-done | bytes 221216 | tf_op jit(solution)/shard_map/ppermute | solution.py:39
  32.3 0.5 collective-permute-start.12
  32.8 0.1 collective-permute-start.15
  32.9 0.6 shard_map.91
  33.5 0.3 collective-permute-done.13.l1
  33.8 0.2 collective-permute-start.21
  34.0 0.1 collective-permute-done.12.m3
  34.1 0.7 collective-permute-start.22
  34.8 1.2 %shard_map.86 = (bf16[384,1152]{1,0:T(8,128)(2,1)S(1)}, bf16[384,1152]{1,0:T(8,128)(2,1)S(1)}, bf16[1152,384]{1,0:T(8,128)(2,1)S(1)}, bf16[1152,384]{1,0:T(8,128)(2,1)S(1)}) custom-call(s32[5]{0:T(128)S(1)} %stack.22.info, bf16[27,32,128]{2,1,0:T(8,128)(2,1)S(1)} %copy-done, bf16[27,32,128]{2,1,0:T(8,128)(2,1)S(1)} %collective-permute-done.10.m1, ...), custom_call_target="tpu_custom_call" | custom-call | flops 1000000 | bytes 6000000 | tf_op jit(solution)/shard_map/pallas_call | solution.py:352
  36.0 0.0 collective-permute-done.9
  36.0 4.0 %shard_map.87 = (bf16[4,4,128,128]{3,2,1,0:T(8,128)(2,1)S(1)}, f32[4,4,128,128]{3,2,1,0:T(8,128)S(1)}, bf16[6,6,128,128]{3,2,1,0:T(8,128)(2,1)S(1)}) custom-call(s32[5]{0:T(128)S(1)} %stack.22.info, bf16[6,2,128,128]{3,2,1,0:T(8,128)(2,1)S(1)} %bitcast.26, bf16[6,2,128,128]{3,2,1,0:T(8,128)(2,1)S(1)} %bitcast.28, bf16[6,2,128,128]{3,2,1,0:T(8,128)(2,1)S(1)} %bitcast.29, ...), custom_call_target="tpu_custom_call" | custom-call | flops 3000000000 | bytes 4000000 | tf_op jit(solution)/shard_map/pallas_call | solution.py:361
  40.0 1.3 %shard_map.90 = (bf16[2,27,32,128]{3,2,1,0:T(8,128)(2,1)S(1)}, bf16[2,27,32,128]{3,2,1,0:T(8,128)(2,1)S(1)}) custom-call(s32[5]{0:T(128)S(1)} %stack.22.info, bf16[4,4,128,128]{3,2,1,0:T(8,128)(2,1)S(1)} %get-tuple-element.27.act_ref.mid_act, bf16[2,2,128,128]{3,2,1,0:T(8,128)(2,1)S(1)} %get-tuple-element.31.cot_own), custom_call_target="tpu_custom_call" | custom-call | flops 500000000 | bytes 3000000 | tf_op jit(solution)/shard_map/pallas_call | solution.py:382
  41.2 2.1 %collective-permute-start.18 = (bf16[2,27,32,128]{3,2,1,0:T(8,128)(2,1)S(1)}, bf16[2,27,32,128]{3,2,1,0:T(8,128)(2,1)S(1)}, u32[]{:S(2)}, u32[]{:S(2)}) collective-permute-start(bf16[2,27,32,128]{3,2,1,0:T(8,128)(2,1)S(1)} %get-tuple-element.33), channel_id=1, source_target_pairs={{0,1},{1,0},{2,3},{3,2},{4,5},{5,4},{6,7},{7,6},{8,9},{9,8},{10,11... | collective-permute-start | bytes 1327112 | tf_op jit(solution)/shard_map/ppermute | solution.py:39
  43.4 0.0 collective-permute-done.21
  43.4 6.1 %shard_map.92 = (bf16[2,37,32,128]{3,2,1,0:T(8,128)(2,1)S(1)}, bf16[2,37,32,128]{3,2,1,0:T(8,128)(2,1)S(1)}) custom-call(s32[5]{0:T(128)S(1)} %stack.22.info, bf16[6,6,128,128]{3,2,1,0:T(8,128)(2,1)S(1)} %get-tuple-element.34.act_window, bf16[6,2,128,128]{3,2,1,0:T(8,128)(2,1)S(1)} %bitcast.27, bf16[6,2,128,128]{3,2,1,0:T(8,128)(2,1)S(1)} %bitcast.30, ...), custom_call_target="tpu_custom_call" | custom-call | flops 4000000000 | bytes 8000000 | tf_op jit(solution)/shard_map/pallas_call | solution.py:392
  49.4 2.7 %collective-permute-start.23 = (bf16[2,37,32,128]{3,2,1,0:T(8,128)(2,1)S(1)}, bf16[2,37,32,128]{3,2,1,0:T(8,128)(2,1)S(1)}, u32[]{:S(2)}, u32[]{:S(2)}) collective-permute-start(bf16[2,37,32,128]{3,2,1,0:T(8,128)(2,1)S(1)} %get-tuple-element.42), channel_id=1, source_target_pairs={{0,1},{1,0},{2,3},{3,2},{4,5},{5,4},{6,7},{7,6},{8,9},{9,8},{10,11... | collective-permute-start | bytes 1818632 | tf_op jit(solution)/shard_map/ppermute | solution.py:39
  52.1 0.0 collective-permute-done.18
  52.1 0.1 add_convert_fusion.1
  52.3 1.5 %collective-permute-done.23 = bf16[2,37,32,128]{3,2,1,0:T(8,128)(2,1)S(1)} collective-permute-done((bf16[2,37,32,128]{3,2,1,0:T(8,128)(2,1)S(1)}, bf16[2,37,32,128]{3,2,1,0:T(8,128)(2,1)S(1)}, u32[]{:S(2)}, u32[]{:S(2)}) %collective-permute-start.23) | collective-permute-done | bytes 606240 | tf_op jit(solution)/shard_map/ppermute | solution.py:39
  53.8 0.2 add_convert_fusion
  54.0 0.1 pad_maximum_fusion
  54.1 38.9 %all_to_all.10.terms_ref = bf16[64,64,128]{2,1,0:T(8,128)(2,1)S(1)} all-to-all(bf16[64,64,128]{2,1,0:T(8,128)(2,1)S(1)} %bitcast.32), channel_id=1, replica_groups=mesh['depth'=32,'chip'=2,'core'=2] {'chip','depth'}, dimensions={0} | all-to-all | bytes 2097152 | tf_op jit(solution)/shard_map/all_to_all | solution.py:421
  93.0 1.0 shard_map.93
  94.0 4.5 %all-to-all-start.1 = ((bf16[32,64,128]{2,1,0:T(8,128)(2,1)}), bf16[32,64,128]{2,1,0:T(8,128)(2,1)S(1)}, u32[]{:S(2)}, u32[]{:S(2)}) async-start(bf16[32,64,128]{2,1,0:T(8,128)(2,1)} %shard_map.93), calls=%async_computation.1 | async-start | bytes 1048576 | tf_op jit(solution)/shard_map/all_to_all | solution.py:423
  98.5 1.5 %shard_map.88 = (bf16[2,2,2,32,128]{4,3,2,1,0:T(8,128)(2,1)S(1)}, bf16[2,2,2,32,128]{4,3,2,1,0:T(8,128)(2,1)S(1)}) custom-call(s32[5]{0:T(128)S(1)} %stack.22.info, bf16[4,4,128,128]{3,2,1,0:T(8,128)(2,1)S(1)} %get-tuple-element.27.act_ref.mid_act, bf16[384,1152]{1,0:T(8,128)(2,1)S(1)} %get-tuple-element.28.weights), custom_call_target="tpu_custom_call" | custom-call | flops 500000000 | bytes 2000000 | tf_op jit(solution)/shard_map/pallas_call | solution.py:370
  100.0 0.1 collective-permute-start.16
  100.1 1.2 %collective-permute-done.16.near = bf16[2,2,2,32,128]{4,3,2,1,0:T(8,128)(2,1)S(1)} collective-permute-done((bf16[2,2,2,32,128]{4,3,2,1,0:T(8,128)(2,1)S(1)}, bf16[2,2,2,32,128]{4,3,2,1,0:T(8,128)(2,1)S(1)}, u32[]{:S(2)}, u32[]{:S(2)}) %collective-permute-start.16) | collective-permute-done | bytes 65568 | tf_op jit(solution)/shard_map/ppermute | solution.py:39
  101.3 1.3 %collective-permute-start.17 = (bf16[2,2,2,32,128]{4,3,2,1,0:T(8,128)(2,1)S(1)}, bf16[2,2,2,32,128]{4,3,2,1,0:T(8,128)(2,1)S(1)}, u32[]{:S(2)}, u32[]{:S(2)}) collective-permute-start(bf16[2,2,2,32,128]{4,3,2,1,0:T(8,128)(2,1)S(1)} %pad_maximum_fusion.1), channel_id=1, source_target_pairs={{0,2},{1,3},{2,0},{3,1},{4,6},{5,7},{6,4},{7,5},{8,10},{9,11},{10,... | collective-permute-start | bytes 196616 | tf_op jit(solution)/shard_map/ppermute | solution.py:39
  102.6 6.1 %collective-permute-done.17.far = bf16[2,2,2,32,128]{4,3,2,1,0:T(8,128)(2,1)S(1)} collective-permute-done((bf16[2,2,2,32,128]{4,3,2,1,0:T(8,128)(2,1)S(1)}, bf16[2,2,2,32,128]{4,3,2,1,0:T(8,128)(2,1)S(1)}, u32[]{:S(2)}, u32[]{:S(2)}) %collective-permute-start.17) | collective-permute-done | bytes 65568 | tf_op jit(solution)/shard_map/ppermute | solution.py:39
  108.7 0.6 shard_map.89
  109.3 0.7 copy.14
  110.0 1.4 %all-to-all-done.1 = bf16[32,64,128]{2,1,0:T(8,128)(2,1)S(1)} async-done(((bf16[32,64,128]{2,1,0:T(8,128)(2,1)}), bf16[32,64,128]{2,1,0:T(8,128)(2,1)S(1)}, u32[]{:S(2)}, u32[]{:S(2)}) %all-to-all-start.1) | async-done | bytes 524320 | tf_op jit(solution)/shard_map/all_to_all | solution.py:423
  111.4 1.0 shard_map.94
  (15 shorter events, 0.1 us)
Async XLA Ops:
  0.6 14.4 %copy-start.2 = (bf16[8,32,64]{2,1,0:T(8,128)(2,1)S(1)}, bf16[8,32,64]{2,1,0:T(8,128)(2,1)}, u32[]{:S(2)}) copy-start(bf16[8,32,64]{2,1,0:T(8,128)(2,1)} %s0.1) | copy-start | bytes 98308
  1.6 5.6 %collective-permute-start.4 = (bf16[4,2,2,32,128]{4,3,2,1,0:T(8,128)(2,1)S(1)}, bf16[4,2,2,32,128]{4,3,2,1,0:T(8,128)(2,1)S(1)}, u32[]{:S(2)}, u32[]{:S(2)}) collective-permute-start(bf16[4,2,2,32,128]{4,3,2,1,0:T(8,128)(2,1)S(1)} %bitcast.22), channel_id=1, source_target_pairs={{0,2},{1,3},{2,0},{3,1},{4,6},{5,7},{6,4},{7,5},{8,10},{9,11},{10,... | collective-permute-start | bytes 393224 | tf_op jit(solution)/shard_map/ppermute | solution.py:39
  3.7 11.3 %collective-permute-start.3 = (bf16[4,2,2,32,128]{4,3,2,1,0:T(8,128)(2,1)S(1)}, bf16[4,2,2,32,128]{4,3,2,1,0:T(8,128)(2,1)S(1)}, u32[]{:S(2)}, u32[]{:S(2)}) collective-permute-start(bf16[4,2,2,32,128]{4,3,2,1,0:T(8,128)(2,1)S(1)} %bitcast.23), channel_id=1, source_target_pairs={{0,1},{1,0},{2,3},{3,2},{4,5},{5,4},{6,7},{7,6},{8,9},{9,8},{10,11... | collective-permute-start | bytes 393224 | tf_op jit(solution)/shard_map/ppermute | solution.py:39
  7.2 7.8 %collective-permute-start.5 = (bf16[4,2,2,32,128]{4,3,2,1,0:T(8,128)(2,1)S(1)}, bf16[4,2,2,32,128]{4,3,2,1,0:T(8,128)(2,1)S(1)}, u32[]{:S(2)}, u32[]{:S(2)}) collective-permute-start(bf16[4,2,2,32,128]{4,3,2,1,0:T(8,128)(2,1)S(1)} %collective-permute-done.4.c2), channel_id=1, source_target_pairs={{0,1},{1,0},{2,3},{3,2},{4,5},{5,4},{6,7},{7,6},{8,9},{9,8},{10,11... | collective-permute-start | bytes 393224 | tf_op jit(solution)/shard_map/ppermute | solution.py:39
  7.2 4.7 %collective-permute-start.1 = (bf16[8,32,64]{2,1,0:T(8,128)(2,1)}, bf16[8,32,64]{2,1,0:T(8,128)(2,1)S(1)}, u32[]{:S(2)}, u32[]{:S(2)}) collective-permute-start(bf16[8,32,64]{2,1,0:T(8,128)(2,1)} %s0.1), channel_id=1, source_target_pairs={{0,2},{1,3},{2,0},{3,1},{4,6},{5,7},{6,4},{7,5},{8,10},{9,11},{10,... | collective-permute-start | bytes 98312 | tf_op jit(solution)/shard_map/ppermute | solution.py:39
  9.0 17.5 %collective-permute-start.10 = (bf16[27,32,128]{2,1,0:T(8,128)(2,1)}, bf16[27,32,128]{2,1,0:T(8,128)(2,1)S(1)}, u32[]{:S(2)}, u32[]{:S(2)}) collective-permute-start(bf16[27,32,128]{2,1,0:T(8,128)(2,1)} %m0.1), channel_id=1, source_target_pairs={{0,1},{1,0},{2,3},{3,2},{4,5},{5,4},{6,7},{7,6},{8,9},{9,8},{10,11... | collective-permute-start | bytes 663560 | tf_op jit(solution)/shard_map/ppermute | solution.py:39
  9.2 2.8 %collective-permute-start = (bf16[8,32,64]{2,1,0:T(8,128)(2,1)}, bf16[8,32,64]{2,1,0:T(8,128)(2,1)S(1)}, u32[]{:S(2)}, u32[]{:S(2)}) collective-permute-start(bf16[8,32,64]{2,1,0:T(8,128)(2,1)} %s0.1), channel_id=1, source_target_pairs={{0,1},{1,0},{2,3},{3,2},{4,5},{5,4},{6,7},{7,6},{8,9},{9,8},{10,11... | collective-permute-start | bytes 98312 | tf_op jit(solution)/shard_map/ppermute | solution.py:39
  11.9 3.1 %collective-permute-start.2 = (bf16[8,32,64]{2,1,0:T(8,128)(2,1)S(1)}, bf16[8,32,64]{2,1,0:T(8,128)(2,1)S(1)}, u32[]{:S(2)}, u32[]{:S(2)}) collective-permute-start(bf16[8,32,64]{2,1,0:T(8,128)(2,1)S(1)} %collective-permute-done.1.s2), channel_id=1, source_target_pairs={{0,1},{1,0},{2,3},{3,2},{4,5},{5,4},{6,7},{7,6},{8,9},{9,8},{10,11... | collective-permute-start | bytes 98312 | tf_op jit(solution)/shard_map/ppermute | solution.py:39
  11.9 15.2 %collective-permute-start.11 = (bf16[27,32,128]{2,1,0:T(8,128)(2,1)}, bf16[27,32,128]{2,1,0:T(8,128)(2,1)S(1)}, u32[]{:S(2)}, u32[]{:S(2)}) collective-permute-start(bf16[27,32,128]{2,1,0:T(8,128)(2,1)} %m0.1), channel_id=1, source_target_pairs={{0,2},{1,3},{2,0},{3,1},{4,6},{5,7},{6,4},{7,5},{8,10},{9,11},{10,... | collective-permute-start | bytes 663560 | tf_op jit(solution)/shard_map/ppermute | solution.py:39
  13.7 5.4 %copy-start.1 = (bf16[27,32,128]{2,1,0:T(8,128)(2,1)S(1)}, bf16[27,32,128]{2,1,0:T(8,128)(2,1)}, u32[]{:S(2)}) copy-start(bf16[27,32,128]{2,1,0:T(8,128)(2,1)} %l0.1) | copy-start | bytes 663556
  15.1 19.7 %copy-start = (bf16[27,32,128]{2,1,0:T(8,128)(2,1)S(1)}, bf16[27,32,128]{2,1,0:T(8,128)(2,1)}, u32[]{:S(2)}) copy-start(bf16[27,32,128]{2,1,0:T(8,128)(2,1)} %m0.1) | copy-start | bytes 663556
  16.7 8.2 %collective-permute-start.6 = (bf16[2,256,128]{2,1,0:T(8,128)(2,1)S(1)}, bf16[2,256,128]{2,1,0:T(8,128)(2,1)S(1)}, u32[]{:S(2)}, u32[]{:S(2)}) collective-permute-start(bf16[2,256,128]{2,1,0:T(8,128)(2,1)S(1)} %get-tuple-element.25.own), channel_id=1, source_target_pairs={{0,4},{1,5},{2,6},{3,7},{4,0},{5,1},{6,2},{7,3},{8,12},{9,13},{10,... | collective-permute-start | bytes 393224 | tf_op jit(solution)/shard_map/ppermute | solution.py:39
  18.4 7.4 %collective-permute-start.7 = (bf16[2,256,128]{2,1,0:T(8,128)(2,1)S(1)}, bf16[2,256,128]{2,1,0:T(8,128)(2,1)S(1)}, u32[]{:S(2)}, u32[]{:S(2)}) collective-permute-start(bf16[2,256,128]{2,1,0:T(8,128)(2,1)S(1)} %get-tuple-element.25.own), channel_id=1, source_target_pairs={{4,8},{5,9},{6,10},{7,11},{8,4},{9,5},{10,6},{11,7},{12,16},{13,17... | collective-permute-start | bytes 393224 | tf_op jit(solution)/shard_map/ppermute | solution.py:39
  19.1 13.2 %collective-permute-start.14 = (bf16[27,32,128]{2,1,0:T(8,128)(2,1)S(1)}, bf16[27,32,128]{2,1,0:T(8,128)(2,1)S(1)}, u32[]{:S(2)}, u32[]{:S(2)}) collective-permute-start(bf16[27,32,128]{2,1,0:T(8,128)(2,1)S(1)} %copy-done.1), channel_id=1, source_target_pairs={{0,18},{1,19},{2,16},{3,17},{4,22},{5,23},{6,20},{7,21},{8,26},{9,... | collective-permute-start | bytes 663560 | tf_op jit(solution)/shard_map/ppermute | solution.py:39
  24.9 7.3 %collective-permute-start.19 = (bf16[2,256,128]{2,1,0:T(8,128)(2,1)S(1)}, bf16[2,256,128]{2,1,0:T(8,128)(2,1)S(1)}, u32[]{:S(2)}, u32[]{:S(2)}) collective-permute-start(bf16[2,256,128]{2,1,0:T(8,128)(2,1)S(1)} %get-tuple-element.35.own), channel_id=1, source_target_pairs={{0,4},{1,5},{2,6},{3,7},{4,0},{5,1},{6,2},{7,3},{8,12},{9,13},{10,... | collective-permute-start | bytes 393224 | tf_op jit(solution)/shard_map/ppermute | solution.py:39
  26.3 9.6 %collective-permute-start.8 = (bf16[6,256,128]{2,1,0:T(8,128)(2,1)S(1)}, bf16[6,256,128]{2,1,0:T(8,128)(2,1)S(1)}, u32[]{:S(2)}, u32[]{:S(2)}) collective-permute-start(bf16[6,256,128]{2,1,0:T(8,128)(2,1)S(1)} %shard_map.85), channel_id=1, source_target_pairs={{0,1},{1,0},{2,3},{3,2},{4,5},{5,4},{6,7},{7,6},{8,9},{9,8},{10,11... | collective-permute-start | bytes 1179656 | tf_op jit(solution)/shard_map/ppermute | solution.py:39
  26.4 9.5 %collective-permute-start.9 = (bf16[6,256,128]{2,1,0:T(8,128)(2,1)S(1)}, bf16[6,256,128]{2,1,0:T(8,128)(2,1)S(1)}, u32[]{:S(2)}, u32[]{:S(2)}) collective-permute-start(bf16[6,256,128]{2,1,0:T(8,128)(2,1)S(1)} %shard_map.85), channel_id=1, source_target_pairs={{1,2},{2,1},{5,6},{6,5},{9,10},{10,9},{13,14},{14,13},{17,18},{18,... | collective-permute-start | bytes 1179656 | tf_op jit(solution)/shard_map/ppermute | solution.py:39
  27.1 5.6 %collective-permute-start.20 = (bf16[2,256,128]{2,1,0:T(8,128)(2,1)S(1)}, bf16[2,256,128]{2,1,0:T(8,128)(2,1)S(1)}, u32[]{:S(2)}, u32[]{:S(2)}) collective-permute-start(bf16[2,256,128]{2,1,0:T(8,128)(2,1)S(1)} %get-tuple-element.35.own), channel_id=1, source_target_pairs={{4,8},{5,9},{6,10},{7,11},{8,4},{9,5},{10,6},{11,7},{12,16},{13,17... | collective-permute-start | bytes 393224 | tf_op jit(solution)/shard_map/ppermute | solution.py:39
  32.3 1.5 %collective-permute-start.13 = (bf16[27,32,128]{2,1,0:T(8,128)(2,1)S(1)}, bf16[27,32,128]{2,1,0:T(8,128)(2,1)S(1)}, u32[]{:S(2)}, u32[]{:S(2)}) collective-permute-start(bf16[27,32,128]{2,1,0:T(8,128)(2,1)S(1)} %copy-done.1), channel_id=1, source_target_pairs={{0,1},{1,0},{2,3},{3,2},{4,5},{5,4},{6,7},{7,6},{8,9},{9,8},{10,11... | collective-permute-start | bytes 663560 | tf_op jit(solution)/shard_map/ppermute | solution.py:39
  32.3 1.8 %collective-permute-start.12 = (bf16[27,32,128]{2,1,0:T(8,128)(2,1)S(1)}, bf16[27,32,128]{2,1,0:T(8,128)(2,1)S(1)}, u32[]{:S(2)}, u32[]{:S(2)}) collective-permute-start(bf16[27,32,128]{2,1,0:T(8,128)(2,1)S(1)} %collective-permute-done.11.m2), channel_id=1, source_target_pairs={{0,1},{1,0},{2,3},{3,2},{4,5},{5,4},{6,7},{7,6},{8,9},{9,8},{10,11... | collective-permute-start | bytes 663560 | tf_op jit(solution)/shard_map/ppermute | solution.py:39
  32.8 2.0 %collective-permute-start.15 = (bf16[27,32,128]{2,1,0:T(8,128)(2,1)S(1)}, bf16[27,32,128]{2,1,0:T(8,128)(2,1)S(1)}, u32[]{:S(2)}, u32[]{:S(2)}) collective-permute-start(bf16[27,32,128]{2,1,0:T(8,128)(2,1)S(1)} %collective-permute-done.14.l2), channel_id=1, source_target_pairs={{0,1},{1,0},{2,3},{3,2},{4,5},{5,4},{6,7},{7,6},{8,9},{9,8},{10,11... | collective-permute-start | bytes 663560 | tf_op jit(solution)/shard_map/ppermute | solution.py:39
  33.8 9.6 %collective-permute-start.21 = (bf16[6,256,128]{2,1,0:T(8,128)(2,1)S(1)}, bf16[6,256,128]{2,1,0:T(8,128)(2,1)S(1)}, u32[]{:S(2)}, u32[]{:S(2)}) collective-permute-start(bf16[6,256,128]{2,1,0:T(8,128)(2,1)S(1)} %shard_map.91), channel_id=1, source_target_pairs={{0,1},{1,0},{2,3},{3,2},{4,5},{5,4},{6,7},{7,6},{8,9},{9,8},{10,11... | collective-permute-start | bytes 1179656 | tf_op jit(solution)/shard_map/ppermute | solution.py:39
  34.1 9.3 %collective-permute-start.22 = (bf16[6,256,128]{2,1,0:T(8,128)(2,1)S(1)}, bf16[6,256,128]{2,1,0:T(8,128)(2,1)S(1)}, u32[]{:S(2)}, u32[]{:S(2)}) collective-permute-start(bf16[6,256,128]{2,1,0:T(8,128)(2,1)S(1)} %shard_map.91), channel_id=1, source_target_pairs={{1,2},{2,1},{5,6},{6,5},{9,10},{10,9},{13,14},{14,13},{17,18},{18,... | collective-permute-start | bytes 1179656 | tf_op jit(solution)/shard_map/ppermute | solution.py:39
  41.2 10.9 %collective-permute-start.18 = (bf16[2,27,32,128]{3,2,1,0:T(8,128)(2,1)S(1)}, bf16[2,27,32,128]{3,2,1,0:T(8,128)(2,1)S(1)}, u32[]{:S(2)}, u32[]{:S(2)}) collective-permute-start(bf16[2,27,32,128]{3,2,1,0:T(8,128)(2,1)S(1)} %get-tuple-element.33), channel_id=1, source_target_pairs={{0,1},{1,0},{2,3},{3,2},{4,5},{5,4},{6,7},{7,6},{8,9},{9,8},{10,11... | collective-permute-start | bytes 1327112 | tf_op jit(solution)/shard_map/ppermute | solution.py:39
  49.4 4.4 %collective-permute-start.23 = (bf16[2,37,32,128]{3,2,1,0:T(8,128)(2,1)S(1)}, bf16[2,37,32,128]{3,2,1,0:T(8,128)(2,1)S(1)}, u32[]{:S(2)}, u32[]{:S(2)}) collective-permute-start(bf16[2,37,32,128]{3,2,1,0:T(8,128)(2,1)S(1)} %get-tuple-element.42), channel_id=1, source_target_pairs={{0,1},{1,0},{2,3},{3,2},{4,5},{5,4},{6,7},{7,6},{8,9},{9,8},{10,11... | collective-permute-start | bytes 1818632 | tf_op jit(solution)/shard_map/ppermute | solution.py:39
  94.0 17.4 %all-to-all-start.1 = ((bf16[32,64,128]{2,1,0:T(8,128)(2,1)}), bf16[32,64,128]{2,1,0:T(8,128)(2,1)S(1)}, u32[]{:S(2)}, u32[]{:S(2)}) async-start(bf16[32,64,128]{2,1,0:T(8,128)(2,1)} %shard_map.93), calls=%async_computation.1 | async-start | bytes 1048576 | tf_op jit(solution)/shard_map/all_to_all | solution.py:423
  100.0 1.3 %collective-permute-start.16 = (bf16[2,2,2,32,128]{4,3,2,1,0:T(8,128)(2,1)S(1)}, bf16[2,2,2,32,128]{4,3,2,1,0:T(8,128)(2,1)S(1)}, u32[]{:S(2)}, u32[]{:S(2)}) collective-permute-start(bf16[2,2,2,32,128]{4,3,2,1,0:T(8,128)(2,1)S(1)} %get-tuple-element.30), channel_id=1, source_target_pairs={{0,1},{1,0},{2,3},{3,2},{4,5},{5,4},{6,7},{7,6},{8,9},{9,8},{10,11... | collective-permute-start | bytes 196616 | tf_op jit(solution)/shard_map/ppermute | solution.py:39
  101.3 7.4 %collective-permute-start.17 = (bf16[2,2,2,32,128]{4,3,2,1,0:T(8,128)(2,1)S(1)}, bf16[2,2,2,32,128]{4,3,2,1,0:T(8,128)(2,1)S(1)}, u32[]{:S(2)}, u32[]{:S(2)}) collective-permute-start(bf16[2,2,2,32,128]{4,3,2,1,0:T(8,128)(2,1)S(1)} %pad_maximum_fusion.1), channel_id=1, source_target_pairs={{0,2},{1,3},{2,0},{3,1},{4,6},{5,7},{6,4},{7,5},{8,10},{9,11},{10,... | collective-permute-start | bytes 196616 | tf_op jit(solution)/shard_map/ppermute | solution.py:39

commit v10 on v9

--- a/solution.py
+++ b/solution.py
@@ -1,3 +1,5 @@
+import functools
+
 import jax
 import jax.numpy as jnp
 from jax import lax
@@ -81,7 +83,7 @@
 
 def stride_body(
     info, u_ref, s0, s1, s2, s3, c0, c1, c2, c3,
-    act_ref, pre_ref, columns_ref, cot_ref, cells_ref, weights,
+    act_ref, pre_ref, columns_ref, cot_ref, cells_ref, pack_ref, weights,
 ):
     filt = info[1]
     for j, part in enumerate((s0, s1, s2, s3)):
@@ -107,17 +109,20 @@
             pre_ref[p, r] = pre
             act = (pre * jax.nn.sigmoid(pre)).astype(jnp.bfloat16)
             act_ref[p, r * 128 : r * 128 + 128] = act
+            pack_ref[p, r * 128 : r * 128 + 128] = act
             for j, part in enumerate((c0, c1, c2, c3)):
                 start = pl.multiple_of((filt ^ j) * 32, 32)
                 cot_ref[p, r, pl.ds(start, 32), :] = part[filt, r, p]
             cot = cot_ref[p, r].astype(jnp.float32).T.astype(jnp.bfloat16)
             cells_ref[p, r * 128 : r * 128 + 128] = cot
-
-
-def join_body(info, own, pair, beyond, column_ref):
+            pack_ref[p, 256 + r * 128 : 384 + r * 128] = cot
+
+
+def join_body(first, info, own, pair, beyond, column_ref):
     odd = info[0] & 1
-    for at, part in ((2, own), (4 - 4 * odd, pair), (4 * odd, beyond)):
-        column_ref[pl.ds(at, 2)] = part[...]
+    column_ref[2:4] = own[...]
+    column_ref[pl.ds(4 - 4 * odd, 2)] = pair[...]
+    column_ref[pl.ds(4 * odd, 2)] = beyond[:, first : first + 256]
 
 
 def fill_window(window, middle, near, cross, core):
@@ -306,14 +311,16 @@
             out_ref[d, at : at + 16] = total
 
 
-def neighbourhood(info, own):
+def neighbourhood(info, own, beyond, first):
     def inner(d, f):
         return (d, 3 - f) if f in (1, 2) else (-1, f)
 
-    beyond = shifted(own, lambda d, f: (d + 1 if d % 2 else d - 1, f))
     pair = shifted(own, lambda d, f: (d ^ 1, f))
     column = call(
-        "join", join_body, shape((6, 256, 128)), in_specs=[SMEM] + [VMEM] * 3
+        "join",
+        functools.partial(join_body, first),
+        shape((6, 256, 128)),
+        in_specs=[SMEM] + [VMEM] * 3,
     )(info, own, pair, beyond)
     cross = shifted(column, inner)
     near = swap_core(column)
@@ -331,7 +338,7 @@
     last_parts = four_parts(last_weight, 4)
     upper = upper_level.transpose(1, 2, 0, 3)
 
-    level_act, level_pre, columns, cot_own, cot_cells = call(
+    level_act, level_pre, columns, cot_own, cot_cells, pack = call(
         "stride",
         stride_body,
         [
@@ -340,14 +347,16 @@
             shape((512, 512)),
             shape((2, 2, 128, 128)),
             shape((2, 256, 128)),
+            shape((2, 512, 128)),
         ],
         [pltpu.VMEM((128, 512), jnp.bfloat16)],
         flops=200_000_000,
         moved=1_500_000,
         in_specs=[SMEM] + [VMEM] * 9,
     )(info, upper, *stride_parts, *cot_parts)
-    act_parts = neighbourhood(info, level_act)
-    back_parts = neighbourhood(info, cot_cells)
+    beyond = shifted(pack, lambda d, f: (d + 1 if d % 2 else d - 1, f))
+    act_parts = neighbourhood(info, level_act, beyond, 0)
+    back_parts = neighbourhood(info, cot_cells, beyond, 256)
 
     forward_m, forward_l, backward_l, backward_m = call(
         "weights",

time: 113 us -> 107 us (0.947)
  blocking collectives: 38.9 us -> 32.6 us
  waiting for transfers between devices: 21.1 us -> 22.7 us
    all_to_all x1, blocking collectives: 38.9 us -> 32.6 us  [whole(): lax.all_to_all(terms.reshape(2 * depth, 64, 128), ('chip', 'depth'), 0, 0...]
    ppermute x24 -> x23, waiting for transfers between devices: 19.7 us -> 21.4 us  [shifted(): return lax.ppermute(value, AXES, pairs_of(move))]
    ppermute x24 -> x23, starting transfers between devices: 24.3 us -> 23.6 us  [shifted(): return lax.ppermute(value, AXES, pairs_of(move))]
  transfers between devices with their start and end apart: 25 -> 24, of which waited for: 9 -> 9; matrix products, arithmetic and copies ran while one was open for 2% -> 2% of each run, Pallas kernels for 15% -> 15%
where the time goes in v10:
time: 107 us
  blocking collectives  32.6 us (30%)
  starting transfers between devices  28.1 us (26%)
  waiting for transfers between devices  22.7 us (21%)
  Pallas kernels  19.2 us (18%)
  local copies, waits for them, and re-layouts  3.05 us (3%)
    all_to_all x1, blocking collectives, whole(): lax.all_to_all(terms.reshape(2 * depth, 64, 128), ('chip', 'depth'), 0, 0...  32.6 us
    ppermute x23, starting transfers between devices, shifted(): return lax.ppermute(value, AXES, pairs_of(move))  23.6 us
    ppermute x23, waiting for transfers between devices, shifted(): return lax.ppermute(value, AXES, pairs_of(move))  21.4 us
    pallas_call x1, Pallas kernels, whole(): call('back', back_body, [shape((2, 37, 32, 128))] * 2, [pltpu.VMEM((6, 6,...  6.06 us
    all_to_all x1, starting transfers between devices, whole(): full = lax.all_to_all(spread, 'depth', 0, 0, tiled=True)  4.55 us
    pallas_call x1, Pallas kernels, whole(): call('middle', middle_body, [shape((4, 4, 128, 128)), shape((4, 4, 128, 1...  3.98 us
    unnamed x9, local copies, waits for them, and re-layouts  2.95 us
  transfers between devices with their start and end apart: 24, of which 9 were waited for; matrix products, arithmetic and copies ran while one was open for 2% of the time, Pallas kernels for 15%

profile of v10, /device:TPU:0, one launch (start us, length us, event | category | flops | bytes accessed | tf_op | source)
XLA Modules:
  0.0 107.0 jit_solution(12783874072032679137)
XLA Ops:
  0.6 0.0 copy-start.2
  0.6 1.0 copy.12
  1.6 2.1 %collective-permute-start.4 = (bf16[4,2,2,32,128]{4,3,2,1,0:T(8,128)(2,1)S(1)}, bf16[4,2,2,32,128]{4,3,2,1,0:T(8,128)(2,1)S(1)}, u32[]{:S(2)}, u32[]{:S(2)}) collective-permute-start(bf16[4,2,2,32,128]{4,3,2,1,0:T(8,128)(2,1)S(1)} %bitcast.22), channel_id=1, source_target_pairs={{0,2},{1,3},{2,0},{3,1},{4,6},{5,7},{6,4},{7,5},{8,10},{9,11},{10,... | collective-permute-start | bytes 393224 | tf_op jit(solution)/shard_map/ppermute | solution.py:41
  3.7 0.0 collective-permute-start.3
  3.7 3.5 %collective-permute-done.4.c2 = bf16[4,2,2,32,128]{4,3,2,1,0:T(8,128)(2,1)S(1)} collective-permute-done((bf16[4,2,2,32,128]{4,3,2,1,0:T(8,128)(2,1)S(1)}, bf16[4,2,2,32,128]{4,3,2,1,0:T(8,128)(2,1)S(1)}, u32[]{:S(2)}, u32[]{:S(2)}) %collective-permute-start.4) | collective-permute-done | bytes 131104 | tf_op jit(solution)/shard_map/ppermute | solution.py:41
  7.2 0.0 collective-permute-start.5
  7.2 1.7 %collective-permute-start.1 = (bf16[8,32,64]{2,1,0:T(8,128)(2,1)}, bf16[8,32,64]{2,1,0:T(8,128)(2,1)S(1)}, u32[]{:S(2)}, u32[]{:S(2)}) collective-permute-start(bf16[8,32,64]{2,1,0:T(8,128)(2,1)} %s0.1), channel_id=1, source_target_pairs={{0,2},{1,3},{2,0},{3,1},{4,6},{5,7},{6,4},{7,5},{8,10},{9,11},{10,... | collective-permute-start | bytes 98312 | tf_op jit(solution)/shard_map/ppermute | solution.py:41
  9.0 0.2 collective-permute-start
  9.2 2.7 %collective-permute-done.1.s2 = bf16[8,32,64]{2,1,0:T(8,128)(2,1)S(1)} collective-permute-done((bf16[8,32,64]{2,1,0:T(8,128)(2,1)}, bf16[8,32,64]{2,1,0:T(8,128)(2,1)S(1)}, u32[]{:S(2)}, u32[]{:S(2)}) %collective-permute-start.1) | collective-permute-done | bytes 32800 | tf_op jit(solution)/shard_map/ppermute | solution.py:41
  11.9 0.0 collective-permute-start.2
  11.9 1.3 %copy.16 = bf16[64,4,4,256]{3,0,2,1:T(8,128)(2,1)S(1)} copy(bf16[64,4,4,256]{3,2,1,0:T(4,128)(2,1)} %param.5) | data formatting | bytes 1048576 | tf_op args[0]
  13.2 0.1 stack.22.info
  13.3 0.0 collective-permute-done.s1
  13.3 0.0 collective-permute-done.3.c1
  13.3 1.6 %shard_map.84 = (bf16[2,256,128]{2,1,0:T(8,128)(2,1)S(1)}, f32[2,2,128,128]{3,2,1,0:T(8,128)S(1)}, bf16[512,512]{1,0:T(8,128)(2,1)S(1)}, bf16[2,2,128,128]{3,2,1...) custom-call(s32[5]{0:T(128)S(1)} %stack.22.info, ...), custom_call_target="tpu_custom_call" | custom-call | flops 200000000 | bytes 1500000 | tf_op jit(solution)/shard_map/pallas_call | solution.py:341
  15.0 0.7 collective-permute-start.7
  15.7 0.6 collective-permute-start.10
  16.3 4.1 %collective-permute-start.6 = (bf16[2,256,128]{2,1,0:T(8,128)(2,1)S(1)}, bf16[2,256,128]{2,1,0:T(8,128)(2,1)S(1)}, u32[]{:S(2)}, u32[]{:S(2)}) collective-permute-start(bf16[2,256,128]{2,1,0:T(8,128)(2,1)S(1)} %get-tuple-element.26.own), channel_id=1, source_target_pairs={{0,4},{1,5},{2,6},{3,7},{4,0},{5,1},{6,2},{7,3},{8,12},{9,13},{10,... | collective-permute-start | bytes 393224 | tf_op jit(solution)/shard_map/ppermute | solution.py:41
  20.4 1.7 %collective-permute-start.11 = (bf16[27,32,128]{2,1,0:T(8,128)(2,1)S(1)}, bf16[27,32,128]{2,1,0:T(8,128)(2,1)S(1)}, u32[]{:S(2)}, u32[]{:S(2)}) collective-permute-start(bf16[27,32,128]{2,1,0:T(8,128)(2,1)S(1)} %copy-done), channel_id=1, source_target_pairs={{0,2},{1,3},{2,0},{3,1},{4,6},{5,7},{6,4},{7,5},{8,10},{9,11},{10,... | collective-permute-start | bytes 663560 | tf_op jit(solution)/shard_map/ppermute | solution.py:41
  22.1 2.5 %collective-permute-start.14 = (bf16[27,32,128]{2,1,0:T(8,128)(2,1)S(1)}, bf16[27,32,128]{2,1,0:T(8,128)(2,1)S(1)}, u32[]{:S(2)}, u32[]{:S(2)}) collective-permute-start(bf16[27,32,128]{2,1,0:T(8,128)(2,1)S(1)} %copy-done.1), channel_id=1, source_target_pairs={{0,18},{1,19},{2,16},{3,17},{4,22},{5,23},{6,20},{7,21},{8,26},{9,... | collective-permute-start | bytes 663560 | tf_op jit(solution)/shard_map/ppermute | solution.py:41
  24.6 0.0 collective-permute-done.6.pair
  24.6 0.0 collective-permute-done.7.beyond
  24.6 0.6 shard_map.85
  25.2 0.1 collective-permute-start.8
  25.3 0.7 collective-permute-start.9
  26.0 2.6 %collective-permute-start.19 = (bf16[2,256,128]{2,1,0:T(8,128)(2,1)S(1)}, bf16[2,256,128]{2,1,0:T(8,128)(2,1)S(1)}, u32[]{:S(2)}, u32[]{:S(2)}) collective-permute-start(bf16[2,256,128]{2,1,0:T(8,128)(2,1)S(1)} %get-tuple-element.37.own), channel_id=1, source_target_pairs={{0,4},{1,5},{2,6},{3,7},{4,0},{5,1},{6,2},{7,3},{8,12},{9,13},{10,... | collective-permute-start | bytes 393224 | tf_op jit(solution)/shard_map/ppermute | solution.py:41
  28.6 4.9 %collective-permute-done.11.m2 = bf16[27,32,128]{2,1,0:T(8,128)(2,1)S(1)} collective-permute-done((bf16[27,32,128]{2,1,0:T(8,128)(2,1)S(1)}, bf16[27,32,128]{2,1,0:T(8,128)(2,1)S(1)}, u32[]{:S(2)}, u32[]{:S(2)}) %collective-permute-start.11) | collective-permute-done | bytes 221216 | tf_op jit(solution)/shard_map/ppermute | solution.py:41
  33.6 0.0 collective-permute-start.13
  33.6 0.7 collective-permute-done.14.l2
  34.2 0.0 collective-permute-start.12
  34.2 0.0 collective-permute-done.19.pair
  34.2 0.5 collective-permute-start.15
  34.7 0.6 shard_map.91
  35.3 0.0 collective-permute-done.13.l1
  35.3 0.1 collective-permute-start.20
  35.4 0.3 collective-permute-done.12.m3
  35.7 0.7 collective-permute-start.21
  36.4 0.0 collective-permute-done.15.l3
  36.4 1.2 %shard_map.86 = (bf16[384,1152]{1,0:T(8,128)(2,1)S(1)}, bf16[384,1152]{1,0:T(8,128)(2,1)S(1)}, bf16[1152,384]{1,0:T(8,128)(2,1)S(1)}, bf16[1152,384]{1,0:T(8,128)(2,1)S(1)}) custom-call(s32[5]{0:T(128)S(1)} %stack.22.info, bf16[27,32,128]{2,1,0:T(8,128)(2,1)S(1)} %copy-done, bf16[27,32,128]{2,1,0:T(8,128)(2,1)S(1)} %collective-permute-done.10.m1, ...), custom_call_target="tpu_custom_call" | custom-call | flops 1000000 | bytes 6000000 | tf_op jit(solution)/shard_map/pallas_call | solution.py:361
  37.6 0.0 collective-permute-done.8
  37.6 4.0 %shard_map.87 = (bf16[4,4,128,128]{3,2,1,0:T(8,128)(2,1)S(1)}, f32[4,4,128,128]{3,2,1,0:T(8,128)S(1)}, bf16[6,6,128,128]{3,2,1,0:T(8,128)(2,1)S(1)}) custom-call(s32[5]{0:T(128)S(1)} %stack.22.info, bf16[6,2,128,128]{3,2,1,0:T(8,128)(2,1)S(1)} %bitcast.26, bf16[6,2,128,128]{3,2,1,0:T(8,128)(2,1)S(1)} %bitcast.28, bf16[6,2,128,128]{3,2,1,0:T(8,128)(2,1)S(1)} %bitcast.29, ...), custom_call_target="tpu_custom_call" | custom-call | flops 3000000000 | bytes 4000000 | tf_op jit(solution)/shard_map/pallas_call | solution.py:370
  41.6 1.3 %shard_map.90 = (bf16[2,27,32,128]{3,2,1,0:T(8,128)(2,1)S(1)}, bf16[2,27,32,128]{3,2,1,0:T(8,128)(2,1)S(1)}) custom-call(s32[5]{0:T(128)S(1)} %stack.22.info, bf16[4,4,128,128]{3,2,1,0:T(8,128)(2,1)S(1)} %get-tuple-element.29.act_ref.mid_act, bf16[2,2,128,128]{3,2,1,0:T(8,128)(2,1)S(1)} %get-tuple-element.33.cot_own), custom_call_target="tpu_custom_call" | custom-call | flops 500000000 | bytes 3000000 | tf_op jit(solution)/shard_map/pallas_call | solution.py:391
  42.9 3.7 %collective-permute-start.18 = (bf16[2,27,32,128]{3,2,1,0:T(8,128)(2,1)S(1)}, bf16[2,27,32,128]{3,2,1,0:T(8,128)(2,1)S(1)}, u32[]{:S(2)}, u32[]{:S(2)}) collective-permute-start(bf16[2,27,32,128]{3,2,1,0:T(8,128)(2,1)S(1)} %get-tuple-element.35), channel_id=1, source_target_pairs={{0,1},{1,0},{2,3},{3,2},{4,5},{5,4},{6,7},{7,6},{8,9},{9,8},{10,11... | collective-permute-start | bytes 1327112 | tf_op jit(solution)/shard_map/ppermute | solution.py:41
  46.6 0.0 collective-permute-done.20
  46.6 0.0 collective-permute-done.21
  46.6 6.1 %shard_map.92 = (bf16[2,37,32,128]{3,2,1,0:T(8,128)(2,1)S(1)}, bf16[2,37,32,128]{3,2,1,0:T(8,128)(2,1)S(1)}) custom-call(s32[5]{0:T(128)S(1)} %stack.22.info, bf16[6,6,128,128]{3,2,1,0:T(8,128)(2,1)S(1)} %get-tuple-element.36.act_window, bf16[6,2,128,128]{3,2,1,0:T(8,128)(2,1)S(1)} %bitcast.27, bf16[6,2,128,128]{3,2,1,0:T(8,128)(2,1)S(1)} %bitcast.30, ...), custom_call_target="tpu_custom_call" | custom-call | flops 4000000000 | bytes 8000000 | tf_op jit(solution)/shard_map/pallas_call | solution.py:401
  52.7 0.1 collective-permute-start.22
  52.8 0.0 collective-permute-done.18
  52.8 0.1 add_convert_fusion.1
  52.9 1.9 %collective-permute-done.22 = bf16[2,37,32,128]{3,2,1,0:T(8,128)(2,1)S(1)} collective-permute-done((bf16[2,37,32,128]{3,2,1,0:T(8,128)(2,1)S(1)}, bf16[2,37,32,128]{3,2,1,0:T(8,128)(2,1)S(1)}, u32[]{:S(2)}, u32[]{:S(2)}) %collective-permute-start.22) | collective-permute-done | bytes 606240 | tf_op jit(solution)/shard_map/ppermute | solution.py:41
  54.8 0.2 add_convert_fusion
  54.9 0.1 pad_maximum_fusion
  55.0 32.6 %all_to_all.10.terms_ref = bf16[64,64,128]{2,1,0:T(8,128)(2,1)S(1)} all-to-all(bf16[64,64,128]{2,1,0:T(8,128)(2,1)S(1)} %bitcast.32), channel_id=1, replica_groups=mesh['depth'=32,'chip'=2,'core'=2] {'chip','depth'}, dimensions={0} | all-to-all | bytes 2097152 | tf_op jit(solution)/shard_map/all_to_all | solution.py:430
  87.6 1.0 shard_map.93
  88.6 4.5 %all-to-all-start.1 = ((bf16[32,64,128]{2,1,0:T(8,128)(2,1)}), bf16[32,64,128]{2,1,0:T(8,128)(2,1)S(1)}, u32[]{:S(2)}, u32[]{:S(2)}) async-start(bf16[32,64,128]{2,1,0:T(8,128)(2,1)} %shard_map.93), calls=%async_computation.1 | async-start | bytes 1048576 | tf_op jit(solution)/shard_map/all_to_all | solution.py:432
  93.1 1.5 %shard_map.88 = (bf16[2,2,2,32,128]{4,3,2,1,0:T(8,128)(2,1)S(1)}, bf16[2,2,2,32,128]{4,3,2,1,0:T(8,128)(2,1)S(1)}) custom-call(s32[5]{0:T(128)S(1)} %stack.22.info, bf16[4,4,128,128]{3,2,1,0:T(8,128)(2,1)S(1)} %get-tuple-element.29.act_ref.mid_act, bf16[384,1152]{1,0:T(8,128)(2,1)S(1)} %get-tuple-element.30.weights), custom_call_target="tpu_custom_call" | custom-call | flops 500000000 | bytes 2000000 | tf_op jit(solution)/shard_map/pallas_call | solution.py:379
  94.6 0.1 collective-permute-start.16
  94.7 1.2 %collective-permute-done.16.near = bf16[2,2,2,32,128]{4,3,2,1,0:T(8,128)(2,1)S(1)} collective-permute-done((bf16[2,2,2,32,128]{4,3,2,1,0:T(8,128)(2,1)S(1)}, bf16[2,2,2,32,128]{4,3,2,1,0:T(8,128)(2,1)S(1)}, u32[]{:S(2)}, u32[]{:S(2)}) %collective-permute-start.16) | collective-permute-done | bytes 65568 | tf_op jit(solution)/shard_map/ppermute | solution.py:41
  95.9 1.3 %collective-permute-start.17 = (bf16[2,2,2,32,128]{4,3,2,1,0:T(8,128)(2,1)S(1)}, bf16[2,2,2,32,128]{4,3,2,1,0:T(8,128)(2,1)S(1)}, u32[]{:S(2)}, u32[]{:S(2)}) collective-permute-start(bf16[2,2,2,32,128]{4,3,2,1,0:T(8,128)(2,1)S(1)} %pad_maximum_fusion.1), channel_id=1, source_target_pairs={{0,2},{1,3},{2,0},{3,1},{4,6},{5,7},{6,4},{7,5},{8,10},{9,11},{10,... | collective-permute-start | bytes 196616 | tf_op jit(solution)/shard_map/ppermute | solution.py:41
  97.2 6.1 %collective-permute-done.17.far = bf16[2,2,2,32,128]{4,3,2,1,0:T(8,128)(2,1)S(1)} collective-permute-done((bf16[2,2,2,32,128]{4,3,2,1,0:T(8,128)(2,1)S(1)}, bf16[2,2,2,32,128]{4,3,2,1,0:T(8,128)(2,1)S(1)}, u32[]{:S(2)}, u32[]{:S(2)}) %collective-permute-start.17) | collective-permute-done | bytes 65568 | tf_op jit(solution)/shard_map/ppermute | solution.py:41
  103.3 0.6 shard_map.89
  103.9 0.7 copy.14
  104.6 1.4 %all-to-all-done.1 = bf16[32,64,128]{2,1,0:T(8,128)(2,1)S(1)} async-done(((bf16[32,64,128]{2,1,0:T(8,128)(2,1)}), bf16[32,64,128]{2,1,0:T(8,128)(2,1)S(1)}, u32[]{:S(2)}, u32[]{:S(2)}) %all-to-all-start.1) | async-done | bytes 524320 | tf_op jit(solution)/shard_map/all_to_all | solution.py:432
  106.0 1.0 shard_map.94
  (13 shorter events, 0.0 us)
Async XLA Ops:
  0.6 12.7 %copy-start.2 = (bf16[8,32,64]{2,1,0:T(8,128)(2,1)S(1)}, bf16[8,32,64]{2,1,0:T(8,128)(2,1)}, u32[]{:S(2)}) copy-start(bf16[8,32,64]{2,1,0:T(8,128)(2,1)} %s0.1) | copy-start | bytes 98308
  1.6 5.6 %collective-permute-start.4 = (bf16[4,2,2,32,128]{4,3,2,1,0:T(8,128)(2,1)S(1)}, bf16[4,2,2,32,128]{4,3,2,1,0:T(8,128)(2,1)S(1)}, u32[]{:S(2)}, u32[]{:S(2)}) collective-permute-start(bf16[4,2,2,32,128]{4,3,2,1,0:T(8,128)(2,1)S(1)} %bitcast.22), channel_id=1, source_target_pairs={{0,2},{1,3},{2,0},{3,1},{4,6},{5,7},{6,4},{7,5},{8,10},{9,11},{10,... | collective-permute-start | bytes 393224 | tf_op jit(solution)/shard_map/ppermute | solution.py:41
  3.7 9.6 %collective-permute-start.3 = (bf16[4,2,2,32,128]{4,3,2,1,0:T(8,128)(2,1)S(1)}, bf16[4,2,2,32,128]{4,3,2,1,0:T(8,128)(2,1)S(1)}, u32[]{:S(2)}, u32[]{:S(2)}) collective-permute-start(bf16[4,2,2,32,128]{4,3,2,1,0:T(8,128)(2,1)S(1)} %bitcast.23), channel_id=1, source_target_pairs={{0,1},{1,0},{2,3},{3,2},{4,5},{5,4},{6,7},{7,6},{8,9},{9,8},{10,11... | collective-permute-start | bytes 393224 | tf_op jit(solution)/shard_map/ppermute | solution.py:41
  7.2 6.1 %collective-permute-start.5 = (bf16[4,2,2,32,128]{4,3,2,1,0:T(8,128)(2,1)S(1)}, bf16[4,2,2,32,128]{4,3,2,1,0:T(8,128)(2,1)S(1)}, u32[]{:S(2)}, u32[]{:S(2)}) collective-permute-start(bf16[4,2,2,32,128]{4,3,2,1,0:T(8,128)(2,1)S(1)} %collective-permute-done.4.c2), channel_id=1, source_target_pairs={{0,1},{1,0},{2,3},{3,2},{4,5},{5,4},{6,7},{7,6},{8,9},{9,8},{10,11... | collective-permute-start | bytes 393224 | tf_op jit(solution)/shard_map/ppermute | solution.py:41
  7.2 4.7 %collective-permute-start.1 = (bf16[8,32,64]{2,1,0:T(8,128)(2,1)}, bf16[8,32,64]{2,1,0:T(8,128)(2,1)S(1)}, u32[]{:S(2)}, u32[]{:S(2)}) collective-permute-start(bf16[8,32,64]{2,1,0:T(8,128)(2,1)} %s0.1), channel_id=1, source_target_pairs={{0,2},{1,3},{2,0},{3,1},{4,6},{5,7},{6,4},{7,5},{8,10},{9,11},{10,... | collective-permute-start | bytes 98312 | tf_op jit(solution)/shard_map/ppermute | solution.py:41
  9.0 4.3 %collective-permute-start = (bf16[8,32,64]{2,1,0:T(8,128)(2,1)}, bf16[8,32,64]{2,1,0:T(8,128)(2,1)S(1)}, u32[]{:S(2)}, u32[]{:S(2)}) collective-permute-start(bf16[8,32,64]{2,1,0:T(8,128)(2,1)} %s0.1), channel_id=1, source_target_pairs={{0,1},{1,0},{2,3},{3,2},{4,5},{5,4},{6,7},{7,6},{8,9},{9,8},{10,11... | collective-permute-start | bytes 98312 | tf_op jit(solution)/shard_map/ppermute | solution.py:41
  11.9 1.4 %collective-permute-start.2 = (bf16[8,32,64]{2,1,0:T(8,128)(2,1)S(1)}, bf16[8,32,64]{2,1,0:T(8,128)(2,1)S(1)}, u32[]{:S(2)}, u32[]{:S(2)}) collective-permute-start(bf16[8,32,64]{2,1,0:T(8,128)(2,1)S(1)} %collective-permute-done.1.s2), channel_id=1, source_target_pairs={{0,1},{1,0},{2,3},{3,2},{4,5},{5,4},{6,7},{7,6},{8,9},{9,8},{10,11... | collective-permute-start | bytes 98312 | tf_op jit(solution)/shard_map/ppermute | solution.py:41
  11.9 3.7 %copy-start = (bf16[27,32,128]{2,1,0:T(8,128)(2,1)S(1)}, bf16[27,32,128]{2,1,0:T(8,128)(2,1)}, u32[]{:S(2)}) copy-start(bf16[27,32,128]{2,1,0:T(8,128)(2,1)} %m0.1) | copy-start | bytes 663556
  11.9 10.2 %copy-start.1 = (bf16[27,32,128]{2,1,0:T(8,128)(2,1)S(1)}, bf16[27,32,128]{2,1,0:T(8,128)(2,1)}, u32[]{:S(2)}) copy-start(bf16[27,32,128]{2,1,0:T(8,128)(2,1)} %l0.1) | copy-start | bytes 663556
  15.0 9.7 %collective-permute-start.7 = (bf16[2,512,128]{2,1,0:T(8,128)(2,1)S(1)}, bf16[2,512,128]{2,1,0:T(8,128)(2,1)S(1)}, u32[]{:S(2)}, u32[]{:S(2)}) collective-permute-start(bf16[2,512,128]{2,1,0:T(8,128)(2,1)S(1)} %get-tuple-element.27), channel_id=1, source_target_pairs={{4,8},{5,9},{6,10},{7,11},{8,4},{9,5},{10,6},{11,7},{12,16},{13,17... | collective-permute-start | bytes 786440 | tf_op jit(solution)/shard_map/ppermute | solution.py:41
  15.7 10.3 %collective-permute-start.10 = (bf16[27,32,128]{2,1,0:T(8,128)(2,1)S(1)}, bf16[27,32,128]{2,1,0:T(8,128)(2,1)S(1)}, u32[]{:S(2)}, u32[]{:S(2)}) collective-permute-start(bf16[27,32,128]{2,1,0:T(8,128)(2,1)S(1)} %copy-done), channel_id=1, source_target_pairs={{0,1},{1,0},{2,3},{3,2},{4,5},{5,4},{6,7},{7,6},{8,9},{9,8},{10,11... | collective-permute-start | bytes 663560 | tf_op jit(solution)/shard_map/ppermute | solution.py:41
  16.3 8.4 %collective-permute-start.6 = (bf16[2,256,128]{2,1,0:T(8,128)(2,1)S(1)}, bf16[2,256,128]{2,1,0:T(8,128)(2,1)S(1)}, u32[]{:S(2)}, u32[]{:S(2)}) collective-permute-start(bf16[2,256,128]{2,1,0:T(8,128)(2,1)S(1)} %get-tuple-element.26.own), channel_id=1, source_target_pairs={{0,4},{1,5},{2,6},{3,7},{4,0},{5,1},{6,2},{7,3},{8,12},{9,13},{10,... | collective-permute-start | bytes 393224 | tf_op jit(solution)/shard_map/ppermute | solution.py:41
  20.4 13.2 %collective-permute-start.11 = (bf16[27,32,128]{2,1,0:T(8,128)(2,1)S(1)}, bf16[27,32,128]{2,1,0:T(8,128)(2,1)S(1)}, u32[]{:S(2)}, u32[]{:S(2)}) collective-permute-start(bf16[27,32,128]{2,1,0:T(8,128)(2,1)S(1)} %copy-done), channel_id=1, source_target_pairs={{0,2},{1,3},{2,0},{3,1},{4,6},{5,7},{6,4},{7,5},{8,10},{9,11},{10,... | collective-permute-start | bytes 663560 | tf_op jit(solution)/shard_map/ppermute | solution.py:41
  22.1 12.1 %collective-permute-start.14 = (bf16[27,32,128]{2,1,0:T(8,128)(2,1)S(1)}, bf16[27,32,128]{2,1,0:T(8,128)(2,1)S(1)}, u32[]{:S(2)}, u32[]{:S(2)}) collective-permute-start(bf16[27,32,128]{2,1,0:T(8,128)(2,1)S(1)} %copy-done.1), channel_id=1, source_target_pairs={{0,18},{1,19},{2,16},{3,17},{4,22},{5,23},{6,20},{7,21},{8,26},{9,... | collective-permute-start | bytes 663560 | tf_op jit(solution)/shard_map/ppermute | solution.py:41
  25.2 12.3 %collective-permute-start.8 = (bf16[6,256,128]{2,1,0:T(8,128)(2,1)S(1)}, bf16[6,256,128]{2,1,0:T(8,128)(2,1)S(1)}, u32[]{:S(2)}, u32[]{:S(2)}) collective-permute-start(bf16[6,256,128]{2,1,0:T(8,128)(2,1)S(1)} %shard_map.85), channel_id=1, source_target_pairs={{0,1},{1,0},{2,3},{3,2},{4,5},{5,4},{6,7},{7,6},{8,9},{9,8},{10,11... | collective-permute-start | bytes 1179656 | tf_op jit(solution)/shard_map/ppermute | solution.py:41
  25.3 12.3 %collective-permute-start.9 = (bf16[6,256,128]{2,1,0:T(8,128)(2,1)S(1)}, bf16[6,256,128]{2,1,0:T(8,128)(2,1)S(1)}, u32[]{:S(2)}, u32[]{:S(2)}) collective-permute-start(bf16[6,256,128]{2,1,0:T(8,128)(2,1)S(1)} %shard_map.85), channel_id=1, source_target_pairs={{1,2},{2,1},{5,6},{6,5},{9,10},{10,9},{13,14},{14,13},{17,18},{18,... | collective-permute-start | bytes 1179656 | tf_op jit(solution)/shard_map/ppermute | solution.py:41
  26.0 8.2 %collective-permute-start.19 = (bf16[2,256,128]{2,1,0:T(8,128)(2,1)S(1)}, bf16[2,256,128]{2,1,0:T(8,128)(2,1)S(1)}, u32[]{:S(2)}, u32[]{:S(2)}) collective-permute-start(bf16[2,256,128]{2,1,0:T(8,128)(2,1)S(1)} %get-tuple-element.37.own), channel_id=1, source_target_pairs={{0,4},{1,5},{2,6},{3,7},{4,0},{5,1},{6,2},{7,3},{8,12},{9,13},{10,... | collective-permute-start | bytes 393224 | tf_op jit(solution)/shard_map/ppermute | solution.py:41
  33.6 1.8 %collective-permute-start.13 = (bf16[27,32,128]{2,1,0:T(8,128)(2,1)S(1)}, bf16[27,32,128]{2,1,0:T(8,128)(2,1)S(1)}, u32[]{:S(2)}, u32[]{:S(2)}) collective-permute-start(bf16[27,32,128]{2,1,0:T(8,128)(2,1)S(1)} %copy-done.1), channel_id=1, source_target_pairs={{0,1},{1,0},{2,3},{3,2},{4,5},{5,4},{6,7},{7,6},{8,9},{9,8},{10,11... | collective-permute-start | bytes 663560 | tf_op jit(solution)/shard_map/ppermute | solution.py:41
  34.2 1.5 %collective-permute-start.12 = (bf16[27,32,128]{2,1,0:T(8,128)(2,1)S(1)}, bf16[27,32,128]{2,1,0:T(8,128)(2,1)S(1)}, u32[]{:S(2)}, u32[]{:S(2)}) collective-permute-start(bf16[27,32,128]{2,1,0:T(8,128)(2,1)S(1)} %collective-permute-done.11.m2), channel_id=1, source_target_pairs={{0,1},{1,0},{2,3},{3,2},{4,5},{5,4},{6,7},{7,6},{8,9},{9,8},{10,11... | collective-permute-start | bytes 663560 | tf_op jit(solution)/shard_map/ppermute | solution.py:41
  34.2 2.1 %collective-permute-start.15 = (bf16[27,32,128]{2,1,0:T(8,128)(2,1)S(1)}, bf16[27,32,128]{2,1,0:T(8,128)(2,1)S(1)}, u32[]{:S(2)}, u32[]{:S(2)}) collective-permute-start(bf16[27,32,128]{2,1,0:T(8,128)(2,1)S(1)} %collective-permute-done.14.l2), channel_id=1, source_target_pairs={{0,1},{1,0},{2,3},{3,2},{4,5},{5,4},{6,7},{7,6},{8,9},{9,8},{10,11... | collective-permute-start | bytes 663560 | tf_op jit(solution)/shard_map/ppermute | solution.py:41
  35.3 11.3 %collective-permute-start.20 = (bf16[6,256,128]{2,1,0:T(8,128)(2,1)S(1)}, bf16[6,256,128]{2,1,0:T(8,128)(2,1)S(1)}, u32[]{:S(2)}, u32[]{:S(2)}) collective-permute-start(bf16[6,256,128]{2,1,0:T(8,128)(2,1)S(1)} %shard_map.91), channel_id=1, source_target_pairs={{0,1},{1,0},{2,3},{3,2},{4,5},{5,4},{6,7},{7,6},{8,9},{9,8},{10,11... | collective-permute-start | bytes 1179656 | tf_op jit(solution)/shard_map/ppermute | solution.py:41
  35.7 10.9 %collective-permute-start.21 = (bf16[6,256,128]{2,1,0:T(8,128)(2,1)S(1)}, bf16[6,256,128]{2,1,0:T(8,128)(2,1)S(1)}, u32[]{:S(2)}, u32[]{:S(2)}) collective-permute-start(bf16[6,256,128]{2,1,0:T(8,128)(2,1)S(1)} %shard_map.91), channel_id=1, source_target_pairs={{1,2},{2,1},{5,6},{6,5},{9,10},{10,9},{13,14},{14,13},{17,18},{18,... | collective-permute-start | bytes 1179656 | tf_op jit(solution)/shard_map/ppermute | solution.py:41
  42.9 9.9 %collective-permute-start.18 = (bf16[2,27,32,128]{3,2,1,0:T(8,128)(2,1)S(1)}, bf16[2,27,32,128]{3,2,1,0:T(8,128)(2,1)S(1)}, u32[]{:S(2)}, u32[]{:S(2)}) collective-permute-start(bf16[2,27,32,128]{3,2,1,0:T(8,128)(2,1)S(1)} %get-tuple-element.35), channel_id=1, source_target_pairs={{0,1},{1,0},{2,3},{3,2},{4,5},{5,4},{6,7},{7,6},{8,9},{9,8},{10,11... | collective-permute-start | bytes 1327112 | tf_op jit(solution)/shard_map/ppermute | solution.py:41
  52.7 2.1 %collective-permute-start.22 = (bf16[2,37,32,128]{3,2,1,0:T(8,128)(2,1)S(1)}, bf16[2,37,32,128]{3,2,1,0:T(8,128)(2,1)S(1)}, u32[]{:S(2)}, u32[]{:S(2)}) collective-permute-start(bf16[2,37,32,128]{3,2,1,0:T(8,128)(2,1)S(1)} %get-tuple-element.44), channel_id=1, source_target_pairs={{0,1},{1,0},{2,3},{3,2},{4,5},{5,4},{6,7},{7,6},{8,9},{9,8},{10,11... | collective-permute-start | bytes 1818632 | tf_op jit(solution)/shard_map/ppermute | solution.py:41
  88.6 17.4 %all-to-all-start.1 = ((bf16[32,64,128]{2,1,0:T(8,128)(2,1)}), bf16[32,64,128]{2,1,0:T(8,128)(2,1)S(1)}, u32[]{:S(2)}, u32[]{:S(2)}) async-start(bf16[32,64,128]{2,1,0:T(8,128)(2,1)} %shard_map.93), calls=%async_computation.1 | async-start | bytes 1048576 | tf_op jit(solution)/shard_map/all_to_all | solution.py:432
  94.6 1.3 %collective-permute-start.16 = (bf16[2,2,2,32,128]{4,3,2,1,0:T(8,128)(2,1)S(1)}, bf16[2,2,2,32,128]{4,3,2,1,0:T(8,128)(2,1)S(1)}, u32[]{:S(2)}, u32[]{:S(2)}) collective-permute-start(bf16[2,2,2,32,128]{4,3,2,1,0:T(8,128)(2,1)S(1)} %get-tuple-element.32), channel_id=1, source_target_pairs={{0,1},{1,0},{2,3},{3,2},{4,5},{5,4},{6,7},{7,6},{8,9},{9,8},{10,11... | collective-permute-start | bytes 196616 | tf_op jit(solution)/shard_map/ppermute | solution.py:41
  95.9 7.4 %collective-permute-start.17 = (bf16[2,2,2,32,128]{4,3,2,1,0:T(8,128)(2,1)S(1)}, bf16[2,2,2,32,128]{4,3,2,1,0:T(8,128)(2,1)S(1)}, u32[]{:S(2)}, u32[]{:S(2)}) collective-permute-start(bf16[2,2,2,32,128]{4,3,2,1,0:T(8,128)(2,1)S(1)} %pad_maximum_fusion.1), channel_id=1, source_target_pairs={{0,2},{1,3},{2,0},{3,1},{4,6},{5,7},{6,4},{7,5},{8,10},{9,11},{10,... | collective-permute-start | bytes 196616 | tf_op jit(solution)/shard_map/ppermute | solution.py:41

commit v11 on v10

--- a/solution.py
+++ b/solution.py
@@ -118,17 +118,21 @@
             pack_ref[p, 256 + r * 128 : 384 + r * 128] = cot
 
 
-def join_body(first, info, own, pair, beyond, column_ref):
+def join_body(first, info, own, pair, beyond, column_ref, halo_ref):
     odd = info[0] & 1
     column_ref[2:4] = own[...]
     column_ref[pl.ds(4 - 4 * odd, 2)] = pair[...]
     column_ref[pl.ds(4 * odd, 2)] = beyond[:, first : first + 256]
-
-
-def fill_window(window, middle, near, cross, core):
+    halo_ref[pl.ds(2 - 2 * odd, 2)] = pair[...]
+    halo_ref[pl.ds(2 * odd, 2)] = beyond[:, first : first + 256]
+
+
+def fill_window(window, middle, near, cross, halo, core):
     window[:, 2:4] = middle[...]
     window[:, pl.ds(4 - 4 * core, 2)] = near[...]
-    window[:, pl.ds(4 * core, 2)] = cross[...]
+    window[0:2, pl.ds(4 * core, 2)] = halo[0:2]
+    window[2:4, pl.ds(4 * core, 2)] = cross[...]
+    window[4:6, pl.ds(4 * core, 2)] = halo[2:4]
 
 
 def fill_forward(weights, parts, filt):
@@ -198,8 +202,8 @@
     return valid & (plane <= last) & (row <= jnp.where(filt == 3, 2, 3))
 
 
-def middle_body(info, mid, near, cross, weights, act_ref, pre_ref, window):
-    fill_window(window, mid, near, cross, info[4])
+def middle_body(info, mid, near, cross, halo, weights, act_ref, pre_ref, window):
+    fill_window(window, mid, near, cross, halo, info[4])
 
     pre = conv_forward(window, 0, 4, 0, 4, weights)
     act = jnp.where(inside(info), pre * jax.nn.sigmoid(pre), 0.0)
@@ -259,12 +263,12 @@
 
 
 def back_body(
-    info, act_window, mid, near, cross, weights_l, weights_m, mid_pre, level_pre, columns,
+    info, act_window, mid, near, cross, halo, weights_l, weights_m, mid_pre, level_pre, columns,
     keep_ref, send_ref, window, delta, turned,
 ):
     core = info[4]
     refs = (keep_ref, send_ref)
-    fill_window(window, mid, near, cross, core)
+    fill_window(window, mid, near, cross, halo, core)
 
     back = conv_backward(window, 0, 4, 0, 4, weights_l)
     here = jnp.where(inside(info), back * silu_slope(mid_pre[...].reshape(16 * CELLS, 128)), 0.0)
@@ -316,15 +320,16 @@
         return (d, 3 - f) if f in (1, 2) else (-1, f)
 
     pair = shifted(own, lambda d, f: (d ^ 1, f))
-    column = call(
+    cross = shifted(own, inner)
+    column, halo = call(
         "join",
         functools.partial(join_body, first),
-        shape((6, 256, 128)),
+        [shape((6, 256, 128)), shape((4, 256, 128))],
         in_specs=[SMEM] + [VMEM] * 3,
     )(info, own, pair, beyond)
-    cross = shifted(column, inner)
+    halo = shifted(halo, inner)
     near = swap_core(column)
-    return [x.reshape(6, 2, 128, 128) for x in (column, near, cross)]
+    return [x.reshape(x.shape[0], 2, 128, 128) for x in (column, near, cross, halo)]
 
 
 def whole(upper_level, stride_weight, middle_weight, last_weight, cotangent):
@@ -373,7 +378,7 @@
         [shape((4, 4, 128, 128)), shape((4, 4, 128, 128), jnp.float32), shape((6, 6, 128, 128))],
         flops=3_000_000_000,
         moved=4_000_000,
-        in_specs=[SMEM] + [VMEM] * 4,
+        in_specs=[SMEM] + [VMEM] * 5,
     )(info, *act_parts, forward_m)
 
     stay, leave = call(
@@ -409,7 +414,7 @@
         ],
         flops=4_000_000_000,
         moved=8_000_000,
-        in_specs=[SMEM] + [VMEM] * 9,
+        in_specs=[SMEM] + [VMEM] * 10,
     )(
         info, act_window, *back_parts, backward_l, backward_m, mid_pre, level_pre, columns
     )

time: 107 us -> 111 us (1.037)
  starting transfers between devices: 28.1 us -> 35.9 us
  blocking collectives: 32.6 us -> 27.2 us
  waiting for transfers between devices: 22.7 us -> 24 us
    ppermute x23 -> x25, starting transfers between devices: 23.6 us -> 31.3 us  [shifted(): return lax.ppermute(value, AXES, pairs_of(move))]
    all_to_all x1, blocking collectives: 32.6 us -> 27.2 us  [whole(): lax.all_to_all(terms.reshape(2 * depth, 64, 128), ('chip', 'depth'), 0, 0...]
    ppermute x23 -> x25, waiting for transfers between devices: 21.4 us -> 22.7 us  [shifted(): return lax.ppermute(value, AXES, pairs_of(move))]
  transfers between devices with their start and end apart: 24 -> 26, of which waited for: 9 -> 10; matrix products, arithmetic and copies ran while one was open for 2% -> 2% of each run, Pallas kernels for 15% -> 14%
where the time goes in v11:
time: 111 us
  starting transfers between devices  35.9 us (32%)
  blocking collectives  27.2 us (25%)
  waiting for transfers between devices  24 us (22%)
  Pallas kernels  19.3 us (17%)
  local copies, waits for them, and re-layouts  3.05 us (3%)
    ppermute x25, starting transfers between devices, shifted(): return lax.ppermute(value, AXES, pairs_of(move))  31.3 us
    all_to_all x1, blocking collectives, whole(): lax.all_to_all(terms.reshape(2 * depth, 64, 128), ('chip', 'depth'), 0, 0...  27.2 us
    ppermute x25, waiting for transfers between devices, shifted(): return lax.ppermute(value, AXES, pairs_of(move))  22.7 us
    pallas_call x1, Pallas kernels, whole(): call('back', back_body, [shape((2, 37, 32, 128))] * 2, [pltpu.VMEM((6, 6,...  6.06 us
    all_to_all x1, starting transfers between devices, whole(): full = lax.all_to_all(spread, 'depth', 0, 0, tiled=True)  4.54 us
    pallas_call x1, Pallas kernels, whole(): call('middle', middle_body, [shape((4, 4, 128, 128)), shape((4, 4, 128, 1...  3.98 us
    unnamed x9, local copies, waits for them, and re-layouts  2.95 us
  transfers between devices with their start and end apart: 26, of which 10 were waited for; matrix products, arithmetic and copies ran while one was open for 2% of the time, Pallas kernels for 14%

profile of v11, /device:TPU:0, one launch (start us, length us, event | category | flops | bytes accessed | tf_op | source)
XLA Modules:
  0.0 110.8 jit_solution(16377909595647458717)
XLA Ops:
  0.6 0.0 copy-start.2
  0.6 1.0 copy.12
  1.6 2.1 %collective-permute-start.4 = (bf16[4,2,2,32,128]{4,3,2,1,0:T(8,128)(2,1)S(1)}, bf16[4,2,2,32,128]{4,3,2,1,0:T(8,128)(2,1)S(1)}, u32[]{:S(2)}, u32[]{:S(2)}) collective-permute-start(bf16[4,2,2,32,128]{4,3,2,1,0:T(8,128)(2,1)S(1)} %bitcast.24), channel_id=1, source_target_pairs={{0,2},{1,3},{2,0},{3,1},{4,6},{5,7},{6,4},{7,5},{8,10},{9,11},{10,... | collective-permute-start | bytes 393224 | tf_op jit(solution)/shard_map/ppermute | solution.py:41
  3.7 0.0 collective-permute-start.3
  3.7 3.5 %collective-permute-done.4.c2 = bf16[4,2,2,32,128]{4,3,2,1,0:T(8,128)(2,1)S(1)} collective-permute-done((bf16[4,2,2,32,128]{4,3,2,1,0:T(8,128)(2,1)S(1)}, bf16[4,2,2,32,128]{4,3,2,1,0:T(8,128)(2,1)S(1)}, u32[]{:S(2)}, u32[]{:S(2)}) %collective-permute-start.4) | collective-permute-done | bytes 131104 | tf_op jit(solution)/shard_map/ppermute | solution.py:41
  7.2 1.7 %collective-permute-start.1 = (bf16[8,32,64]{2,1,0:T(8,128)(2,1)}, bf16[8,32,64]{2,1,0:T(8,128)(2,1)S(1)}, u32[]{:S(2)}, u32[]{:S(2)}) collective-permute-start(bf16[8,32,64]{2,1,0:T(8,128)(2,1)} %s0.1), channel_id=1, source_target_pairs={{0,2},{1,3},{2,0},{3,1},{4,6},{5,7},{6,4},{7,5},{8,10},{9,11},{10,... | collective-permute-start | bytes 98312 | tf_op jit(solution)/shard_map/ppermute | solution.py:41
  9.0 0.2 collective-permute-start
  9.2 2.7 %collective-permute-done.1.s2 = bf16[8,32,64]{2,1,0:T(8,128)(2,1)S(1)} collective-permute-done((bf16[8,32,64]{2,1,0:T(8,128)(2,1)}, bf16[8,32,64]{2,1,0:T(8,128)(2,1)S(1)}, u32[]{:S(2)}, u32[]{:S(2)}) %collective-permute-start.1) | collective-permute-done | bytes 32800 | tf_op jit(solution)/shard_map/ppermute | solution.py:41
  11.9 0.0 collective-permute-start.2
  11.9 1.3 %copy.16 = bf16[64,4,4,256]{3,0,2,1:T(8,128)(2,1)S(1)} copy(bf16[64,4,4,256]{3,2,1,0:T(4,128)(2,1)} %param.5) | data formatting | bytes 1048576 | tf_op args[0]
  13.2 0.1 stack.22.info
  13.3 0.0 collective-permute-done.3.c1
  13.3 1.6 %shard_map.84 = (bf16[2,256,128]{2,1,0:T(8,128)(2,1)S(1)}, f32[2,2,128,128]{3,2,1,0:T(8,128)S(1)}, bf16[512,512]{1,0:T(8,128)(2,1)S(1)}, bf16[2,2,128,128]{3,2,1...) custom-call(s32[5]{0:T(128)S(1)} %stack.22.info, ...), custom_call_target="tpu_custom_call" | custom-call | flops 200000000 | bytes 1500000 | tf_op jit(solution)/shard_map/pallas_call | solution.py:346
  15.0 0.7 collective-permute-start.7
  15.7 4.5 %collective-permute-start.6 = (bf16[2,256,128]{2,1,0:T(8,128)(2,1)S(1)}, bf16[2,256,128]{2,1,0:T(8,128)(2,1)S(1)}, u32[]{:S(2)}, u32[]{:S(2)}) collective-permute-start(bf16[2,256,128]{2,1,0:T(8,128)(2,1)S(1)} %get-tuple-element.30.own), channel_id=1, source_target_pairs={{0,4},{1,5},{2,6},{3,7},{4,0},{5,1},{6,2},{7,3},{8,12},{9,13},{10,... | collective-permute-start | bytes 393224 | tf_op jit(solution)/shard_map/ppermute | solution.py:41
  20.1 1.7 %collective-permute-start.12 = (bf16[27,32,128]{2,1,0:T(8,128)(2,1)S(1)}, bf16[27,32,128]{2,1,0:T(8,128)(2,1)S(1)}, u32[]{:S(2)}, u32[]{:S(2)}) collective-permute-start(bf16[27,32,128]{2,1,0:T(8,128)(2,1)S(1)} %copy-done), channel_id=1, source_target_pairs={{0,2},{1,3},{2,0},{3,1},{4,6},{5,7},{6,4},{7,5},{8,10},{9,11},{10,... | collective-permute-start | bytes 663560 | tf_op jit(solution)/shard_map/ppermute | solution.py:41
  21.9 0.0 collective-permute-start.11
  21.9 0.5 collective-permute-start.14
  22.4 1.6 %collective-permute-done.6.pair = bf16[2,256,128]{2,1,0:T(8,128)(2,1)S(1)} collective-permute-done((bf16[2,256,128]{2,1,0:T(8,128)(2,1)S(1)}, bf16[2,256,128]{2,1,0:T(8,128)(2,1)S(1)}, u32[]{:S(2)}, u32[]{:S(2)}) %collective-permute-start.6) | collective-permute-done | bytes 131104 | tf_op jit(solution)/shard_map/ppermute | solution.py:41
  24.0 5.5 %collective-permute-start.15 = (bf16[27,32,128]{2,1,0:T(8,128)(2,1)S(1)}, bf16[27,32,128]{2,1,0:T(8,128)(2,1)S(1)}, u32[]{:S(2)}, u32[]{:S(2)}) collective-permute-start(bf16[27,32,128]{2,1,0:T(8,128)(2,1)S(1)} %copy-done.1), channel_id=1, source_target_pairs={{0,18},{1,19},{2,16},{3,17},{4,22},{5,23},{6,20},{7,21},{8,26},{9,... | collective-permute-start | bytes 663560 | tf_op jit(solution)/shard_map/ppermute | solution.py:41
  29.5 0.0 collective-permute-done.7.beyond
  29.5 0.6 shard_map.85
  30.1 0.1 collective-permute-start.8
  30.2 2.8 %collective-permute-done.12.m2 = bf16[27,32,128]{2,1,0:T(8,128)(2,1)S(1)} collective-permute-done((bf16[27,32,128]{2,1,0:T(8,128)(2,1)S(1)}, bf16[27,32,128]{2,1,0:T(8,128)(2,1)S(1)}, u32[]{:S(2)}, u32[]{:S(2)}) %collective-permute-start.12) | collective-permute-done | bytes 221216 | tf_op jit(solution)/shard_map/ppermute | solution.py:41
  33.0 0.0 collective-permute-start.13
  33.0 0.0 collective-permute-done.11.m1
  33.0 0.0 collective-permute-start.20
  33.1 0.7 collective-permute-start.10
  33.7 0.7 collective-permute-done.15.l2
  34.4 2.5 %collective-permute-start.16 = (bf16[27,32,128]{2,1,0:T(8,128)(2,1)S(1)}, bf16[27,32,128]{2,1,0:T(8,128)(2,1)S(1)}, u32[]{:S(2)}, u32[]{:S(2)}) collective-permute-start(bf16[27,32,128]{2,1,0:T(8,128)(2,1)S(1)} %collective-permute-done.15.l2), channel_id=1, source_target_pairs={{0,1},{1,0},{2,3},{3,2},{4,5},{5,4},{6,7},{7,6},{8,9},{9,8},{10,11... | collective-permute-start | bytes 663560 | tf_op jit(solution)/shard_map/ppermute | solution.py:41
  36.9 2.0 %collective-permute-done.20.pair = bf16[2,256,128]{2,1,0:T(8,128)(2,1)S(1)} collective-permute-done((bf16[2,256,128]{2,1,0:T(8,128)(2,1)S(1)}, bf16[2,256,128]{2,1,0:T(8,128)(2,1)S(1)}, u32[]{:S(2)}, u32[]{:S(2)}) %collective-permute-start.20) | collective-permute-done | bytes 131104 | tf_op jit(solution)/shard_map/ppermute | solution.py:41
  39.0 0.7 collective-permute-start.9
  39.6 0.6 shard_map.91
  40.3 0.0 collective-permute-done.13.m3
  40.3 3.2 %collective-permute-start.21 = (bf16[6,256,128]{2,1,0:T(8,128)(2,1)S(1)}, bf16[6,256,128]{2,1,0:T(8,128)(2,1)S(1)}, u32[]{:S(2)}, u32[]{:S(2)}) collective-permute-start(bf16[6,256,128]{2,1,0:T(8,128)(2,1)S(1)} %get-tuple-element.44), channel_id=1, source_target_pairs={{0,1},{1,0},{2,3},{3,2},{4,5},{5,4},{6,7},{7,6},{8,9},{9,8},{10,11... | collective-permute-start | bytes 1179656 | tf_op jit(solution)/shard_map/ppermute | solution.py:41
  43.4 0.0 collective-permute-done.16.l3
  43.4 0.7 collective-permute-start.22
  44.1 1.2 %shard_map.86 = (bf16[384,1152]{1,0:T(8,128)(2,1)S(1)}, bf16[384,1152]{1,0:T(8,128)(2,1)S(1)}, bf16[1152,384]{1,0:T(8,128)(2,1)S(1)}, bf16[1152,384]{1,0:T(8,128)(2,1)S(1)}) custom-call(s32[5]{0:T(128)S(1)} %stack.22.info, bf16[27,32,128]{2,1,0:T(8,128)(2,1)S(1)} %copy-done, bf16[27,32,128]{2,1,0:T(8,128)(2,1)S(1)} %collective-permute-done.11.m1, ...), custom_call_target="tpu_custom_call" | custom-call | flops 1000000 | bytes 6000000 | tf_op jit(solution)/shard_map/pallas_call | solution.py:366
  45.3 0.0 collective-permute-done.9
  45.3 0.7 collective-permute-start.23
  46.0 0.0 collective-permute-done.8
  46.0 4.0 %shard_map.87 = (bf16[4,4,128,128]{3,2,1,0:T(8,128)(2,1)S(1)}, f32[4,4,128,128]{3,2,1,0:T(8,128)S(1)}, bf16[6,6,128,128]{3,2,1,0:T(8,128)(2,1)S(1)}) custom-call(s32[5]{0:T(128)S(1)} %stack.22.info, bf16[6,2,128,128]{3,2,1,0:T(8,128)(2,1)S(1)} %bitcast.28, bf16[6,2,128,128]{3,2,1,0:T(8,128)(2,1)S(1)} %bitcast.29, bf16[2,2,128,128]{3,2,1,0:T(8,128)(2,1)S(1)} %bitcast.35, ...), custom_call_target="tpu_custom_call" | custom-call | flops 3000000000 | bytes 4000000 | tf_op jit(solution)/shard_map/pallas_call | solution.py:375
  50.0 1.3 %shard_map.90 = (bf16[2,27,32,128]{3,2,1,0:T(8,128)(2,1)S(1)}, bf16[2,27,32,128]{3,2,1,0:T(8,128)(2,1)S(1)}) custom-call(s32[5]{0:T(128)S(1)} %stack.22.info, bf16[4,4,128,128]{3,2,1,0:T(8,128)(2,1)S(1)} %get-tuple-element.35.act_ref.mid_act, bf16[2,2,128,128]{3,2,1,0:T(8,128)(2,1)S(1)} %get-tuple-element.39.cot_own), custom_call_target="tpu_custom_call" | custom-call | flops 500000000 | bytes 3000000 | tf_op jit(solution)/shard_map/pallas_call | solution.py:396
  51.3 4.5 %collective-permute-start.19 = (bf16[2,27,32,128]{3,2,1,0:T(8,128)(2,1)S(1)}, bf16[2,27,32,128]{3,2,1,0:T(8,128)(2,1)S(1)}, u32[]{:S(2)}, u32[]{:S(2)}) collective-permute-start(bf16[2,27,32,128]{3,2,1,0:T(8,128)(2,1)S(1)} %get-tuple-element.41), channel_id=1, source_target_pairs={{0,1},{1,0},{2,3},{3,2},{4,5},{5,4},{6,7},{7,6},{8,9},{9,8},{10,11... | collective-permute-start | bytes 1327112 | tf_op jit(solution)/shard_map/ppermute | solution.py:41
  55.8 0.0 collective-permute-done.22
  55.8 0.0 collective-permute-done.23
  55.8 6.1 %shard_map.92 = (bf16[2,37,32,128]{3,2,1,0:T(8,128)(2,1)S(1)}, bf16[2,37,32,128]{3,2,1,0:T(8,128)(2,1)S(1)}) custom-call(s32[5]{0:T(128)S(1)} %stack.22.info, bf16[6,6,128,128]{3,2,1,0:T(8,128)(2,1)S(1)} %get-tuple-element.42.act_window, bf16[6,2,128,128]{3,2,1,0:T(8,128)(2,1)S(1)} %bitcast.30, bf16[6,2,128,128]{3,2,1,0:T(8,128)(2,1)S(1)} %bitcast.31, ...), custom_call_target="tpu_custom_call" | custom-call | flops 4000000000 | bytes 8000000 | tf_op jit(solution)/shard_map/pallas_call | solution.py:406
  61.9 0.1 collective-permute-start.24
  62.0 0.1 add_convert_fusion.1
  62.1 1.9 %collective-permute-done.24 = bf16[2,37,32,128]{3,2,1,0:T(8,128)(2,1)S(1)} collective-permute-done((bf16[2,37,32,128]{3,2,1,0:T(8,128)(2,1)S(1)}, bf16[2,37,32,128]{3,2,1,0:T(8,128)(2,1)S(1)}, u32[]{:S(2)}, u32[]{:S(2)}) %collective-permute-start.24) | collective-permute-done | bytes 606240 | tf_op jit(solution)/shard_map/ppermute | solution.py:41
  64.0 0.2 add_convert_fusion
  64.1 0.1 pad_maximum_fusion
  64.2 27.2 %all_to_all.10.terms_ref = bf16[64,64,128]{2,1,0:T(8,128)(2,1)S(1)} all-to-all(bf16[64,64,128]{2,1,0:T(8,128)(2,1)S(1)} %bitcast.36), channel_id=1, replica_groups=mesh['depth'=32,'chip'=2,'core'=2] {'chip','depth'}, dimensions={0} | all-to-all | bytes 2097152 | tf_op jit(solution)/shard_map/all_to_all | solution.py:435
  91.4 1.0 shard_map.93
  92.4 4.5 %all-to-all-start.1 = ((bf16[32,64,128]{2,1,0:T(8,128)(2,1)}), bf16[32,64,128]{2,1,0:T(8,128)(2,1)S(1)}, u32[]{:S(2)}, u32[]{:S(2)}) async-start(bf16[32,64,128]{2,1,0:T(8,128)(2,1)} %shard_map.93), calls=%async_computation.1 | async-start | bytes 1048576 | tf_op jit(solution)/shard_map/all_to_all | solution.py:437
  97.0 1.5 %shard_map.88 = (bf16[2,2,2,32,128]{4,3,2,1,0:T(8,128)(2,1)S(1)}, bf16[2,2,2,32,128]{4,3,2,1,0:T(8,128)(2,1)S(1)}) custom-call(s32[5]{0:T(128)S(1)} %stack.22.info, bf16[4,4,128,128]{3,2,1,0:T(8,128)(2,1)S(1)} %get-tuple-element.35.act_ref.mid_act, bf16[384,1152]{1,0:T(8,128)(2,1)S(1)} %get-tuple-element.36.weights), custom_call_target="tpu_custom_call" | custom-call | flops 500000000 | bytes 2000000 | tf_op jit(solution)/shard_map/pallas_call | solution.py:384
  98.4 0.1 collective-permute-start.17
  98.5 1.2 %collective-permute-done.17.near = bf16[2,2,2,32,128]{4,3,2,1,0:T(8,128)(2,1)S(1)} collective-permute-done((bf16[2,2,2,32,128]{4,3,2,1,0:T(8,128)(2,1)S(1)}, bf16[2,2,2,32,128]{4,3,2,1,0:T(8,128)(2,1)S(1)}, u32[]{:S(2)}, u32[]{:S(2)}) %collective-permute-start.17) | collective-permute-done | bytes 65568 | tf_op jit(solution)/shard_map/ppermute | solution.py:41
  99.8 1.3 %collective-permute-start.18 = (bf16[2,2,2,32,128]{4,3,2,1,0:T(8,128)(2,1)S(1)}, bf16[2,2,2,32,128]{4,3,2,1,0:T(8,128)(2,1)S(1)}, u32[]{:S(2)}, u32[]{:S(2)}) collective-permute-start(bf16[2,2,2,32,128]{4,3,2,1,0:T(8,128)(2,1)S(1)} %pad_maximum_fusion.1), channel_id=1, source_target_pairs={{0,2},{1,3},{2,0},{3,1},{4,6},{5,7},{6,4},{7,5},{8,10},{9,11},{10,... | collective-permute-start | bytes 196616 | tf_op jit(solution)/shard_map/ppermute | solution.py:41
  101.1 6.1 %collective-permute-done.18.far = bf16[2,2,2,32,128]{4,3,2,1,0:T(8,128)(2,1)S(1)} collective-permute-done((bf16[2,2,2,32,128]{4,3,2,1,0:T(8,128)(2,1)S(1)}, bf16[2,2,2,32,128]{4,3,2,1,0:T(8,128)(2,1)S(1)}, u32[]{:S(2)}, u32[]{:S(2)}) %collective-permute-start.18) | collective-permute-done | bytes 65568 | tf_op jit(solution)/shard_map/ppermute | solution.py:41
  107.2 0.6 shard_map.89
  107.8 0.7 copy.14
  108.5 1.3 %all-to-all-done.1 = bf16[32,64,128]{2,1,0:T(8,128)(2,1)S(1)} async-done(((bf16[32,64,128]{2,1,0:T(8,128)(2,1)}), bf16[32,64,128]{2,1,0:T(8,128)(2,1)S(1)}, u32[]{:S(2)}, u32[]{:S(2)}) %all-to-all-start.1) | async-done | bytes 524320 | tf_op jit(solution)/shard_map/all_to_all | solution.py:437
  109.8 1.0 shard_map.94
  (17 shorter events, 0.1 us)
Async XLA Ops:
  0.6 12.7 %copy-start.2 = (bf16[8,32,64]{2,1,0:T(8,128)(2,1)S(1)}, bf16[8,32,64]{2,1,0:T(8,128)(2,1)}, u32[]{:S(2)}) copy-start(bf16[8,32,64]{2,1,0:T(8,128)(2,1)} %s0.1) | copy-start | bytes 98308
  1.6 5.6 %collective-permute-start.4 = (bf16[4,2,2,32,128]{4,3,2,1,0:T(8,128)(2,1)S(1)}, bf16[4,2,2,32,128]{4,3,2,1,0:T(8,128)(2,1)S(1)}, u32[]{:S(2)}, u32[]{:S(2)}) collective-permute-start(bf16[4,2,2,32,128]{4,3,2,1,0:T(8,128)(2,1)S(1)} %bitcast.24), channel_id=1, source_target_pairs={{0,2},{1,3},{2,0},{3,1},{4,6},{5,7},{6,4},{7,5},{8,10},{9,11},{10,... | collective-permute-start | bytes 393224 | tf_op jit(solution)/shard_map/ppermute | solution.py:41
  3.7 9.6 %collective-permute-start.3 = (bf16[4,2,2,32,128]{4,3,2,1,0:T(8,128)(2,1)S(1)}, bf16[4,2,2,32,128]{4,3,2,1,0:T(8,128)(2,1)S(1)}, u32[]{:S(2)}, u32[]{:S(2)}) collective-permute-start(bf16[4,2,2,32,128]{4,3,2,1,0:T(8,128)(2,1)S(1)} %bitcast.25), channel_id=1, source_target_pairs={{0,1},{1,0},{2,3},{3,2},{4,5},{5,4},{6,7},{7,6},{8,9},{9,8},{10,11... | collective-permute-start | bytes 393224 | tf_op jit(solution)/shard_map/ppermute | solution.py:41
  7.2 6.1 %collective-permute-start.5 = (bf16[4,2,2,32,128]{4,3,2,1,0:T(8,128)(2,1)S(1)}, bf16[4,2,2,32,128]{4,3,2,1,0:T(8,128)(2,1)S(1)}, u32[]{:S(2)}, u32[]{:S(2)}) collective-permute-start(bf16[4,2,2,32,128]{4,3,2,1,0:T(8,128)(2,1)S(1)} %collective-permute-done.4.c2), channel_id=1, source_target_pairs={{0,1},{1,0},{2,3},{3,2},{4,5},{5,4},{6,7},{7,6},{8,9},{9,8},{10,11... | collective-permute-start | bytes 393224 | tf_op jit(solution)/shard_map/ppermute | solution.py:41
  7.2 4.7 %collective-permute-start.1 = (bf16[8,32,64]{2,1,0:T(8,128)(2,1)}, bf16[8,32,64]{2,1,0:T(8,128)(2,1)S(1)}, u32[]{:S(2)}, u32[]{:S(2)}) collective-permute-start(bf16[8,32,64]{2,1,0:T(8,128)(2,1)} %s0.1), channel_id=1, source_target_pairs={{0,2},{1,3},{2,0},{3,1},{4,6},{5,7},{6,4},{7,5},{8,10},{9,11},{10,... | collective-permute-start | bytes 98312 | tf_op jit(solution)/shard_map/ppermute | solution.py:41
  9.0 4.3 %collective-permute-start = (bf16[8,32,64]{2,1,0:T(8,128)(2,1)}, bf16[8,32,64]{2,1,0:T(8,128)(2,1)S(1)}, u32[]{:S(2)}, u32[]{:S(2)}) collective-permute-start(bf16[8,32,64]{2,1,0:T(8,128)(2,1)} %s0.1), channel_id=1, source_target_pairs={{0,1},{1,0},{2,3},{3,2},{4,5},{5,4},{6,7},{7,6},{8,9},{9,8},{10,11... | collective-permute-start | bytes 98312 | tf_op jit(solution)/shard_map/ppermute | solution.py:41
  11.9 1.4 %collective-permute-start.2 = (bf16[8,32,64]{2,1,0:T(8,128)(2,1)S(1)}, bf16[8,32,64]{2,1,0:T(8,128)(2,1)S(1)}, u32[]{:S(2)}, u32[]{:S(2)}) collective-permute-start(bf16[8,32,64]{2,1,0:T(8,128)(2,1)S(1)} %collective-permute-done.1.s2), channel_id=1, source_target_pairs={{0,1},{1,0},{2,3},{3,2},{4,5},{5,4},{6,7},{7,6},{8,9},{9,8},{10,11... | collective-permute-start | bytes 98312 | tf_op jit(solution)/shard_map/ppermute | solution.py:41
  11.9 8.2 %copy-start = (bf16[27,32,128]{2,1,0:T(8,128)(2,1)S(1)}, bf16[27,32,128]{2,1,0:T(8,128)(2,1)}, u32[]{:S(2)}) copy-start(bf16[27,32,128]{2,1,0:T(8,128)(2,1)} %m0.1) | copy-start | bytes 663556
  11.9 9.9 %copy-start.1 = (bf16[27,32,128]{2,1,0:T(8,128)(2,1)S(1)}, bf16[27,32,128]{2,1,0:T(8,128)(2,1)}, u32[]{:S(2)}) copy-start(bf16[27,32,128]{2,1,0:T(8,128)(2,1)} %l0.1) | copy-start | bytes 663556
  15.0 14.5 %collective-permute-start.7 = (bf16[2,512,128]{2,1,0:T(8,128)(2,1)S(1)}, bf16[2,512,128]{2,1,0:T(8,128)(2,1)S(1)}, u32[]{:S(2)}, u32[]{:S(2)}) collective-permute-start(bf16[2,512,128]{2,1,0:T(8,128)(2,1)S(1)} %get-tuple-element.31), channel_id=1, source_target_pairs={{4,8},{5,9},{6,10},{7,11},{8,4},{9,5},{10,6},{11,7},{12,16},{13,17... | collective-permute-start | bytes 786440 | tf_op jit(solution)/shard_map/ppermute | solution.py:41
  15.7 8.4 %collective-permute-start.6 = (bf16[2,256,128]{2,1,0:T(8,128)(2,1)S(1)}, bf16[2,256,128]{2,1,0:T(8,128)(2,1)S(1)}, u32[]{:S(2)}, u32[]{:S(2)}) collective-permute-start(bf16[2,256,128]{2,1,0:T(8,128)(2,1)S(1)} %get-tuple-element.30.own), channel_id=1, source_target_pairs={{0,4},{1,5},{2,6},{3,7},{4,0},{5,1},{6,2},{7,3},{8,12},{9,13},{10,... | collective-permute-start | bytes 393224 | tf_op jit(solution)/shard_map/ppermute | solution.py:41
  20.1 12.9 %collective-permute-start.12 = (bf16[27,32,128]{2,1,0:T(8,128)(2,1)S(1)}, bf16[27,32,128]{2,1,0:T(8,128)(2,1)S(1)}, u32[]{:S(2)}, u32[]{:S(2)}) collective-permute-start(bf16[27,32,128]{2,1,0:T(8,128)(2,1)S(1)} %copy-done), channel_id=1, source_target_pairs={{0,2},{1,3},{2,0},{3,1},{4,6},{5,7},{6,4},{7,5},{8,10},{9,11},{10,... | collective-permute-start | bytes 663560 | tf_op jit(solution)/shard_map/ppermute | solution.py:41
  21.9 11.2 %collective-permute-start.11 = (bf16[27,32,128]{2,1,0:T(8,128)(2,1)S(1)}, bf16[27,32,128]{2,1,0:T(8,128)(2,1)S(1)}, u32[]{:S(2)}, u32[]{:S(2)}) collective-permute-start(bf16[27,32,128]{2,1,0:T(8,128)(2,1)S(1)} %copy-done), channel_id=1, source_target_pairs={{0,1},{1,0},{2,3},{3,2},{4,5},{5,4},{6,7},{7,6},{8,9},{9,8},{10,11... | collective-permute-start | bytes 663560 | tf_op jit(solution)/shard_map/ppermute | solution.py:41
  21.9 11.2 %collective-permute-start.14 = (bf16[27,32,128]{2,1,0:T(8,128)(2,1)S(1)}, bf16[27,32,128]{2,1,0:T(8,128)(2,1)S(1)}, u32[]{:S(2)}, u32[]{:S(2)}) collective-permute-start(bf16[27,32,128]{2,1,0:T(8,128)(2,1)S(1)} %copy-done.1), channel_id=1, source_target_pairs={{0,1},{1,0},{2,3},{3,2},{4,5},{5,4},{6,7},{7,6},{8,9},{9,8},{10,11... | collective-permute-start | bytes 663560 | tf_op jit(solution)/shard_map/ppermute | solution.py:41
  24.0 10.4 %collective-permute-start.15 = (bf16[27,32,128]{2,1,0:T(8,128)(2,1)S(1)}, bf16[27,32,128]{2,1,0:T(8,128)(2,1)S(1)}, u32[]{:S(2)}, u32[]{:S(2)}) collective-permute-start(bf16[27,32,128]{2,1,0:T(8,128)(2,1)S(1)} %copy-done.1), channel_id=1, source_target_pairs={{0,18},{1,19},{2,16},{3,17},{4,22},{5,23},{6,20},{7,21},{8,26},{9,... | collective-permute-start | bytes 663560 | tf_op jit(solution)/shard_map/ppermute | solution.py:41
  30.1 15.9 %collective-permute-start.8 = (bf16[6,256,128]{2,1,0:T(8,128)(2,1)S(1)}, bf16[6,256,128]{2,1,0:T(8,128)(2,1)S(1)}, u32[]{:S(2)}, u32[]{:S(2)}) collective-permute-start(bf16[6,256,128]{2,1,0:T(8,128)(2,1)S(1)} %get-tuple-element.32), channel_id=1, source_target_pairs={{0,1},{1,0},{2,3},{3,2},{4,5},{5,4},{6,7},{7,6},{8,9},{9,8},{10,11... | collective-permute-start | bytes 1179656 | tf_op jit(solution)/shard_map/ppermute | solution.py:41
  33.0 7.2 %collective-permute-start.13 = (bf16[27,32,128]{2,1,0:T(8,128)(2,1)S(1)}, bf16[27,32,128]{2,1,0:T(8,128)(2,1)S(1)}, u32[]{:S(2)}, u32[]{:S(2)}) collective-permute-start(bf16[27,32,128]{2,1,0:T(8,128)(2,1)S(1)} %collective-permute-done.12.m2), channel_id=1, source_target_pairs={{0,1},{1,0},{2,3},{3,2},{4,5},{5,4},{6,7},{7,6},{8,9},{9,8},{10,11... | collective-permute-start | bytes 663560 | tf_op jit(solution)/shard_map/ppermute | solution.py:41
  33.0 5.9 %collective-permute-start.20 = (bf16[2,256,128]{2,1,0:T(8,128)(2,1)S(1)}, bf16[2,256,128]{2,1,0:T(8,128)(2,1)S(1)}, u32[]{:S(2)}, u32[]{:S(2)}) collective-permute-start(bf16[2,256,128]{2,1,0:T(8,128)(2,1)S(1)} %get-tuple-element.43.own), channel_id=1, source_target_pairs={{0,4},{1,5},{2,6},{3,7},{4,0},{5,1},{6,2},{7,3},{8,12},{9,13},{10,... | collective-permute-start | bytes 393224 | tf_op jit(solution)/shard_map/ppermute | solution.py:41
  33.1 12.9 %collective-permute-start.10 = (bf16[4,256,128]{2,1,0:T(8,128)(2,1)S(1)}, bf16[4,256,128]{2,1,0:T(8,128)(2,1)S(1)}, u32[]{:S(2)}, u32[]{:S(2)}) collective-permute-start(bf16[4,256,128]{2,1,0:T(8,128)(2,1)S(1)} %get-tuple-element.33), channel_id=1, source_target_pairs={{1,2},{2,1},{5,6},{6,5},{9,10},{10,9},{13,14},{14,13},{17,18},{18,... | collective-permute-start | bytes 786440 | tf_op jit(solution)/shard_map/ppermute | solution.py:41
  34.4 9.0 %collective-permute-start.16 = (bf16[27,32,128]{2,1,0:T(8,128)(2,1)S(1)}, bf16[27,32,128]{2,1,0:T(8,128)(2,1)S(1)}, u32[]{:S(2)}, u32[]{:S(2)}) collective-permute-start(bf16[27,32,128]{2,1,0:T(8,128)(2,1)S(1)} %collective-permute-done.15.l2), channel_id=1, source_target_pairs={{0,1},{1,0},{2,3},{3,2},{4,5},{5,4},{6,7},{7,6},{8,9},{9,8},{10,11... | collective-permute-start | bytes 663560 | tf_op jit(solution)/shard_map/ppermute | solution.py:41
  39.0 6.3 %collective-permute-start.9 = (bf16[2,256,128]{2,1,0:T(8,128)(2,1)S(1)}, bf16[2,256,128]{2,1,0:T(8,128)(2,1)S(1)}, u32[]{:S(2)}, u32[]{:S(2)}) collective-permute-start(bf16[2,256,128]{2,1,0:T(8,128)(2,1)S(1)} %get-tuple-element.30.own), channel_id=1, source_target_pairs={{1,2},{2,1},{5,6},{6,5},{9,10},{10,9},{13,14},{14,13},{17,18},{18,... | collective-permute-start | bytes 393224 | tf_op jit(solution)/shard_map/ppermute | solution.py:41
  40.3 15.5 %collective-permute-start.21 = (bf16[6,256,128]{2,1,0:T(8,128)(2,1)S(1)}, bf16[6,256,128]{2,1,0:T(8,128)(2,1)S(1)}, u32[]{:S(2)}, u32[]{:S(2)}) collective-permute-start(bf16[6,256,128]{2,1,0:T(8,128)(2,1)S(1)} %get-tuple-element.44), channel_id=1, source_target_pairs={{0,1},{1,0},{2,3},{3,2},{4,5},{5,4},{6,7},{7,6},{8,9},{9,8},{10,11... | collective-permute-start | bytes 1179656 | tf_op jit(solution)/shard_map/ppermute | solution.py:41
  43.4 12.3 %collective-permute-start.22 = (bf16[2,256,128]{2,1,0:T(8,128)(2,1)S(1)}, bf16[2,256,128]{2,1,0:T(8,128)(2,1)S(1)}, u32[]{:S(2)}, u32[]{:S(2)}) collective-permute-start(bf16[2,256,128]{2,1,0:T(8,128)(2,1)S(1)} %get-tuple-element.43.own), channel_id=1, source_target_pairs={{1,2},{2,1},{5,6},{6,5},{9,10},{10,9},{13,14},{14,13},{17,18},{18,... | collective-permute-start | bytes 393224 | tf_op jit(solution)/shard_map/ppermute | solution.py:41
  45.3 10.5 %collective-permute-start.23 = (bf16[4,256,128]{2,1,0:T(8,128)(2,1)S(1)}, bf16[4,256,128]{2,1,0:T(8,128)(2,1)S(1)}, u32[]{:S(2)}, u32[]{:S(2)}) collective-permute-start(bf16[4,256,128]{2,1,0:T(8,128)(2,1)S(1)} %get-tuple-element.45), channel_id=1, source_target_pairs={{1,2},{2,1},{5,6},{6,5},{9,10},{10,9},{13,14},{14,13},{17,18},{18,... | collective-permute-start | bytes 786440 | tf_op jit(solution)/shard_map/ppermute | solution.py:41
  51.3 10.7 %collective-permute-start.19 = (bf16[2,27,32,128]{3,2,1,0:T(8,128)(2,1)S(1)}, bf16[2,27,32,128]{3,2,1,0:T(8,128)(2,1)S(1)}, u32[]{:S(2)}, u32[]{:S(2)}) collective-permute-start(bf16[2,27,32,128]{3,2,1,0:T(8,128)(2,1)S(1)} %get-tuple-element.41), channel_id=1, source_target_pairs={{0,1},{1,0},{2,3},{3,2},{4,5},{5,4},{6,7},{7,6},{8,9},{9,8},{10,11... | collective-permute-start | bytes 1327112 | tf_op jit(solution)/shard_map/ppermute | solution.py:41
  61.9 2.1 %collective-permute-start.24 = (bf16[2,37,32,128]{3,2,1,0:T(8,128)(2,1)S(1)}, bf16[2,37,32,128]{3,2,1,0:T(8,128)(2,1)S(1)}, u32[]{:S(2)}, u32[]{:S(2)}) collective-permute-start(bf16[2,37,32,128]{3,2,1,0:T(8,128)(2,1)S(1)} %get-tuple-element.52), channel_id=1, source_target_pairs={{0,1},{1,0},{2,3},{3,2},{4,5},{5,4},{6,7},{7,6},{8,9},{9,8},{10,11... | collective-permute-start | bytes 1818632 | tf_op jit(solution)/shard_map/ppermute | solution.py:41
  92.4 17.4 %all-to-all-start.1 = ((bf16[32,64,128]{2,1,0:T(8,128)(2,1)}), bf16[32,64,128]{2,1,0:T(8,128)(2,1)S(1)}, u32[]{:S(2)}, u32[]{:S(2)}) async-start(bf16[32,64,128]{2,1,0:T(8,128)(2,1)} %shard_map.93), calls=%async_computation.1 | async-start | bytes 1048576 | tf_op jit(solution)/shard_map/all_to_all | solution.py:437
  98.4 1.3 %collective-permute-start.17 = (bf16[2,2,2,32,128]{4,3,2,1,0:T(8,128)(2,1)S(1)}, bf16[2,2,2,32,128]{4,3,2,1,0:T(8,128)(2,1)S(1)}, u32[]{:S(2)}, u32[]{:S(2)}) collective-permute-start(bf16[2,2,2,32,128]{4,3,2,1,0:T(8,128)(2,1)S(1)} %get-tuple-element.38), channel_id=1, source_target_pairs={{0,1},{1,0},{2,3},{3,2},{4,5},{5,4},{6,7},{7,6},{8,9},{9,8},{10,11... | collective-permute-start | bytes 196616 | tf_op jit(solution)/shard_map/ppermute | solution.py:41
  99.8 7.4 %collective-permute-start.18 = (bf16[2,2,2,32,128]{4,3,2,1,0:T(8,128)(2,1)S(1)}, bf16[2,2,2,32,128]{4,3,2,1,0:T(8,128)(2,1)S(1)}, u32[]{:S(2)}, u32[]{:S(2)}) collective-permute-start(bf16[2,2,2,32,128]{4,3,2,1,0:T(8,128)(2,1)S(1)} %pad_maximum_fusion.1), channel_id=1, source_target_pairs={{0,2},{1,3},{2,0},{3,1},{4,6},{5,7},{6,4},{7,5},{8,10},{9,11},{10,... | collective-permute-start | bytes 196616 | tf_op jit(solution)/shard_map/ppermute | solution.py:41

commit v12 on v10

--- a/solution.py
+++ b/solution.py
@@ -118,17 +118,25 @@
             pack_ref[p, 256 + r * 128 : 384 + r * 128] = cot
 
 
-def join_body(first, info, own, pair, beyond, column_ref):
+def join_body(first, info, own, pair, beyond, column_ref, *halo):
     odd = info[0] & 1
     column_ref[2:4] = own[...]
     column_ref[pl.ds(4 - 4 * odd, 2)] = pair[...]
     column_ref[pl.ds(4 * odd, 2)] = beyond[:, first : first + 256]
+    for halo_ref in halo:
+        halo_ref[pl.ds(2 - 2 * odd, 2)] = pair[...]
+        halo_ref[pl.ds(2 * odd, 2)] = beyond[:, first : first + 256]
 
 
 def fill_window(window, middle, near, cross, core):
     window[:, 2:4] = middle[...]
     window[:, pl.ds(4 - 4 * core, 2)] = near[...]
-    window[:, pl.ds(4 * core, 2)] = cross[...]
+    if len(cross) == 1:
+        window[:, pl.ds(4 * core, 2)] = cross[0][...]
+    else:
+        window[0:2, pl.ds(4 * core, 2)] = cross[1][0:2]
+        window[2:4, pl.ds(4 * core, 2)] = cross[0][...]
+        window[4:6, pl.ds(4 * core, 2)] = cross[1][2:4]
 
 
 def fill_forward(weights, parts, filt):
@@ -198,8 +206,8 @@
     return valid & (plane <= last) & (row <= jnp.where(filt == 3, 2, 3))
 
 
-def middle_body(info, mid, near, cross, weights, act_ref, pre_ref, window):
-    fill_window(window, mid, near, cross, info[4])
+def middle_body(info, mid, near, cross, halo, weights, act_ref, pre_ref, window):
+    fill_window(window, mid, near, (cross, halo), info[4])
 
     pre = conv_forward(window, 0, 4, 0, 4, weights)
     act = jnp.where(inside(info), pre * jax.nn.sigmoid(pre), 0.0)
@@ -264,7 +272,7 @@
 ):
     core = info[4]
     refs = (keep_ref, send_ref)
-    fill_window(window, mid, near, cross, core)
+    fill_window(window, mid, near, (cross,), core)
 
     back = conv_backward(window, 0, 4, 0, 4, weights_l)
     here = jnp.where(inside(info), back * silu_slope(mid_pre[...].reshape(16 * CELLS, 128)), 0.0)
@@ -311,20 +319,21 @@
             out_ref[d, at : at + 16] = total
 
 
-def neighbourhood(info, own, beyond, first):
+def neighbourhood(info, own, beyond, first, split):
     def inner(d, f):
         return (d, 3 - f) if f in (1, 2) else (-1, f)
 
     pair = shifted(own, lambda d, f: (d ^ 1, f))
-    column = call(
+    cross = [shifted(own, inner)] if split else []
+    column, *halo = call(
         "join",
         functools.partial(join_body, first),
-        shape((6, 256, 128)),
+        [shape((6, 256, 128))] + [shape((4, 256, 128))] * split,
         in_specs=[SMEM] + [VMEM] * 3,
     )(info, own, pair, beyond)
-    cross = shifted(column, inner)
+    cross += [shifted(halo[0] if split else column, inner)]
     near = swap_core(column)
-    return [x.reshape(6, 2, 128, 128) for x in (column, near, cross)]
+    return [x.reshape(x.shape[0], 2, 128, 128) for x in (column, near, *cross)]
 
 
 def whole(upper_level, stride_weight, middle_weight, last_weight, cotangent):
@@ -355,8 +364,8 @@
         in_specs=[SMEM] + [VMEM] * 9,
     )(info, upper, *stride_parts, *cot_parts)
     beyond = shifted(pack, lambda d, f: (d + 1 if d % 2 else d - 1, f))
-    act_parts = neighbourhood(info, level_act, beyond, 0)
-    back_parts = neighbourhood(info, cot_cells, beyond, 256)
+    act_parts = neighbourhood(info, level_act, beyond, 0, True)
+    back_parts = neighbourhood(info, cot_cells, beyond, 256, False)
 
     forward_m, forward_l, backward_l, backward_m = call(
         "weights",
@@ -373,7 +382,7 @@
         [shape((4, 4, 128, 128)), shape((4, 4, 128, 128), jnp.float32), shape((6, 6, 128, 128))],
         flops=3_000_000_000,
         moved=4_000_000,
-        in_specs=[SMEM] + [VMEM] * 4,
+        in_specs=[SMEM] + [VMEM] * 5,
     )(info, *act_parts, forward_m)
 
     stay, leave = call(

time: 107 us -> 110 us (1.028)
  waiting for transfers between devices: 22.7 us -> 30.9 us
  blocking collectives: 32.6 us -> 28.3 us
  starting transfers between devices: 28.1 us -> 26.5 us
    ppermute x23 -> x24, waiting for transfers between devices: 21.4 us -> 29.3 us  [shifted(): return lax.ppermute(value, AXES, pairs_of(move))]
    all_to_all x1, blocking collectives: 32.6 us -> 28.3 us  [whole(): lax.all_to_all(terms.reshape(2 * depth, 64, 128), ('chip', 'depth'), 0, 0...]
    ppermute x23 -> x24, starting transfers between devices: 23.6 us -> 21.7 us  [shifted(): return lax.ppermute(value, AXES, pairs_of(move))]
  transfers between devices with their start and end apart: 24 -> 25, of which waited for: 9 -> 9; matrix products, arithmetic and copies ran while one was open for 2% -> 2% of each run, Pallas kernels for 15% -> 14%
where the time goes in v12:
time: 110 us; the launch traced here: 109 us
  waiting for transfers between devices  30.9 us (28%)
  blocking collectives  28.3 us (26%)
  starting transfers between devices  26.5 us (24%)
  Pallas kernels  19.3 us (18%)
  local copies, waits for them, and re-layouts  3.05 us (3%)
    ppermute x24, waiting for transfers between devices, shifted(): return lax.ppermute(value, AXES, pairs_of(move))  29.3 us
    all_to_all x1, blocking collectives, whole(): lax.all_to_all(terms.reshape(2 * depth, 64, 128), ('chip', 'depth'), 0, 0...  28.3 us
    ppermute x24, starting transfers between devices, shifted(): return lax.ppermute(value, AXES, pairs_of(move))  21.7 us
    pallas_call x1, Pallas kernels, whole(): call('back', back_body, [shape((2, 37, 32, 128))] * 2, [pltpu.VMEM((6, 6,...  6.06 us
    all_to_all x1, starting transfers between devices, whole(): full = lax.all_to_all(spread, 'depth', 0, 0, tiled=True)  4.78 us
    pallas_call x1, Pallas kernels, whole(): call('middle', middle_body, [shape((4, 4, 128, 128)), shape((4, 4, 128, 1...  3.99 us
    unnamed x9, local copies, waits for them, and re-layouts  2.95 us
  transfers between devices with their start and end apart: 25, of which 9 were waited for; matrix products, arithmetic and copies ran while one was open for 2% of the time, Pallas kernels for 14%

profile of v12, /device:TPU:0, one launch (start us, length us, event | category | flops | bytes accessed | tf_op | source)
XLA Modules:
  0.0 109.3 jit_solution(764361880789014025)
XLA Ops:
  0.6 0.0 copy-start.2
  0.6 1.0 copy.12
  1.6 2.1 %collective-permute-start.4 = (bf16[4,2,2,32,128]{4,3,2,1,0:T(8,128)(2,1)S(1)}, bf16[4,2,2,32,128]{4,3,2,1,0:T(8,128)(2,1)S(1)}, u32[]{:S(2)}, u32[]{:S(2)}) collective-permute-start(bf16[4,2,2,32,128]{4,3,2,1,0:T(8,128)(2,1)S(1)} %bitcast.23), channel_id=1, source_target_pairs={{0,2},{1,3},{2,0},{3,1},{4,6},{5,7},{6,4},{7,5},{8,10},{9,11},{10,... | collective-permute-start | bytes 393224 | tf_op jit(solution)/shard_map/ppermute | solution.py:41
  3.7 0.0 collective-permute-start.3
  3.7 3.5 %collective-permute-done.4.c2 = bf16[4,2,2,32,128]{4,3,2,1,0:T(8,128)(2,1)S(1)} collective-permute-done((bf16[4,2,2,32,128]{4,3,2,1,0:T(8,128)(2,1)S(1)}, bf16[4,2,2,32,128]{4,3,2,1,0:T(8,128)(2,1)S(1)}, u32[]{:S(2)}, u32[]{:S(2)}) %collective-permute-start.4) | collective-permute-done | bytes 131104 | tf_op jit(solution)/shard_map/ppermute | solution.py:41
  7.2 0.0 collective-permute-start.5
  7.2 1.7 %collective-permute-start.1 = (bf16[8,32,64]{2,1,0:T(8,128)(2,1)}, bf16[8,32,64]{2,1,0:T(8,128)(2,1)S(1)}, u32[]{:S(2)}, u32[]{:S(2)}) collective-permute-start(bf16[8,32,64]{2,1,0:T(8,128)(2,1)} %s0.1), channel_id=1, source_target_pairs={{0,2},{1,3},{2,0},{3,1},{4,6},{5,7},{6,4},{7,5},{8,10},{9,11},{10,... | collective-permute-start | bytes 98312 | tf_op jit(solution)/shard_map/ppermute | solution.py:41
  9.0 0.2 collective-permute-start
  9.2 2.7 %collective-permute-done.1.s2 = bf16[8,32,64]{2,1,0:T(8,128)(2,1)S(1)} collective-permute-done((bf16[8,32,64]{2,1,0:T(8,128)(2,1)}, bf16[8,32,64]{2,1,0:T(8,128)(2,1)S(1)}, u32[]{:S(2)}, u32[]{:S(2)}) %collective-permute-start.1) | collective-permute-done | bytes 32800 | tf_op jit(solution)/shard_map/ppermute | solution.py:41
  11.9 0.0 collective-permute-start.2
  11.9 1.3 %copy.16 = bf16[64,4,4,256]{3,0,2,1:T(8,128)(2,1)S(1)} copy(bf16[64,4,4,256]{3,2,1,0:T(4,128)(2,1)} %param.5) | data formatting | bytes 1048576 | tf_op args[0]
  13.2 0.1 stack.22.info
  13.3 0.0 collective-permute-done.s1
  13.3 0.0 collective-permute-done.2.s3
  13.3 0.0 collective-permute-done.3.c1
  13.3 0.0 collective-permute-done.5.c3
  13.3 1.6 %shard_map.84 = (bf16[2,256,128]{2,1,0:T(8,128)(2,1)S(1)}, f32[2,2,128,128]{3,2,1,0:T(8,128)S(1)}, bf16[512,512]{1,0:T(8,128)(2,1)S(1)}, bf16[2,2,128,128]{3,2,1...) custom-call(s32[5]{0:T(128)S(1)} %stack.22.info, ...), custom_call_target="tpu_custom_call" | custom-call | flops 200000000 | bytes 1500000 | tf_op jit(solution)/shard_map/pallas_call | solution.py:350
  15.0 0.7 collective-permute-start.7
  15.7 4.5 %collective-permute-start.6 = (bf16[2,256,128]{2,1,0:T(8,128)(2,1)S(1)}, bf16[2,256,128]{2,1,0:T(8,128)(2,1)S(1)}, u32[]{:S(2)}, u32[]{:S(2)}) collective-permute-start(bf16[2,256,128]{2,1,0:T(8,128)(2,1)S(1)} %get-tuple-element.28.own), channel_id=1, source_target_pairs={{0,4},{1,5},{2,6},{3,7},{4,0},{5,1},{6,2},{7,3},{8,12},{9,13},{10,... | collective-permute-start | bytes 393224 | tf_op jit(solution)/shard_map/ppermute | solution.py:41
  20.1 1.7 %collective-permute-start.12 = (bf16[27,32,128]{2,1,0:T(8,128)(2,1)S(1)}, bf16[27,32,128]{2,1,0:T(8,128)(2,1)S(1)}, u32[]{:S(2)}, u32[]{:S(2)}) collective-permute-start(bf16[27,32,128]{2,1,0:T(8,128)(2,1)S(1)} %copy-done), channel_id=1, source_target_pairs={{0,2},{1,3},{2,0},{3,1},{4,6},{5,7},{6,4},{7,5},{8,10},{9,11},{10,... | collective-permute-start | bytes 663560 | tf_op jit(solution)/shard_map/ppermute | solution.py:41
  21.9 2.5 %collective-permute-start.15 = (bf16[27,32,128]{2,1,0:T(8,128)(2,1)S(1)}, bf16[27,32,128]{2,1,0:T(8,128)(2,1)S(1)}, u32[]{:S(2)}, u32[]{:S(2)}) collective-permute-start(bf16[27,32,128]{2,1,0:T(8,128)(2,1)S(1)} %copy-done.1), channel_id=1, source_target_pairs={{0,18},{1,19},{2,16},{3,17},{4,22},{5,23},{6,20},{7,21},{8,26},{9,... | collective-permute-start | bytes 663560 | tf_op jit(solution)/shard_map/ppermute | solution.py:41
  24.4 0.0 collective-permute-start.11
  24.4 0.0 collective-permute-done.6.pair
  24.4 0.5 collective-permute-start.14
  24.9 0.0 collective-permute-done.7.beyond
  24.9 0.6 shard_map.85
  25.6 0.1 collective-permute-start.8
  25.6 7.4 %collective-permute-done.12.m2 = bf16[27,32,128]{2,1,0:T(8,128)(2,1)S(1)} collective-permute-done((bf16[27,32,128]{2,1,0:T(8,128)(2,1)S(1)}, bf16[27,32,128]{2,1,0:T(8,128)(2,1)S(1)}, u32[]{:S(2)}, u32[]{:S(2)}) %collective-permute-start.12) | collective-permute-done | bytes 221216 | tf_op jit(solution)/shard_map/ppermute | solution.py:41
  33.0 0.0 collective-permute-start.13
  33.0 1.2 %collective-permute-done.15.l2 = bf16[27,32,128]{2,1,0:T(8,128)(2,1)S(1)} collective-permute-done((bf16[27,32,128]{2,1,0:T(8,128)(2,1)S(1)}, bf16[27,32,128]{2,1,0:T(8,128)(2,1)S(1)}, u32[]{:S(2)}, u32[]{:S(2)}) %collective-permute-start.15) | collective-permute-done | bytes 221216 | tf_op jit(solution)/shard_map/ppermute | solution.py:41
  34.2 0.0 collective-permute-start.16
  34.2 0.0 collective-permute-done.11.m1
  34.3 0.7 collective-permute-start.10
  34.9 5.2 %collective-permute-done.20.pair = bf16[2,256,128]{2,1,0:T(8,128)(2,1)S(1)} collective-permute-done((bf16[2,256,128]{2,1,0:T(8,128)(2,1)S(1)}, bf16[2,256,128]{2,1,0:T(8,128)(2,1)S(1)}, u32[]{:S(2)}, u32[]{:S(2)}) %collective-permute-start.20) | collective-permute-done | bytes 131104 | tf_op jit(solution)/shard_map/ppermute | solution.py:41
  40.1 0.7 collective-permute-start.9
  40.8 0.6 shard_map.91
  41.4 2.4 %collective-permute-start.21 = (bf16[6,256,128]{2,1,0:T(8,128)(2,1)S(1)}, bf16[6,256,128]{2,1,0:T(8,128)(2,1)S(1)}, u32[]{:S(2)}, u32[]{:S(2)}) collective-permute-start(bf16[6,256,128]{2,1,0:T(8,128)(2,1)S(1)} %shard_map.91), channel_id=1, source_target_pairs={{0,1},{1,0},{2,3},{3,2},{4,5},{5,4},{6,7},{7,6},{8,9},{9,8},{10,11... | collective-permute-start | bytes 1179656 | tf_op jit(solution)/shard_map/ppermute | solution.py:41
  43.8 0.7 collective-permute-start.22
  44.5 1.2 %shard_map.86 = (bf16[384,1152]{1,0:T(8,128)(2,1)S(1)}, bf16[384,1152]{1,0:T(8,128)(2,1)S(1)}, bf16[1152,384]{1,0:T(8,128)(2,1)S(1)}, bf16[1152,384]{1,0:T(8,128)(2,1)S(1)}) custom-call(s32[5]{0:T(128)S(1)} %stack.22.info, bf16[27,32,128]{2,1,0:T(8,128)(2,1)S(1)} %copy-done, bf16[27,32,128]{2,1,0:T(8,128)(2,1)S(1)} %collective-permute-done.11.m1, ...), custom_call_target="tpu_custom_call" | custom-call | flops 1000000 | bytes 6000000 | tf_op jit(solution)/shard_map/pallas_call | solution.py:370
  45.7 0.0 collective-permute-done.9
  45.7 0.0 collective-permute-done.10
  45.7 4.0 %shard_map.87 = (bf16[4,4,128,128]{3,2,1,0:T(8,128)(2,1)S(1)}, f32[4,4,128,128]{3,2,1,0:T(8,128)S(1)}, bf16[6,6,128,128]{3,2,1,0:T(8,128)(2,1)S(1)}) custom-call(s32[5]{0:T(128)S(1)} %stack.22.info, bf16[6,2,128,128]{3,2,1,0:T(8,128)(2,1)S(1)} %bitcast.28, bf16[6,2,128,128]{3,2,1,0:T(8,128)(2,1)S(1)} %bitcast.29, bf16[2,2,128,128]{3,2,1,0:T(8,128)(2,1)S(1)} %bitcast.33, ...), custom_call_target="tpu_custom_call" | custom-call | flops 3000000000 | bytes 4000000 | tf_op jit(solution)/shard_map/pallas_call | solution.py:379
  49.7 1.3 %shard_map.90 = (bf16[2,27,32,128]{3,2,1,0:T(8,128)(2,1)S(1)}, bf16[2,27,32,128]{3,2,1,0:T(8,128)(2,1)S(1)}) custom-call(s32[5]{0:T(128)S(1)} %stack.22.info, bf16[4,4,128,128]{3,2,1,0:T(8,128)(2,1)S(1)} %get-tuple-element.33.act_ref.mid_act, bf16[2,2,128,128]{3,2,1,0:T(8,128)(2,1)S(1)} %get-tuple-element.37.cot_own), custom_call_target="tpu_custom_call" | custom-call | flops 500000000 | bytes 3000000 | tf_op jit(solution)/shard_map/pallas_call | solution.py:400
  51.0 1.8 %collective-permute-start.19 = (bf16[2,27,32,128]{3,2,1,0:T(8,128)(2,1)S(1)}, bf16[2,27,32,128]{3,2,1,0:T(8,128)(2,1)S(1)}, u32[]{:S(2)}, u32[]{:S(2)}) collective-permute-start(bf16[2,27,32,128]{3,2,1,0:T(8,128)(2,1)S(1)} %get-tuple-element.39), channel_id=1, source_target_pairs={{0,1},{1,0},{2,3},{3,2},{4,5},{5,4},{6,7},{7,6},{8,9},{9,8},{10,11... | collective-permute-start | bytes 1327112 | tf_op jit(solution)/shard_map/ppermute | solution.py:41
  52.8 0.0 collective-permute-done.21
  52.8 6.1 %shard_map.92 = (bf16[2,37,32,128]{3,2,1,0:T(8,128)(2,1)S(1)}, bf16[2,37,32,128]{3,2,1,0:T(8,128)(2,1)S(1)}) custom-call(s32[5]{0:T(128)S(1)} %stack.22.info, bf16[6,6,128,128]{3,2,1,0:T(8,128)(2,1)S(1)} %get-tuple-element.40.act_window, bf16[6,2,128,128]{3,2,1,0:T(8,128)(2,1)S(1)} %bitcast.27, bf16[6,2,128,128]{3,2,1,0:T(8,128)(2,1)S(1)} %bitcast.30, ...), custom_call_target="tpu_custom_call" | custom-call | flops 4000000000 | bytes 8000000 | tf_op jit(solution)/shard_map/pallas_call | solution.py:410
  58.9 0.3 collective-permute-start.23
  59.1 0.0 collective-permute-done.19
  59.1 0.1 add_convert_fusion.1
  59.2 1.7 %collective-permute-done.23 = bf16[2,37,32,128]{3,2,1,0:T(8,128)(2,1)S(1)} collective-permute-done((bf16[2,37,32,128]{3,2,1,0:T(8,128)(2,1)S(1)}, bf16[2,37,32,128]{3,2,1,0:T(8,128)(2,1)S(1)}, u32[]{:S(2)}, u32[]{:S(2)}) %collective-permute-start.23) | collective-permute-done | bytes 606240 | tf_op jit(solution)/shard_map/ppermute | solution.py:41
  61.0 0.2 add_convert_fusion
  61.1 0.1 pad_maximum_fusion
  61.2 28.3 %all_to_all.10.terms_ref = bf16[64,64,128]{2,1,0:T(8,128)(2,1)S(1)} all-to-all(bf16[64,64,128]{2,1,0:T(8,128)(2,1)S(1)} %bitcast.34), channel_id=1, replica_groups=mesh['depth'=32,'chip'=2,'core'=2] {'chip','depth'}, dimensions={0} | all-to-all | bytes 2097152 | tf_op jit(solution)/shard_map/all_to_all | solution.py:439
  89.6 1.0 shard_map.93
  90.5 4.8 %all-to-all-start.1 = ((bf16[32,64,128]{2,1,0:T(8,128)(2,1)}), bf16[32,64,128]{2,1,0:T(8,128)(2,1)S(1)}, u32[]{:S(2)}, u32[]{:S(2)}) async-start(bf16[32,64,128]{2,1,0:T(8,128)(2,1)} %shard_map.93), calls=%async_computation.1 | async-start | bytes 1048576 | tf_op jit(solution)/shard_map/all_to_all | solution.py:441
  95.3 1.5 %shard_map.88 = (bf16[2,2,2,32,128]{4,3,2,1,0:T(8,128)(2,1)S(1)}, bf16[2,2,2,32,128]{4,3,2,1,0:T(8,128)(2,1)S(1)}) custom-call(s32[5]{0:T(128)S(1)} %stack.22.info, bf16[4,4,128,128]{3,2,1,0:T(8,128)(2,1)S(1)} %get-tuple-element.33.act_ref.mid_act, bf16[384,1152]{1,0:T(8,128)(2,1)S(1)} %get-tuple-element.34.weights), custom_call_target="tpu_custom_call" | custom-call | flops 500000000 | bytes 2000000 | tf_op jit(solution)/shard_map/pallas_call | solution.py:388
  96.8 0.1 collective-permute-start.17
  96.9 1.2 %collective-permute-done.17.near = bf16[2,2,2,32,128]{4,3,2,1,0:T(8,128)(2,1)S(1)} collective-permute-done((bf16[2,2,2,32,128]{4,3,2,1,0:T(8,128)(2,1)S(1)}, bf16[2,2,2,32,128]{4,3,2,1,0:T(8,128)(2,1)S(1)}, u32[]{:S(2)}, u32[]{:S(2)}) %collective-permute-start.17) | collective-permute-done | bytes 65568 | tf_op jit(solution)/shard_map/ppermute | solution.py:41
  98.1 1.1 collective-permute-start.18
  99.2 6.3 %collective-permute-done.18.far = bf16[2,2,2,32,128]{4,3,2,1,0:T(8,128)(2,1)S(1)} collective-permute-done((bf16[2,2,2,32,128]{4,3,2,1,0:T(8,128)(2,1)S(1)}, bf16[2,2,2,32,128]{4,3,2,1,0:T(8,128)(2,1)S(1)}, u32[]{:S(2)}, u32[]{:S(2)}) %collective-permute-start.18) | collective-permute-done | bytes 65568 | tf_op jit(solution)/shard_map/ppermute | solution.py:41
  105.5 0.6 shard_map.89
  106.1 0.7 copy.14
  106.8 1.6 %all-to-all-done.1 = bf16[32,64,128]{2,1,0:T(8,128)(2,1)S(1)} async-done(((bf16[32,64,128]{2,1,0:T(8,128)(2,1)}), bf16[32,64,128]{2,1,0:T(8,128)(2,1)S(1)}, u32[]{:S(2)}, u32[]{:S(2)}) %all-to-all-start.1) | async-done | bytes 524320 | tf_op jit(solution)/shard_map/all_to_all | solution.py:441
  108.3 1.0 shard_map.94
  (15 shorter events, 0.1 us)
Async XLA Ops:
  0.6 12.7 %copy-start.2 = (bf16[8,32,64]{2,1,0:T(8,128)(2,1)S(1)}, bf16[8,32,64]{2,1,0:T(8,128)(2,1)}, u32[]{:S(2)}) copy-start(bf16[8,32,64]{2,1,0:T(8,128)(2,1)} %s0.1) | copy-start | bytes 98308
  1.6 5.6 %collective-permute-start.4 = (bf16[4,2,2,32,128]{4,3,2,1,0:T(8,128)(2,1)S(1)}, bf16[4,2,2,32,128]{4,3,2,1,0:T(8,128)(2,1)S(1)}, u32[]{:S(2)}, u32[]{:S(2)}) collective-permute-start(bf16[4,2,2,32,128]{4,3,2,1,0:T(8,128)(2,1)S(1)} %bitcast.23), channel_id=1, source_target_pairs={{0,2},{1,3},{2,0},{3,1},{4,6},{5,7},{6,4},{7,5},{8,10},{9,11},{10,... | collective-permute-start | bytes 393224 | tf_op jit(solution)/shard_map/ppermute | solution.py:41
  3.7 9.6 %collective-permute-start.3 = (bf16[4,2,2,32,128]{4,3,2,1,0:T(8,128)(2,1)S(1)}, bf16[4,2,2,32,128]{4,3,2,1,0:T(8,128)(2,1)S(1)}, u32[]{:S(2)}, u32[]{:S(2)}) collective-permute-start(bf16[4,2,2,32,128]{4,3,2,1,0:T(8,128)(2,1)S(1)} %bitcast.24), channel_id=1, source_target_pairs={{0,1},{1,0},{2,3},{3,2},{4,5},{5,4},{6,7},{7,6},{8,9},{9,8},{10,11... | collective-permute-start | bytes 393224 | tf_op jit(solution)/shard_map/ppermute | solution.py:41
  7.2 6.1 %collective-permute-start.5 = (bf16[4,2,2,32,128]{4,3,2,1,0:T(8,128)(2,1)S(1)}, bf16[4,2,2,32,128]{4,3,2,1,0:T(8,128)(2,1)S(1)}, u32[]{:S(2)}, u32[]{:S(2)}) collective-permute-start(bf16[4,2,2,32,128]{4,3,2,1,0:T(8,128)(2,1)S(1)} %collective-permute-done.4.c2), channel_id=1, source_target_pairs={{0,1},{1,0},{2,3},{3,2},{4,5},{5,4},{6,7},{7,6},{8,9},{9,8},{10,11... | collective-permute-start | bytes 393224 | tf_op jit(solution)/shard_map/ppermute | solution.py:41
  7.2 4.7 %collective-permute-start.1 = (bf16[8,32,64]{2,1,0:T(8,128)(2,1)}, bf16[8,32,64]{2,1,0:T(8,128)(2,1)S(1)}, u32[]{:S(2)}, u32[]{:S(2)}) collective-permute-start(bf16[8,32,64]{2,1,0:T(8,128)(2,1)} %s0.1), channel_id=1, source_target_pairs={{0,2},{1,3},{2,0},{3,1},{4,6},{5,7},{6,4},{7,5},{8,10},{9,11},{10,... | collective-permute-start | bytes 98312 | tf_op jit(solution)/shard_map/ppermute | solution.py:41
  9.0 4.3 %collective-permute-start = (bf16[8,32,64]{2,1,0:T(8,128)(2,1)}, bf16[8,32,64]{2,1,0:T(8,128)(2,1)S(1)}, u32[]{:S(2)}, u32[]{:S(2)}) collective-permute-start(bf16[8,32,64]{2,1,0:T(8,128)(2,1)} %s0.1), channel_id=1, source_target_pairs={{0,1},{1,0},{2,3},{3,2},{4,5},{5,4},{6,7},{7,6},{8,9},{9,8},{10,11... | collective-permute-start | bytes 98312 | tf_op jit(solution)/shard_map/ppermute | solution.py:41
  11.9 1.4 %collective-permute-start.2 = (bf16[8,32,64]{2,1,0:T(8,128)(2,1)S(1)}, bf16[8,32,64]{2,1,0:T(8,128)(2,1)S(1)}, u32[]{:S(2)}, u32[]{:S(2)}) collective-permute-start(bf16[8,32,64]{2,1,0:T(8,128)(2,1)S(1)} %collective-permute-done.1.s2), channel_id=1, source_target_pairs={{0,1},{1,0},{2,3},{3,2},{4,5},{5,4},{6,7},{7,6},{8,9},{9,8},{10,11... | collective-permute-start | bytes 98312 | tf_op jit(solution)/shard_map/ppermute | solution.py:41
  11.9 8.2 %copy-start = (bf16[27,32,128]{2,1,0:T(8,128)(2,1)S(1)}, bf16[27,32,128]{2,1,0:T(8,128)(2,1)}, u32[]{:S(2)}) copy-start(bf16[27,32,128]{2,1,0:T(8,128)(2,1)} %m0.1) | copy-start | bytes 663556
  11.9 9.9 %copy-start.1 = (bf16[27,32,128]{2,1,0:T(8,128)(2,1)S(1)}, bf16[27,32,128]{2,1,0:T(8,128)(2,1)}, u32[]{:S(2)}) copy-start(bf16[27,32,128]{2,1,0:T(8,128)(2,1)} %l0.1) | copy-start | bytes 663556
  15.0 9.9 %collective-permute-start.7 = (bf16[2,512,128]{2,1,0:T(8,128)(2,1)S(1)}, bf16[2,512,128]{2,1,0:T(8,128)(2,1)S(1)}, u32[]{:S(2)}, u32[]{:S(2)}) collective-permute-start(bf16[2,512,128]{2,1,0:T(8,128)(2,1)S(1)} %get-tuple-element.29), channel_id=1, source_target_pairs={{4,8},{5,9},{6,10},{7,11},{8,4},{9,5},{10,6},{11,7},{12,16},{13,17... | collective-permute-start | bytes 786440 | tf_op jit(solution)/shard_map/ppermute | solution.py:41
  15.7 8.7 %collective-permute-start.6 = (bf16[2,256,128]{2,1,0:T(8,128)(2,1)S(1)}, bf16[2,256,128]{2,1,0:T(8,128)(2,1)S(1)}, u32[]{:S(2)}, u32[]{:S(2)}) collective-permute-start(bf16[2,256,128]{2,1,0:T(8,128)(2,1)S(1)} %get-tuple-element.28.own), channel_id=1, source_target_pairs={{0,4},{1,5},{2,6},{3,7},{4,0},{5,1},{6,2},{7,3},{8,12},{9,13},{10,... | collective-permute-start | bytes 393224 | tf_op jit(solution)/shard_map/ppermute | solution.py:41
  20.1 12.9 %collective-permute-start.12 = (bf16[27,32,128]{2,1,0:T(8,128)(2,1)S(1)}, bf16[27,32,128]{2,1,0:T(8,128)(2,1)S(1)}, u32[]{:S(2)}, u32[]{:S(2)}) collective-permute-start(bf16[27,32,128]{2,1,0:T(8,128)(2,1)S(1)} %copy-done), channel_id=1, source_target_pairs={{0,2},{1,3},{2,0},{3,1},{4,6},{5,7},{6,4},{7,5},{8,10},{9,11},{10,... | collective-permute-start | bytes 663560 | tf_op jit(solution)/shard_map/ppermute | solution.py:41
  21.9 12.3 %collective-permute-start.15 = (bf16[27,32,128]{2,1,0:T(8,128)(2,1)S(1)}, bf16[27,32,128]{2,1,0:T(8,128)(2,1)S(1)}, u32[]{:S(2)}, u32[]{:S(2)}) collective-permute-start(bf16[27,32,128]{2,1,0:T(8,128)(2,1)S(1)} %copy-done.1), channel_id=1, source_target_pairs={{0,18},{1,19},{2,16},{3,17},{4,22},{5,23},{6,20},{7,21},{8,26},{9,... | collective-permute-start | bytes 663560 | tf_op jit(solution)/shard_map/ppermute | solution.py:41
  24.4 9.8 %collective-permute-start.11 = (bf16[27,32,128]{2,1,0:T(8,128)(2,1)S(1)}, bf16[27,32,128]{2,1,0:T(8,128)(2,1)S(1)}, u32[]{:S(2)}, u32[]{:S(2)}) collective-permute-start(bf16[27,32,128]{2,1,0:T(8,128)(2,1)S(1)} %copy-done), channel_id=1, source_target_pairs={{0,1},{1,0},{2,3},{3,2},{4,5},{5,4},{6,7},{7,6},{8,9},{9,8},{10,11... | collective-permute-start | bytes 663560 | tf_op jit(solution)/shard_map/ppermute | solution.py:41
  24.4 9.8 %collective-permute-start.14 = (bf16[27,32,128]{2,1,0:T(8,128)(2,1)S(1)}, bf16[27,32,128]{2,1,0:T(8,128)(2,1)S(1)}, u32[]{:S(2)}, u32[]{:S(2)}) collective-permute-start(bf16[27,32,128]{2,1,0:T(8,128)(2,1)S(1)} %copy-done.1), channel_id=1, source_target_pairs={{0,1},{1,0},{2,3},{3,2},{4,5},{5,4},{6,7},{7,6},{8,9},{9,8},{10,11... | collective-permute-start | bytes 663560 | tf_op jit(solution)/shard_map/ppermute | solution.py:41
  25.6 20.2 %collective-permute-start.8 = (bf16[6,256,128]{2,1,0:T(8,128)(2,1)S(1)}, bf16[6,256,128]{2,1,0:T(8,128)(2,1)S(1)}, u32[]{:S(2)}, u32[]{:S(2)}) collective-permute-start(bf16[6,256,128]{2,1,0:T(8,128)(2,1)S(1)} %get-tuple-element.30), channel_id=1, source_target_pairs={{0,1},{1,0},{2,3},{3,2},{4,5},{5,4},{6,7},{7,6},{8,9},{9,8},{10,11... | collective-permute-start | bytes 1179656 | tf_op jit(solution)/shard_map/ppermute | solution.py:41
  33.0 8.4 %collective-permute-start.13 = (bf16[27,32,128]{2,1,0:T(8,128)(2,1)S(1)}, bf16[27,32,128]{2,1,0:T(8,128)(2,1)S(1)}, u32[]{:S(2)}, u32[]{:S(2)}) collective-permute-start(bf16[27,32,128]{2,1,0:T(8,128)(2,1)S(1)} %collective-permute-done.12.m2), channel_id=1, source_target_pairs={{0,1},{1,0},{2,3},{3,2},{4,5},{5,4},{6,7},{7,6},{8,9},{9,8},{10,11... | collective-permute-start | bytes 663560 | tf_op jit(solution)/shard_map/ppermute | solution.py:41
  34.2 9.6 %collective-permute-start.16 = (bf16[27,32,128]{2,1,0:T(8,128)(2,1)S(1)}, bf16[27,32,128]{2,1,0:T(8,128)(2,1)S(1)}, u32[]{:S(2)}, u32[]{:S(2)}) collective-permute-start(bf16[27,32,128]{2,1,0:T(8,128)(2,1)S(1)} %collective-permute-done.15.l2), channel_id=1, source_target_pairs={{0,1},{1,0},{2,3},{3,2},{4,5},{5,4},{6,7},{7,6},{8,9},{9,8},{10,11... | collective-permute-start | bytes 663560 | tf_op jit(solution)/shard_map/ppermute | solution.py:41
  34.2 5.9 %collective-permute-start.20 = (bf16[2,256,128]{2,1,0:T(8,128)(2,1)S(1)}, bf16[2,256,128]{2,1,0:T(8,128)(2,1)S(1)}, u32[]{:S(2)}, u32[]{:S(2)}) collective-permute-start(bf16[2,256,128]{2,1,0:T(8,128)(2,1)S(1)} %get-tuple-element.41.own), channel_id=1, source_target_pairs={{0,4},{1,5},{2,6},{3,7},{4,0},{5,1},{6,2},{7,3},{8,12},{9,13},{10,... | collective-permute-start | bytes 393224 | tf_op jit(solution)/shard_map/ppermute | solution.py:41
  34.3 11.5 %collective-permute-start.10 = (bf16[4,256,128]{2,1,0:T(8,128)(2,1)S(1)}, bf16[4,256,128]{2,1,0:T(8,128)(2,1)S(1)}, u32[]{:S(2)}, u32[]{:S(2)}) collective-permute-start(bf16[4,256,128]{2,1,0:T(8,128)(2,1)S(1)} %get-tuple-element.31), channel_id=1, source_target_pairs={{1,2},{2,1},{5,6},{6,5},{9,10},{10,9},{13,14},{14,13},{17,18},{18,... | collective-permute-start | bytes 786440 | tf_op jit(solution)/shard_map/ppermute | solution.py:41
  40.1 5.6 %collective-permute-start.9 = (bf16[2,256,128]{2,1,0:T(8,128)(2,1)S(1)}, bf16[2,256,128]{2,1,0:T(8,128)(2,1)S(1)}, u32[]{:S(2)}, u32[]{:S(2)}) collective-permute-start(bf16[2,256,128]{2,1,0:T(8,128)(2,1)S(1)} %get-tuple-element.28.own), channel_id=1, source_target_pairs={{1,2},{2,1},{5,6},{6,5},{9,10},{10,9},{13,14},{14,13},{17,18},{18,... | collective-permute-start | bytes 393224 | tf_op jit(solution)/shard_map/ppermute | solution.py:41
  41.4 11.4 %collective-permute-start.21 = (bf16[6,256,128]{2,1,0:T(8,128)(2,1)S(1)}, bf16[6,256,128]{2,1,0:T(8,128)(2,1)S(1)}, u32[]{:S(2)}, u32[]{:S(2)}) collective-permute-start(bf16[6,256,128]{2,1,0:T(8,128)(2,1)S(1)} %shard_map.91), channel_id=1, source_target_pairs={{0,1},{1,0},{2,3},{3,2},{4,5},{5,4},{6,7},{7,6},{8,9},{9,8},{10,11... | collective-permute-start | bytes 1179656 | tf_op jit(solution)/shard_map/ppermute | solution.py:41
  43.8 8.9 %collective-permute-start.22 = (bf16[6,256,128]{2,1,0:T(8,128)(2,1)S(1)}, bf16[6,256,128]{2,1,0:T(8,128)(2,1)S(1)}, u32[]{:S(2)}, u32[]{:S(2)}) collective-permute-start(bf16[6,256,128]{2,1,0:T(8,128)(2,1)S(1)} %shard_map.91), channel_id=1, source_target_pairs={{1,2},{2,1},{5,6},{6,5},{9,10},{10,9},{13,14},{14,13},{17,18},{18,... | collective-permute-start | bytes 1179656 | tf_op jit(solution)/shard_map/ppermute | solution.py:41
  51.0 8.1 %collective-permute-start.19 = (bf16[2,27,32,128]{3,2,1,0:T(8,128)(2,1)S(1)}, bf16[2,27,32,128]{3,2,1,0:T(8,128)(2,1)S(1)}, u32[]{:S(2)}, u32[]{:S(2)}) collective-permute-start(bf16[2,27,32,128]{3,2,1,0:T(8,128)(2,1)S(1)} %get-tuple-element.39), channel_id=1, source_target_pairs={{0,1},{1,0},{2,3},{3,2},{4,5},{5,4},{6,7},{7,6},{8,9},{9,8},{10,11... | collective-permute-start | bytes 1327112 | tf_op jit(solution)/shard_map/ppermute | solution.py:41
  58.9 2.1 %collective-permute-start.23 = (bf16[2,37,32,128]{3,2,1,0:T(8,128)(2,1)S(1)}, bf16[2,37,32,128]{3,2,1,0:T(8,128)(2,1)S(1)}, u32[]{:S(2)}, u32[]{:S(2)}) collective-permute-start(bf16[2,37,32,128]{3,2,1,0:T(8,128)(2,1)S(1)} %get-tuple-element.48), channel_id=1, source_target_pairs={{0,1},{1,0},{2,3},{3,2},{4,5},{5,4},{6,7},{7,6},{8,9},{9,8},{10,11... | collective-permute-start | bytes 1818632 | tf_op jit(solution)/shard_map/ppermute | solution.py:41
  90.5 17.8 %all-to-all-start.1 = ((bf16[32,64,128]{2,1,0:T(8,128)(2,1)}), bf16[32,64,128]{2,1,0:T(8,128)(2,1)S(1)}, u32[]{:S(2)}, u32[]{:S(2)}) async-start(bf16[32,64,128]{2,1,0:T(8,128)(2,1)} %shard_map.93), calls=%async_computation.1 | async-start | bytes 1048576 | tf_op jit(solution)/shard_map/all_to_all | solution.py:441
  96.8 1.3 %collective-permute-start.17 = (bf16[2,2,2,32,128]{4,3,2,1,0:T(8,128)(2,1)S(1)}, bf16[2,2,2,32,128]{4,3,2,1,0:T(8,128)(2,1)S(1)}, u32[]{:S(2)}, u32[]{:S(2)}) collective-permute-start(bf16[2,2,2,32,128]{4,3,2,1,0:T(8,128)(2,1)S(1)} %get-tuple-element.36), channel_id=1, source_target_pairs={{0,1},{1,0},{2,3},{3,2},{4,5},{5,4},{6,7},{7,6},{8,9},{9,8},{10,11... | collective-permute-start | bytes 196616 | tf_op jit(solution)/shard_map/ppermute | solution.py:41
  98.1 7.4 %collective-permute-start.18 = (bf16[2,2,2,32,128]{4,3,2,1,0:T(8,128)(2,1)S(1)}, bf16[2,2,2,32,128]{4,3,2,1,0:T(8,128)(2,1)S(1)}, u32[]{:S(2)}, u32[]{:S(2)}) collective-permute-start(bf16[2,2,2,32,128]{4,3,2,1,0:T(8,128)(2,1)S(1)} %pad_maximum_fusion.1), channel_id=1, source_target_pairs={{0,2},{1,3},{2,0},{3,1},{4,6},{5,7},{6,4},{7,5},{8,10},{9,11},{10,... | collective-permute-start | bytes 196616 | tf_op jit(solution)/shard_map/ppermute | solution.py:41
